TPU v7x, 256 devices: a whole 4x4x8 slice. The times are simulated.
256 devices in a mesh: pts: 16 (over z, core), row: 4 (over x), col: 4 (over y).
Axes of the slice: x: 4, y: 4, z: 8, core: 2. Of those that a mesh axis runs over, the one named last changes fastest.
Arguments:
- weights: bfloat16 [12, 32768, 256], P(None, ('pts', 'row', 'col')), as said below
- visibility: int32 [4, 32768], P(None, ('pts', 'row', 'col')), may hold values from 0 to 16, as said below
- inverses: bfloat16 [6, 32768], P(None, ('pts', 'row', 'col')), as said below
- grad_points: bfloat16 [3, 32768], P(None, ('pts', 'row', 'col')), may hold values from -6 to 6
- camera_blocks: float32 [4096, 256], P(('pts', 'row')), as said below
- grad_cams: float32 [4096], P(('pts', 'row')), may hold values from -6 to 6
Outputs:
- schur: float32 [4096, 4096], P(('pts', 'row'), 'col')
- reduced_rhs: float32 [4096], P(('pts', 'row'))
- solution: float32 [4096], P(('pts', 'row'))
Inputs may be any that keep to these rules, and one draw needn't show every extreme that they name: `weights`: entries of a slot whose visibility entry is 16 are arbitrary. `visibility`: column p lists the camera blocks point p sees: its first c entries are distinct blocks, with 1 <= c <= min(4, 16); the remaining entries are 16 and mark empty slots. `inverses`: rows 0 to 2 hold the diagonal of a symmetric positive definite 3 x 3 matrix, rows 3, 4, 5 its entries (0,1), (0,2), (1,2). `camera_blocks`: the 256 rows of block b hold a symmetric 256 x 256 matrix.
All inputs are finite; a program needn't handle non-finite values.
Results may differ from a plain program's by a relative error of at most 0.0048.
Values may be sent and summed in bfloat16 or wider, within the bound.
No kernel may reach another device: no remote copies, remote signals or barrier semaphores. Data moves between devices by JAX's collectives and lax.ppermute only.
A program may use at most 64 MiB of HBM per device.

v0:
```python
import math

import jax
import jax.numpy as jnp
from jax import lax
from jax.sharding import PartitionSpec as P

ITERS = 3


def apply_inverse(coefs, rows):
    target_shape = coefs.shape[1:] + (1,) * (rows.ndim - 2)
    entries = [coefs[entry].reshape(target_shape) for entry in range(6)]
    first = entries[0] * rows[0] + entries[3] * rows[1] + entries[4] * rows[2]
    second = entries[3] * rows[0] + entries[1] * rows[1] + entries[5] * rows[2]
    third = entries[4] * rows[0] + entries[5] * rows[1] + entries[2] * rows[2]
    return jnp.stack([first, second, third], 0)


def total_one(first, second, view):
    return lax.psum(jnp.sum(view(first) * view(second)), ("pts", "row"))


def run_minres(operate, view, rhs_vec):
    beta_first = jnp.sqrt(total_one(rhs_vec, rhs_vec, view))
    r_older = rhs_vec
    r_old = rhs_vec
    lanczos = rhs_vec
    beta_old = jnp.float32(0.0)
    beta_now = beta_first
    d_bar = jnp.float32(0.0)
    eps_now = jnp.float32(0.0)
    phi_bar = beta_first
    cos_now = jnp.float32(-1.0)
    sin_now = jnp.float32(0.0)
    w_now = jnp.zeros_like(rhs_vec)
    w_old = jnp.zeros_like(rhs_vec)
    answer = jnp.zeros_like(rhs_vec)
    for turn in range(ITERS):
        v_now = lanczos / beta_now
        lanczos = operate(v_now)
        if turn > 0:
            lanczos = lanczos - beta_now / beta_old * r_older
        alpha_now = total_one(v_now, lanczos, view)
        lanczos = lanczos - alpha_now / beta_now * r_old
        beta_old = beta_now
        beta_now = jnp.sqrt(total_one(lanczos, lanczos, view))
        r_older = r_old
        r_old = lanczos
        eps_old = eps_now
        delta_now = cos_now * d_bar + sin_now * alpha_now
        g_bar = sin_now * d_bar - cos_now * alpha_now
        eps_now = sin_now * beta_now
        d_bar = -cos_now * beta_now
        gamma_now = jnp.sqrt(g_bar * g_bar + beta_now * beta_now)
        cos_now = g_bar / gamma_now
        sin_now = beta_now / gamma_now
        phi_now = cos_now * phi_bar
        phi_bar = sin_now * phi_bar
        w_older = w_old
        w_old = w_now
        w_now = (v_now - eps_old * w_older - delta_now * w_old) / gamma_now
        answer = answer + phi_now * w_now
    return answer


def per_device(weights, visibility, inverses, grad_points, camera_blocks, grad_cams):
    n_row = lax.axis_size("row")
    n_col = lax.axis_size("col")
    blocks = lax.axis_size("pts")
    pts_idx = lax.axis_index("pts")
    row_idx = lax.axis_index("row")
    col_idx = lax.axis_index("col")
    width = weights.shape[2]
    slots = visibility.shape[0]
    per_dev = weights.shape[1]
    total = blocks * width
    strip = width // n_row
    set_rows = blocks * strip
    col_count = total // n_col
    col_blocks = max(1, col_count // width)
    first_block = col_idx * col_count // width
    shards = n_row * n_col
    contract = (((0, 1), (0, 1)), ((), ()))
    all_ids = jnp.arange(blocks, dtype=jnp.int32).astype(jnp.bfloat16)
    col_ids = (first_block + jnp.arange(col_blocks, dtype=jnp.int32)).astype(jnp.bfloat16)
    init = (
        jnp.zeros((set_rows, col_count), jnp.float32),
        jnp.zeros((shards, set_rows), jnp.float32),
    )
    vis_values = visibility.astype(jnp.bfloat16)
    w_all = lax.all_gather(weights, ("row", "col"), axis=1, tiled=True)
    vis_all = lax.all_gather(vis_values, ("row", "col"), axis=1, tiled=True)
    inv_all = lax.all_gather(inverses, ("row", "col"), axis=1, tiled=True)
    grad_all = lax.all_gather(grad_points, ("row", "col"), axis=1, tiled=True)
    n_points = w_all.shape[1]
    block_len = math.gcd(n_points, math.gcd(per_dev, 256))

    def one_block(index_blk, acc):
        tile_acc, parts_acc = acc
        offset_pts = index_blk * block_len
        w_blk = lax.dynamic_slice_in_dim(w_all, offset_pts, block_len, 1).reshape(
            slots, 3, block_len, width
        )
        vis_blk = lax.dynamic_slice_in_dim(vis_all, offset_pts, block_len, 1)
        inv_blk = lax.dynamic_slice_in_dim(inv_all, offset_pts, block_len, 1).astype(jnp.float32)
        grad_blk = lax.dynamic_slice_in_dim(grad_all, offset_pts, block_len, 1).astype(jnp.float32)
        mask_all = (vis_blk[:, :, None] == all_ids[None, None, :]).astype(jnp.bfloat16)
        w_rows = lax.dynamic_slice_in_dim(w_blk, row_idx * strip, strip, 3)
        row_terms = jnp.einsum(
            "kpb,kapi->apbi", mask_all, w_rows, preferred_element_type=jnp.float32
        )
        row_terms = row_terms.astype(jnp.bfloat16).reshape(3, block_len, set_rows)
        mask_col = (vis_blk[:, :, None] == col_ids[None, None, :]).astype(jnp.bfloat16)
        col_terms = jnp.einsum(
            "kpb,kapi->apbi", mask_col, w_blk, preferred_element_type=jnp.float32
        )
        col_terms = col_terms.reshape(3, block_len, col_count)
        scaled = apply_inverse(inv_blk, col_terms).astype(jnp.bfloat16)
        moved = apply_inverse(inv_blk, grad_blk).astype(jnp.bfloat16)
        tile_acc = tile_acc + lax.dot_general(
            row_terms, scaled, contract, preferred_element_type=jnp.float32
        )
        rhs_term = lax.dot_general(row_terms, moved, contract, preferred_element_type=jnp.float32)
        shard_slot = offset_pts // per_dev
        current = lax.dynamic_index_in_dim(parts_acc, shard_slot, 0, False)
        parts_acc = lax.dynamic_update_index_in_dim(parts_acc, current + rhs_term, shard_slot, 0)
        return (tile_acc, parts_acc)

    tile, parts = lax.fori_loop(0, n_points // block_len, one_block, init)
    reduced = jnp.sum(parts, axis=0)
    glob_cols = col_idx * col_count + jnp.arange(col_count, dtype=jnp.int32)
    inside = glob_cols // width == pts_idx
    local_cols = jnp.clip(glob_cols - pts_idx * width, 0, width - 1)
    placed = jnp.where(inside[None, :], jnp.take(camera_blocks, local_cols, axis=1), 0.0)
    row_start = pts_idx * strip
    own_tile = lax.dynamic_slice_in_dim(tile, row_start, strip, 0)
    term_tile = lax.dynamic_update_slice_in_dim(-tile, placed - own_tile, row_start, 0)
    own_rhs = lax.dynamic_slice_in_dim(reduced, row_start, strip, 0)
    term_rhs = lax.dynamic_update_slice_in_dim(-reduced, grad_cams - own_rhs, row_start, 0)
    schur_part, rhs_part = (
        lax.psum_scatter(term_tile, "pts", scatter_dimension=0, tiled=True),
        lax.psum_scatter(term_rhs, "pts", scatter_dimension=0, tiled=True),
    )

    def operate_strips(vector):
        gathered = lax.all_gather(vector, ("pts", "row"), axis=0, tiled=True)
        col_piece = lax.dynamic_slice_in_dim(gathered, col_idx * col_count, col_count, 0)
        local_part = jnp.dot(schur_part, col_piece, precision=lax.Precision.HIGHEST)
        return lax.psum(local_part, "col")

    def view_same(vector):
        return vector

    answer = run_minres(operate_strips, view_same, rhs_part)
    return (schur_part, rhs_part, answer)


def solution(mesh):
    return jax.shard_map(
        per_device,
        mesh=mesh,
        in_specs=(
            P(None, ("pts", "row", "col"), None),
            P(None, ("pts", "row", "col")),
            P(None, ("pts", "row", "col")),
            P(None, ("pts", "row", "col")),
            P(("pts", "row"), None),
            P(("pts", "row")),
        ),
        out_specs=(P(("pts", "row"), "col"), P(("pts", "row")), P(("pts", "row"))),
        check_vma=False,
    )
```

profile of v0, /device:TPU:2, one launch (start us, length us, event | category | flops | bytes accessed | tf_op | source)
XLA Modules:
  0.0 2022.5 jit_solution(15879753510746175105)
XLA Ops:
  13.7 23.3 %all_gather.24 = bf16[3,2048]{1,0:T(4,128)(2,1)S(1)} all-gather(bf16[3,128]{1,0:T(4,128)(2,1)} %param.11), channel_id=1, replica_groups=mesh['pts'=16,'row'=4,'col'=4] {'row','col'}, dimensions={1}, use_global_device_ids=true | all-gather | bytes 13056 | tf_op jit(solution)/shard_map/all_gather | solution.py:95
  37.0 21.1 %all_gather.22 = bf16[4,2048]{1,0:T(4,128)(2,1)S(1)} all-gather(bf16[4,128]{1,0:T(4,128)(2,1)S(1)} %convert_element_type.64), channel_id=1, replica_groups=mesh['pts'=16,'row'=4,'col'=4] {'row','col'}, dimensions={1}, use_global_device_ids=true | all-gather | bytes 17408 | tf_op jit(solution)/shard_map/all_gather | solution.py:93
  58.0 22.7 %all_gather.23 = bf16[6,2048]{1,0:T(8,128)(2,1)S(1)} all-gather(bf16[6,128]{1,0:T(8,128)(2,1)} %param.10), channel_id=1, replica_groups=mesh['pts'=16,'row'=4,'col'=4] {'row','col'}, dimensions={1}, use_global_device_ids=true | all-gather | bytes 26112 | tf_op jit(solution)/shard_map/all_gather | solution.py:94
  80.8 27.9 %all-gather.2.cloned.1.call-done = bf16[12,2048,256]{2,1,0:T(8,128)(2,1)} async-done(((bf16[12,128,256]{2,1,0:T(8,128)(2,1)}), bf16[12,2048,256]{2,1,0:T(8,128)(2,1)}) %all-gather.2.cloned.1.call-update) | async-done | bytes 12582928 | tf_op jit(solution)/shard_map/all_gather | solution.py:92
  108.6 200.1 %while.18 = (s32[]{:T(128)}, f32[1024,1024]{1,0:T(8,128)}, f32[16,1024]{1,0:T(8,128)S(1)}, bf16[12,2048,256]{2,1,0:T(8,128)(2,1)}, s32[]{:T(128)}, /*index=5*/bf...) while((s32[]{:T(128)}, f32[1024,1024]{1,0:T(8,128)}, ...), condition=%wide.region_1.2_spmd.clone, body=%wide.region_0.1_spmd.clone.sunk | while | flops 818057856 | bytes 27751116 | solution.py:130
  125.8 5.4 bitcast_add_fusion.2
  138.5 5.4 bitcast_add_fusion.2
  151.1 5.4 bitcast_add_fusion.2
  163.8 5.4 bitcast_add_fusion.2
  176.4 5.4 bitcast_add_fusion.2
  189.1 5.4 bitcast_add_fusion.2
  201.7 5.4 bitcast_add_fusion.2
  214.4 5.4 bitcast_add_fusion.2
  227.0 5.4 bitcast_add_fusion.2
  252.3 5.4 bitcast_add_fusion.2
  264.9 5.4 bitcast_add_fusion.2
  290.2 5.4 bitcast_add_fusion.2
  302.9 5.4 bitcast_add_fusion.2
  324.3 26.3 %all-reduce.3 = f32[1024]{0:T(1024)S(1)} all-reduce(f32[1024]{0:T(1024)S(1)} %subtract_dynamic-update-slice_fusion), channel_id=3, replica_groups=mesh['pts'=16,'row'=4,'col'=4] {'pts'}, use_global_device_ids=true, to_apply=%region_4.5.clone | all-reduce | flops 1024 | bytes 8192
  351.3 125.6 %psum.70 = f32[]{:T(128)} all-reduce(f32[]{:T(128)} %get-tuple-element.322), channel_id=1, replica_groups=mesh['pts'=16,'row'=4,'col'=4] {'pts','row'}, use_global_device_ids=true, to_apply=%region_6.7 | all-reduce | flops 1 | bytes 8 | tf_op jit(solution)/shard_map/psum | solution.py:21
  477.7 245.2 %all-reduce = f32[4096]{0:T(1024)S(1)} all-reduce(f32[4096]{0:T(1024)S(1)} %fusion.32), channel_id=1, replica_groups=mesh['pts'=16,'row'=4,'col'=4] {'pts','row'}, use_global_device_ids=true, to_apply=%add | all-reduce | flops 4096 | bytes 32768
  724.1 9.2 psum.71
  733.9 129.2 %psum.72 = f32[]{:T(128)} all-reduce(f32[]{:T(128)} %multiply_reduce_fusion.5), channel_id=1, replica_groups=mesh['pts'=16,'row'=4,'col'=4] {'pts','row'}, use_global_device_ids=true, to_apply=%region_9.10 | all-reduce | flops 1 | bytes 8 | tf_op jit(solution)/shard_map/psum | solution.py:21
  864.4 124.6 %psum.73 = f32[]{:T(128)} all-reduce(f32[]{:T(128)} %get-tuple-element.320), channel_id=1, replica_groups=mesh['pts'=16,'row'=4,'col'=4] {'pts','row'}, use_global_device_ids=true, to_apply=%region_11.12 | all-reduce | flops 1 | bytes 8 | tf_op jit(solution)/shard_map/psum | solution.py:21
  990.6 245.9 %all-reduce.1 = f32[4096]{0:T(1024)S(1)} all-reduce(f32[4096]{0:T(1024)S(1)} %fusion.33), channel_id=1, replica_groups=mesh['pts'=16,'row'=4,'col'=4] {'pts','row'}, use_global_device_ids=true, to_apply=%add.1 | all-reduce | flops 4096 | bytes 32768
  1237.7 7.8 psum.74
  1246.2 127.1 %psum.75 = f32[]{:T(128)} all-reduce(f32[]{:T(128)} %multiply_reduce_fusion.3), channel_id=1, replica_groups=mesh['pts'=16,'row'=4,'col'=4] {'pts','row'}, use_global_device_ids=true, to_apply=%region_14.15 | all-reduce | flops 1 | bytes 8 | tf_op jit(solution)/shard_map/psum | solution.py:21
  1376.0 124.6 %psum.76 = f32[]{:T(128)} all-reduce(f32[]{:T(128)} %get-tuple-element.318), channel_id=1, replica_groups=mesh['pts'=16,'row'=4,'col'=4] {'pts','row'}, use_global_device_ids=true, to_apply=%region_16.17 | all-reduce | flops 1 | bytes 8 | tf_op jit(solution)/shard_map/psum | solution.py:21
  1501.5 245.9 %all-reduce.2 = f32[4096]{0:T(1024)S(1)} all-reduce(f32[4096]{0:T(1024)S(1)} %get-tuple-element.316), channel_id=1, replica_groups=mesh['pts'=16,'row'=4,'col'=4] {'pts','row'}, use_global_device_ids=true, to_apply=%add.2 | all-reduce | flops 4096 | bytes 32768
  1748.6 9.8 psum.77
  1759.1 127.1 %psum.78 = f32[]{:T(128)} all-reduce(f32[]{:T(128)} %multiply_reduce_fusion.1), channel_id=1, replica_groups=mesh['pts'=16,'row'=4,'col'=4] {'pts','row'}, use_global_device_ids=true, to_apply=%region_19.20 | all-reduce | flops 1 | bytes 8 | tf_op jit(solution)/shard_map/psum | solution.py:21
  1889.0 124.6 %psum.79 = f32[]{:T(128)} all-reduce(f32[]{:T(128)} %multiply_reduce_fusion), channel_id=1, replica_groups=mesh['pts'=16,'row'=4,'col'=4] {'pts','row'}, use_global_device_ids=true, to_apply=%region_21.22 | all-reduce | flops 1 | bytes 8 | tf_op jit(solution)/shard_map/psum | solution.py:21
  (425 shorter events, 157.1 us)
Async XLA Ops:
  7.2 101.5 %all-gather.2.cloned.1.call-start = ((), (), s32[]{:S(2)}) async-start(), calls=%async_computation.1 | async-start | bytes 13369344 | tf_op jit(solution)/shard_map/all_gather | solution.py:92
  7.9 715.0 %reduce-scatter.2.cloned.1.call-start = ((), (), s32[]{:S(2)}) async-start(), calls=%async_computation.2 | async-start | bytes 4456448 | tf_op jit(solution)/shard_map/reduce_scatter | solution.py:142
  314.1 5.0 copy-start
  319.1 2.5 copy-start.4
  319.1 3.7 copy-start.3
  319.1 5.0 copy-start.2
  351.3 1664.3 %copy-start.1 = (f32[64]{0:T(128)}, f32[64]{0:T(128)S(1)}, u32[]{:S(2)}) copy-start(f32[64]{0:T(128)S(1)} %get-tuple-element.323) | copy-start | bytes 772
Sparse Core Ops, SparseCore 0:
  10.5 98.0 all-gather.1
  321.7 62.5 reduce-scatter.1
where the time goes:
time: 2020 us
  blocking collectives  1740 us (86%)
  matrix products  125 us (6%)
  local copies, waits for them, and re-layouts  81.3 us (4%)
  waiting for transfers between devices  28.6 us (1%)
  between operations  24.7 us (1%)
    psum x7, blocking collectives, total_one(): return lax.psum(jnp.sum(view(first) * view(second)), ('pts', 'row'))  883 us
    unnamed x4, blocking collectives  763 us
    dot_general x16, matrix products, one_block(): lax.dot_general(row_terms, scaled, contract, preferred_element_type=jnp.f...  84.3 us
  transfers between devices with their start and end apart: 2, of which 1 were waited for; matrix products, arithmetic and copies ran while one was open for 0% of the time, Pallas kernels for 0%

commit v1 on v0

v1 whole, which is shorter than its diff:
```python
import functools

import jax
import jax.numpy as jnp
from jax import lax
from jax.experimental import pallas as pl
from jax.experimental.pallas import tpu as pltpu
from jax.sharding import PartitionSpec as P

ITERS = 3
NT = (((1,), (1,)), ((), ()))
AUX = 16


def total(first, second):
    return jnp.sum(jnp.sum(first * second, axis=1, keepdims=True), axis=0, keepdims=True)


def minres(rhs_vec, products):
    beta_first = jnp.sqrt(total(rhs_vec, rhs_vec))
    r_older = rhs_vec
    r_old = rhs_vec
    lanczos = rhs_vec
    zero = jnp.zeros_like(beta_first)
    beta_old = zero
    beta_now = beta_first
    d_bar = zero
    eps_now = zero
    phi_bar = beta_first
    cos_now = zero - 1.0
    sin_now = zero
    w_now = jnp.zeros_like(rhs_vec)
    w_old = jnp.zeros_like(rhs_vec)
    answer = jnp.zeros_like(rhs_vec)
    for turn in range(ITERS):
        v_now = lanczos / beta_now
        if turn == len(products):
            return v_now
        lanczos = products[turn]
        if turn > 0:
            lanczos = lanczos - beta_now / beta_old * r_older
        alpha_now = total(v_now, lanczos)
        lanczos = lanczos - alpha_now / beta_now * r_old
        beta_old = beta_now
        beta_now = jnp.sqrt(total(lanczos, lanczos))
        r_older = r_old
        r_old = lanczos
        eps_old = eps_now
        delta_now = cos_now * d_bar + sin_now * alpha_now
        g_bar = sin_now * d_bar - cos_now * alpha_now
        eps_now = sin_now * beta_now
        d_bar = -cos_now * beta_now
        gamma_now = jnp.sqrt(g_bar * g_bar + beta_now * beta_now)
        cos_now = g_bar / gamma_now
        sin_now = beta_now / gamma_now
        phi_now = cos_now * phi_bar
        phi_bar = sin_now * phi_bar
        w_older = w_old
        w_old = w_now
        w_now = (v_now - eps_old * w_older - delta_now * w_old) / gamma_now
        answer = answer + phi_now * w_now
    return answer


def apply_inverse(inv, rows):
    return (
        inv[0] * rows[0] + inv[3] * rows[1] + inv[4] * rows[2],
        inv[3] * rows[0] + inv[1] * rows[1] + inv[5] * rows[2],
        inv[4] * rows[0] + inv[5] * rows[1] + inv[2] * rows[2],
    )


def slot_masks(vis, blocks):
    points = vis.shape[1]
    ids = lax.broadcasted_iota(jnp.int32, (blocks, points), 0)
    return [(vis[k : k + 1, :] == ids).astype(jnp.float32) for k in range(vis.shape[0])]


def prepare_kernel(slots, blocks, w_ref, vis_ref, inv_ref, grad_ref, cams_ref, send_ref, zw_ref, part_ref):
    points = vis_ref.shape[1]
    width = w_ref.shape[1]
    inv = inv_ref[...].astype(jnp.float32)
    inv_rows = [inv[e : e + 1, :] for e in range(6)]
    grad = grad_ref[...].astype(jnp.float32)
    vis = vis_ref[...]
    for k in range(slots):
        turned = []
        for a in range(3):
            at = 3 * k + a
            t = jnp.transpose(w_ref[at * points : (at + 1) * points, :].astype(jnp.float32))
            turned.append(t)
            send_ref[at * width : (at + 1) * width, :] = t.astype(jnp.bfloat16)
        for a, z in enumerate(apply_inverse(inv_rows, turned)):
            at = 3 * k + a
            zw_ref[:, at * points : (at + 1) * points] = z.astype(jnp.bfloat16)
    pad = jnp.zeros((AUX - slots - 6, points), jnp.float32)
    aux = jnp.concatenate([vis.astype(jnp.float32), inv, pad], axis=0)
    send_ref[3 * slots * width :, :] = aux.astype(jnp.bfloat16)
    masks = slot_masks(vis, blocks)
    moved = apply_inverse(inv_rows, [grad[a : a + 1, :] for a in range(3)])
    moved = [e.astype(jnp.bfloat16).astype(jnp.float32) for e in moved]
    lhs = jnp.concatenate([masks[k] * moved[a] for k in range(slots) for a in range(3)], axis=1)
    terms = jnp.dot(lhs.astype(jnp.bfloat16), w_ref[...], preferred_element_type=jnp.float32)
    part_ref[...] = cams_ref[...] - terms


def split(x):
    high = x.astype(jnp.bfloat16)
    low = (x - high.astype(jnp.float32)).astype(jnp.bfloat16)
    return high, low


def product_kernel(slots, blocks, n_known, *refs):
    place_ref, vis_ref, w_ref, zw_ref, cam_ref = refs[:5]
    known = refs[5 : 5 + n_known]
    out_ref = refs[5 + n_known]
    points = vis_ref.shape[1]
    v = minres(known[0][...], [r[...] for r in known[1:]])
    masks = slot_masks(vis_ref[...], blocks)
    v2 = jnp.concatenate(split(v), axis=0)
    dots = jnp.dot(v2, zw_ref[...], preferred_element_type=jnp.float32)
    dots = dots[:blocks] + dots[blocks:]
    t = []
    for a in range(3):
        s = None
        for k in range(slots):
            at = 3 * k + a
            term = masks[k] * dots[:, at * points : (at + 1) * points]
            s = term if s is None else s + term
        t.append(jnp.sum(s, axis=0, keepdims=True))
    lhs = jnp.concatenate([masks[k] * t[a] for k in range(slots) for a in range(3)], axis=1)
    lhs2 = jnp.concatenate(split(lhs), axis=0)
    terms = jnp.dot(lhs2, w_ref[...], preferred_element_type=jnp.float32)
    rows = lax.broadcasted_iota(jnp.int32, v.shape, 0)
    own = jnp.where(rows == place_ref[0], v, 0.0)
    cams = jnp.dot(own, cam_ref[...], precision=lax.Precision.HIGHEST, preferred_element_type=jnp.float32)
    out_ref[...] = cams - terms[:blocks] - terms[blocks:]


def answer_kernel(rhs_ref, s1_ref, s2_ref, s3_ref, out_ref):
    out_ref[...] = minres(rhs_ref[...], [s1_ref[...], s2_ref[...], s3_ref[...]])


def tile_kernel(slots, blocks, width, strip, place_ref, got_ref, cam_ref, out_ref, row_ref, col_ref):
    pts_idx, row_idx, col_idx = place_ref[0], place_ref[1], place_ref[2]
    sources, _, points = got_ref.shape
    col_blocks = out_ref.shape[1] // width

    @pl.when(pl.program_id(0) == 0)
    def _():
        out_ref[...] = jnp.zeros_like(out_ref)
        for c in range(col_blocks):

            @pl.when(col_idx * col_blocks + c == pts_idx)
            def _():
                start = pl.multiple_of(pts_idx * strip, strip)
                out_ref[pl.ds(start, strip), c * width : (c + 1) * width] = cam_ref[...]

    base_aux = 3 * slots * width
    for s in range(sources):
        aux = got_ref[s, base_aux : base_aux + AUX, :].astype(jnp.float32)
        vis = [aux[k : k + 1, :] for k in range(slots)]
        inv = [aux[slots + e : slots + e + 1, :] for e in range(6)]

        @pl.loop(0, col_blocks)
        def _(c):
            block = (col_idx * col_blocks + c).astype(jnp.float32)
            picks = [jnp.where(vis[k] == block, 1.0, 0.0).astype(jnp.bfloat16) for k in range(slots)]
            start = pl.multiple_of(c * width, width)
            for h in range(0, width, 64):
                rows = []
                for a in range(3):
                    y = None
                    for k in range(slots):
                        at = (3 * k + a) * width + h
                        term = picks[k] * got_ref[s, at : at + 64, :]
                        y = term if y is None else y + term
                    rows.append(y.astype(jnp.float32))
                for a, z in enumerate(apply_inverse(inv, rows)):
                    at = (a * sources + s) * points
                    col_ref[pl.ds(start + h, 64), at : at + points] = z.astype(jnp.bfloat16)

        @pl.loop(0, blocks)
        def _(b):
            block = b.astype(jnp.float32)
            picks = [jnp.where(vis[k] == block, -1.0, 0.0).astype(jnp.bfloat16) for k in range(slots)]
            start = pl.multiple_of(b * strip, strip)
            for a in range(3):
                y = None
                for k in range(slots):
                    at = pl.multiple_of((3 * k + a) * width + row_idx * strip, strip)
                    term = picks[k] * got_ref[s, pl.ds(at, strip), :]
                    y = term if y is None else y + term
                at = (a * sources + s) * points
                row_ref[pl.ds(start, strip), at : at + points] = y

    step = 256

    @pl.loop(0, out_ref.shape[0] // step)
    def _(m):
        start = pl.multiple_of(m * step, step)
        out_ref[pl.ds(start, step), :] += lax.dot_general(
            row_ref[pl.ds(start, step), :], col_ref[...], NT, preferred_element_type=jnp.float32
        )


def swap(value, axis, size, bit):
    return lax.ppermute(value, axis, [(i, i ^ bit) for i in range(size)])


def tree(values):
    while len(values) > 1:
        values = [values[i] + values[i + 1] for i in range(0, len(values), 2)]
    return values[0]


def all_sum(value, n_pts, n_row, n_col):
    value = value + swap(value, "pts", n_pts, 1)
    for axis, size, unit in (("row", n_row, 1), ("col", n_col, 1), ("pts", n_pts, 2)):
        value = tree([value] + [swap(value, axis, size, b) for b in range(unit, size, unit)])
    return value


def per_device(weights, visibility, inverses, grad_points, camera_blocks, grad_cams):
    n_row = lax.axis_size("row")
    n_col = lax.axis_size("col")
    blocks = lax.axis_size("pts")
    pts_idx = lax.axis_index("pts")
    row_idx = lax.axis_index("row")
    col_idx = lax.axis_index("col")
    slots, points = visibility.shape
    width = weights.shape[2]
    strip = width // n_row
    total_rows = blocks * width
    col_count = total_rows // n_col
    set_rows = blocks * strip
    shards = n_row * n_col
    send_rows = 3 * slots * width + AUX
    place = jnp.stack([pts_idx, row_idx, col_idx]).astype(jnp.int32)
    w_flat = weights.reshape(3 * slots * points, width)
    first_col = (col_idx == 0).astype(jnp.float32)
    lanes = jnp.arange(width, dtype=jnp.int32)[None, :]
    own_lanes = (lanes // strip == row_idx) & (jnp.arange(blocks, dtype=jnp.int32)[:, None] == pts_idx)
    cams_placed = jnp.where(own_lanes, jnp.tile(grad_cams, n_row)[None, :] * first_col, 0.0)
    cam_wide = lax.dynamic_update_slice(
        jnp.zeros((width, width), jnp.float32), camera_blocks * first_col, (row_idx * strip, 0)
    )
    vmem = pl.BlockSpec(memory_space=pltpu.VMEM)
    smem = pl.BlockSpec(memory_space=pltpu.SMEM)
    vec = jax.ShapeDtypeStruct((blocks, width), jnp.float32)

    send, zw, part = pl.pallas_call(
        functools.partial(prepare_kernel, slots, blocks),
        out_shape=(
            jax.ShapeDtypeStruct((send_rows, points), jnp.bfloat16),
            jax.ShapeDtypeStruct((width, 3 * slots * points), jnp.bfloat16),
            vec,
        ),
        in_specs=[vmem] * 5,
        out_specs=(vmem,) * 3,
        name="prepare",
    )(w_flat, visibility, inverses, grad_points, cams_placed)

    got = lax.all_gather(send, ("row", "col"), axis=0, tiled=False)

    def product(known):
        return pl.pallas_call(
            functools.partial(product_kernel, slots, blocks, len(known)),
            out_shape=vec,
            in_specs=[smem] + [vmem] * (4 + len(known)),
            out_specs=vmem,
            name="product",
        )(place, visibility, w_flat, zw, cam_wide, *known)

    def reduce_all(value):
        return all_sum(value, blocks, n_row, n_col)

    rhs = reduce_all(part)
    known = [rhs]
    known.append(reduce_all(product(known)))
    got, known = lax.optimization_barrier((got, known))

    pair = 2
    tile = pl.pallas_call(
        functools.partial(tile_kernel, slots, blocks, width, strip),
        out_shape=jax.ShapeDtypeStruct((set_rows, col_count), jnp.float32),
        grid=(shards // pair,),
        in_specs=[
            smem,
            pl.BlockSpec((pair, send_rows, points), lambda i: (i, 0, 0)),
            pl.BlockSpec((strip, width), lambda i: (0, 0)),
        ],
        out_specs=pl.BlockSpec((set_rows, col_count), lambda i: (0, 0)),
        scratch_shapes=[
            pltpu.VMEM((set_rows, 3 * pair * points), jnp.bfloat16),
            pltpu.VMEM((col_count, 3 * pair * points), jnp.bfloat16),
        ],
        compiler_params=pltpu.CompilerParams(
            dimension_semantics=("arbitrary",), vmem_limit_bytes=40 * 1024 * 1024
        ),
        cost_estimate=pl.CostEstimate(
            flops=2 * set_rows * col_count * 3 * shards * points,
            bytes_accessed=2 * shards * send_rows * points + 4 * set_rows * col_count,
            transcendentals=0,
        ),
        name="tile",
    )(place, got, camera_blocks)

    tile, known = lax.optimization_barrier((tile, known))
    schur = lax.psum_scatter(tile, "pts", scatter_dimension=0, tiled=True)
    for _ in range(1, ITERS):
        known.append(reduce_all(product(known)))
    answer = pl.pallas_call(answer_kernel, out_shape=vec, in_specs=[vmem] * 4, out_specs=vmem, name="answer")(*known)

    def own(value):
        return lax.dynamic_slice(value, (pts_idx, row_idx * strip), (1, strip)).reshape(strip)

    return (schur, own(rhs), own(answer))


def solution(mesh):
    return jax.shard_map(
        per_device,
        mesh=mesh,
        in_specs=(
            P(None, ("pts", "row", "col"), None),
            P(None, ("pts", "row", "col")),
            P(None, ("pts", "row", "col")),
            P(None, ("pts", "row", "col")),
            P(("pts", "row"), None),
            P(("pts", "row")),
        ),
        out_specs=(P(("pts", "row"), "col"), P(("pts", "row")), P(("pts", "row"))),
        check_vma=False,
    )
```

time: 2020 us -> 242 us (0.12)
  blocking collectives: 1740 us -> 0 us
  matrix products: 125 us -> 0 us
  starting transfers between devices: 0.08 us -> 92.8 us
  local copies, waits for them, and re-layouts: 81.3 us -> 6.06 us
  Pallas kernels: 0 us -> 50.5 us
  waiting for transfers between devices: 28.6 us -> 67.2 us
    psum x10 -> x0, blocking collectives: 909 us -> none  [the longest x7 883 us: total_one(): return lax.psum(jnp.sum(view(first) * view(second)), ('pts', 'row'))]
    unnamed x4 -> x0, blocking collectives: 763 us -> none
    dot_general x67 -> x0, matrix products: 125 us -> none  [the longest x16 84.3 us: one_block(): lax.dot_general(row_terms, scaled, contract, preferred_element_type=jnp.f...]
    ppermute x0 -> x56, starting transfers between devices: none -> 92.7 us  [swap(): return lax.ppermute(value, axis, [(i, i ^ bit) for i in range(size)])]
    all_gather x3 -> x0, blocking collectives: 67.1 us -> none  [the longest x1 23.3 us: per_device(): grad_all = lax.all_gather(grad_points, ('row', 'col'), axis=1, tiled=True)]
    pallas_call x0 -> x6, Pallas kernels: none -> 50.5 us  [the longest x1 36.9 us: per_device(): pl.pallas_call(functools.partial(tile_kernel, slots, blocks, width, strip...]
    ppermute x0 -> x56, waiting for transfers between devices: none -> 47.9 us  [swap(): return lax.ppermute(value, axis, [(i, i ^ bit) for i in range(size)])]
    dynamic_slice x67 -> x0, local copies, waits for them, and re-layouts: 21.6 us -> none  [the longest x16 19.1 us: one_block(): lax.dynamic_slice_in_dim(w_all, offset_pts, block_len, 1)]
  transfers between devices with their start and end apart: 2 -> 58, of which waited for: 1 -> 29; matrix products, arithmetic and copies ran while one was open for 0% -> 4% of each run, Pallas kernels for 0% -> 5%
where the time goes in v1:
time: 242 us; the launch traced here: 239 us
  starting transfers between devices  92.8 us (38%)
  waiting for transfers between devices  67.2 us (28%)
  Pallas kernels  50.5 us (21%)
  between operations  14.2 us (6%)
  other arithmetic  8.2 us (3%)
  local copies, waits for them, and re-layouts  6.06 us (3%)
    ppermute x56, starting transfers between devices, swap(): return lax.ppermute(value, axis, [(i, i ^ bit) for i in range(size)])  92.7 us
    ppermute x56, waiting for transfers between devices, swap(): return lax.ppermute(value, axis, [(i, i ^ bit) for i in range(size)])  47.9 us
    pallas_call x1, Pallas kernels, per_device(): pl.pallas_call(functools.partial(tile_kernel, slots, blocks, width, strip...  36.9 us
    all_gather x1, waiting for transfers between devices, per_device(): got = lax.all_gather(send, ('row', 'col'), axis=0, tiled=False)  19.2 us
    pallas_call x3, Pallas kernels, product(): pl.pallas_call(functools.partial(product_kernel, slots, blocks, len(known...  8.71 us
  transfers between devices with their start and end apart: 58, of which 29 were waited for; matrix products, arithmetic and copies ran while one was open for 4% of the time, Pallas kernels for 5%

profile of v1, /device:TPU:2, one launch (start us, length us, event | category | flops | bytes accessed | tf_op | source)
XLA Modules:
  0.0 239.0 jit_solution(6665305430342374912)
XLA Ops:
  8.7 2.8 %prepare.1 = (bf16[3088,128]{1,0:T(8,128)(2,1)}, bf16[256,1536]{1,0:T(8,128)(2,1)}, f32[16,256]{1,0:T(8,128)}) custom-call(bf16[1536,256]{1,0:T(8,128)(2,1)} %bitcast.9, s32[4,128]{1,0:T(4,128)} %refs_1_.5, bf16[6,128]{1,0:T(8,128)(2,1)} %inv_ref.1, bf16[3,128]{1,0:T(4,128)(2,1)} %grad_ref.1, f32[16,256]{1,0:T(8,128)} %and_select_fusion.cams_ref), custom_call_target="tpu_custom_call" | custom-call | tf_op jit(solution)/shard_map/prepare/pallas_call | solution.py:252
  17.8 3.5 %collective-permute-done.2 = f32[16,256]{1,0:T(8,128)S(1)} collective-permute-done((f32[16,256]{1,0:T(8,128)S(1)}, f32[16,256]{1,0:T(8,128)S(1)}, u32[]{:S(2)}, u32[]{:S(2)}) %collective-permute-start.2) | collective-permute-done | bytes 16416 | tf_op jit(solution)/shard_map/ppermute | solution.py:208
  22.2 2.9 %collective-permute-start.5 = (f32[16,256]{1,0:T(8,128)S(1)}, f32[16,256]{1,0:T(8,128)S(1)}, u32[]{:S(2)}, u32[]{:S(2)}) collective-permute-start(f32[16,256]{1,0:T(8,128)S(1)} %add_add_fusion.11), channel_id=1, source_target_pairs={{0,2},{1,3},{2,0},{3,1},{4,6},{5,7},{6,4},{7,5},{8,10},{9,11},{10,... | collective-permute-start | bytes 49160 | tf_op jit(solution)/shard_map/ppermute | solution.py:208
  27.4 2.6 %collective-permute-done.6 = f32[16,256]{1,0:T(8,128)S(1)} collective-permute-done((f32[16,256]{1,0:T(8,128)S(1)}, f32[16,256]{1,0:T(8,128)S(1)}, u32[]{:S(2)}, u32[]{:S(2)}) %collective-permute-start.6) | collective-permute-done | bytes 16416 | tf_op jit(solution)/shard_map/ppermute | solution.py:208
  30.0 7.3 %collective-permute-start.10 = (f32[16,256]{1,0:T(8,128)S(1)}, f32[16,256]{1,0:T(8,128)S(1)}, u32[]{:S(2)}, u32[]{:S(2)}) collective-permute-start(f32[16,256]{1,0:T(8,128)S(1)} %add_add_fusion.10), channel_id=1, source_target_pairs={{0,128},{16,144},{32,160},{48,176},{64,192},{80,208},{96,224},{112... | collective-permute-start | bytes 49160 | tf_op jit(solution)/shard_map/ppermute | solution.py:208
  38.2 4.7 %collective-permute-start.12 = (f32[16,256]{1,0:T(8,128)S(1)}, f32[16,256]{1,0:T(8,128)S(1)}, u32[]{:S(2)}, u32[]{:S(2)}) collective-permute-start(f32[16,256]{1,0:T(8,128)S(1)} %add_add_fusion.10), channel_id=1, source_target_pairs={{0,192},{16,208},{32,224},{48,240},{64,128},{80,144},{96,160},{112... | collective-permute-start | bytes 49160 | tf_op jit(solution)/shard_map/ppermute | solution.py:208
  51.6 2.7 %product.3 = f32[16,256]{1,0:T(8,128)} custom-call(s32[3]{0:T(128)} %pad_add_fusion.refs_0_.place_ref, s32[4,128]{1,0:T(4,128)} %refs_1_.5, bf16[1536,256]{1,0:T(8,128)(2,1)} %bitcast.10, bf16[256,1536]{1,0:T(8,128)(2,1)} %get-tuple-element.14.refs_3_, f32[256,256]{1,0:T(8,128)} %copy-done.3, f32[16,256]{1,0:T(8,128)} %add_add_fusion.9.refs_5_.rhs_ref), custom_call_target="tpu_custom_call" | custom-call | tf_op jit(solution)/shard_map/product/pallas_call | solution.py:267
  56.4 3.2 %collective-permute-start.15 = (f32[16,256]{1,0:T(8,128)S(1)}, f32[16,256]{1,0:T(8,128)S(1)}, u32[]{:S(2)}, u32[]{:S(2)}) collective-permute-start(f32[16,256]{1,0:T(8,128)S(1)} %add.200), channel_id=1, source_target_pairs={{0,4},{4,0},{8,12},{12,8},{1,5},{5,1},{9,13},{13,9},{2,6},{6,2},{1... | collective-permute-start | bytes 49160 | tf_op jit(solution)/shard_map/ppermute | solution.py:208
  61.7 3.5 %collective-permute-done.16 = f32[16,256]{1,0:T(8,128)S(1)} collective-permute-done((f32[16,256]{1,0:T(8,128)S(1)}, f32[16,256]{1,0:T(8,128)S(1)}, u32[]{:S(2)}, u32[]{:S(2)}) %collective-permute-start.16) | collective-permute-done | bytes 16416 | tf_op jit(solution)/shard_map/ppermute | solution.py:208
  66.9 3.2 %collective-permute-start.20 = (f32[16,256]{1,0:T(8,128)S(1)}, f32[16,256]{1,0:T(8,128)S(1)}, u32[]{:S(2)}, u32[]{:S(2)}) collective-permute-start(f32[16,256]{1,0:T(8,128)S(1)} %add_add_fusion.8), channel_id=1, source_target_pairs={{0,3},{1,2},{2,1},{3,0},{4,7},{5,6},{6,5},{7,4},{8,11},{9,10},{10,... | collective-permute-start | bytes 49160 | tf_op jit(solution)/shard_map/ppermute | solution.py:208
  72.2 2.6 %collective-permute-start.22 = (f32[16,256]{1,0:T(8,128)S(1)}, f32[16,256]{1,0:T(8,128)S(1)}, u32[]{:S(2)}, u32[]{:S(2)}) collective-permute-start(f32[16,256]{1,0:T(8,128)S(1)} %add_add_fusion.7), channel_id=1, source_target_pairs={{0,64},{16,80},{32,96},{48,112},{64,0},{80,16},{96,32},{112,48},{1... | collective-permute-start | bytes 49160 | tf_op jit(solution)/shard_map/ppermute | solution.py:208
  76.6 4.7 %collective-permute-start.24 = (f32[16,256]{1,0:T(8,128)S(1)}, f32[16,256]{1,0:T(8,128)S(1)}, u32[]{:S(2)}, u32[]{:S(2)}) collective-permute-start(f32[16,256]{1,0:T(8,128)S(1)} %add_add_fusion.7), channel_id=1, source_target_pairs={{0,128},{16,144},{32,160},{48,176},{64,192},{80,208},{96,224},{112... | collective-permute-start | bytes 49160 | tf_op jit(solution)/shard_map/ppermute | solution.py:208
  81.3 4.4 %collective-permute-start.26 = (f32[16,256]{1,0:T(8,128)S(1)}, f32[16,256]{1,0:T(8,128)S(1)}, u32[]{:S(2)}, u32[]{:S(2)}) collective-permute-start(f32[16,256]{1,0:T(8,128)S(1)} %add_add_fusion.7), channel_id=1, source_target_pairs={{0,192},{16,208},{32,224},{48,240},{64,128},{80,144},{96,160},{112... | collective-permute-start | bytes 49160 | tf_op jit(solution)/shard_map/ppermute | solution.py:208
  88.1 2.6 %collective-permute-done.27 = f32[16,256]{1,0:T(8,128)S(1)} collective-permute-done((f32[16,256]{1,0:T(8,128)S(1)}, f32[16,256]{1,0:T(8,128)S(1)}, u32[]{:S(2)}, u32[]{:S(2)}) %collective-permute-start.27) | collective-permute-done | bytes 16416 | tf_op jit(solution)/shard_map/ppermute | solution.py:208
  91.3 19.2 %all-gather.3.cloned.1.call-done = bf16[49408,128]{1,0:T(8,128)(2,1)} async-done(((bf16[3088,128]{1,0:T(8,128)(2,1)}), bf16[49408,128]{1,0:T(8,128)(2,1)}) %all-gather.3.cloned.1.call-update) | async-done | bytes 12648464 | tf_op jit(solution)/shard_map/all_gather | solution.py:264
  112.0 36.9 %tile.8 = f32[1024,1024]{1,0:T(8,128)S(1)} custom-call(s32[3]{0:T(128)S(1)} %copy-done.2, bf16[16,3088,128]{2,1,0:T(8,128)(2,1)} %bitcast.13, f32[64,256]{1,0:T(8,128)S(1)} %copy-done.1), custom_call_target="tpu_custom_call" | custom-call | flops 12884901888 | bytes 16842752 | tf_op jit(solution)/shard_map/tile/pallas_call | solution.py:284
  151.0 2.9 %product.4 = f32[16,256]{1,0:T(8,128)} custom-call(s32[3]{0:T(128)} %pad_add_fusion.refs_0_.place_ref, s32[4,128]{1,0:T(4,128)} %refs_1_.5, bf16[1536,256]{1,0:T(8,128)(2,1)} %bitcast.11, bf16[256,1536]{1,0:T(8,128)(2,1)} %get-tuple-element.14.refs_3_, f32[256,256]{1,0:T(8,128)} %copy-done.3, f32[16,256]{1,0:T(8,128)} %add_add_fusion.9.refs_5_.rhs_ref, ...), custom_call_target="tpu_custom_call" | custom-call | tf_op jit(solution)/shard_map/product/pallas_call | solution.py:267
  156.6 2.3 collective-permute-start.30
  163.4 2.7 %collective-permute-start.33 = (f32[16,256]{1,0:T(8,128)S(1)}, f32[16,256]{1,0:T(8,128)S(1)}, u32[]{:S(2)}, u32[]{:S(2)}) collective-permute-start(f32[16,256]{1,0:T(8,128)S(1)} %add_add_fusion.5), channel_id=1, source_target_pairs={{0,2},{1,3},{2,0},{3,1},{4,6},{5,7},{6,4},{7,5},{8,10},{9,11},{10,... | collective-permute-start | bytes 49160 | tf_op jit(solution)/shard_map/ppermute | solution.py:208
  168.6 2.4 %collective-permute-done.34 = f32[16,256]{1,0:T(8,128)S(1)} collective-permute-done((f32[16,256]{1,0:T(8,128)S(1)}, f32[16,256]{1,0:T(8,128)S(1)}, u32[]{:S(2)}, u32[]{:S(2)}) %collective-permute-start.34) | collective-permute-done | bytes 16416 | tf_op jit(solution)/shard_map/ppermute | solution.py:208
  172.7 2.5 %collective-permute-start.36 = (f32[16,256]{1,0:T(8,128)S(1)}, f32[16,256]{1,0:T(8,128)S(1)}, u32[]{:S(2)}, u32[]{:S(2)}) collective-permute-start(f32[16,256]{1,0:T(8,128)S(1)} %add_add_fusion.4), channel_id=1, source_target_pairs={{0,64},{16,80},{32,96},{48,112},{64,0},{80,16},{96,32},{112,48},{1... | collective-permute-start | bytes 49160 | tf_op jit(solution)/shard_map/ppermute | solution.py:208
  175.5 5.7 %collective-permute-start.38 = (f32[16,256]{1,0:T(8,128)S(1)}, f32[16,256]{1,0:T(8,128)S(1)}, u32[]{:S(2)}, u32[]{:S(2)}) collective-permute-start(f32[16,256]{1,0:T(8,128)S(1)} %add_add_fusion.4), channel_id=1, source_target_pairs={{0,128},{16,144},{32,160},{48,176},{64,192},{80,208},{96,224},{112... | collective-permute-start | bytes 49160 | tf_op jit(solution)/shard_map/ppermute | solution.py:208
  181.3 3.5 %collective-permute-start.40 = (f32[16,256]{1,0:T(8,128)S(1)}, f32[16,256]{1,0:T(8,128)S(1)}, u32[]{:S(2)}, u32[]{:S(2)}) collective-permute-start(f32[16,256]{1,0:T(8,128)S(1)} %add_add_fusion.4), channel_id=1, source_target_pairs={{0,192},{16,208},{32,224},{48,240},{64,128},{80,144},{96,160},{112... | collective-permute-start | bytes 49160 | tf_op jit(solution)/shard_map/ppermute | solution.py:208
  184.8 3.3 %collective-permute-done.39 = f32[16,256]{1,0:T(8,128)S(1)} collective-permute-done((f32[16,256]{1,0:T(8,128)S(1)}, f32[16,256]{1,0:T(8,128)S(1)}, u32[]{:S(2)}, u32[]{:S(2)}) %collective-permute-start.39) | collective-permute-done | bytes 16416 | tf_op jit(solution)/shard_map/ppermute | solution.py:208
  190.3 3.1 %product.5 = f32[16,256]{1,0:T(8,128)} custom-call(s32[3]{0:T(128)} %pad_add_fusion.refs_0_.place_ref, s32[4,128]{1,0:T(4,128)} %refs_1_.5, bf16[1536,256]{1,0:T(8,128)(2,1)} %bitcast.12, bf16[256,1536]{1,0:T(8,128)(2,1)} %get-tuple-element.14.refs_3_, f32[256,256]{1,0:T(8,128)} %copy-done.3, f32[16,256]{1,0:T(8,128)} %add_add_fusion.9.refs_5_.rhs_ref, ...), custom_call_target="tpu_custom_call" | custom-call | tf_op jit(solution)/shard_map/product/pallas_call | solution.py:267
  199.3 3.5 %collective-permute-done.44 = f32[16,256]{1,0:T(8,128)S(1)} collective-permute-done((f32[16,256]{1,0:T(8,128)S(1)}, f32[16,256]{1,0:T(8,128)S(1)}, u32[]{:S(2)}, u32[]{:S(2)}) %collective-permute-start.44) | collective-permute-done | bytes 16416 | tf_op jit(solution)/shard_map/ppermute | solution.py:208
  202.9 3.8 %collective-permute-start.47 = (f32[16,256]{1,0:T(8,128)S(1)}, f32[16,256]{1,0:T(8,128)S(1)}, u32[]{:S(2)}, u32[]{:S(2)}) collective-permute-start(f32[16,256]{1,0:T(8,128)S(1)} %add_add_fusion.2), channel_id=1, source_target_pairs={{0,2},{1,3},{2,0},{3,1},{4,6},{5,7},{6,4},{7,5},{8,10},{9,11},{10,... | collective-permute-start | bytes 49160 | tf_op jit(solution)/shard_map/ppermute | solution.py:208
  208.6 3.1 %collective-permute-done.48 = f32[16,256]{1,0:T(8,128)S(1)} collective-permute-done((f32[16,256]{1,0:T(8,128)S(1)}, f32[16,256]{1,0:T(8,128)S(1)}, u32[]{:S(2)}, u32[]{:S(2)}) %collective-permute-start.48) | collective-permute-done | bytes 16416 | tf_op jit(solution)/shard_map/ppermute | solution.py:208
  211.7 2.5 %collective-permute-start.49 = (f32[16,256]{1,0:T(8,128)S(1)}, f32[16,256]{1,0:T(8,128)S(1)}, u32[]{:S(2)}, u32[]{:S(2)}) collective-permute-start(f32[16,256]{1,0:T(8,128)S(1)} %add_add_fusion.1), channel_id=1, source_target_pairs={{0,32},{16,48},{32,0},{48,16},{64,96},{80,112},{96,64},{112,80},{1... | collective-permute-start | bytes 49160 | tf_op jit(solution)/shard_map/ppermute | solution.py:208
  216.6 2.6 %collective-permute-start.52 = (f32[16,256]{1,0:T(8,128)S(1)}, f32[16,256]{1,0:T(8,128)S(1)}, u32[]{:S(2)}, u32[]{:S(2)}) collective-permute-start(f32[16,256]{1,0:T(8,128)S(1)} %add_add_fusion.1), channel_id=1, source_target_pairs={{0,128},{16,144},{32,160},{48,176},{64,192},{80,208},{96,224},{112... | collective-permute-start | bytes 49160 | tf_op jit(solution)/shard_map/ppermute | solution.py:208
  219.2 2.9 %collective-permute-start.53 = (f32[16,256]{1,0:T(8,128)S(1)}, f32[16,256]{1,0:T(8,128)S(1)}, u32[]{:S(2)}, u32[]{:S(2)}) collective-permute-start(f32[16,256]{1,0:T(8,128)S(1)} %add_add_fusion.1), channel_id=1, source_target_pairs={{0,160},{16,176},{32,128},{48,144},{64,224},{80,240},{96,192},{112... | collective-permute-start | bytes 49160 | tf_op jit(solution)/shard_map/ppermute | solution.py:208
  223.3 2.5 %collective-permute-start.55 = (f32[16,256]{1,0:T(8,128)S(1)}, f32[16,256]{1,0:T(8,128)S(1)}, u32[]{:S(2)}, u32[]{:S(2)}) collective-permute-start(f32[16,256]{1,0:T(8,128)S(1)} %add_add_fusion.1), channel_id=1, source_target_pairs={{0,224},{16,240},{32,192},{48,208},{64,160},{80,176},{96,128},{112... | collective-permute-start | bytes 49160 | tf_op jit(solution)/shard_map/ppermute | solution.py:208
  (127 shorter events, 68.4 us)
Async XLA Ops:
  7.2 103.4 %all-gather.3.cloned.1.call-start = ((), (), s32[]{:S(2)}) async-start(), calls=%async_computation.2 | async-start | bytes 13438976 | tf_op jit(solution)/shard_map/all_gather | solution.py:264
  11.5 220.6 %reduce-scatter.2.cloned.1.call-start = ((), (), s32[]{:S(2)}) async-start(), calls=%async_computation.1 | async-start | bytes 4456448 | tf_op jit(solution)/shard_map/reduce_scatter | solution.py:310
  16.1 5.2 %collective-permute-start.2 = (f32[16,256]{1,0:T(8,128)S(1)}, f32[16,256]{1,0:T(8,128)S(1)}, u32[]{:S(2)}, u32[]{:S(2)}) collective-permute-start(f32[16,256]{1,0:T(8,128)S(1)} %add.185), channel_id=1, source_target_pairs={{0,8},{4,12},{8,0},{12,4},{1,9},{5,13},{9,1},{13,5},{2,10},{6,14},... | collective-permute-start | bytes 49160 | tf_op jit(solution)/shard_map/ppermute | solution.py:208
  22.2 5.2 %collective-permute-start.5 = (f32[16,256]{1,0:T(8,128)S(1)}, f32[16,256]{1,0:T(8,128)S(1)}, u32[]{:S(2)}, u32[]{:S(2)}) collective-permute-start(f32[16,256]{1,0:T(8,128)S(1)} %add_add_fusion.11), channel_id=1, source_target_pairs={{0,2},{1,3},{2,0},{3,1},{4,6},{5,7},{6,4},{7,5},{8,10},{9,11},{10,... | collective-permute-start | bytes 49160 | tf_op jit(solution)/shard_map/ppermute | solution.py:208
  30.0 14.4 %collective-permute-start.10 = (f32[16,256]{1,0:T(8,128)S(1)}, f32[16,256]{1,0:T(8,128)S(1)}, u32[]{:S(2)}, u32[]{:S(2)}) collective-permute-start(f32[16,256]{1,0:T(8,128)S(1)} %add_add_fusion.10), channel_id=1, source_target_pairs={{0,128},{16,144},{32,160},{48,176},{64,192},{80,208},{96,224},{112... | collective-permute-start | bytes 49160 | tf_op jit(solution)/shard_map/ppermute | solution.py:208
  37.3 8.1 %collective-permute-start.11 = (f32[16,256]{1,0:T(8,128)S(1)}, f32[16,256]{1,0:T(8,128)S(1)}, u32[]{:S(2)}, u32[]{:S(2)}) collective-permute-start(f32[16,256]{1,0:T(8,128)S(1)} %add_add_fusion.10), channel_id=1, source_target_pairs={{0,160},{16,176},{32,128},{48,144},{64,224},{80,240},{96,192},{112... | collective-permute-start | bytes 49160 | tf_op jit(solution)/shard_map/ppermute | solution.py:208
  38.2 9.7 %collective-permute-start.12 = (f32[16,256]{1,0:T(8,128)S(1)}, f32[16,256]{1,0:T(8,128)S(1)}, u32[]{:S(2)}, u32[]{:S(2)}) collective-permute-start(f32[16,256]{1,0:T(8,128)S(1)} %add_add_fusion.10), channel_id=1, source_target_pairs={{0,192},{16,208},{32,224},{48,240},{64,128},{80,144},{96,160},{112... | collective-permute-start | bytes 49160 | tf_op jit(solution)/shard_map/ppermute | solution.py:208
  45.4 5.5 %collective-permute-start.9 = (f32[16,256]{1,0:T(8,128)S(1)}, f32[16,256]{1,0:T(8,128)S(1)}, u32[]{:S(2)}, u32[]{:S(2)}) collective-permute-start(f32[16,256]{1,0:T(8,128)S(1)} %add_add_fusion.10), channel_id=1, source_target_pairs={{0,96},{16,112},{32,64},{48,80},{64,32},{80,48},{96,0},{112,16},{1... | collective-permute-start | bytes 49160 | tf_op jit(solution)/shard_map/ppermute | solution.py:208
  56.4 5.3 %collective-permute-start.15 = (f32[16,256]{1,0:T(8,128)S(1)}, f32[16,256]{1,0:T(8,128)S(1)}, u32[]{:S(2)}, u32[]{:S(2)}) collective-permute-start(f32[16,256]{1,0:T(8,128)S(1)} %add.200), channel_id=1, source_target_pairs={{0,4},{4,0},{8,12},{12,8},{1,5},{5,1},{9,13},{13,9},{2,6},{6,2},{1... | collective-permute-start | bytes 49160 | tf_op jit(solution)/shard_map/ppermute | solution.py:208
  59.6 5.6 %collective-permute-start.16 = (f32[16,256]{1,0:T(8,128)S(1)}, f32[16,256]{1,0:T(8,128)S(1)}, u32[]{:S(2)}, u32[]{:S(2)}) collective-permute-start(f32[16,256]{1,0:T(8,128)S(1)} %add.200), channel_id=1, source_target_pairs={{0,8},{4,12},{8,0},{12,4},{1,9},{5,13},{9,1},{13,5},{2,10},{6,14},... | collective-permute-start | bytes 49160 | tf_op jit(solution)/shard_map/ppermute | solution.py:208
  59.6 5.6 %collective-permute-start.17 = (f32[16,256]{1,0:T(8,128)S(1)}, f32[16,256]{1,0:T(8,128)S(1)}, u32[]{:S(2)}, u32[]{:S(2)}) collective-permute-start(f32[16,256]{1,0:T(8,128)S(1)} %add.200), channel_id=1, source_target_pairs={{0,12},{4,8},{8,4},{12,0},{1,13},{5,9},{9,5},{13,1},{2,14},{6,10},... | collective-permute-start | bytes 49160 | tf_op jit(solution)/shard_map/ppermute | solution.py:208
  65.3 5.8 %collective-permute-start.19 = (f32[16,256]{1,0:T(8,128)S(1)}, f32[16,256]{1,0:T(8,128)S(1)}, u32[]{:S(2)}, u32[]{:S(2)}) collective-permute-start(f32[16,256]{1,0:T(8,128)S(1)} %add_add_fusion.8), channel_id=1, source_target_pairs={{0,2},{1,3},{2,0},{3,1},{4,6},{5,7},{6,4},{7,5},{8,10},{9,11},{10,... | collective-permute-start | bytes 49160 | tf_op jit(solution)/shard_map/ppermute | solution.py:208
  66.9 5.3 %collective-permute-start.20 = (f32[16,256]{1,0:T(8,128)S(1)}, f32[16,256]{1,0:T(8,128)S(1)}, u32[]{:S(2)}, u32[]{:S(2)}) collective-permute-start(f32[16,256]{1,0:T(8,128)S(1)} %add_add_fusion.8), channel_id=1, source_target_pairs={{0,3},{1,2},{2,1},{3,0},{4,7},{5,6},{6,5},{7,4},{8,11},{9,10},{10,... | collective-permute-start | bytes 49160 | tf_op jit(solution)/shard_map/ppermute | solution.py:208
  72.1 9.2 %collective-permute-start.21 = (f32[16,256]{1,0:T(8,128)S(1)}, f32[16,256]{1,0:T(8,128)S(1)}, u32[]{:S(2)}, u32[]{:S(2)}) collective-permute-start(f32[16,256]{1,0:T(8,128)S(1)} %add_add_fusion.7), channel_id=1, source_target_pairs={{0,32},{16,48},{32,0},{48,16},{64,96},{80,112},{96,64},{112,80},{1... | collective-permute-start | bytes 49160 | tf_op jit(solution)/shard_map/ppermute | solution.py:208
  72.2 13.5 %collective-permute-start.22 = (f32[16,256]{1,0:T(8,128)S(1)}, f32[16,256]{1,0:T(8,128)S(1)}, u32[]{:S(2)}, u32[]{:S(2)}) collective-permute-start(f32[16,256]{1,0:T(8,128)S(1)} %add_add_fusion.7), channel_id=1, source_target_pairs={{0,64},{16,80},{32,96},{48,112},{64,0},{80,16},{96,32},{112,48},{1... | collective-permute-start | bytes 49160 | tf_op jit(solution)/shard_map/ppermute | solution.py:208
  74.8 11.0 %collective-permute-start.23 = (f32[16,256]{1,0:T(8,128)S(1)}, f32[16,256]{1,0:T(8,128)S(1)}, u32[]{:S(2)}, u32[]{:S(2)}) collective-permute-start(f32[16,256]{1,0:T(8,128)S(1)} %add_add_fusion.7), channel_id=1, source_target_pairs={{0,96},{16,112},{32,64},{48,80},{64,32},{80,48},{96,0},{112,16},{1... | collective-permute-start | bytes 49160 | tf_op jit(solution)/shard_map/ppermute | solution.py:208
  76.6 9.2 %collective-permute-start.24 = (f32[16,256]{1,0:T(8,128)S(1)}, f32[16,256]{1,0:T(8,128)S(1)}, u32[]{:S(2)}, u32[]{:S(2)}) collective-permute-start(f32[16,256]{1,0:T(8,128)S(1)} %add_add_fusion.7), channel_id=1, source_target_pairs={{0,128},{16,144},{32,160},{48,176},{64,192},{80,208},{96,224},{112... | collective-permute-start | bytes 49160 | tf_op jit(solution)/shard_map/ppermute | solution.py:208
  81.3 6.7 %collective-permute-start.25 = (f32[16,256]{1,0:T(8,128)S(1)}, f32[16,256]{1,0:T(8,128)S(1)}, u32[]{:S(2)}, u32[]{:S(2)}) collective-permute-start(f32[16,256]{1,0:T(8,128)S(1)} %add_add_fusion.7), channel_id=1, source_target_pairs={{0,160},{16,176},{32,128},{48,144},{64,224},{80,240},{96,192},{112... | collective-permute-start | bytes 49160 | tf_op jit(solution)/shard_map/ppermute | solution.py:208
  81.3 6.7 %collective-permute-start.26 = (f32[16,256]{1,0:T(8,128)S(1)}, f32[16,256]{1,0:T(8,128)S(1)}, u32[]{:S(2)}, u32[]{:S(2)}) collective-permute-start(f32[16,256]{1,0:T(8,128)S(1)} %add_add_fusion.7), channel_id=1, source_target_pairs={{0,192},{16,208},{32,224},{48,240},{64,128},{80,144},{96,160},{112... | collective-permute-start | bytes 49160 | tf_op jit(solution)/shard_map/ppermute | solution.py:208
  171.0 10.2 %collective-permute-start.35 = (f32[16,256]{1,0:T(8,128)S(1)}, f32[16,256]{1,0:T(8,128)S(1)}, u32[]{:S(2)}, u32[]{:S(2)}) collective-permute-start(f32[16,256]{1,0:T(8,128)S(1)} %add_add_fusion.4), channel_id=1, source_target_pairs={{0,32},{16,48},{32,0},{48,16},{64,96},{80,112},{96,64},{112,80},{1... | collective-permute-start | bytes 49160 | tf_op jit(solution)/shard_map/ppermute | solution.py:208
  172.7 12.1 %collective-permute-start.36 = (f32[16,256]{1,0:T(8,128)S(1)}, f32[16,256]{1,0:T(8,128)S(1)}, u32[]{:S(2)}, u32[]{:S(2)}) collective-permute-start(f32[16,256]{1,0:T(8,128)S(1)} %add_add_fusion.4), channel_id=1, source_target_pairs={{0,64},{16,80},{32,96},{48,112},{64,0},{80,16},{96,32},{112,48},{1... | collective-permute-start | bytes 49160 | tf_op jit(solution)/shard_map/ppermute | solution.py:208
  175.2 9.6 %collective-permute-start.37 = (f32[16,256]{1,0:T(8,128)S(1)}, f32[16,256]{1,0:T(8,128)S(1)}, u32[]{:S(2)}, u32[]{:S(2)}) collective-permute-start(f32[16,256]{1,0:T(8,128)S(1)} %add_add_fusion.4), channel_id=1, source_target_pairs={{0,96},{16,112},{32,64},{48,80},{64,32},{80,48},{96,0},{112,16},{1... | collective-permute-start | bytes 49160 | tf_op jit(solution)/shard_map/ppermute | solution.py:208
  175.5 9.3 %collective-permute-start.38 = (f32[16,256]{1,0:T(8,128)S(1)}, f32[16,256]{1,0:T(8,128)S(1)}, u32[]{:S(2)}, u32[]{:S(2)}) collective-permute-start(f32[16,256]{1,0:T(8,128)S(1)} %add_add_fusion.4), channel_id=1, source_target_pairs={{0,128},{16,144},{32,160},{48,176},{64,192},{80,208},{96,224},{112... | collective-permute-start | bytes 49160 | tf_op jit(solution)/shard_map/ppermute | solution.py:208
  181.2 6.8 %collective-permute-start.39 = (f32[16,256]{1,0:T(8,128)S(1)}, f32[16,256]{1,0:T(8,128)S(1)}, u32[]{:S(2)}, u32[]{:S(2)}) collective-permute-start(f32[16,256]{1,0:T(8,128)S(1)} %add_add_fusion.4), channel_id=1, source_target_pairs={{0,160},{16,176},{32,128},{48,144},{64,224},{80,240},{96,192},{112... | collective-permute-start | bytes 49160 | tf_op jit(solution)/shard_map/ppermute | solution.py:208
  181.3 6.8 %collective-permute-start.40 = (f32[16,256]{1,0:T(8,128)S(1)}, f32[16,256]{1,0:T(8,128)S(1)}, u32[]{:S(2)}, u32[]{:S(2)}) collective-permute-start(f32[16,256]{1,0:T(8,128)S(1)} %add_add_fusion.4), channel_id=1, source_target_pairs={{0,192},{16,208},{32,224},{48,240},{64,128},{80,144},{96,160},{112... | collective-permute-start | bytes 49160 | tf_op jit(solution)/shard_map/ppermute | solution.py:208
  202.9 5.6 %collective-permute-start.47 = (f32[16,256]{1,0:T(8,128)S(1)}, f32[16,256]{1,0:T(8,128)S(1)}, u32[]{:S(2)}, u32[]{:S(2)}) collective-permute-start(f32[16,256]{1,0:T(8,128)S(1)} %add_add_fusion.2), channel_id=1, source_target_pairs={{0,2},{1,3},{2,0},{3,1},{4,6},{5,7},{6,4},{7,5},{8,10},{9,11},{10,... | collective-permute-start | bytes 49160 | tf_op jit(solution)/shard_map/ppermute | solution.py:208
  211.7 10.5 %collective-permute-start.49 = (f32[16,256]{1,0:T(8,128)S(1)}, f32[16,256]{1,0:T(8,128)S(1)}, u32[]{:S(2)}, u32[]{:S(2)}) collective-permute-start(f32[16,256]{1,0:T(8,128)S(1)} %add_add_fusion.1), channel_id=1, source_target_pairs={{0,32},{16,48},{32,0},{48,16},{64,96},{80,112},{96,64},{112,80},{1... | collective-permute-start | bytes 49160 | tf_op jit(solution)/shard_map/ppermute | solution.py:208
  214.1 9.1 %collective-permute-start.50 = (f32[16,256]{1,0:T(8,128)S(1)}, f32[16,256]{1,0:T(8,128)S(1)}, u32[]{:S(2)}, u32[]{:S(2)}) collective-permute-start(f32[16,256]{1,0:T(8,128)S(1)} %add_add_fusion.1), channel_id=1, source_target_pairs={{0,64},{16,80},{32,96},{48,112},{64,0},{80,16},{96,32},{112,48},{1... | collective-permute-start | bytes 49160 | tf_op jit(solution)/shard_map/ppermute | solution.py:208
  215.3 11.7 %collective-permute-start.51 = (f32[16,256]{1,0:T(8,128)S(1)}, f32[16,256]{1,0:T(8,128)S(1)}, u32[]{:S(2)}, u32[]{:S(2)}) collective-permute-start(f32[16,256]{1,0:T(8,128)S(1)} %add_add_fusion.1), channel_id=1, source_target_pairs={{0,96},{16,112},{32,64},{48,80},{64,32},{80,48},{96,0},{112,16},{1... | collective-permute-start | bytes 49160 | tf_op jit(solution)/shard_map/ppermute | solution.py:208
  216.6 10.4 %collective-permute-start.52 = (f32[16,256]{1,0:T(8,128)S(1)}, f32[16,256]{1,0:T(8,128)S(1)}, u32[]{:S(2)}, u32[]{:S(2)}) collective-permute-start(f32[16,256]{1,0:T(8,128)S(1)} %add_add_fusion.1), channel_id=1, source_target_pairs={{0,128},{16,144},{32,160},{48,176},{64,192},{80,208},{96,224},{112... | collective-permute-start | bytes 49160 | tf_op jit(solution)/shard_map/ppermute | solution.py:208
  219.2 7.9 %collective-permute-start.53 = (f32[16,256]{1,0:T(8,128)S(1)}, f32[16,256]{1,0:T(8,128)S(1)}, u32[]{:S(2)}, u32[]{:S(2)}) collective-permute-start(f32[16,256]{1,0:T(8,128)S(1)} %add_add_fusion.1), channel_id=1, source_target_pairs={{0,160},{16,176},{32,128},{48,144},{64,224},{80,240},{96,192},{112... | collective-permute-start | bytes 49160 | tf_op jit(solution)/shard_map/ppermute | solution.py:208
  222.1 5.8 %collective-permute-start.54 = (f32[16,256]{1,0:T(8,128)S(1)}, f32[16,256]{1,0:T(8,128)S(1)}, u32[]{:S(2)}, u32[]{:S(2)}) collective-permute-start(f32[16,256]{1,0:T(8,128)S(1)} %add_add_fusion.1), channel_id=1, source_target_pairs={{0,192},{16,208},{32,224},{48,240},{64,128},{80,144},{96,160},{112... | collective-permute-start | bytes 49160 | tf_op jit(solution)/shard_map/ppermute | solution.py:208
  (30 other events, 125.6 us)
Sparse Core Ops, SparseCore 0:
  11.7 98.8 all-gather.2
  151.1 63.9 reduce-scatter.1

commit v2 on v1

--- a/solution.py
+++ b/solution.py
@@ -5,6 +5,7 @@
 from jax import lax
 from jax.experimental import pallas as pl
 from jax.experimental.pallas import tpu as pltpu
+from jax.sharding import Mesh
 from jax.sharding import PartitionSpec as P
 
 ITERS = 3
@@ -132,7 +133,7 @@
     lhs2 = jnp.concatenate(split(lhs), axis=0)
     terms = jnp.dot(lhs2, w_ref[...], preferred_element_type=jnp.float32)
     rows = lax.broadcasted_iota(jnp.int32, v.shape, 0)
-    own = jnp.where(rows == place_ref[0], v, 0.0)
+    own = jnp.where(rows == 2 * place_ref[0] + place_ref[1], v, 0.0)
     cams = jnp.dot(own, cam_ref[...], precision=lax.Precision.HIGHEST, preferred_element_type=jnp.float32)
     out_ref[...] = cams - terms[:blocks] - terms[blocks:]
 
@@ -141,71 +142,76 @@
     out_ref[...] = minres(rhs_ref[...], [s1_ref[...], s2_ref[...], s3_ref[...]])
 
 
-def tile_kernel(slots, blocks, width, strip, place_ref, got_ref, cam_ref, out_ref, row_ref, col_ref):
-    pts_idx, row_idx, col_idx = place_ref[0], place_ref[1], place_ref[2]
+def chosen(picks, terms):
+    value = None
+    for pick, term in zip(picks, terms):
+        part = pick * term
+        value = part if value is None else value + part
+    return value
+
+
+def tile_kernel(slots, blocks, width, strip, fine, place_ref, got_ref, cam_ref, own_ref, peer_ref, acc_ref, row_ref, col_ref):
+    z_idx, core_idx, row_idx, col_idx = place_ref[0], place_ref[1], place_ref[2], place_ref[3]
     sources, _, points = got_ref.shape
-    col_blocks = out_ref.shape[1] // width
+    half, col_count = own_ref.shape
+    col_blocks = col_count // width
+    base_aux = 3 * slots * width
 
     @pl.when(pl.program_id(0) == 0)
     def _():
-        out_ref[...] = jnp.zeros_like(out_ref)
+        own_ref[...] = jnp.zeros_like(own_ref)
+        acc_ref[...] = jnp.zeros_like(acc_ref)
         for c in range(col_blocks):
 
-            @pl.when(col_idx * col_blocks + c == pts_idx)
+            @pl.when(col_idx * col_blocks + c == 2 * z_idx + core_idx)
             def _():
-                start = pl.multiple_of(pts_idx * strip, strip)
-                out_ref[pl.ds(start, strip), c * width : (c + 1) * width] = cam_ref[...]
-
-    base_aux = 3 * slots * width
+                start = pl.multiple_of(z_idx * strip, strip)
+                own_ref[pl.ds(start, strip), c * width : (c + 1) * width] = cam_ref[...]
+
     for s in range(sources):
         aux = got_ref[s, base_aux : base_aux + AUX, :].astype(jnp.float32)
         vis = [aux[k : k + 1, :] for k in range(slots)]
         inv = [aux[slots + e : slots + e + 1, :] for e in range(6)]
 
-        @pl.loop(0, col_blocks)
-        def _(c):
-            block = (col_idx * col_blocks + c).astype(jnp.float32)
-            picks = [jnp.where(vis[k] == block, 1.0, 0.0).astype(jnp.bfloat16) for k in range(slots)]
-            start = pl.multiple_of(c * width, width)
-            for h in range(0, width, 64):
-                rows = []
-                for a in range(3):
-                    y = None
-                    for k in range(slots):
-                        at = (3 * k + a) * width + h
-                        term = picks[k] * got_ref[s, at : at + 64, :]
-                        y = term if y is None else y + term
-                    rows.append(y.astype(jnp.float32))
+        def picks_of(block, one):
+            block = block.astype(jnp.float32)
+            return [jnp.where(v == block, one, 0.0).astype(jnp.bfloat16) for v in vis]
+
+        col_picks = [picks_of(col_idx * col_blocks + c, 1.0) for c in range(col_blocks)]
+
+        @pl.loop(0, width // fine)
+        def _(h):
+            terms = []
+            for at in range(3 * slots):
+                start = pl.multiple_of(at * width + h * fine, fine)
+                terms.append(got_ref[s, pl.ds(start, fine), :])
+            for c in range(col_blocks):
+                rows = [chosen(col_picks[c], terms[a::3]).astype(jnp.float32) for a in range(3)]
+                start = pl.multiple_of(c * width + h * fine, fine)
                 for a, z in enumerate(apply_inverse(inv, rows)):
                     at = (a * sources + s) * points
-                    col_ref[pl.ds(start + h, 64), at : at + points] = z.astype(jnp.bfloat16)
-
-        @pl.loop(0, blocks)
-        def _(b):
-            block = b.astype(jnp.float32)
-            picks = [jnp.where(vis[k] == block, -1.0, 0.0).astype(jnp.bfloat16) for k in range(slots)]
-            start = pl.multiple_of(b * strip, strip)
-            for a in range(3):
-                y = None
-                for k in range(slots):
-                    at = pl.multiple_of((3 * k + a) * width + row_idx * strip, strip)
-                    term = picks[k] * got_ref[s, pl.ds(at, strip), :]
-                    y = term if y is None else y + term
-                at = (a * sources + s) * points
-                row_ref[pl.ds(start, strip), at : at + points] = y
-
-    step = 256
-
-    @pl.loop(0, out_ref.shape[0] // step)
-    def _(m):
-        start = pl.multiple_of(m * step, step)
-        out_ref[pl.ds(start, step), :] += lax.dot_general(
-            row_ref[pl.ds(start, step), :], col_ref[...], NT, preferred_element_type=jnp.float32
-        )
-
-
-def swap(value, axis, size, bit):
-    return lax.ppermute(value, axis, [(i, i ^ bit) for i in range(size)])
+                    col_ref[pl.ds(start, fine), at : at + points] = z.astype(jnp.bfloat16)
+
+        @pl.loop(0, strip // fine)
+        def _(h):
+            terms = []
+            for at in range(3 * slots):
+                start = pl.multiple_of(at * width + row_idx * strip + h * fine, fine)
+                terms.append(got_ref[s, pl.ds(start, fine), :])
+            for b in range(blocks):
+                other = b >= blocks // 2
+                picks = picks_of(2 * (b % (blocks // 2)) + (1 - core_idx if other else core_idx), -1.0)
+                start = pl.multiple_of(b * strip + h * fine, fine)
+                for a in range(3):
+                    at = (a * sources + s) * points
+                    row_ref[pl.ds(start, fine), at : at + points] = chosen(picks, terms[a::3])
+
+    acc_ref[...] += lax.dot_general(row_ref[half:, :], col_ref[...], NT, preferred_element_type=jnp.float32)
+    own_ref[...] += lax.dot_general(row_ref[:half, :], col_ref[...], NT, preferred_element_type=jnp.float32)
+
+    @pl.when(pl.program_id(0) == pl.num_programs(0) - 1)
+    def _():
+        peer_ref[...] = acc_ref[...].astype(jnp.bfloat16)
 
 
 def tree(values):
@@ -214,18 +220,29 @@
     return values[0]
 
 
-def all_sum(value, n_pts, n_row, n_col):
-    value = value + swap(value, "pts", n_pts, 1)
-    for axis, size, unit in (("row", n_row, 1), ("col", n_col, 1), ("pts", n_pts, 2)):
-        value = tree([value] + [swap(value, axis, size, b) for b in range(unit, size, unit)])
-    return value
+def core_sum(value):
+    return value + lax.ppermute(value, "core", [(0, 1), (1, 0)])
+
+
+def all_sum(value, n_z, n_row, n_col):
+    value = core_sum(value)
+    far = n_z // 2
+    pairs = [[(2 * z + c, 2 * (z ^ (j + c * far)) + c) for z in range(n_z) for c in range(2)] for j in range(far)]
+    value = tree([lax.ppermute(value, ("z", "core"), p) for p in pairs])
+    for axis, size in (("row", n_row), ("col", n_col)):
+        swaps = [lax.ppermute(value, axis, [(i, i ^ b) for i in range(size)]) for b in range(1, size)]
+        value = tree([value] + swaps)
+    return core_sum(value)
 
 
 def per_device(weights, visibility, inverses, grad_points, camera_blocks, grad_cams):
     n_row = lax.axis_size("row")
     n_col = lax.axis_size("col")
-    blocks = lax.axis_size("pts")
-    pts_idx = lax.axis_index("pts")
+    n_z = lax.axis_size("z")
+    blocks = 2 * n_z
+    z_idx = lax.axis_index("z")
+    core_idx = lax.axis_index("core")
+    pts_idx = 2 * z_idx + core_idx
     row_idx = lax.axis_index("row")
     col_idx = lax.axis_index("col")
     slots, points = visibility.shape
@@ -236,7 +253,7 @@
     set_rows = blocks * strip
     shards = n_row * n_col
     send_rows = 3 * slots * width + AUX
-    place = jnp.stack([pts_idx, row_idx, col_idx]).astype(jnp.int32)
+    place = jnp.stack([z_idx, core_idx, row_idx, col_idx]).astype(jnp.int32)
     w_flat = weights.reshape(3 * slots * points, width)
     first_col = (col_idx == 0).astype(jnp.float32)
     lanes = jnp.arange(width, dtype=jnp.int32)[None, :]
@@ -273,30 +290,39 @@
         )(place, visibility, w_flat, zw, cam_wide, *known)
 
     def reduce_all(value):
-        return all_sum(value, blocks, n_row, n_col)
+        return all_sum(value, n_z, n_row, n_col)
 
     rhs = reduce_all(part)
     known = [rhs]
-    known.append(reduce_all(product(known)))
+    for _ in range(1, ITERS):
+        known.append(reduce_all(product(known)))
     got, known = lax.optimization_barrier((got, known))
 
     pair = 2
-    tile = pl.pallas_call(
-        functools.partial(tile_kernel, slots, blocks, width, strip),
-        out_shape=jax.ShapeDtypeStruct((set_rows, col_count), jnp.float32),
+    half = set_rows // 2
+    own_half, peer_half = pl.pallas_call(
+        functools.partial(tile_kernel, slots, blocks, width, strip, 64),
+        out_shape=(
+            jax.ShapeDtypeStruct((half, col_count), jnp.float32),
+            jax.ShapeDtypeStruct((half, col_count), jnp.bfloat16),
+        ),
         grid=(shards // pair,),
         in_specs=[
             smem,
             pl.BlockSpec((pair, send_rows, points), lambda i: (i, 0, 0)),
             pl.BlockSpec((strip, width), lambda i: (0, 0)),
         ],
-        out_specs=pl.BlockSpec((set_rows, col_count), lambda i: (0, 0)),
+        out_specs=(
+            pl.BlockSpec((half, col_count), lambda i: (0, 0)),
+            pl.BlockSpec((half, col_count), lambda i: (0, 0)),
+        ),
         scratch_shapes=[
+            pltpu.VMEM((half, col_count), jnp.float32),
             pltpu.VMEM((set_rows, 3 * pair * points), jnp.bfloat16),
             pltpu.VMEM((col_count, 3 * pair * points), jnp.bfloat16),
         ],
         compiler_params=pltpu.CompilerParams(
-            dimension_semantics=("arbitrary",), vmem_limit_bytes=40 * 1024 * 1024
+            dimension_semantics=("arbitrary",), vmem_limit_bytes=56 * 1024 * 1024
         ),
         cost_estimate=pl.CostEstimate(
             flops=2 * set_rows * col_count * 3 * shards * points,
@@ -305,11 +331,11 @@
         ),
         name="tile",
     )(place, got, camera_blocks)
-
+    taken = lax.ppermute(peer_half, "core", [(0, 1), (1, 0)])
+    tile = own_half + taken.astype(jnp.float32)
     tile, known = lax.optimization_barrier((tile, known))
-    schur = lax.psum_scatter(tile, "pts", scatter_dimension=0, tiled=True)
-    for _ in range(1, ITERS):
-        known.append(reduce_all(product(known)))
+    schur = lax.psum_scatter(tile, "z", scatter_dimension=0, tiled=True)
+    known.append(reduce_all(product(known)))
     answer = pl.pallas_call(answer_kernel, out_shape=vec, in_specs=[vmem] * 4, out_specs=vmem, name="answer")(*known)
 
     def own(value):
@@ -319,17 +345,20 @@
 
 
 def solution(mesh):
+    n_pts, n_row, n_col = (mesh.shape[axis] for axis in ("pts", "row", "col"))
+    cores = Mesh(mesh.devices.reshape(n_pts // 2, 2, n_row, n_col), ("z", "core", "row", "col"))
+    pts = ("z", "core")
     return jax.shard_map(
         per_device,
-        mesh=mesh,
+        mesh=cores,
         in_specs=(
-            P(None, ("pts", "row", "col"), None),
-            P(None, ("pts", "row", "col")),
-            P(None, ("pts", "row", "col")),
-            P(None, ("pts", "row", "col")),
-            P(("pts", "row"), None),
-            P(("pts", "row")),
-        ),
-        out_specs=(P(("pts", "row"), "col"), P(("pts", "row")), P(("pts", "row"))),
+            P(None, (*pts, "row", "col"), None),
+            P(None, (*pts, "row", "col")),
+            P(None, (*pts, "row", "col")),
+            P(None, (*pts, "row", "col")),
+            P((*pts, "row"), None),
+            P((*pts, "row")),
+        ),
+        out_specs=(P((*pts, "row"), "col"), P((*pts, "row")), P((*pts, "row"))),
         check_vma=False,
     )

time: 242 us -> 201 us (0.83)
  starting transfers between devices: 92.8 us -> 70.1 us
  waiting for transfers between devices: 67.2 us -> 57.3 us
  Pallas kernels: 50.5 us -> 44.7 us
  local copies, waits for them, and re-layouts: 6.06 us -> 2.67 us
  other arithmetic: 8.2 us -> 10.8 us
    ppermute x56 -> x49, starting transfers between devices: 92.7 us -> 70.1 us  [the longest x24 35.5 us: all_sum(): lax.ppermute(value, axis, [(i, i ^ b) for i in range(size)])]
    all_gather x1, waiting for transfers between devices: 19.2 us -> 0.01 us  [per_device(): got = lax.all_gather(send, ('row', 'col'), axis=0, tiled=False)]
    ppermute x56 -> x49, waiting for transfers between devices: 47.9 us -> 54.9 us  [the longest x24 29.2 us: all_sum(): lax.ppermute(value, axis, [(i, i ^ b) for i in range(size)])]
    pallas_call x1, Pallas kernels: 36.9 us -> 31.1 us  [per_device(): pl.pallas_call(functools.partial(tile_kernel, slots, blocks, width, strip...]
    add x4 -> x9, other arithmetic: 2.9 us -> 8.71 us  [the longest x8 5.31 us: core_sum(): return value + lax.ppermute(value, 'core', [(0, 1), (1, 0)])]
    unnamed x8 -> x4, local copies, waits for them, and re-layouts: 3.44 us -> 0.01 us
  transfers between devices with their start and end apart: 58 -> 51, of which waited for: 29 -> 36; matrix products, arithmetic and copies ran while one was open for 4% -> 4% of each run, Pallas kernels for 5% -> 5%
where the time goes in v2:
time: 201 us; the launch traced here: 200 us
  starting transfers between devices  70.1 us (35%)
  waiting for transfers between devices  57.3 us (29%)
  Pallas kernels  44.7 us (22%)
  between operations  14.2 us (7%)
  other arithmetic  10.8 us (5%)
  local copies, waits for them, and re-layouts  2.67 us (1%)
    ppermute x24, starting transfers between devices, all_sum(): lax.ppermute(value, axis, [(i, i ^ b) for i in range(size)])  35.5 us
    pallas_call x1, Pallas kernels, per_device(): pl.pallas_call(functools.partial(tile_kernel, slots, blocks, width, strip...  31.1 us
    ppermute x24, waiting for transfers between devices, all_sum(): lax.ppermute(value, axis, [(i, i ^ b) for i in range(size)])  29.2 us
    ppermute x16, starting transfers between devices, all_sum(): value = tree([lax.ppermute(value, ('z', 'core'), p) for p in pairs])  25 us
    ppermute x16, waiting for transfers between devices, all_sum(): value = tree([lax.ppermute(value, ('z', 'core'), p) for p in pairs])  16.7 us
    ppermute x8, starting transfers between devices, core_sum(): return value + lax.ppermute(value, 'core', [(0, 1), (1, 0)])  9.17 us
    pallas_call x3, Pallas kernels, product(): pl.pallas_call(functools.partial(product_kernel, slots, blocks, len(known...  8.68 us
    ppermute x8, waiting for transfers between devices, core_sum(): return value + lax.ppermute(value, 'core', [(0, 1), (1, 0)])  6.46 us
  transfers between devices with their start and end apart: 51, of which 36 were waited for; matrix products, arithmetic and copies ran while one was open for 4% of the time, Pallas kernels for 5%

profile of v2, /device:TPU:2, one launch (start us, length us, event | category | flops | bytes accessed | tf_op | source)
XLA Modules:
  0.0 199.8 jit_solution(16155113455685888997)
XLA Ops:
  8.7 2.8 %prepare.1 = (bf16[3088,128]{1,0:T(8,128)(2,1)}, bf16[256,1536]{1,0:T(8,128)(2,1)}, f32[16,256]{1,0:T(8,128)}) custom-call(bf16[1536,256]{1,0:T(8,128)(2,1)} %bitcast.10, s32[4,128]{1,0:T(4,128)} %refs_1_.5, bf16[6,128]{1,0:T(8,128)(2,1)} %inv_ref.1, bf16[3,128]{1,0:T(4,128)(2,1)} %grad_ref.1, f32[16,256]{1,0:T(8,128)} %and_select_fusion.cams_ref), custom_call_target="tpu_custom_call" | custom-call | tf_op jit(solution)/shard_map/prepare/pallas_call | solution.py:269
  16.5 3.3 %collective-permute-start.3 = (f32[16,256]{1,0:T(8,128)S(1)}, f32[16,256]{1,0:T(8,128)S(1)}, u32[]{:S(2)}, u32[]{:S(2)}) collective-permute-start(f32[16,256]{1,0:T(8,128)S(1)} %add.156), channel_id=1, source_target_pairs={{0,64},{16,208},{32,96},{48,240},{64,0},{80,144},{96,32},{112,176}... | collective-permute-start | bytes 49160 | tf_op jit(solution)/shard_map/ppermute | solution.py:231
  21.5 3.8 %collective-permute-done.4 = f32[16,256]{1,0:T(8,128)S(1)} collective-permute-done((f32[16,256]{1,0:T(8,128)S(1)}, f32[16,256]{1,0:T(8,128)S(1)}, u32[]{:S(2)}, u32[]{:S(2)}) %collective-permute-start.4) | collective-permute-done | bytes 16416 | tf_op jit(solution)/shard_map/ppermute | solution.py:231
  25.9 2.4 %collective-permute-start.6 = (f32[16,256]{1,0:T(8,128)S(1)}, f32[16,256]{1,0:T(8,128)S(1)}, u32[]{:S(2)}, u32[]{:S(2)}) collective-permute-start(f32[16,256]{1,0:T(8,128)S(1)} %add_add_fusion.11), channel_id=1, source_target_pairs={{0,8},{4,12},{8,0},{12,4},{1,9},{5,13},{9,1},{13,5},{2,10},{6,14},... | collective-permute-start | bytes 49160 | tf_op jit(solution)/shard_map/ppermute | solution.py:233
  29.2 2.0 %collective-permute-done.6 = f32[16,256]{1,0:T(8,128)S(1)} collective-permute-done((f32[16,256]{1,0:T(8,128)S(1)}, f32[16,256]{1,0:T(8,128)S(1)}, u32[]{:S(2)}, u32[]{:S(2)}) %collective-permute-start.6) | collective-permute-done | bytes 16416 | tf_op jit(solution)/shard_map/ppermute | solution.py:233
  32.3 3.2 %collective-permute-start.10 = (f32[16,256]{1,0:T(8,128)S(1)}, f32[16,256]{1,0:T(8,128)S(1)}, u32[]{:S(2)}, u32[]{:S(2)}) collective-permute-start(f32[16,256]{1,0:T(8,128)S(1)} %add_add_fusion.10), channel_id=1, source_target_pairs={{0,3},{1,2},{2,1},{3,0},{4,7},{5,6},{6,5},{7,4},{8,11},{9,10},{10,... | collective-permute-start | bytes 49160 | tf_op jit(solution)/shard_map/ppermute | solution.py:233
  40.9 3.4 %collective-permute-start.11 = (f32[16,256]{1,0:T(8,128)S(1)}, f32[16,256]{1,0:T(8,128)S(1)}, u32[]{:S(2)}, u32[]{:S(2)}) collective-permute-start(f32[16,256]{1,0:T(8,128)S(1)} %add_add_fusion.9), channel_id=1, source_target_pairs={{0,16},{16,0},{1,17},{17,1},{2,18},{18,2},{3,19},{19,3},{4,20},{20... | collective-permute-start | bytes 49160 | tf_op jit(solution)/shard_map/ppermute | solution.py:224
  45.7 2.7 %product.3 = f32[16,256]{1,0:T(8,128)} custom-call(s32[4]{0:T(128)} %pad_add_fusion.refs_0_.place_ref, s32[4,128]{1,0:T(4,128)} %refs_1_.5, bf16[1536,256]{1,0:T(8,128)(2,1)} %bitcast.11, bf16[256,1536]{1,0:T(8,128)(2,1)} %get-tuple-element.18.refs_3_, f32[256,256]{1,0:T(8,128)} %copy-done, f32[16,256]{1,0:T(8,128)} %add.166.refs_5_.rhs_ref), custom_call_target="tpu_custom_call" | custom-call | tf_op jit(solution)/shard_map/product/pallas_call | solution.py:284
  51.2 2.5 %collective-permute-start.14 = (f32[16,256]{1,0:T(8,128)S(1)}, f32[16,256]{1,0:T(8,128)S(1)}, u32[]{:S(2)}, u32[]{:S(2)}) collective-permute-start(f32[16,256]{1,0:T(8,128)S(1)} %add.168), channel_id=1, source_target_pairs={{0,32},{16,176},{32,0},{48,144},{64,96},{80,240},{96,64},{112,208}... | collective-permute-start | bytes 49160 | tf_op jit(solution)/shard_map/ppermute | solution.py:231
  56.2 2.2 %collective-permute-done.15 = f32[16,256]{1,0:T(8,128)S(1)} collective-permute-done((f32[16,256]{1,0:T(8,128)S(1)}, f32[16,256]{1,0:T(8,128)S(1)}, u32[]{:S(2)}, u32[]{:S(2)}) %collective-permute-start.15) | collective-permute-done | bytes 16416 | tf_op jit(solution)/shard_map/ppermute | solution.py:231
  59.8 2.7 %collective-permute-start.17 = (f32[16,256]{1,0:T(8,128)S(1)}, f32[16,256]{1,0:T(8,128)S(1)}, u32[]{:S(2)}, u32[]{:S(2)}) collective-permute-start(f32[16,256]{1,0:T(8,128)S(1)} %add_add_fusion.8), channel_id=1, source_target_pairs={{0,4},{4,0},{8,12},{12,8},{1,5},{5,1},{9,13},{13,9},{2,6},{6,2},{1... | collective-permute-start | bytes 49160 | tf_op jit(solution)/shard_map/ppermute | solution.py:233
  64.6 3.7 %collective-permute-done.18 = f32[16,256]{1,0:T(8,128)S(1)} collective-permute-done((f32[16,256]{1,0:T(8,128)S(1)}, f32[16,256]{1,0:T(8,128)S(1)}, u32[]{:S(2)}, u32[]{:S(2)}) %collective-permute-start.18) | collective-permute-done | bytes 16416 | tf_op jit(solution)/shard_map/ppermute | solution.py:233
  73.0 2.5 %collective-permute-done.21 = f32[16,256]{1,0:T(8,128)S(1)} collective-permute-done((f32[16,256]{1,0:T(8,128)S(1)}, f32[16,256]{1,0:T(8,128)S(1)}, u32[]{:S(2)}, u32[]{:S(2)}) %collective-permute-start.21) | collective-permute-done | bytes 16416 | tf_op jit(solution)/shard_map/ppermute | solution.py:233
  79.6 2.9 %product.4 = f32[16,256]{1,0:T(8,128)} custom-call(s32[4]{0:T(128)} %pad_add_fusion.refs_0_.place_ref, s32[4,128]{1,0:T(4,128)} %refs_1_.5, bf16[1536,256]{1,0:T(8,128)(2,1)} %bitcast.12, bf16[256,1536]{1,0:T(8,128)(2,1)} %get-tuple-element.18.refs_3_, f32[256,256]{1,0:T(8,128)} %copy-done, f32[16,256]{1,0:T(8,128)} %add.166.refs_5_.rhs_ref, ...), custom_call_target="tpu_custom_call" | custom-call | tf_op jit(solution)/shard_map/product/pallas_call | solution.py:284
  85.3 2.7 %collective-permute-start.26 = (f32[16,256]{1,0:T(8,128)S(1)}, f32[16,256]{1,0:T(8,128)S(1)}, u32[]{:S(2)}, u32[]{:S(2)}) collective-permute-start(f32[16,256]{1,0:T(8,128)S(1)} %add.179), channel_id=1, source_target_pairs={{0,32},{16,176},{32,0},{48,144},{64,96},{80,240},{96,64},{112,208}... | collective-permute-start | bytes 49160 | tf_op jit(solution)/shard_map/ppermute | solution.py:231
  90.5 2.2 %collective-permute-done.27 = f32[16,256]{1,0:T(8,128)S(1)} collective-permute-done((f32[16,256]{1,0:T(8,128)S(1)}, f32[16,256]{1,0:T(8,128)S(1)}, u32[]{:S(2)}, u32[]{:S(2)}) %collective-permute-start.27) | collective-permute-done | bytes 16416 | tf_op jit(solution)/shard_map/ppermute | solution.py:231
  98.2 2.7 %collective-permute-done.30 = f32[16,256]{1,0:T(8,128)S(1)} collective-permute-done((f32[16,256]{1,0:T(8,128)S(1)}, f32[16,256]{1,0:T(8,128)S(1)}, u32[]{:S(2)}, u32[]{:S(2)}) %collective-permute-start.30) | collective-permute-done | bytes 16416 | tf_op jit(solution)/shard_map/ppermute | solution.py:233
  101.5 3.6 %collective-permute-start.33 = (f32[16,256]{1,0:T(8,128)S(1)}, f32[16,256]{1,0:T(8,128)S(1)}, u32[]{:S(2)}, u32[]{:S(2)}) collective-permute-start(f32[16,256]{1,0:T(8,128)S(1)} %add_add_fusion.4), channel_id=1, source_target_pairs={{0,2},{1,3},{2,0},{3,1},{4,6},{5,7},{6,4},{7,5},{8,10},{9,11},{10,... | collective-permute-start | bytes 49160 | tf_op jit(solution)/shard_map/ppermute | solution.py:233
  107.7 2.7 %collective-permute-done.34 = f32[16,256]{1,0:T(8,128)S(1)} collective-permute-done((f32[16,256]{1,0:T(8,128)S(1)}, f32[16,256]{1,0:T(8,128)S(1)}, u32[]{:S(2)}, u32[]{:S(2)}) %collective-permute-start.34) | collective-permute-done | bytes 16416 | tf_op jit(solution)/shard_map/ppermute | solution.py:233
  113.2 31.1 %tile.8 = (f32[512,1024]{1,0:T(8,128)}, bf16[512,1024]{1,0:T(8,128)(2,1)}) custom-call(s32[4]{0:T(128)} %pad_add_fusion.refs_0_.place_ref, bf16[16,3088,128]{2,1,0:T(8,128)(2,1)} %bitcast.14, f32[64,256]{1,0:T(8,128)} %cam_ref.1), custom_call_target="tpu_custom_call" | custom-call | flops 12884901888 | bytes 16842752 | tf_op jit(solution)/shard_map/tile/pallas_call | solution.py:303
  144.7 2.5 %collective-permute-done.36 = bf16[512,1024]{1,0:T(8,128)(2,1)S(1)} collective-permute-done((bf16[512,1024]{1,0:T(8,128)(2,1)}, bf16[512,1024]{1,0:T(8,128)(2,1)S(1)}, u32[]{:S(2)}, u32[]{:S(2)}) %collective-permute-start.36) | collective-permute-done | bytes 1048608 | tf_op jit(solution)/shard_map/ppermute | solution.py:334
  147.2 3.4 %convert_add_fusion = f32[512,1024]{1,0:T(8,128)} fusion(f32[512,1024]{1,0:T(8,128)} %get-tuple-element.20, bf16[512,1024]{1,0:T(8,128)(2,1)S(1)} %collective-permute-done.36), kind=kLoop, calls=%fused_computation | loop fusion | flops 1048576 | bytes 5242880 | tf_op jit(solution)/shard_map/add | solution.py:335
  150.6 3.1 %product.5 = f32[16,256]{1,0:T(8,128)} custom-call(s32[4]{0:T(128)} %pad_add_fusion.refs_0_.place_ref, s32[4,128]{1,0:T(4,128)} %refs_1_.5, bf16[1536,256]{1,0:T(8,128)(2,1)} %bitcast.13, bf16[256,1536]{1,0:T(8,128)(2,1)} %get-tuple-element.18.refs_3_, f32[256,256]{1,0:T(8,128)} %copy-done, f32[16,256]{1,0:T(8,128)} %add.166.refs_5_.rhs_ref, ...), custom_call_target="tpu_custom_call" | custom-call | tf_op jit(solution)/shard_map/product/pallas_call | solution.py:284
  156.5 4.6 %collective-permute-start.39 = (f32[16,256]{1,0:T(8,128)S(1)}, f32[16,256]{1,0:T(8,128)S(1)}, u32[]{:S(2)}, u32[]{:S(2)}) collective-permute-start(f32[16,256]{1,0:T(8,128)S(1)} %add.192), channel_id=1, source_target_pairs={{0,32},{16,176},{32,0},{48,144},{64,96},{80,240},{96,64},{112,208}... | collective-permute-start | bytes 49160 | tf_op jit(solution)/shard_map/ppermute | solution.py:231
  163.6 2.5 %collective-permute-done.40 = f32[16,256]{1,0:T(8,128)S(1)} collective-permute-done((f32[16,256]{1,0:T(8,128)S(1)}, f32[16,256]{1,0:T(8,128)S(1)}, u32[]{:S(2)}, u32[]{:S(2)}) %collective-permute-start.40) | collective-permute-done | bytes 16416 | tf_op jit(solution)/shard_map/ppermute | solution.py:231
  167.5 3.3 %collective-permute-start.42 = (f32[16,256]{1,0:T(8,128)S(1)}, f32[16,256]{1,0:T(8,128)S(1)}, u32[]{:S(2)}, u32[]{:S(2)}) collective-permute-start(f32[16,256]{1,0:T(8,128)S(1)} %add_add_fusion.2), channel_id=1, source_target_pairs={{0,4},{4,0},{8,12},{12,8},{1,5},{5,1},{9,13},{13,9},{2,6},{6,2},{1... | collective-permute-start | bytes 49160 | tf_op jit(solution)/shard_map/ppermute | solution.py:233
  172.5 3.5 %collective-permute-done.43 = f32[16,256]{1,0:T(8,128)S(1)} collective-permute-done((f32[16,256]{1,0:T(8,128)S(1)}, f32[16,256]{1,0:T(8,128)S(1)}, u32[]{:S(2)}, u32[]{:S(2)}) %collective-permute-start.43) | collective-permute-done | bytes 16416 | tf_op jit(solution)/shard_map/ppermute | solution.py:233
  176.2 2.6 %collective-permute-start.46 = (f32[16,256]{1,0:T(8,128)S(1)}, f32[16,256]{1,0:T(8,128)S(1)}, u32[]{:S(2)}, u32[]{:S(2)}) collective-permute-start(f32[16,256]{1,0:T(8,128)S(1)} %add_add_fusion.1), channel_id=1, source_target_pairs={{0,2},{1,3},{2,0},{3,1},{4,6},{5,7},{6,4},{7,5},{8,10},{9,11},{10,... | collective-permute-start | bytes 49160 | tf_op jit(solution)/shard_map/ppermute | solution.py:233
  178.7 2.1 %collective-permute-start.47 = (f32[16,256]{1,0:T(8,128)S(1)}, f32[16,256]{1,0:T(8,128)S(1)}, u32[]{:S(2)}, u32[]{:S(2)}) collective-permute-start(f32[16,256]{1,0:T(8,128)S(1)} %add_add_fusion.1), channel_id=1, source_target_pairs={{0,3},{1,2},{2,1},{3,0},{4,7},{5,6},{6,5},{7,4},{8,11},{9,10},{10,... | collective-permute-start | bytes 49160 | tf_op jit(solution)/shard_map/ppermute | solution.py:233
  181.5 2.3 %collective-permute-done.47 = f32[16,256]{1,0:T(8,128)S(1)} collective-permute-done((f32[16,256]{1,0:T(8,128)S(1)}, f32[16,256]{1,0:T(8,128)S(1)}, u32[]{:S(2)}, u32[]{:S(2)}) %collective-permute-start.47) | collective-permute-done | bytes 16416 | tf_op jit(solution)/shard_map/ppermute | solution.py:233
  187.2 2.1 %answer.1 = f32[16,256]{1,0:T(8,128)} custom-call(f32[16,256]{1,0:T(8,128)} %add.166.refs_5_.rhs_ref, f32[16,256]{1,0:T(8,128)} %add.178.refs_6_.s1_ref, f32[16,256]{1,0:T(8,128)} %add.189.refs_7_.s2_ref, f32[16,256]{1,0:T(8,128)} %add.202.s3_ref), custom_call_target="tpu_custom_call" | custom-call | tf_op jit(solution)/shard_map/answer/pallas_call | solution.py:339
  190.5 2.4 %reduce-scatter.2.cloned.1.call-done = f32[64,1024]{1,0:T(8,128)} async-done(((f32[512,1024]{1,0:T(8,128)}), f32[64,1024]{1,0:T(8,128)}) %reduce-scatter.2.cloned.1.call-update) | async-done | bytes 262160 | tf_op jit(solution)/shard_map/reduce_scatter | solution.py:337
  (114 shorter events, 66.2 us)
Async XLA Ops:
  7.2 106.0 %all-gather.3.cloned.1.call-start = ((), (), s32[]{:S(2)}) async-start(), calls=%async_computation.2 | async-start | bytes 13438976 | tf_op jit(solution)/shard_map/all_gather | solution.py:281
  11.6 181.4 %reduce-scatter.2.cloned.1.call-start = ((), (), s32[]{:S(2)}) async-start(), calls=%async_computation.1 | async-start | bytes 2359296 | tf_op jit(solution)/shard_map/reduce_scatter | solution.py:337
  13.8 5.9 %collective-permute-start.1 = (f32[16,256]{1,0:T(8,128)S(1)}, f32[16,256]{1,0:T(8,128)S(1)}, u32[]{:S(2)}, u32[]{:S(2)}) collective-permute-start(f32[16,256]{1,0:T(8,128)S(1)} %add.156), channel_id=1, source_target_pairs={{0,0},{16,144},{32,32},{48,176},{64,64},{80,208},{96,96},{112,240}... | collective-permute-start | bytes 49160 | tf_op jit(solution)/shard_map/ppermute | solution.py:231
  14.5 5.3 %collective-permute-start.2 = (f32[16,256]{1,0:T(8,128)S(1)}, f32[16,256]{1,0:T(8,128)S(1)}, u32[]{:S(2)}, u32[]{:S(2)}) collective-permute-start(f32[16,256]{1,0:T(8,128)S(1)} %add.156), channel_id=1, source_target_pairs={{0,32},{16,176},{32,0},{48,144},{64,96},{80,240},{96,64},{112,208}... | collective-permute-start | bytes 49160 | tf_op jit(solution)/shard_map/ppermute | solution.py:231
  16.5 5.0 %collective-permute-start.3 = (f32[16,256]{1,0:T(8,128)S(1)}, f32[16,256]{1,0:T(8,128)S(1)}, u32[]{:S(2)}, u32[]{:S(2)}) collective-permute-start(f32[16,256]{1,0:T(8,128)S(1)} %add.156), channel_id=1, source_target_pairs={{0,64},{16,208},{32,96},{48,240},{64,0},{80,144},{96,32},{112,176}... | collective-permute-start | bytes 49160 | tf_op jit(solution)/shard_map/ppermute | solution.py:231
  19.7 5.5 %collective-permute-start.4 = (f32[16,256]{1,0:T(8,128)S(1)}, f32[16,256]{1,0:T(8,128)S(1)}, u32[]{:S(2)}, u32[]{:S(2)}) collective-permute-start(f32[16,256]{1,0:T(8,128)S(1)} %add.156), channel_id=1, source_target_pairs={{0,96},{16,240},{32,64},{48,208},{64,32},{80,176},{96,0},{112,144}... | collective-permute-start | bytes 49160 | tf_op jit(solution)/shard_map/ppermute | solution.py:231
  25.9 5.4 %collective-permute-start.6 = (f32[16,256]{1,0:T(8,128)S(1)}, f32[16,256]{1,0:T(8,128)S(1)}, u32[]{:S(2)}, u32[]{:S(2)}) collective-permute-start(f32[16,256]{1,0:T(8,128)S(1)} %add_add_fusion.11), channel_id=1, source_target_pairs={{0,8},{4,12},{8,0},{12,4},{1,9},{5,13},{9,1},{13,5},{2,10},{6,14},... | collective-permute-start | bytes 49160 | tf_op jit(solution)/shard_map/ppermute | solution.py:233
  32.3 5.1 %collective-permute-start.10 = (f32[16,256]{1,0:T(8,128)S(1)}, f32[16,256]{1,0:T(8,128)S(1)}, u32[]{:S(2)}, u32[]{:S(2)}) collective-permute-start(f32[16,256]{1,0:T(8,128)S(1)} %add_add_fusion.10), channel_id=1, source_target_pairs={{0,3},{1,2},{2,1},{3,0},{4,7},{5,6},{6,5},{7,4},{8,11},{9,10},{10,... | collective-permute-start | bytes 49160 | tf_op jit(solution)/shard_map/ppermute | solution.py:233
  35.6 5.4 %collective-permute-start.9 = (f32[16,256]{1,0:T(8,128)S(1)}, f32[16,256]{1,0:T(8,128)S(1)}, u32[]{:S(2)}, u32[]{:S(2)}) collective-permute-start(f32[16,256]{1,0:T(8,128)S(1)} %add_add_fusion.10), channel_id=1, source_target_pairs={{0,2},{1,3},{2,0},{3,1},{4,6},{5,7},{6,4},{7,5},{8,10},{9,11},{10,... | collective-permute-start | bytes 49160 | tf_op jit(solution)/shard_map/ppermute | solution.py:233
  50.6 5.6 %collective-permute-start.13 = (f32[16,256]{1,0:T(8,128)S(1)}, f32[16,256]{1,0:T(8,128)S(1)}, u32[]{:S(2)}, u32[]{:S(2)}) collective-permute-start(f32[16,256]{1,0:T(8,128)S(1)} %add.168), channel_id=1, source_target_pairs={{0,0},{16,144},{32,32},{48,176},{64,64},{80,208},{96,96},{112,240}... | collective-permute-start | bytes 49160 | tf_op jit(solution)/shard_map/ppermute | solution.py:231
  51.2 5.0 %collective-permute-start.14 = (f32[16,256]{1,0:T(8,128)S(1)}, f32[16,256]{1,0:T(8,128)S(1)}, u32[]{:S(2)}, u32[]{:S(2)}) collective-permute-start(f32[16,256]{1,0:T(8,128)S(1)} %add.168), channel_id=1, source_target_pairs={{0,32},{16,176},{32,0},{48,144},{64,96},{80,240},{96,64},{112,208}... | collective-permute-start | bytes 49160 | tf_op jit(solution)/shard_map/ppermute | solution.py:231
  54.3 5.5 %collective-permute-start.16 = (f32[16,256]{1,0:T(8,128)S(1)}, f32[16,256]{1,0:T(8,128)S(1)}, u32[]{:S(2)}, u32[]{:S(2)}) collective-permute-start(f32[16,256]{1,0:T(8,128)S(1)} %add.168), channel_id=1, source_target_pairs={{0,96},{16,240},{32,64},{48,208},{64,32},{80,176},{96,0},{112,144}... | collective-permute-start | bytes 49160 | tf_op jit(solution)/shard_map/ppermute | solution.py:231
  62.5 5.7 %collective-permute-start.18 = (f32[16,256]{1,0:T(8,128)S(1)}, f32[16,256]{1,0:T(8,128)S(1)}, u32[]{:S(2)}, u32[]{:S(2)}) collective-permute-start(f32[16,256]{1,0:T(8,128)S(1)} %add_add_fusion.8), channel_id=1, source_target_pairs={{0,8},{4,12},{8,0},{12,4},{1,9},{5,13},{9,1},{13,5},{2,10},{6,14},... | collective-permute-start | bytes 49160 | tf_op jit(solution)/shard_map/ppermute | solution.py:233
  62.6 5.7 %collective-permute-start.19 = (f32[16,256]{1,0:T(8,128)S(1)}, f32[16,256]{1,0:T(8,128)S(1)}, u32[]{:S(2)}, u32[]{:S(2)}) collective-permute-start(f32[16,256]{1,0:T(8,128)S(1)} %add_add_fusion.8), channel_id=1, source_target_pairs={{0,12},{4,8},{8,4},{12,0},{1,13},{5,9},{9,5},{13,1},{2,14},{6,10},... | collective-permute-start | bytes 49160 | tf_op jit(solution)/shard_map/ppermute | solution.py:233
  68.2 4.8 %collective-permute-start.20 = (f32[16,256]{1,0:T(8,128)S(1)}, f32[16,256]{1,0:T(8,128)S(1)}, u32[]{:S(2)}, u32[]{:S(2)}) collective-permute-start(f32[16,256]{1,0:T(8,128)S(1)} %add_add_fusion.7), channel_id=1, source_target_pairs={{0,1},{1,0},{2,3},{3,2},{4,5},{5,4},{6,7},{7,6},{8,9},{9,8},{10,11... | collective-permute-start | bytes 49160 | tf_op jit(solution)/shard_map/ppermute | solution.py:233
  69.9 5.6 %collective-permute-start.21 = (f32[16,256]{1,0:T(8,128)S(1)}, f32[16,256]{1,0:T(8,128)S(1)}, u32[]{:S(2)}, u32[]{:S(2)}) collective-permute-start(f32[16,256]{1,0:T(8,128)S(1)} %add_add_fusion.7), channel_id=1, source_target_pairs={{0,2},{1,3},{2,0},{3,1},{4,6},{5,7},{6,4},{7,5},{8,10},{9,11},{10,... | collective-permute-start | bytes 49160 | tf_op jit(solution)/shard_map/ppermute | solution.py:233
  71.1 5.3 %collective-permute-start.22 = (f32[16,256]{1,0:T(8,128)S(1)}, f32[16,256]{1,0:T(8,128)S(1)}, u32[]{:S(2)}, u32[]{:S(2)}) collective-permute-start(f32[16,256]{1,0:T(8,128)S(1)} %add_add_fusion.7), channel_id=1, source_target_pairs={{0,3},{1,2},{2,1},{3,0},{4,7},{5,6},{6,5},{7,4},{8,11},{9,10},{10,... | collective-permute-start | bytes 49160 | tf_op jit(solution)/shard_map/ppermute | solution.py:233
  84.7 5.8 %collective-permute-start.25 = (f32[16,256]{1,0:T(8,128)S(1)}, f32[16,256]{1,0:T(8,128)S(1)}, u32[]{:S(2)}, u32[]{:S(2)}) collective-permute-start(f32[16,256]{1,0:T(8,128)S(1)} %add.179), channel_id=1, source_target_pairs={{0,0},{16,144},{32,32},{48,176},{64,64},{80,208},{96,96},{112,240}... | collective-permute-start | bytes 49160 | tf_op jit(solution)/shard_map/ppermute | solution.py:231
  85.3 5.1 %collective-permute-start.26 = (f32[16,256]{1,0:T(8,128)S(1)}, f32[16,256]{1,0:T(8,128)S(1)}, u32[]{:S(2)}, u32[]{:S(2)}) collective-permute-start(f32[16,256]{1,0:T(8,128)S(1)} %add.179), channel_id=1, source_target_pairs={{0,32},{16,176},{32,0},{48,144},{64,96},{80,240},{96,64},{112,208}... | collective-permute-start | bytes 49160 | tf_op jit(solution)/shard_map/ppermute | solution.py:231
  88.5 5.5 %collective-permute-start.28 = (f32[16,256]{1,0:T(8,128)S(1)}, f32[16,256]{1,0:T(8,128)S(1)}, u32[]{:S(2)}, u32[]{:S(2)}) collective-permute-start(f32[16,256]{1,0:T(8,128)S(1)} %add.179), channel_id=1, source_target_pairs={{0,96},{16,240},{32,64},{48,208},{64,32},{80,176},{96,0},{112,144}... | collective-permute-start | bytes 49160 | tf_op jit(solution)/shard_map/ppermute | solution.py:231
  95.3 5.6 %collective-permute-start.30 = (f32[16,256]{1,0:T(8,128)S(1)}, f32[16,256]{1,0:T(8,128)S(1)}, u32[]{:S(2)}, u32[]{:S(2)}) collective-permute-start(f32[16,256]{1,0:T(8,128)S(1)} %add_add_fusion.5), channel_id=1, source_target_pairs={{0,8},{4,12},{8,0},{12,4},{1,9},{5,13},{9,1},{13,5},{2,10},{6,14},... | collective-permute-start | bytes 49160 | tf_op jit(solution)/shard_map/ppermute | solution.py:233
  101.5 6.1 %collective-permute-start.33 = (f32[16,256]{1,0:T(8,128)S(1)}, f32[16,256]{1,0:T(8,128)S(1)}, u32[]{:S(2)}, u32[]{:S(2)}) collective-permute-start(f32[16,256]{1,0:T(8,128)S(1)} %add_add_fusion.4), channel_id=1, source_target_pairs={{0,2},{1,3},{2,0},{3,1},{4,6},{5,7},{6,4},{7,5},{8,10},{9,11},{10,... | collective-permute-start | bytes 49160 | tf_op jit(solution)/shard_map/ppermute | solution.py:233
  105.1 5.3 %collective-permute-start.34 = (f32[16,256]{1,0:T(8,128)S(1)}, f32[16,256]{1,0:T(8,128)S(1)}, u32[]{:S(2)}, u32[]{:S(2)}) collective-permute-start(f32[16,256]{1,0:T(8,128)S(1)} %add_add_fusion.4), channel_id=1, source_target_pairs={{0,3},{1,2},{2,1},{3,0},{4,7},{5,6},{6,5},{7,4},{8,11},{9,10},{10,... | collective-permute-start | bytes 49160 | tf_op jit(solution)/shard_map/ppermute | solution.py:233
  155.8 7.7 %collective-permute-start.38 = (f32[16,256]{1,0:T(8,128)S(1)}, f32[16,256]{1,0:T(8,128)S(1)}, u32[]{:S(2)}, u32[]{:S(2)}) collective-permute-start(f32[16,256]{1,0:T(8,128)S(1)} %add.192), channel_id=1, source_target_pairs={{0,0},{16,144},{32,32},{48,176},{64,64},{80,208},{96,96},{112,240}... | collective-permute-start | bytes 49160 | tf_op jit(solution)/shard_map/ppermute | solution.py:231
  156.5 7.1 %collective-permute-start.39 = (f32[16,256]{1,0:T(8,128)S(1)}, f32[16,256]{1,0:T(8,128)S(1)}, u32[]{:S(2)}, u32[]{:S(2)}) collective-permute-start(f32[16,256]{1,0:T(8,128)S(1)} %add.192), channel_id=1, source_target_pairs={{0,32},{16,176},{32,0},{48,144},{64,96},{80,240},{96,64},{112,208}... | collective-permute-start | bytes 49160 | tf_op jit(solution)/shard_map/ppermute | solution.py:231
  161.1 4.9 %collective-permute-start.40 = (f32[16,256]{1,0:T(8,128)S(1)}, f32[16,256]{1,0:T(8,128)S(1)}, u32[]{:S(2)}, u32[]{:S(2)}) collective-permute-start(f32[16,256]{1,0:T(8,128)S(1)} %add.192), channel_id=1, source_target_pairs={{0,64},{16,208},{32,96},{48,240},{64,0},{80,144},{96,32},{112,176}... | collective-permute-start | bytes 49160 | tf_op jit(solution)/shard_map/ppermute | solution.py:231
  161.6 5.9 %collective-permute-start.41 = (f32[16,256]{1,0:T(8,128)S(1)}, f32[16,256]{1,0:T(8,128)S(1)}, u32[]{:S(2)}, u32[]{:S(2)}) collective-permute-start(f32[16,256]{1,0:T(8,128)S(1)} %add.192), channel_id=1, source_target_pairs={{0,96},{16,240},{32,64},{48,208},{64,32},{80,176},{96,0},{112,144}... | collective-permute-start | bytes 49160 | tf_op jit(solution)/shard_map/ppermute | solution.py:231
  167.5 5.0 %collective-permute-start.42 = (f32[16,256]{1,0:T(8,128)S(1)}, f32[16,256]{1,0:T(8,128)S(1)}, u32[]{:S(2)}, u32[]{:S(2)}) collective-permute-start(f32[16,256]{1,0:T(8,128)S(1)} %add_add_fusion.2), channel_id=1, source_target_pairs={{0,4},{4,0},{8,12},{12,8},{1,5},{5,1},{9,13},{13,9},{2,6},{6,2},{1... | collective-permute-start | bytes 49160 | tf_op jit(solution)/shard_map/ppermute | solution.py:233
  170.8 5.2 %collective-permute-start.43 = (f32[16,256]{1,0:T(8,128)S(1)}, f32[16,256]{1,0:T(8,128)S(1)}, u32[]{:S(2)}, u32[]{:S(2)}) collective-permute-start(f32[16,256]{1,0:T(8,128)S(1)} %add_add_fusion.2), channel_id=1, source_target_pairs={{0,8},{4,12},{8,0},{12,4},{1,9},{5,13},{9,1},{13,5},{2,10},{6,14},... | collective-permute-start | bytes 49160 | tf_op jit(solution)/shard_map/ppermute | solution.py:233
  171.0 5.1 %collective-permute-start.44 = (f32[16,256]{1,0:T(8,128)S(1)}, f32[16,256]{1,0:T(8,128)S(1)}, u32[]{:S(2)}, u32[]{:S(2)}) collective-permute-start(f32[16,256]{1,0:T(8,128)S(1)} %add_add_fusion.2), channel_id=1, source_target_pairs={{0,12},{4,8},{8,4},{12,0},{1,13},{5,9},{9,5},{13,1},{2,14},{6,10},... | collective-permute-start | bytes 49160 | tf_op jit(solution)/shard_map/ppermute | solution.py:233
  176.2 5.3 %collective-permute-start.46 = (f32[16,256]{1,0:T(8,128)S(1)}, f32[16,256]{1,0:T(8,128)S(1)}, u32[]{:S(2)}, u32[]{:S(2)}) collective-permute-start(f32[16,256]{1,0:T(8,128)S(1)} %add_add_fusion.1), channel_id=1, source_target_pairs={{0,2},{1,3},{2,0},{3,1},{4,6},{5,7},{6,4},{7,5},{8,10},{9,11},{10,... | collective-permute-start | bytes 49160 | tf_op jit(solution)/shard_map/ppermute | solution.py:233
  178.7 5.0 %collective-permute-start.47 = (f32[16,256]{1,0:T(8,128)S(1)}, f32[16,256]{1,0:T(8,128)S(1)}, u32[]{:S(2)}, u32[]{:S(2)}) collective-permute-start(f32[16,256]{1,0:T(8,128)S(1)} %add_add_fusion.1), channel_id=1, source_target_pairs={{0,3},{1,2},{2,1},{3,0},{4,7},{5,6},{6,5},{7,4},{8,11},{9,10},{10,... | collective-permute-start | bytes 49160 | tf_op jit(solution)/shard_map/ppermute | solution.py:233
  (21 other events, 102.5 us)
Sparse Core Ops, SparseCore 0:
  11.7 100.1 all-gather.2
  150.7 42.1 reduce-scatter.1

commit v3 on v2

--- a/solution.py
+++ b/solution.py
@@ -138,8 +138,17 @@
     out_ref[...] = cams - terms[:blocks] - terms[blocks:]
 
 
-def answer_kernel(rhs_ref, s1_ref, s2_ref, s3_ref, out_ref):
-    out_ref[...] = minres(rhs_ref[...], [s1_ref[...], s2_ref[...], s3_ref[...]])
+def answer_kernel(strip, place_ref, rhs_ref, s1_ref, s2_ref, s3_ref, own_rhs_ref, own_ref):
+    rhs = rhs_ref[...]
+    answer = minres(rhs, [s1_ref[...], s2_ref[...], s3_ref[...]])
+    rows = lax.broadcasted_iota(jnp.int32, rhs.shape, 0)
+    for value, ref in ((rhs, own_rhs_ref), (answer, own_ref)):
+        line = jnp.sum(jnp.where(rows == 2 * place_ref[0] + place_ref[1], value, 0.0), axis=0, keepdims=True)
+        for r in range(rhs.shape[1] // strip):
+
+            @pl.when(place_ref[2] == r)
+            def _():
+                ref[...] = line[:, r * strip : (r + 1) * strip]
 
 
 def chosen(picks, terms):
@@ -150,25 +159,28 @@
     return value
 
 
-def tile_kernel(slots, blocks, width, strip, fine, place_ref, got_ref, cam_ref, own_ref, peer_ref, acc_ref, row_ref, col_ref):
+def tile_kernel(slots, blocks, width, strip, fine, offsets, place_ref, got_ref, cam_ref, *refs):
+    count = len(offsets)
+    out_refs, (acc_ref, row_ref, col_ref) = refs[:count], refs[count:]
     z_idx, core_idx, row_idx, col_idx = place_ref[0], place_ref[1], place_ref[2], place_ref[3]
     sources, _, points = got_ref.shape
-    half, col_count = own_ref.shape
+    col_count = acc_ref.shape[2]
     col_blocks = col_count // width
     base_aux = 3 * slots * width
 
     @pl.when(pl.program_id(0) == 0)
     def _():
-        own_ref[...] = jnp.zeros_like(own_ref)
         acc_ref[...] = jnp.zeros_like(acc_ref)
-        for c in range(col_blocks):
-
-            @pl.when(col_idx * col_blocks + c == 2 * z_idx + core_idx)
-            def _():
-                start = pl.multiple_of(z_idx * strip, strip)
-                own_ref[pl.ds(start, strip), c * width : (c + 1) * width] = cam_ref[...]
-
-    for s in range(sources):
+        if offsets[0] == 0:
+            for c in range(col_blocks):
+
+                @pl.when(col_idx * col_blocks + c == 2 * z_idx + core_idx)
+                def _():
+                    start = pl.multiple_of(z_idx * strip, strip)
+                    acc_ref[0, pl.ds(start, strip), c * width : (c + 1) * width] = cam_ref[...]
+
+    @pl.loop(0, sources)
+    def _(s):
         aux = got_ref[s, base_aux : base_aux + AUX, :].astype(jnp.float32)
         vis = [aux[k : k + 1, :] for k in range(slots)]
         inv = [aux[slots + e : slots + e + 1, :] for e in range(6)]
@@ -177,20 +189,23 @@
             block = block.astype(jnp.float32)
             return [jnp.where(v == block, one, 0.0).astype(jnp.bfloat16) for v in vis]
 
-        col_picks = [picks_of(col_idx * col_blocks + c, 1.0) for c in range(col_blocks)]
-
-        @pl.loop(0, width // fine)
-        def _(h):
-            terms = []
-            for at in range(3 * slots):
-                start = pl.multiple_of(at * width + h * fine, fine)
-                terms.append(got_ref[s, pl.ds(start, fine), :])
-            for c in range(col_blocks):
-                rows = [chosen(col_picks[c], terms[a::3]).astype(jnp.float32) for a in range(3)]
-                start = pl.multiple_of(c * width + h * fine, fine)
-                for a, z in enumerate(apply_inverse(inv, rows)):
-                    at = (a * sources + s) * points
-                    col_ref[pl.ds(start, fine), at : at + points] = z.astype(jnp.bfloat16)
+        @pl.loop(0, count)
+        def _(d):
+            first = (col_idx ^ (d + offsets[0])) * col_blocks
+            col_picks = [picks_of(first + c, 1.0) for c in range(col_blocks)]
+
+            @pl.loop(0, width // fine)
+            def _(h):
+                terms = []
+                for at in range(3 * slots):
+                    start = pl.multiple_of(at * width + h * fine, fine)
+                    terms.append(got_ref[s, pl.ds(start, fine), :])
+                for c in range(col_blocks):
+                    rows = [chosen(col_picks[c], terms[a::3]).astype(jnp.float32) for a in range(3)]
+                    start = pl.multiple_of(c * width + h * fine, fine)
+                    for a, z in enumerate(apply_inverse(inv, rows)):
+                        at = pl.multiple_of((a * sources + s) * points, points)
+                        col_ref[d, pl.ds(start, fine), pl.ds(at, points)] = z.astype(jnp.bfloat16)
 
         @pl.loop(0, strip // fine)
         def _(h):
@@ -198,20 +213,21 @@
             for at in range(3 * slots):
                 start = pl.multiple_of(at * width + row_idx * strip + h * fine, fine)
                 terms.append(got_ref[s, pl.ds(start, fine), :])
-            for b in range(blocks):
-                other = b >= blocks // 2
-                picks = picks_of(2 * (b % (blocks // 2)) + (1 - core_idx if other else core_idx), -1.0)
+            for b in range(blocks // 2):
+                picks = picks_of(2 * b + core_idx, -1.0)
                 start = pl.multiple_of(b * strip + h * fine, fine)
                 for a in range(3):
-                    at = (a * sources + s) * points
-                    row_ref[pl.ds(start, fine), at : at + points] = chosen(picks, terms[a::3])
-
-    acc_ref[...] += lax.dot_general(row_ref[half:, :], col_ref[...], NT, preferred_element_type=jnp.float32)
-    own_ref[...] += lax.dot_general(row_ref[:half, :], col_ref[...], NT, preferred_element_type=jnp.float32)
+                    at = pl.multiple_of((a * sources + s) * points, points)
+                    row_ref[pl.ds(start, fine), pl.ds(at, points)] = chosen(picks, terms[a::3])
+
+    @pl.loop(0, count)
+    def _(d):
+        acc_ref[d] += lax.dot_general(row_ref[...], col_ref[d], NT, preferred_element_type=jnp.float32)
 
     @pl.when(pl.program_id(0) == pl.num_programs(0) - 1)
     def _():
-        peer_ref[...] = acc_ref[...].astype(jnp.bfloat16)
+        for d in range(count):
+            out_refs[d][...] = acc_ref[d].astype(out_refs[d].dtype)
 
 
 def tree(values):
@@ -224,11 +240,13 @@
     return value + lax.ppermute(value, "core", [(0, 1), (1, 0)])
 
 
-def all_sum(value, n_z, n_row, n_col):
+def all_sum(value, n_z, n_row, n_col, between=None):
     value = core_sum(value)
     far = n_z // 2
     pairs = [[(2 * z + c, 2 * (z ^ (j + c * far)) + c) for z in range(n_z) for c in range(2)] for j in range(far)]
     value = tree([lax.ppermute(value, ("z", "core"), p) for p in pairs])
+    if between is not None:
+        value = between(value)
     for axis, size in (("row", n_row), ("col", n_col)):
         swaps = [lax.ppermute(value, axis, [(i, i ^ b) for i in range(size)]) for b in range(1, size)]
         value = tree([value] + swaps)
@@ -251,7 +269,7 @@
     total_rows = blocks * width
     col_count = total_rows // n_col
     set_rows = blocks * strip
-    shards = n_row * n_col
+    shards = 2 * n_row
     send_rows = 3 * slots * width + AUX
     place = jnp.stack([z_idx, core_idx, row_idx, col_idx]).astype(jnp.int32)
     w_flat = weights.reshape(3 * slots * points, width)
@@ -278,7 +296,7 @@
         name="prepare",
     )(w_flat, visibility, inverses, grad_points, cams_placed)
 
-    got = lax.all_gather(send, ("row", "col"), axis=0, tiled=False)
+    got = lax.all_gather(send, ("core", "row"), axis=0, tiled=False)
 
     def product(known):
         return pl.pallas_call(
@@ -289,59 +307,66 @@
             name="product",
         )(place, visibility, w_flat, zw, cam_wide, *known)
 
-    def reduce_all(value):
-        return all_sum(value, n_z, n_row, n_col)
-
-    rhs = reduce_all(part)
-    known = [rhs]
-    for _ in range(1, ITERS):
-        known.append(reduce_all(product(known)))
-    got, known = lax.optimization_barrier((got, known))
-
     pair = 2
     half = set_rows // 2
-    own_half, peer_half = pl.pallas_call(
-        functools.partial(tile_kernel, slots, blocks, width, strip, 64),
-        out_shape=(
-            jax.ShapeDtypeStruct((half, col_count), jnp.float32),
-            jax.ShapeDtypeStruct((half, col_count), jnp.bfloat16),
-        ),
-        grid=(shards // pair,),
-        in_specs=[
-            smem,
-            pl.BlockSpec((pair, send_rows, points), lambda i: (i, 0, 0)),
-            pl.BlockSpec((strip, width), lambda i: (0, 0)),
-        ],
-        out_specs=(
-            pl.BlockSpec((half, col_count), lambda i: (0, 0)),
-            pl.BlockSpec((half, col_count), lambda i: (0, 0)),
-        ),
-        scratch_shapes=[
-            pltpu.VMEM((half, col_count), jnp.float32),
-            pltpu.VMEM((set_rows, 3 * pair * points), jnp.bfloat16),
-            pltpu.VMEM((col_count, 3 * pair * points), jnp.bfloat16),
-        ],
-        compiler_params=pltpu.CompilerParams(
-            dimension_semantics=("arbitrary",), vmem_limit_bytes=56 * 1024 * 1024
-        ),
-        cost_estimate=pl.CostEstimate(
-            flops=2 * set_rows * col_count * 3 * shards * points,
-            bytes_accessed=2 * shards * send_rows * points + 4 * set_rows * col_count,
-            transcendentals=0,
-        ),
-        name="tile",
-    )(place, got, camera_blocks)
-    taken = lax.ppermute(peer_half, "core", [(0, 1), (1, 0)])
-    tile = own_half + taken.astype(jnp.float32)
-    tile, known = lax.optimization_barrier((tile, known))
-    schur = lax.psum_scatter(tile, "z", scatter_dimension=0, tiled=True)
-    known.append(reduce_all(product(known)))
-    answer = pl.pallas_call(answer_kernel, out_shape=vec, in_specs=[vmem] * 4, out_specs=vmem, name="answer")(*known)
-
-    def own(value):
-        return lax.dynamic_slice(value, (pts_idx, row_idx * strip), (1, strip)).reshape(strip)
-
-    return (schur, own(rhs), own(answer))
+
+    def pieces_of(got, offsets, dtype):
+        return pl.pallas_call(
+            functools.partial(tile_kernel, slots, blocks, width, strip, 64, offsets),
+            out_shape=(jax.ShapeDtypeStruct((half, col_count), dtype),) * len(offsets),
+            grid=(shards // pair,),
+            in_specs=[
+                smem,
+                pl.BlockSpec((pair, send_rows, points), lambda i: (i, 0, 0)),
+                pl.BlockSpec((strip, width), lambda i: (0, 0)),
+            ],
+            out_specs=(pl.BlockSpec((half, col_count), lambda i: (0, 0)),) * len(offsets),
+            scratch_shapes=[
+                pltpu.VMEM((len(offsets), half, col_count), jnp.float32),
+                pltpu.VMEM((half, 3 * pair * points), jnp.bfloat16),
+                pltpu.VMEM((len(offsets), col_count, 3 * pair * points), jnp.bfloat16),
+            ],
+            compiler_params=pltpu.CompilerParams(
+                dimension_semantics=("arbitrary",), vmem_limit_bytes=56 * 1024 * 1024
+            ),
+            cost_estimate=pl.CostEstimate(
+                flops=2 * len(offsets) * half * col_count * 3 * shards * points,
+                bytes_accessed=2 * shards * send_rows * points + 4 * len(offsets) * half * col_count,
+                transcendentals=0,
+            ),
+            name="tile",
+        )(place, got, camera_blocks)
+
+    held = {}
+
+    def make_tile(value):
+        here, value = lax.optimization_barrier((got, value))
+        offsets = tuple(range(1, n_col))
+        pieces, value = lax.optimization_barrier((pieces_of(here, offsets, jnp.bfloat16), value))
+        held["taken"] = [
+            lax.ppermute(piece, "col", [(i, i ^ offset) for i in range(n_col)]) for piece, offset in zip(pieces, offsets)
+        ]
+        (held["own"],), value = lax.optimization_barrier((pieces_of(here, (0,), jnp.float32), value))
+        return value
+
+    def reduce_tile(value):
+        tile = tree([held["own"]] + [piece.astype(jnp.float32) for piece in held["taken"]])
+        tile, value = lax.optimization_barrier((tile, value))
+        held["schur"] = lax.psum_scatter(tile, "z", scatter_dimension=0, tiled=True)
+        return value
+
+    known = [all_sum(part, n_z, n_row, n_col)]
+    for between in (make_tile, reduce_tile, None):
+        known.append(all_sum(product(known), n_z, n_row, n_col, between))
+    own = jax.ShapeDtypeStruct((1, strip), jnp.float32)
+    own_rhs, answer = pl.pallas_call(
+        functools.partial(answer_kernel, strip),
+        out_shape=(own, own),
+        in_specs=[smem] + [vmem] * 4,
+        out_specs=(vmem, vmem),
+        name="answer",
+    )(place, *known)
+    return (held["schur"], own_rhs.reshape(strip), answer.reshape(strip))
 
 
 def solution(mesh):

time: 201 us -> 232 us (1.15)
  starting transfers between devices: 70.1 us -> 86.7 us
  Pallas kernels: 44.7 us -> 60.8 us
  local copies, waits for them, and re-layouts: 2.67 us -> 0.12 us
    ppermute x8, starting transfers between devices: 9.17 us -> 28.1 us  [core_sum(): return value + lax.ppermute(value, 'core', [(0, 1), (1, 0)])]
    pallas_call x2 -> x3, Pallas kernels: 33.2 us -> 49.2 us  [the longest x2 47.1 us: pieces_of(): pl.pallas_call(functools.partial(tile_kernel, slots, blocks, width, strip...]
    ppermute x24, waiting for transfers between devices: 29.2 us -> 36.4 us  [all_sum(): lax.ppermute(value, axis, [(i, i ^ b) for i in range(size)])]
    ppermute x16, starting transfers between devices: 25 us -> 20.1 us  [all_sum(): value = tree([lax.ppermute(value, ('z', 'core'), p) for p in pairs])]
    ppermute x1 -> x3, starting transfers between devices: 0.34 us -> 4.7 us  [make_tile(): lax.ppermute(piece, 'col', [(i, i ^ offset) for i in range(n_col)])]
    ppermute x16, waiting for transfers between devices: 16.7 us -> 12.9 us  [all_sum(): value = tree([lax.ppermute(value, ('z', 'core'), p) for p in pairs])]
    add x12 -> x13, other arithmetic: 0.09 us -> 3.66 us  [tree(): values = [values[i] + values[i + 1] for i in range(0, len(values), 2)]]
    add x1 -> x0, other arithmetic: 3.39 us -> none  [per_device(): tile = own_half + taken.astype(jnp.float32)]
  transfers between devices with their start and end apart: 51 -> 53, of which waited for: 36 -> 33; matrix products, arithmetic and copies ran while one was open for 4% -> 3% of each run, Pallas kernels for 5% -> 11%
where the time goes in v3:
time: 232 us; the launch traced here: 229 us
  starting transfers between devices  86.7 us (37%)
  Pallas kernels  60.8 us (26%)
  waiting for transfers between devices  56.6 us (24%)
  between operations  14.3 us (6%)
  other arithmetic  10.9 us (5%)
    pallas_call x2, Pallas kernels, pieces_of(): pl.pallas_call(functools.partial(tile_kernel, slots, blocks, width, strip...  47.1 us
    ppermute x24, waiting for transfers between devices, all_sum(): lax.ppermute(value, axis, [(i, i ^ b) for i in range(size)])  36.4 us
    ppermute x24, starting transfers between devices, all_sum(): lax.ppermute(value, axis, [(i, i ^ b) for i in range(size)])  33.7 us
    ppermute x8, starting transfers between devices, core_sum(): return value + lax.ppermute(value, 'core', [(0, 1), (1, 0)])  28.1 us
    ppermute x16, starting transfers between devices, all_sum(): value = tree([lax.ppermute(value, ('z', 'core'), p) for p in pairs])  20.1 us
    ppermute x16, waiting for transfers between devices, all_sum(): value = tree([lax.ppermute(value, ('z', 'core'), p) for p in pairs])  12.9 us
    pallas_call x3, Pallas kernels, product(): pl.pallas_call(functools.partial(product_kernel, slots, blocks, len(known...  8.74 us
    ppermute x8, waiting for transfers between devices, core_sum(): return value + lax.ppermute(value, 'core', [(0, 1), (1, 0)])  7.28 us
  transfers between devices with their start and end apart: 53, of which 33 were waited for; matrix products, arithmetic and copies ran while one was open for 3% of the time, Pallas kernels for 11%

profile of v3, /device:TPU:2, one launch (start us, length us, event | category | flops | bytes accessed | tf_op | source)
XLA Modules:
  0.0 229.4 jit_solution(10089005502029261954)
XLA Ops:
  8.7 2.9 %prepare.1 = (bf16[3088,128]{1,0:T(8,128)(2,1)}, bf16[256,1536]{1,0:T(8,128)(2,1)}, f32[16,256]{1,0:T(8,128)}) custom-call(bf16[1536,256]{1,0:T(8,128)(2,1)} %bitcast.8, s32[4,128]{1,0:T(4,128)} %refs_1_.5, bf16[6,128]{1,0:T(8,128)(2,1)} %inv_ref.1, bf16[3,128]{1,0:T(4,128)(2,1)} %grad_ref.1, f32[16,256]{1,0:T(8,128)} %and_select_fusion.cams_ref), custom_call_target="tpu_custom_call" | custom-call | tf_op jit(solution)/shard_map/prepare/pallas_call | solution.py:287
  13.8 4.6 %collective-permute-start.4 = (f32[16,256]{1,0:T(8,128)S(1)}, f32[16,256]{1,0:T(8,128)S(1)}, u32[]{:S(2)}, u32[]{:S(2)}) collective-permute-start(f32[16,256]{1,0:T(8,128)S(1)} %add.157), channel_id=1, source_target_pairs={{0,96},{16,240},{32,64},{48,208},{64,32},{80,176},{96,0},{112,144}... | collective-permute-start | bytes 49160 | tf_op jit(solution)/shard_map/ppermute | solution.py:247
  20.2 2.9 %collective-permute-done.3 = f32[16,256]{1,0:T(8,128)S(1)} collective-permute-done((f32[16,256]{1,0:T(8,128)S(1)}, f32[16,256]{1,0:T(8,128)S(1)}, u32[]{:S(2)}, u32[]{:S(2)}) %collective-permute-start.3) | collective-permute-done | bytes 16416 | tf_op jit(solution)/shard_map/ppermute | solution.py:247
  27.3 2.6 %collective-permute-done.6 = f32[16,256]{1,0:T(8,128)S(1)} collective-permute-done((f32[16,256]{1,0:T(8,128)S(1)}, f32[16,256]{1,0:T(8,128)S(1)}, u32[]{:S(2)}, u32[]{:S(2)}) %collective-permute-start.6) | collective-permute-done | bytes 16416 | tf_op jit(solution)/shard_map/ppermute | solution.py:251
  29.9 3.1 %collective-permute-start.10 = (f32[16,256]{1,0:T(8,128)S(1)}, f32[16,256]{1,0:T(8,128)S(1)}, u32[]{:S(2)}, u32[]{:S(2)}) collective-permute-start(f32[16,256]{1,0:T(8,128)S(1)} %add_add_fusion.11), channel_id=1, source_target_pairs={{0,3},{1,2},{2,1},{3,0},{4,7},{5,6},{6,5},{7,4},{8,11},{9,10},{10,... | collective-permute-start | bytes 49160 | tf_op jit(solution)/shard_map/ppermute | solution.py:251
  35.0 3.3 %collective-permute-done.9 = f32[16,256]{1,0:T(8,128)S(1)} collective-permute-done((f32[16,256]{1,0:T(8,128)S(1)}, f32[16,256]{1,0:T(8,128)S(1)}, u32[]{:S(2)}, u32[]{:S(2)}) %collective-permute-start.9) | collective-permute-done | bytes 16416 | tf_op jit(solution)/shard_map/ppermute | solution.py:251
  38.3 6.5 %collective-permute-start.11 = (f32[16,256]{1,0:T(8,128)S(1)}, f32[16,256]{1,0:T(8,128)S(1)}, u32[]{:S(2)}, u32[]{:S(2)}) collective-permute-start(f32[16,256]{1,0:T(8,128)S(1)} %add_add_fusion.10), channel_id=1, source_target_pairs={{0,16},{16,0},{1,17},{17,1},{2,18},{18,2},{3,19},{19,3},{4,20},{20... | collective-permute-start | bytes 49160 | tf_op jit(solution)/shard_map/ppermute | solution.py:240
  46.2 2.7 %product.3 = f32[16,256]{1,0:T(8,128)} custom-call(s32[4]{0:T(128)} %pad_add_fusion.refs_0_.place_ref, s32[4,128]{1,0:T(4,128)} %refs_1_.5, bf16[1536,256]{1,0:T(8,128)(2,1)} %bitcast.9, bf16[256,1536]{1,0:T(8,128)(2,1)} %get-tuple-element.22.refs_3_, f32[256,256]{1,0:T(8,128)} %copy-done, f32[16,256]{1,0:T(8,128)} %add.167.refs_5_.rhs_ref), custom_call_target="tpu_custom_call" | custom-call | tf_op jit(solution)/shard_map/product/pallas_call | solution.py:302
  51.1 2.0 collective-permute-start.16
  58.4 33.4 %tile.10 = (bf16[512,1024]{1,0:T(8,128)(2,1)}, bf16[512,1024]{1,0:T(8,128)(2,1)}, bf16[512,1024]{1,0:T(8,128)(2,1)}) custom-call(s32[4]{0:T(128)} %pad_add_fusion.refs_0_.place_ref, bf16[8,3088,128]{2,1,0:T(8,128)(2,1)} %bitcast.12, f32[64,256]{1,0:T(8,128)} %cam_ref.3), custom_call_target="tpu_custom_call" | custom-call | flops 9663676416 | bytes 12615680 | tf_op jit(solution)/shard_map/tile/pallas_call | solution.py:314
  92.5 2.7 %collective-permute-start.18 = (bf16[512,1024]{1,0:T(8,128)(2,1)}, bf16[512,1024]{1,0:T(8,128)(2,1)}, u32[]{:S(2)}, u32[]{:S(2)}) collective-permute-start(bf16[512,1024]{1,0:T(8,128)(2,1)} %get-tuple-element.32), channel_id=1, source_target_pairs={{0,2},{1,3},{2,0},{3,1},{4,6},{5,7},{6,4},{7,5},{8,10},{9,11},{10,... | collective-permute-start | bytes 3145736 | tf_op jit(solution)/shard_map/ppermute | solution.py:347
  96.5 13.7 %tile.9 = f32[512,1024]{1,0:T(8,128)} custom-call(s32[4]{0:T(128)} %pad_add_fusion.refs_0_.place_ref, bf16[8,3088,128]{2,1,0:T(8,128)(2,1)} %bitcast.13, f32[64,256]{1,0:T(8,128)} %cam_ref.3), custom_call_target="tpu_custom_call" | custom-call | flops 3221225472 | bytes 8421376 | tf_op jit(solution)/shard_map/tile/pallas_call | solution.py:314
  112.0 2.1 collective-permute-start.21
  114.1 2.9 %collective-permute-start.20 = (f32[16,256]{1,0:T(8,128)S(1)}, f32[16,256]{1,0:T(8,128)S(1)}, u32[]{:S(2)}, u32[]{:S(2)}) collective-permute-start(f32[16,256]{1,0:T(8,128)S(1)} %add_add_fusion.9), channel_id=1, source_target_pairs={{0,4},{4,0},{8,12},{12,8},{1,5},{5,1},{9,13},{13,9},{2,6},{6,2},{1... | collective-permute-start | bytes 49160 | tf_op jit(solution)/shard_map/ppermute | solution.py:251
  120.6 3.8 %collective-permute-done.25 = f32[16,256]{1,0:T(8,128)S(1)} collective-permute-done((f32[16,256]{1,0:T(8,128)S(1)}, f32[16,256]{1,0:T(8,128)S(1)}, u32[]{:S(2)}, u32[]{:S(2)}) %collective-permute-start.25) | collective-permute-done | bytes 16416 | tf_op jit(solution)/shard_map/ppermute | solution.py:251
  124.4 12.6 %collective-permute-done.24 = f32[16,256]{1,0:T(8,128)S(1)} collective-permute-done((f32[16,256]{1,0:T(8,128)S(1)}, f32[16,256]{1,0:T(8,128)S(1)}, u32[]{:S(2)}, u32[]{:S(2)}) %collective-permute-start.24) | collective-permute-done | bytes 16416 | tf_op jit(solution)/shard_map/ppermute | solution.py:251
  137.0 11.4 %collective-permute-start.26 = (f32[16,256]{1,0:T(8,128)S(1)}, f32[16,256]{1,0:T(8,128)S(1)}, u32[]{:S(2)}, u32[]{:S(2)}) collective-permute-start(f32[16,256]{1,0:T(8,128)S(1)} %add_add_fusion.7), channel_id=1, source_target_pairs={{0,16},{16,0},{1,17},{17,1},{2,18},{18,2},{3,19},{19,3},{4,20},{20... | collective-permute-start | bytes 49160 | tf_op jit(solution)/shard_map/ppermute | solution.py:240
  149.8 2.9 %product.4 = f32[16,256]{1,0:T(8,128)} custom-call(s32[4]{0:T(128)} %pad_add_fusion.refs_0_.place_ref, s32[4,128]{1,0:T(4,128)} %refs_1_.5, bf16[1536,256]{1,0:T(8,128)(2,1)} %bitcast.10, bf16[256,1536]{1,0:T(8,128)(2,1)} %get-tuple-element.22.refs_3_, f32[256,256]{1,0:T(8,128)} %copy-done, f32[16,256]{1,0:T(8,128)} %add.167.refs_5_.rhs_ref, ...), custom_call_target="tpu_custom_call" | custom-call | tf_op jit(solution)/shard_map/product/pallas_call | solution.py:302
  154.8 3.5 %collective-permute-start.31 = (f32[16,256]{1,0:T(8,128)S(1)}, f32[16,256]{1,0:T(8,128)S(1)}, u32[]{:S(2)}, u32[]{:S(2)}) collective-permute-start(f32[16,256]{1,0:T(8,128)S(1)} %add.182), channel_id=1, source_target_pairs={{0,96},{16,240},{32,64},{48,208},{64,32},{80,176},{96,0},{112,144}... | collective-permute-start | bytes 49160 | tf_op jit(solution)/shard_map/ppermute | solution.py:247
  158.4 2.0 collective-permute-done.31
  160.4 2.6 %collective-permute-done.30 = f32[16,256]{1,0:T(8,128)S(1)} collective-permute-done((f32[16,256]{1,0:T(8,128)S(1)}, f32[16,256]{1,0:T(8,128)S(1)}, u32[]{:S(2)}, u32[]{:S(2)}) %collective-permute-start.30) | collective-permute-done | bytes 16416 | tf_op jit(solution)/shard_map/ppermute | solution.py:247
  164.2 3.6 %add_add_fusion = f32[512,1024]{1,0:T(8,128)} fusion(bf16[512,1024]{1,0:T(8,128)(2,1)} %collective-permute-done.19, bf16[512,1024]{1,0:T(8,128)(2,1)} %collective-permute-done.18, f32[512,1024]{1,0:T(8,128)S(1)} %copy-done.1, bf16[512,1024]{1,0:T(8,128)(2,1)S(1)} %collective-permute-done.17), kind=kLoop, calls=%fused_computation | loop fusion | flops 3145728 | bytes 7340032 | tf_op jit(solution)/shard_map/add | solution.py:235
  169.2 2.3 %collective-permute-start.33 = (f32[16,256]{1,0:T(8,128)S(1)}, f32[16,256]{1,0:T(8,128)S(1)}, u32[]{:S(2)}, u32[]{:S(2)}) collective-permute-start(f32[16,256]{1,0:T(8,128)S(1)} %add_add_fusion.6), channel_id=1, source_target_pairs={{0,8},{4,12},{8,0},{12,4},{1,9},{5,13},{9,1},{13,5},{2,10},{6,14},... | collective-permute-start | bytes 49160 | tf_op jit(solution)/shard_map/ppermute | solution.py:251
  172.0 2.5 %collective-permute-done.33 = f32[16,256]{1,0:T(8,128)S(1)} collective-permute-done((f32[16,256]{1,0:T(8,128)S(1)}, f32[16,256]{1,0:T(8,128)S(1)}, u32[]{:S(2)}, u32[]{:S(2)}) %collective-permute-start.33) | collective-permute-done | bytes 16416 | tf_op jit(solution)/shard_map/ppermute | solution.py:251
  182.1 6.2 %collective-permute-start.38 = (f32[16,256]{1,0:T(8,128)S(1)}, f32[16,256]{1,0:T(8,128)S(1)}, u32[]{:S(2)}, u32[]{:S(2)}) collective-permute-start(f32[16,256]{1,0:T(8,128)S(1)} %add_add_fusion.4), channel_id=1, source_target_pairs={{0,16},{16,0},{1,17},{17,1},{2,18},{18,2},{3,19},{19,3},{4,20},{20... | collective-permute-start | bytes 49160 | tf_op jit(solution)/shard_map/ppermute | solution.py:240
  189.8 3.1 %product.5 = f32[16,256]{1,0:T(8,128)} custom-call(s32[4]{0:T(128)} %pad_add_fusion.refs_0_.place_ref, s32[4,128]{1,0:T(4,128)} %refs_1_.5, bf16[1536,256]{1,0:T(8,128)(2,1)} %bitcast.11, bf16[256,1536]{1,0:T(8,128)(2,1)} %get-tuple-element.22.refs_3_, f32[256,256]{1,0:T(8,128)} %copy-done, f32[16,256]{1,0:T(8,128)} %add.167.refs_5_.rhs_ref, ...), custom_call_target="tpu_custom_call" | custom-call | tf_op jit(solution)/shard_map/product/pallas_call | solution.py:302
  196.8 2.6 %collective-permute-start.41 = (f32[16,256]{1,0:T(8,128)S(1)}, f32[16,256]{1,0:T(8,128)S(1)}, u32[]{:S(2)}, u32[]{:S(2)}) collective-permute-start(f32[16,256]{1,0:T(8,128)S(1)} %add.193), channel_id=1, source_target_pairs={{0,32},{16,176},{32,0},{48,144},{64,96},{80,240},{96,64},{112,208}... | collective-permute-start | bytes 49160 | tf_op jit(solution)/shard_map/ppermute | solution.py:247
  202.3 2.6 %collective-permute-start.45 = (f32[16,256]{1,0:T(8,128)S(1)}, f32[16,256]{1,0:T(8,128)S(1)}, u32[]{:S(2)}, u32[]{:S(2)}) collective-permute-start(f32[16,256]{1,0:T(8,128)S(1)} %add_add_fusion.3), channel_id=1, source_target_pairs={{0,8},{4,12},{8,0},{12,4},{1,9},{5,13},{9,1},{13,5},{2,10},{6,14},... | collective-permute-start | bytes 49160 | tf_op jit(solution)/shard_map/ppermute | solution.py:251
  208.7 2.2 collective-permute-start.49
  213.7 2.5 %collective-permute-done.48 = f32[16,256]{1,0:T(8,128)S(1)} collective-permute-done((f32[16,256]{1,0:T(8,128)S(1)}, f32[16,256]{1,0:T(8,128)S(1)}, u32[]{:S(2)}, u32[]{:S(2)}) %collective-permute-start.48) | collective-permute-done | bytes 16416 | tf_op jit(solution)/shard_map/ppermute | solution.py:251
  216.2 2.9 %collective-permute-start.50 = (f32[16,256]{1,0:T(8,128)S(1)}, f32[16,256]{1,0:T(8,128)S(1)}, u32[]{:S(2)}, u32[]{:S(2)}) collective-permute-start(f32[16,256]{1,0:T(8,128)S(1)} %add_add_fusion.1), channel_id=1, source_target_pairs={{0,16},{16,0},{1,17},{17,1},{2,18},{18,2},{3,19},{19,3},{4,20},{20... | collective-permute-start | bytes 49160 | tf_op jit(solution)/shard_map/ppermute | solution.py:240
  220.5 2.1 answer.1
  (119 shorter events, 58.3 us)
Async XLA Ops:
  7.2 51.2 %all-gather.3.cloned.1.call-start = ((), (), s32[]{:S(2)}) async-start(), calls=%async_computation.2 | async-start | bytes 7114752 | tf_op jit(solution)/shard_map/all_gather | solution.py:299
  11.6 211.0 %reduce-scatter.2.cloned.1.call-start = ((), (), s32[]{:S(2)}) async-start(), calls=%async_computation.1 | async-start | bytes 2359296 | tf_op jit(solution)/shard_map/reduce_scatter | solution.py:355
  13.8 6.3 %collective-permute-start.4 = (f32[16,256]{1,0:T(8,128)S(1)}, f32[16,256]{1,0:T(8,128)S(1)}, u32[]{:S(2)}, u32[]{:S(2)}) collective-permute-start(f32[16,256]{1,0:T(8,128)S(1)} %add.157), channel_id=1, source_target_pairs={{0,96},{16,240},{32,64},{48,208},{64,32},{80,176},{96,0},{112,144}... | collective-permute-start | bytes 49160 | tf_op jit(solution)/shard_map/ppermute | solution.py:247
  18.5 4.6 %collective-permute-start.3 = (f32[16,256]{1,0:T(8,128)S(1)}, f32[16,256]{1,0:T(8,128)S(1)}, u32[]{:S(2)}, u32[]{:S(2)}) collective-permute-start(f32[16,256]{1,0:T(8,128)S(1)} %add.157), channel_id=1, source_target_pairs={{0,64},{16,208},{32,96},{48,240},{64,0},{80,144},{96,32},{112,176}... | collective-permute-start | bytes 49160 | tf_op jit(solution)/shard_map/ppermute | solution.py:247
  18.5 4.6 %collective-permute-start.2 = (f32[16,256]{1,0:T(8,128)S(1)}, f32[16,256]{1,0:T(8,128)S(1)}, u32[]{:S(2)}, u32[]{:S(2)}) collective-permute-start(f32[16,256]{1,0:T(8,128)S(1)} %add.157), channel_id=1, source_target_pairs={{0,32},{16,176},{32,0},{48,144},{64,96},{80,240},{96,64},{112,208}... | collective-permute-start | bytes 49160 | tf_op jit(solution)/shard_map/ppermute | solution.py:247
  24.7 5.2 %collective-permute-start.6 = (f32[16,256]{1,0:T(8,128)S(1)}, f32[16,256]{1,0:T(8,128)S(1)}, u32[]{:S(2)}, u32[]{:S(2)}) collective-permute-start(f32[16,256]{1,0:T(8,128)S(1)} %add_add_fusion.12), channel_id=1, source_target_pairs={{0,8},{4,12},{8,0},{12,4},{1,9},{5,13},{9,1},{13,5},{2,10},{6,14},... | collective-permute-start | bytes 49160 | tf_op jit(solution)/shard_map/ppermute | solution.py:251
  29.9 5.0 %collective-permute-start.10 = (f32[16,256]{1,0:T(8,128)S(1)}, f32[16,256]{1,0:T(8,128)S(1)}, u32[]{:S(2)}, u32[]{:S(2)}) collective-permute-start(f32[16,256]{1,0:T(8,128)S(1)} %add_add_fusion.11), channel_id=1, source_target_pairs={{0,3},{1,2},{2,1},{3,0},{4,7},{5,6},{6,5},{7,4},{8,11},{9,10},{10,... | collective-permute-start | bytes 49160 | tf_op jit(solution)/shard_map/ppermute | solution.py:251
  33.0 5.2 %collective-permute-start.9 = (f32[16,256]{1,0:T(8,128)S(1)}, f32[16,256]{1,0:T(8,128)S(1)}, u32[]{:S(2)}, u32[]{:S(2)}) collective-permute-start(f32[16,256]{1,0:T(8,128)S(1)} %add_add_fusion.11), channel_id=1, source_target_pairs={{0,2},{1,3},{2,0},{3,1},{4,6},{5,7},{6,4},{7,5},{8,10},{9,11},{10,... | collective-permute-start | bytes 49160 | tf_op jit(solution)/shard_map/ppermute | solution.py:251
  33.7 4.6 %collective-permute-start.8 = (f32[16,256]{1,0:T(8,128)S(1)}, f32[16,256]{1,0:T(8,128)S(1)}, u32[]{:S(2)}, u32[]{:S(2)}) collective-permute-start(f32[16,256]{1,0:T(8,128)S(1)} %add_add_fusion.11), channel_id=1, source_target_pairs={{0,1},{1,0},{2,3},{3,2},{4,5},{5,4},{6,7},{7,6},{8,9},{9,8},{10,11... | collective-permute-start | bytes 49160 | tf_op jit(solution)/shard_map/ppermute | solution.py:251
  38.3 7.3 %collective-permute-start.11 = (f32[16,256]{1,0:T(8,128)S(1)}, f32[16,256]{1,0:T(8,128)S(1)}, u32[]{:S(2)}, u32[]{:S(2)}) collective-permute-start(f32[16,256]{1,0:T(8,128)S(1)} %add_add_fusion.10), channel_id=1, source_target_pairs={{0,16},{16,0},{1,17},{17,1},{2,18},{18,2},{3,19},{19,3},{4,20},{20... | collective-permute-start | bytes 49160 | tf_op jit(solution)/shard_map/ppermute | solution.py:240
  51.1 5.6 %collective-permute-start.16 = (f32[16,256]{1,0:T(8,128)S(1)}, f32[16,256]{1,0:T(8,128)S(1)}, u32[]{:S(2)}, u32[]{:S(2)}) collective-permute-start(f32[16,256]{1,0:T(8,128)S(1)} %add.168), channel_id=1, source_target_pairs={{0,96},{16,240},{32,64},{48,208},{64,32},{80,176},{96,0},{112,144}... | collective-permute-start | bytes 49160 | tf_op jit(solution)/shard_map/ppermute | solution.py:247
  53.1 4.6 %collective-permute-start.15 = (f32[16,256]{1,0:T(8,128)S(1)}, f32[16,256]{1,0:T(8,128)S(1)}, u32[]{:S(2)}, u32[]{:S(2)}) collective-permute-start(f32[16,256]{1,0:T(8,128)S(1)} %add.168), channel_id=1, source_target_pairs={{0,64},{16,208},{32,96},{48,240},{64,0},{80,144},{96,32},{112,176}... | collective-permute-start | bytes 49160 | tf_op jit(solution)/shard_map/ppermute | solution.py:247
  91.8 72.4 %collective-permute-start.17 = (bf16[512,1024]{1,0:T(8,128)(2,1)}, bf16[512,1024]{1,0:T(8,128)(2,1)S(1)}, u32[]{:S(2)}, u32[]{:S(2)}) collective-permute-start(bf16[512,1024]{1,0:T(8,128)(2,1)} %get-tuple-element.31), channel_id=1, source_target_pairs={{0,1},{1,0},{2,3},{3,2},{4,5},{5,4},{6,7},{7,6},{8,9},{9,8},{10,11... | collective-permute-start | bytes 3145736 | tf_op jit(solution)/shard_map/ppermute | solution.py:347
  92.5 71.6 %collective-permute-start.18 = (bf16[512,1024]{1,0:T(8,128)(2,1)}, bf16[512,1024]{1,0:T(8,128)(2,1)}, u32[]{:S(2)}, u32[]{:S(2)}) collective-permute-start(bf16[512,1024]{1,0:T(8,128)(2,1)} %get-tuple-element.32), channel_id=1, source_target_pairs={{0,2},{1,3},{2,0},{3,1},{4,6},{5,7},{6,4},{7,5},{8,10},{9,11},{10,... | collective-permute-start | bytes 3145736 | tf_op jit(solution)/shard_map/ppermute | solution.py:347
  95.3 68.9 %collective-permute-start.19 = (bf16[512,1024]{1,0:T(8,128)(2,1)}, bf16[512,1024]{1,0:T(8,128)(2,1)}, u32[]{:S(2)}, u32[]{:S(2)}) collective-permute-start(bf16[512,1024]{1,0:T(8,128)(2,1)} %get-tuple-element.33), channel_id=1, source_target_pairs={{0,3},{1,2},{2,1},{3,0},{4,7},{5,6},{6,5},{7,4},{8,11},{9,10},{10,... | collective-permute-start | bytes 3145736 | tf_op jit(solution)/shard_map/ppermute | solution.py:347
  112.0 5.2 %collective-permute-start.21 = (f32[16,256]{1,0:T(8,128)S(1)}, f32[16,256]{1,0:T(8,128)S(1)}, u32[]{:S(2)}, u32[]{:S(2)}) collective-permute-start(f32[16,256]{1,0:T(8,128)S(1)} %add_add_fusion.9), channel_id=1, source_target_pairs={{0,8},{4,12},{8,0},{12,4},{1,9},{5,13},{9,1},{13,5},{2,10},{6,14},... | collective-permute-start | bytes 49160 | tf_op jit(solution)/shard_map/ppermute | solution.py:251
  118.7 5.7 %collective-permute-start.25 = (f32[16,256]{1,0:T(8,128)S(1)}, f32[16,256]{1,0:T(8,128)S(1)}, u32[]{:S(2)}, u32[]{:S(2)}) collective-permute-start(f32[16,256]{1,0:T(8,128)S(1)} %add_add_fusion.8), channel_id=1, source_target_pairs={{0,3},{1,2},{2,1},{3,0},{4,7},{5,6},{6,5},{7,4},{8,11},{9,10},{10,... | collective-permute-start | bytes 49160 | tf_op jit(solution)/shard_map/ppermute | solution.py:251
  120.6 16.4 %collective-permute-start.24 = (f32[16,256]{1,0:T(8,128)S(1)}, f32[16,256]{1,0:T(8,128)S(1)}, u32[]{:S(2)}, u32[]{:S(2)}) collective-permute-start(f32[16,256]{1,0:T(8,128)S(1)} %add_add_fusion.8), channel_id=1, source_target_pairs={{0,2},{1,3},{2,0},{3,1},{4,6},{5,7},{6,4},{7,5},{8,10},{9,11},{10,... | collective-permute-start | bytes 49160 | tf_op jit(solution)/shard_map/ppermute | solution.py:251
  124.4 12.6 %collective-permute-start.23 = (f32[16,256]{1,0:T(8,128)S(1)}, f32[16,256]{1,0:T(8,128)S(1)}, u32[]{:S(2)}, u32[]{:S(2)}) collective-permute-start(f32[16,256]{1,0:T(8,128)S(1)} %add_add_fusion.8), channel_id=1, source_target_pairs={{0,1},{1,0},{2,3},{3,2},{4,5},{5,4},{6,7},{7,6},{8,9},{9,8},{10,11... | collective-permute-start | bytes 49160 | tf_op jit(solution)/shard_map/ppermute | solution.py:251
  137.0 12.2 %collective-permute-start.26 = (f32[16,256]{1,0:T(8,128)S(1)}, f32[16,256]{1,0:T(8,128)S(1)}, u32[]{:S(2)}, u32[]{:S(2)}) collective-permute-start(f32[16,256]{1,0:T(8,128)S(1)} %add_add_fusion.7), channel_id=1, source_target_pairs={{0,16},{16,0},{1,17},{17,1},{2,18},{18,2},{3,19},{19,3},{4,20},{20... | collective-permute-start | bytes 49160 | tf_op jit(solution)/shard_map/ppermute | solution.py:240
  154.8 5.5 %collective-permute-start.31 = (f32[16,256]{1,0:T(8,128)S(1)}, f32[16,256]{1,0:T(8,128)S(1)}, u32[]{:S(2)}, u32[]{:S(2)}) collective-permute-start(f32[16,256]{1,0:T(8,128)S(1)} %add.182), channel_id=1, source_target_pairs={{0,96},{16,240},{32,64},{48,208},{64,32},{80,176},{96,0},{112,144}... | collective-permute-start | bytes 49160 | tf_op jit(solution)/shard_map/ppermute | solution.py:247
  158.4 4.6 %collective-permute-start.30 = (f32[16,256]{1,0:T(8,128)S(1)}, f32[16,256]{1,0:T(8,128)S(1)}, u32[]{:S(2)}, u32[]{:S(2)}) collective-permute-start(f32[16,256]{1,0:T(8,128)S(1)} %add.182), channel_id=1, source_target_pairs={{0,64},{16,208},{32,96},{48,240},{64,0},{80,144},{96,32},{112,176}... | collective-permute-start | bytes 49160 | tf_op jit(solution)/shard_map/ppermute | solution.py:247
  169.2 5.2 %collective-permute-start.33 = (f32[16,256]{1,0:T(8,128)S(1)}, f32[16,256]{1,0:T(8,128)S(1)}, u32[]{:S(2)}, u32[]{:S(2)}) collective-permute-start(f32[16,256]{1,0:T(8,128)S(1)} %add_add_fusion.6), channel_id=1, source_target_pairs={{0,8},{4,12},{8,0},{12,4},{1,9},{5,13},{9,1},{13,5},{2,10},{6,14},... | collective-permute-start | bytes 49160 | tf_op jit(solution)/shard_map/ppermute | solution.py:251
  175.3 5.0 %collective-permute-start.37 = (f32[16,256]{1,0:T(8,128)S(1)}, f32[16,256]{1,0:T(8,128)S(1)}, u32[]{:S(2)}, u32[]{:S(2)}) collective-permute-start(f32[16,256]{1,0:T(8,128)S(1)} %add_add_fusion.5), channel_id=1, source_target_pairs={{0,3},{1,2},{2,1},{3,0},{4,7},{5,6},{6,5},{7,4},{8,11},{9,10},{10,... | collective-permute-start | bytes 49160 | tf_op jit(solution)/shard_map/ppermute | solution.py:251
  176.8 5.2 %collective-permute-start.36 = (f32[16,256]{1,0:T(8,128)S(1)}, f32[16,256]{1,0:T(8,128)S(1)}, u32[]{:S(2)}, u32[]{:S(2)}) collective-permute-start(f32[16,256]{1,0:T(8,128)S(1)} %add_add_fusion.5), channel_id=1, source_target_pairs={{0,2},{1,3},{2,0},{3,1},{4,6},{5,7},{6,4},{7,5},{8,10},{9,11},{10,... | collective-permute-start | bytes 49160 | tf_op jit(solution)/shard_map/ppermute | solution.py:251
  182.1 7.1 %collective-permute-start.38 = (f32[16,256]{1,0:T(8,128)S(1)}, f32[16,256]{1,0:T(8,128)S(1)}, u32[]{:S(2)}, u32[]{:S(2)}) collective-permute-start(f32[16,256]{1,0:T(8,128)S(1)} %add_add_fusion.4), channel_id=1, source_target_pairs={{0,16},{16,0},{1,17},{17,1},{2,18},{18,2},{3,19},{19,3},{4,20},{20... | collective-permute-start | bytes 49160 | tf_op jit(solution)/shard_map/ppermute | solution.py:240
  195.0 5.8 %collective-permute-start.43 = (f32[16,256]{1,0:T(8,128)S(1)}, f32[16,256]{1,0:T(8,128)S(1)}, u32[]{:S(2)}, u32[]{:S(2)}) collective-permute-start(f32[16,256]{1,0:T(8,128)S(1)} %add.193), channel_id=1, source_target_pairs={{0,96},{16,240},{32,64},{48,208},{64,32},{80,176},{96,0},{112,144}... | collective-permute-start | bytes 49160 | tf_op jit(solution)/shard_map/ppermute | solution.py:247
  196.8 5.3 %collective-permute-start.42 = (f32[16,256]{1,0:T(8,128)S(1)}, f32[16,256]{1,0:T(8,128)S(1)}, u32[]{:S(2)}, u32[]{:S(2)}) collective-permute-start(f32[16,256]{1,0:T(8,128)S(1)} %add.193), channel_id=1, source_target_pairs={{0,64},{16,208},{32,96},{48,240},{64,0},{80,144},{96,32},{112,176}... | collective-permute-start | bytes 49160 | tf_op jit(solution)/shard_map/ppermute | solution.py:247
  196.8 5.3 %collective-permute-start.41 = (f32[16,256]{1,0:T(8,128)S(1)}, f32[16,256]{1,0:T(8,128)S(1)}, u32[]{:S(2)}, u32[]{:S(2)}) collective-permute-start(f32[16,256]{1,0:T(8,128)S(1)} %add.193), channel_id=1, source_target_pairs={{0,32},{16,176},{32,0},{48,144},{64,96},{80,240},{96,64},{112,208}... | collective-permute-start | bytes 49160 | tf_op jit(solution)/shard_map/ppermute | solution.py:247
  202.3 5.3 %collective-permute-start.45 = (f32[16,256]{1,0:T(8,128)S(1)}, f32[16,256]{1,0:T(8,128)S(1)}, u32[]{:S(2)}, u32[]{:S(2)}) collective-permute-start(f32[16,256]{1,0:T(8,128)S(1)} %add_add_fusion.3), channel_id=1, source_target_pairs={{0,8},{4,12},{8,0},{12,4},{1,9},{5,13},{9,1},{13,5},{2,10},{6,14},... | collective-permute-start | bytes 49160 | tf_op jit(solution)/shard_map/ppermute | solution.py:251
  208.7 5.0 %collective-permute-start.49 = (f32[16,256]{1,0:T(8,128)S(1)}, f32[16,256]{1,0:T(8,128)S(1)}, u32[]{:S(2)}, u32[]{:S(2)}) collective-permute-start(f32[16,256]{1,0:T(8,128)S(1)} %add_add_fusion.2), channel_id=1, source_target_pairs={{0,3},{1,2},{2,1},{3,0},{4,7},{5,6},{6,5},{7,4},{8,11},{9,10},{10,... | collective-permute-start | bytes 49160 | tf_op jit(solution)/shard_map/ppermute | solution.py:251
  210.9 5.2 %collective-permute-start.48 = (f32[16,256]{1,0:T(8,128)S(1)}, f32[16,256]{1,0:T(8,128)S(1)}, u32[]{:S(2)}, u32[]{:S(2)}) collective-permute-start(f32[16,256]{1,0:T(8,128)S(1)} %add_add_fusion.2), channel_id=1, source_target_pairs={{0,2},{1,3},{2,0},{3,1},{4,6},{5,7},{6,4},{7,5},{8,10},{9,11},{10,... | collective-permute-start | bytes 49160 | tf_op jit(solution)/shard_map/ppermute | solution.py:251
  (24 other events, 161.9 us)
Sparse Core Ops, SparseCore 0:
  11.7 45.9 all-gather.2
  167.9 46.4 reduce-scatter.1

commit v4 on v2

--- a/solution.py
+++ b/solution.py
@@ -138,8 +138,17 @@
     out_ref[...] = cams - terms[:blocks] - terms[blocks:]
 
 
-def answer_kernel(rhs_ref, s1_ref, s2_ref, s3_ref, out_ref):
-    out_ref[...] = minres(rhs_ref[...], [s1_ref[...], s2_ref[...], s3_ref[...]])
+def answer_kernel(strip, place_ref, rhs_ref, s1_ref, s2_ref, s3_ref, own_rhs_ref, own_ref):
+    rhs = rhs_ref[...]
+    answer = minres(rhs, [s1_ref[...], s2_ref[...], s3_ref[...]])
+    rows = lax.broadcasted_iota(jnp.int32, rhs.shape, 0)
+    for value, ref in ((rhs, own_rhs_ref), (answer, own_ref)):
+        line = jnp.sum(jnp.where(rows == 2 * place_ref[0] + place_ref[1], value, 0.0), axis=0, keepdims=True)
+        for r in range(rhs.shape[1] // strip):
+
+            @pl.when(place_ref[2] == r)
+            def _():
+                ref[...] = line[:, r * strip : (r + 1) * strip]
 
 
 def chosen(picks, terms):
@@ -150,14 +159,16 @@
     return value
 
 
-def tile_kernel(slots, blocks, width, strip, fine, place_ref, got_ref, cam_ref, own_ref, peer_ref, acc_ref, row_ref, col_ref):
+def tile_kernel(slots, blocks, width, strip, parts, place_ref, got_ref, cam_ref, own_ref, peer_ref, acc_ref, *operands):
     z_idx, core_idx, row_idx, col_idx = place_ref[0], place_ref[1], place_ref[2], place_ref[3]
     sources, _, points = got_ref.shape
     half, col_count = own_ref.shape
     col_blocks = col_count // width
     base_aux = 3 * slots * width
-
-    @pl.when(pl.program_id(0) == 0)
+    fine = 64
+    step = pl.program_id(0)
+
+    @pl.when(step == 0)
     def _():
         own_ref[...] = jnp.zeros_like(own_ref)
         acc_ref[...] = jnp.zeros_like(acc_ref)
@@ -168,48 +179,66 @@
                 start = pl.multiple_of(z_idx * strip, strip)
                 own_ref[pl.ds(start, strip), c * width : (c + 1) * width] = cam_ref[...]
 
-    for s in range(sources):
-        aux = got_ref[s, base_aux : base_aux + AUX, :].astype(jnp.float32)
-        vis = [aux[k : k + 1, :] for k in range(slots)]
-        inv = [aux[slots + e : slots + e + 1, :] for e in range(6)]
-
-        def picks_of(block, one):
-            block = block.astype(jnp.float32)
-            return [jnp.where(v == block, one, 0.0).astype(jnp.bfloat16) for v in vis]
-
-        col_picks = [picks_of(col_idx * col_blocks + c, 1.0) for c in range(col_blocks)]
-
-        @pl.loop(0, width // fine)
-        def _(h):
+    def build(part, row_ref, col_ref):
+        for s in range(sources):
+            aux = got_ref[s, base_aux : base_aux + AUX, :].astype(jnp.float32)
+            vis = [aux[k : k + 1, :] for k in range(slots)]
+            inv = [aux[slots + e : slots + e + 1, :] for e in range(6)]
+
+            def picks_of(block, one):
+                block = block.astype(jnp.float32)
+                return [jnp.where(v == block, one, 0.0).astype(jnp.bfloat16) for v in vis]
+
+            col_picks = [picks_of(col_idx * col_blocks + c, 1.0) for c in range(col_blocks)]
+            for h in range(0, width // parts, fine):
+                terms = []
+                for at in range(3 * slots):
+                    start = pl.multiple_of(at * width + part * (width // parts) + h, fine)
+                    terms.append(got_ref[s, pl.ds(start, fine), :])
+                for c in range(col_blocks):
+                    rows = [chosen(col_picks[c], terms[a::3]).astype(jnp.float32) for a in range(3)]
+                    start = pl.multiple_of(c * width + part * (width // parts) + h, fine)
+                    for a, z in enumerate(apply_inverse(inv, rows)):
+                        at = (a * sources + s) * points
+                        col_ref[pl.ds(start, fine), at : at + points] = z.astype(jnp.bfloat16)
+            deep = strip // parts
             terms = []
             for at in range(3 * slots):
-                start = pl.multiple_of(at * width + h * fine, fine)
-                terms.append(got_ref[s, pl.ds(start, fine), :])
-            for c in range(col_blocks):
-                rows = [chosen(col_picks[c], terms[a::3]).astype(jnp.float32) for a in range(3)]
-                start = pl.multiple_of(c * width + h * fine, fine)
-                for a, z in enumerate(apply_inverse(inv, rows)):
-                    at = (a * sources + s) * points
-                    col_ref[pl.ds(start, fine), at : at + points] = z.astype(jnp.bfloat16)
-
-        @pl.loop(0, strip // fine)
-        def _(h):
-            terms = []
-            for at in range(3 * slots):
-                start = pl.multiple_of(at * width + row_idx * strip + h * fine, fine)
-                terms.append(got_ref[s, pl.ds(start, fine), :])
+                start = pl.multiple_of(at * width + row_idx * strip + part * deep, deep)
+                terms.append(got_ref[s, pl.ds(start, deep), :])
             for b in range(blocks):
                 other = b >= blocks // 2
                 picks = picks_of(2 * (b % (blocks // 2)) + (1 - core_idx if other else core_idx), -1.0)
-                start = pl.multiple_of(b * strip + h * fine, fine)
+                start = pl.multiple_of(b * strip + part * deep, deep)
                 for a in range(3):
                     at = (a * sources + s) * points
-                    row_ref[pl.ds(start, fine), at : at + points] = chosen(picks, terms[a::3])
-
-    acc_ref[...] += lax.dot_general(row_ref[half:, :], col_ref[...], NT, preferred_element_type=jnp.float32)
-    own_ref[...] += lax.dot_general(row_ref[:half, :], col_ref[...], NT, preferred_element_type=jnp.float32)
-
-    @pl.when(pl.program_id(0) == pl.num_programs(0) - 1)
+                    row_ref[pl.ds(start, deep), at : at + points] = chosen(picks, terms[a::3])
+
+    def multiply(part, row_ref, col_ref):
+        span = col_count // parts
+        cols = pl.ds(pl.multiple_of(part * span, span), span)
+        terms = lax.dot_general(row_ref[...], col_ref[cols, :], NT, preferred_element_type=jnp.float32)
+        own_ref[:, cols] += terms[:half]
+        acc_ref[:, cols] += terms[half:]
+
+    even, odd = operands[:2], operands[2:]
+
+    @pl.when(step == 0)
+    def _():
+        @pl.loop(0, parts)
+        def _(part):
+            build(part, *even)
+
+    for parity, ready, coming in ((1, even, odd), (0, odd, even)):
+
+        @pl.when((step > 0) & (step % 2 == parity))
+        def _():
+            @pl.loop(0, parts)
+            def _(part):
+                multiply(part, *ready)
+                build(part, *coming)
+
+    @pl.when(step == pl.num_programs(0) - 1)
     def _():
         peer_ref[...] = acc_ref[...].astype(jnp.bfloat16)
 
@@ -224,11 +253,13 @@
     return value + lax.ppermute(value, "core", [(0, 1), (1, 0)])
 
 
-def all_sum(value, n_z, n_row, n_col):
+def all_sum(value, n_z, n_row, n_col, between=None):
     value = core_sum(value)
     far = n_z // 2
     pairs = [[(2 * z + c, 2 * (z ^ (j + c * far)) + c) for z in range(n_z) for c in range(2)] for j in range(far)]
     value = tree([lax.ppermute(value, ("z", "core"), p) for p in pairs])
+    if between is not None:
+        value = between(value)
     for axis, size in (("row", n_row), ("col", n_col)):
         swaps = [lax.ppermute(value, axis, [(i, i ^ b) for i in range(size)]) for b in range(1, size)]
         value = tree([value] + swaps)
@@ -265,6 +296,7 @@
     vmem = pl.BlockSpec(memory_space=pltpu.VMEM)
     smem = pl.BlockSpec(memory_space=pltpu.SMEM)
     vec = jax.ShapeDtypeStruct((blocks, width), jnp.float32)
+    small = pltpu.CompilerParams(vmem_limit_bytes=16 * 1024 * 1024)
 
     send, zw, part = pl.pallas_call(
         functools.partial(prepare_kernel, slots, blocks),
@@ -275,6 +307,7 @@
         ),
         in_specs=[vmem] * 5,
         out_specs=(vmem,) * 3,
+        compiler_params=small,
         name="prepare",
     )(w_flat, visibility, inverses, grad_points, cams_placed)
 
@@ -286,30 +319,23 @@
             out_shape=vec,
             in_specs=[smem] + [vmem] * (4 + len(known)),
             out_specs=vmem,
+            compiler_params=small,
             name="product",
         )(place, visibility, w_flat, zw, cam_wide, *known)
 
-    def reduce_all(value):
-        return all_sum(value, n_z, n_row, n_col)
-
-    rhs = reduce_all(part)
-    known = [rhs]
-    for _ in range(1, ITERS):
-        known.append(reduce_all(product(known)))
-    got, known = lax.optimization_barrier((got, known))
-
     pair = 2
     half = set_rows // 2
-    own_half, peer_half = pl.pallas_call(
-        functools.partial(tile_kernel, slots, blocks, width, strip, 64),
+    steps = shards // pair
+    make_halves = pl.pallas_call(
+        functools.partial(tile_kernel, slots, blocks, width, strip, 2),
         out_shape=(
             jax.ShapeDtypeStruct((half, col_count), jnp.float32),
             jax.ShapeDtypeStruct((half, col_count), jnp.bfloat16),
         ),
-        grid=(shards // pair,),
+        grid=(steps + 1,),
         in_specs=[
             smem,
-            pl.BlockSpec((pair, send_rows, points), lambda i: (i, 0, 0)),
+            pl.BlockSpec((pair, send_rows, points), lambda i: (jnp.minimum(i, steps - 1), 0, 0)),
             pl.BlockSpec((strip, width), lambda i: (0, 0)),
         ],
         out_specs=(
@@ -320,9 +346,11 @@
             pltpu.VMEM((half, col_count), jnp.float32),
             pltpu.VMEM((set_rows, 3 * pair * points), jnp.bfloat16),
             pltpu.VMEM((col_count, 3 * pair * points), jnp.bfloat16),
+            pltpu.VMEM((set_rows, 3 * pair * points), jnp.bfloat16),
+            pltpu.VMEM((col_count, 3 * pair * points), jnp.bfloat16),
         ],
         compiler_params=pltpu.CompilerParams(
-            dimension_semantics=("arbitrary",), vmem_limit_bytes=56 * 1024 * 1024
+            dimension_semantics=("arbitrary",), vmem_limit_bytes=52 * 1024 * 1024
         ),
         cost_estimate=pl.CostEstimate(
             flops=2 * set_rows * col_count * 3 * shards * points,
@@ -330,18 +358,31 @@
             transcendentals=0,
         ),
         name="tile",
-    )(place, got, camera_blocks)
-    taken = lax.ppermute(peer_half, "core", [(0, 1), (1, 0)])
-    tile = own_half + taken.astype(jnp.float32)
-    tile, known = lax.optimization_barrier((tile, known))
-    schur = lax.psum_scatter(tile, "z", scatter_dimension=0, tiled=True)
-    known.append(reduce_all(product(known)))
-    answer = pl.pallas_call(answer_kernel, out_shape=vec, in_specs=[vmem] * 4, out_specs=vmem, name="answer")(*known)
-
-    def own(value):
-        return lax.dynamic_slice(value, (pts_idx, row_idx * strip), (1, strip)).reshape(strip)
-
-    return (schur, own(rhs), own(answer))
+    )
+
+    held = {}
+
+    def make_tile(value):
+        here, value = lax.optimization_barrier((got, value))
+        own_half, peer_half = make_halves(place, here, camera_blocks)
+        taken = lax.ppermute(peer_half, "core", [(0, 1), (1, 0)])
+        tile, value = lax.optimization_barrier((own_half + taken.astype(jnp.float32), value))
+        held["schur"] = lax.psum_scatter(tile, "z", scatter_dimension=0, tiled=True)
+        return value
+
+    known = [all_sum(part, n_z, n_row, n_col)]
+    for between in (None,) * (ITERS - 1) + (make_tile,):
+        known.append(all_sum(product(known), n_z, n_row, n_col, between))
+    own = jax.ShapeDtypeStruct((1, strip), jnp.float32)
+    own_rhs, answer = pl.pallas_call(
+        functools.partial(answer_kernel, strip),
+        out_shape=(own, own),
+        in_specs=[smem] + [vmem] * 4,
+        out_specs=(vmem, vmem),
+        compiler_params=small,
+        name="answer",
+    )(place, *known)
+    return (held["schur"], own_rhs.reshape(strip), answer.reshape(strip))
 
 
 def solution(mesh):

time: 201 us -> 203 us (level)
  Pallas kernels: 44.7 us -> 32 us
  waiting for transfers between devices: 57.3 us -> 68.7 us
  starting transfers between devices: 70.1 us -> 79.7 us
  other arithmetic: 10.8 us -> 4.35 us
    reduce_scatter x1, waiting for transfers between devices: 2.41 us -> 23.8 us  [make_tile(): held['schur'] = lax.psum_scatter(tile, 'z', scatter_dimension=0, tiled=True)]
    ppermute x8, starting transfers between devices: 9.17 us -> 17 us  [core_sum(): return value + lax.ppermute(value, 'core', [(0, 1), (1, 0)])]
    ppermute x16, waiting for transfers between devices: 16.7 us -> 10 us  [all_sum(): value = tree([lax.ppermute(value, ('z', 'core'), p) for p in pairs])]
    ppermute x1, starting transfers between devices: 0.34 us -> 6.99 us  [make_tile(): taken = lax.ppermute(peer_half, 'core', [(0, 1), (1, 0)])]
    pallas_call x2, Pallas kernels: 33.2 us -> 26.6 us  [the longest x1 24.7 us: make_tile(): own_half, peer_half = make_halves(place, here, camera_blocks)]
    add x8, other arithmetic: 5.31 us -> 0.03 us  [core_sum(): return value + lax.ppermute(value, 'core', [(0, 1), (1, 0)])]
    pallas_call x3, Pallas kernels: 8.68 us -> 3.98 us  [product(): pl.pallas_call(functools.partial(product_kernel, slots, blocks, len(known...]
    ppermute x24, waiting for transfers between devices: 29.2 us -> 25.3 us  [all_sum(): lax.ppermute(value, axis, [(i, i ^ b) for i in range(size)])]
  transfers between devices with their start and end apart: 51 -> 51, of which waited for: 36 -> 34; matrix products, arithmetic and copies ran while one was open for 4% -> 0% of each run, Pallas kernels for 5% -> 3%
where the time goes in v4:
time: 203 us; the launch traced here: 202 us
  starting transfers between devices  79.7 us (39%)
  waiting for transfers between devices  68.7 us (34%)
  Pallas kernels  32 us (16%)
  between operations  14.3 us (7%)
  other arithmetic  4.35 us (2%)
  local copies, waits for them, and re-layouts  3.29 us (2%)
    ppermute x24, starting transfers between devices, all_sum(): lax.ppermute(value, axis, [(i, i ^ b) for i in range(size)])  33.4 us
    ppermute x24, waiting for transfers between devices, all_sum(): lax.ppermute(value, axis, [(i, i ^ b) for i in range(size)])  25.3 us
    pallas_call x1, Pallas kernels, make_tile(): own_half, peer_half = make_halves(place, here, camera_blocks)  24.7 us
    reduce_scatter x1, waiting for transfers between devices, make_tile(): held['schur'] = lax.psum_scatter(tile, 'z', scatter_dimension=0, tiled=True)  23.8 us
    ppermute x16, starting transfers between devices, all_sum(): value = tree([lax.ppermute(value, ('z', 'core'), p) for p in pairs])  22.2 us
    ppermute x8, starting transfers between devices, core_sum(): return value + lax.ppermute(value, 'core', [(0, 1), (1, 0)])  17 us
    ppermute x16, waiting for transfers between devices, all_sum(): value = tree([lax.ppermute(value, ('z', 'core'), p) for p in pairs])  10 us
    ppermute x8, waiting for transfers between devices, core_sum(): return value + lax.ppermute(value, 'core', [(0, 1), (1, 0)])  7.3 us
  transfers between devices with their start and end apart: 51, of which 34 were waited for; matrix products, arithmetic and copies ran while one was open for 0% of the time, Pallas kernels for 3%

profile of v4, /device:TPU:2, one launch (start us, length us, event | category | flops | bytes accessed | tf_op | source)
XLA Modules:
  0.0 202.3 jit_solution(3590139901461780621)
XLA Ops:
  14.0 4.6 %collective-permute-start.4 = (f32[16,256]{1,0:T(8,128)S(1)}, f32[16,256]{1,0:T(8,128)S(1)}, u32[]{:S(2)}, u32[]{:S(2)}) collective-permute-start(f32[16,256]{1,0:T(8,128)S(1)} %add.151), channel_id=1, source_target_pairs={{0,96},{16,240},{32,64},{48,208},{64,32},{80,176},{96,0},{112,144}... | collective-permute-start | bytes 49160 | tf_op jit(solution)/shard_map/ppermute | solution.py:260
  20.4 2.9 %collective-permute-done.3 = f32[16,256]{1,0:T(8,128)S(1)} collective-permute-done((f32[16,256]{1,0:T(8,128)S(1)}, f32[16,256]{1,0:T(8,128)S(1)}, u32[]{:S(2)}, u32[]{:S(2)}) %collective-permute-start.3) | collective-permute-done | bytes 16416 | tf_op jit(solution)/shard_map/ppermute | solution.py:260
  23.3 1.6 collective-permute-start.7
  27.5 2.6 %collective-permute-done.6 = f32[16,256]{1,0:T(8,128)S(1)} collective-permute-done((f32[16,256]{1,0:T(8,128)S(1)}, f32[16,256]{1,0:T(8,128)S(1)}, u32[]{:S(2)}, u32[]{:S(2)}) %collective-permute-start.6) | collective-permute-done | bytes 16416 | tf_op jit(solution)/shard_map/ppermute | solution.py:264
  30.2 3.1 %collective-permute-start.10 = (f32[16,256]{1,0:T(8,128)S(1)}, f32[16,256]{1,0:T(8,128)S(1)}, u32[]{:S(2)}, u32[]{:S(2)}) collective-permute-start(f32[16,256]{1,0:T(8,128)S(1)} %add_add_fusion.10), channel_id=1, source_target_pairs={{0,3},{1,2},{2,1},{3,0},{4,7},{5,6},{6,5},{7,4},{8,11},{9,10},{10,... | collective-permute-start | bytes 49160 | tf_op jit(solution)/shard_map/ppermute | solution.py:264
  35.5 3.3 %collective-permute-done.9 = f32[16,256]{1,0:T(8,128)S(1)} collective-permute-done((f32[16,256]{1,0:T(8,128)S(1)}, f32[16,256]{1,0:T(8,128)S(1)}, u32[]{:S(2)}, u32[]{:S(2)}) %collective-permute-start.9) | collective-permute-done | bytes 16416 | tf_op jit(solution)/shard_map/ppermute | solution.py:264
  38.8 6.6 %collective-permute-start.11 = (f32[16,256]{1,0:T(8,128)S(1)}, f32[16,256]{1,0:T(8,128)S(1)}, u32[]{:S(2)}, u32[]{:S(2)}) collective-permute-start(f32[16,256]{1,0:T(8,128)S(1)} %add_add_fusion.9), channel_id=1, source_target_pairs={{0,16},{16,0},{1,17},{17,1},{2,18},{18,2},{3,19},{19,3},{4,20},{20... | collective-permute-start | bytes 49160 | tf_op jit(solution)/shard_map/ppermute | solution.py:253
  48.7 2.3 %collective-permute-start.16 = (f32[16,256]{1,0:T(8,128)S(1)}, f32[16,256]{1,0:T(8,128)S(1)}, u32[]{:S(2)}, u32[]{:S(2)}) collective-permute-start(f32[16,256]{1,0:T(8,128)S(1)} %add.162), channel_id=1, source_target_pairs={{0,96},{16,240},{32,64},{48,208},{64,32},{80,176},{96,0},{112,144}... | collective-permute-start | bytes 49160 | tf_op jit(solution)/shard_map/ppermute | solution.py:260
  56.0 1.7 collective-permute-start.19
  57.7 1.8 collective-permute-start.18
  60.2 3.1 %collective-permute-done.18 = f32[16,256]{1,0:T(8,128)S(1)} collective-permute-done((f32[16,256]{1,0:T(8,128)S(1)}, f32[16,256]{1,0:T(8,128)S(1)}, u32[]{:S(2)}, u32[]{:S(2)}) %collective-permute-start.18) | collective-permute-done | bytes 16416 | tf_op jit(solution)/shard_map/ppermute | solution.py:264
  68.9 1.7 collective-permute-done.21
  70.6 4.5 %collective-permute-start.23 = (f32[16,256]{1,0:T(8,128)S(1)}, f32[16,256]{1,0:T(8,128)S(1)}, u32[]{:S(2)}, u32[]{:S(2)}) collective-permute-start(f32[16,256]{1,0:T(8,128)S(1)} %add_add_fusion.6), channel_id=1, source_target_pairs={{0,16},{16,0},{1,17},{17,1},{2,18},{18,2},{3,19},{19,3},{4,20},{20... | collective-permute-start | bytes 49160 | tf_op jit(solution)/shard_map/ppermute | solution.py:253
  78.5 1.9 collective-permute-start.28
  80.6 2.3 %collective-permute-start.26 = (f32[16,256]{1,0:T(8,128)S(1)}, f32[16,256]{1,0:T(8,128)S(1)}, u32[]{:S(2)}, u32[]{:S(2)}) collective-permute-start(f32[16,256]{1,0:T(8,128)S(1)} %add.173), channel_id=1, source_target_pairs={{0,32},{16,176},{32,0},{48,144},{64,96},{80,240},{96,64},{112,208}... | collective-permute-start | bytes 49160 | tf_op jit(solution)/shard_map/ppermute | solution.py:260
  86.2 1.9 collective-permute-start.30
  89.3 2.5 %collective-permute-done.30 = f32[16,256]{1,0:T(8,128)S(1)} collective-permute-done((f32[16,256]{1,0:T(8,128)S(1)}, f32[16,256]{1,0:T(8,128)S(1)}, u32[]{:S(2)}, u32[]{:S(2)}) %collective-permute-start.30) | collective-permute-done | bytes 16416 | tf_op jit(solution)/shard_map/ppermute | solution.py:264
  92.2 2.1 %collective-permute-start.34 = (f32[16,256]{1,0:T(8,128)S(1)}, f32[16,256]{1,0:T(8,128)S(1)}, u32[]{:S(2)}, u32[]{:S(2)}) collective-permute-start(f32[16,256]{1,0:T(8,128)S(1)} %add_add_fusion.4), channel_id=1, source_target_pairs={{0,3},{1,2},{2,1},{3,0},{4,7},{5,6},{6,5},{7,4},{8,11},{9,10},{10,... | collective-permute-start | bytes 49160 | tf_op jit(solution)/shard_map/ppermute | solution.py:264
  97.6 2.3 %collective-permute-done.33 = f32[16,256]{1,0:T(8,128)S(1)} collective-permute-done((f32[16,256]{1,0:T(8,128)S(1)}, f32[16,256]{1,0:T(8,128)S(1)}, u32[]{:S(2)}, u32[]{:S(2)}) %collective-permute-start.33) | collective-permute-done | bytes 16416 | tf_op jit(solution)/shard_map/ppermute | solution.py:264
  99.9 4.6 %collective-permute-start.35 = (f32[16,256]{1,0:T(8,128)S(1)}, f32[16,256]{1,0:T(8,128)S(1)}, u32[]{:S(2)}, u32[]{:S(2)}) collective-permute-start(f32[16,256]{1,0:T(8,128)S(1)} %add_add_fusion.3), channel_id=1, source_target_pairs={{0,16},{16,0},{1,17},{17,1},{2,18},{18,2},{3,19},{19,3},{4,20},{20... | collective-permute-start | bytes 49160 | tf_op jit(solution)/shard_map/ppermute | solution.py:253
  108.1 2.0 %collective-permute-start.40 = (f32[16,256]{1,0:T(8,128)S(1)}, f32[16,256]{1,0:T(8,128)S(1)}, u32[]{:S(2)}, u32[]{:S(2)}) collective-permute-start(f32[16,256]{1,0:T(8,128)S(1)} %add.184), channel_id=1, source_target_pairs={{0,96},{16,240},{32,64},{48,208},{64,32},{80,176},{96,0},{112,144}... | collective-permute-start | bytes 49160 | tf_op jit(solution)/shard_map/ppermute | solution.py:260
  110.1 3.3 %collective-permute-start.39 = (f32[16,256]{1,0:T(8,128)S(1)}, f32[16,256]{1,0:T(8,128)S(1)}, u32[]{:S(2)}, u32[]{:S(2)}) collective-permute-start(f32[16,256]{1,0:T(8,128)S(1)} %add.184), channel_id=1, source_target_pairs={{0,64},{16,208},{32,96},{48,240},{64,0},{80,144},{96,32},{112,176}... | collective-permute-start | bytes 49160 | tf_op jit(solution)/shard_map/ppermute | solution.py:260
  115.3 1.9 collective-permute-done.38
  117.2 24.7 %tile.8 = (f32[512,1024]{1,0:T(8,128)}, bf16[512,1024]{1,0:T(8,128)(2,1)S(1)}) custom-call(s32[4]{0:T(128)S(1)} %pad_add_fusion.refs_0_.place_ref, bf16[16,3088,128]{2,1,0:T(8,128)(2,1)} %bitcast.12, f32[64,256]{1,0:T(8,128)S(1)} %copy-done.2), custom_call_target="tpu_custom_call" | custom-call | flops 12884901888 | bytes 16842752 | tf_op jit(solution)/shard_map/tile/pallas_call | solution.py:367
  141.9 7.0 %collective-permute-start.41 = (bf16[512,1024]{1,0:T(8,128)(2,1)S(1)}, bf16[512,1024]{1,0:T(8,128)(2,1)S(1)}, u32[]{:S(2)}, u32[]{:S(2)}) collective-permute-start(bf16[512,1024]{1,0:T(8,128)(2,1)S(1)} %get-tuple-element.19), channel_id=1, source_target_pairs={{0,16},{16,0},{1,17},{17,1},{2,18},{18,2},{3,19},{19,3},{4,20},{20... | collective-permute-start | bytes 3145736 | tf_op jit(solution)/shard_map/ppermute | solution.py:368
  148.9 2.3 %collective-permute-done.41 = bf16[512,1024]{1,0:T(8,128)(2,1)S(1)} collective-permute-done((bf16[512,1024]{1,0:T(8,128)(2,1)S(1)}, bf16[512,1024]{1,0:T(8,128)(2,1)S(1)}, u32[]{:S(2)}, u32[]{:S(2)}) %collective-permute-start.41) | collective-permute-done | bytes 1048608 | tf_op jit(solution)/shard_map/ppermute | solution.py:368
  151.2 3.4 %convert_add_fusion = f32[512,1024]{1,0:T(8,128)} fusion(f32[512,1024]{1,0:T(8,128)} %get-tuple-element.18, bf16[512,1024]{1,0:T(8,128)(2,1)S(1)} %collective-permute-done.41), kind=kLoop, calls=%fused_computation | loop fusion | flops 1048576 | bytes 5242880 | tf_op jit(solution)/shard_map/add | solution.py:369
  156.0 2.1 %collective-permute-start.43 = (f32[16,256]{1,0:T(8,128)S(1)}, f32[16,256]{1,0:T(8,128)S(1)}, u32[]{:S(2)}, u32[]{:S(2)}) collective-permute-start(f32[16,256]{1,0:T(8,128)S(1)} %add_add_fusion.2), channel_id=1, source_target_pairs={{0,8},{4,12},{8,0},{12,4},{1,9},{5,13},{9,1},{13,5},{2,10},{6,14},... | collective-permute-start | bytes 49160 | tf_op jit(solution)/shard_map/ppermute | solution.py:264
  158.8 2.4 %collective-permute-done.43 = f32[16,256]{1,0:T(8,128)S(1)} collective-permute-done((f32[16,256]{1,0:T(8,128)S(1)}, f32[16,256]{1,0:T(8,128)S(1)}, u32[]{:S(2)}, u32[]{:S(2)}) %collective-permute-start.43) | collective-permute-done | bytes 16416 | tf_op jit(solution)/shard_map/ppermute | solution.py:264
  166.8 1.7 collective-permute-done.46
  169.8 1.9 answer.1
  171.7 23.8 %reduce-scatter.2.cloned.1.call-done = f32[64,1024]{1,0:T(8,128)} async-done(((f32[512,1024]{1,0:T(8,128)}), f32[64,1024]{1,0:T(8,128)}) %reduce-scatter.2.cloned.1.call-update) | async-done | bytes 262160 | tf_op jit(solution)/shard_map/reduce_scatter | solution.py:370
  (122 shorter events, 54.2 us)
Async XLA Ops:
  7.2 110.0 %all-gather.3.cloned.1.call-start = ((), (), s32[]{:S(2)}) async-start(), calls=%async_computation.2 | async-start | bytes 13438976 | tf_op jit(solution)/shard_map/all_gather | solution.py:314
  12.7 182.7 %reduce-scatter.2.cloned.1.call-start = ((), (), s32[]{:S(2)}) async-start(), calls=%async_computation.1 | async-start | bytes 2359296 | tf_op jit(solution)/shard_map/reduce_scatter | solution.py:370
  14.0 6.3 %collective-permute-start.4 = (f32[16,256]{1,0:T(8,128)S(1)}, f32[16,256]{1,0:T(8,128)S(1)}, u32[]{:S(2)}, u32[]{:S(2)}) collective-permute-start(f32[16,256]{1,0:T(8,128)S(1)} %add.151), channel_id=1, source_target_pairs={{0,96},{16,240},{32,64},{48,208},{64,32},{80,176},{96,0},{112,144}... | collective-permute-start | bytes 49160 | tf_op jit(solution)/shard_map/ppermute | solution.py:260
  18.7 4.6 %collective-permute-start.3 = (f32[16,256]{1,0:T(8,128)S(1)}, f32[16,256]{1,0:T(8,128)S(1)}, u32[]{:S(2)}, u32[]{:S(2)}) collective-permute-start(f32[16,256]{1,0:T(8,128)S(1)} %add.151), channel_id=1, source_target_pairs={{0,64},{16,208},{32,96},{48,240},{64,0},{80,144},{96,32},{112,176}... | collective-permute-start | bytes 49160 | tf_op jit(solution)/shard_map/ppermute | solution.py:260
  18.7 4.6 %collective-permute-start.2 = (f32[16,256]{1,0:T(8,128)S(1)}, f32[16,256]{1,0:T(8,128)S(1)}, u32[]{:S(2)}, u32[]{:S(2)}) collective-permute-start(f32[16,256]{1,0:T(8,128)S(1)} %add.151), channel_id=1, source_target_pairs={{0,32},{16,176},{32,0},{48,144},{64,96},{80,240},{96,64},{112,208}... | collective-permute-start | bytes 49160 | tf_op jit(solution)/shard_map/ppermute | solution.py:260
  24.9 5.2 %collective-permute-start.6 = (f32[16,256]{1,0:T(8,128)S(1)}, f32[16,256]{1,0:T(8,128)S(1)}, u32[]{:S(2)}, u32[]{:S(2)}) collective-permute-start(f32[16,256]{1,0:T(8,128)S(1)} %add_add_fusion.11), channel_id=1, source_target_pairs={{0,8},{4,12},{8,0},{12,4},{1,9},{5,13},{9,1},{13,5},{2,10},{6,14},... | collective-permute-start | bytes 49160 | tf_op jit(solution)/shard_map/ppermute | solution.py:264
  30.2 5.4 %collective-permute-start.10 = (f32[16,256]{1,0:T(8,128)S(1)}, f32[16,256]{1,0:T(8,128)S(1)}, u32[]{:S(2)}, u32[]{:S(2)}) collective-permute-start(f32[16,256]{1,0:T(8,128)S(1)} %add_add_fusion.10), channel_id=1, source_target_pairs={{0,3},{1,2},{2,1},{3,0},{4,7},{5,6},{6,5},{7,4},{8,11},{9,10},{10,... | collective-permute-start | bytes 49160 | tf_op jit(solution)/shard_map/ppermute | solution.py:264
  33.3 5.6 %collective-permute-start.9 = (f32[16,256]{1,0:T(8,128)S(1)}, f32[16,256]{1,0:T(8,128)S(1)}, u32[]{:S(2)}, u32[]{:S(2)}) collective-permute-start(f32[16,256]{1,0:T(8,128)S(1)} %add_add_fusion.10), channel_id=1, source_target_pairs={{0,2},{1,3},{2,0},{3,1},{4,6},{5,7},{6,4},{7,5},{8,10},{9,11},{10,... | collective-permute-start | bytes 49160 | tf_op jit(solution)/shard_map/ppermute | solution.py:264
  33.9 4.9 %collective-permute-start.8 = (f32[16,256]{1,0:T(8,128)S(1)}, f32[16,256]{1,0:T(8,128)S(1)}, u32[]{:S(2)}, u32[]{:S(2)}) collective-permute-start(f32[16,256]{1,0:T(8,128)S(1)} %add_add_fusion.10), channel_id=1, source_target_pairs={{0,1},{1,0},{2,3},{3,2},{4,5},{5,4},{6,7},{7,6},{8,9},{9,8},{10,11... | collective-permute-start | bytes 49160 | tf_op jit(solution)/shard_map/ppermute | solution.py:264
  38.8 7.4 %collective-permute-start.11 = (f32[16,256]{1,0:T(8,128)S(1)}, f32[16,256]{1,0:T(8,128)S(1)}, u32[]{:S(2)}, u32[]{:S(2)}) collective-permute-start(f32[16,256]{1,0:T(8,128)S(1)} %add_add_fusion.9), channel_id=1, source_target_pairs={{0,16},{16,0},{1,17},{17,1},{2,18},{18,2},{3,19},{19,3},{4,20},{20... | collective-permute-start | bytes 49160 | tf_op jit(solution)/shard_map/ppermute | solution.py:253
  48.7 5.6 %collective-permute-start.16 = (f32[16,256]{1,0:T(8,128)S(1)}, f32[16,256]{1,0:T(8,128)S(1)}, u32[]{:S(2)}, u32[]{:S(2)}) collective-permute-start(f32[16,256]{1,0:T(8,128)S(1)} %add.162), channel_id=1, source_target_pairs={{0,96},{16,240},{32,64},{48,208},{64,32},{80,176},{96,0},{112,144}... | collective-permute-start | bytes 49160 | tf_op jit(solution)/shard_map/ppermute | solution.py:260
  50.9 4.6 %collective-permute-start.15 = (f32[16,256]{1,0:T(8,128)S(1)}, f32[16,256]{1,0:T(8,128)S(1)}, u32[]{:S(2)}, u32[]{:S(2)}) collective-permute-start(f32[16,256]{1,0:T(8,128)S(1)} %add.162), channel_id=1, source_target_pairs={{0,64},{16,208},{32,96},{48,240},{64,0},{80,144},{96,32},{112,176}... | collective-permute-start | bytes 49160 | tf_op jit(solution)/shard_map/ppermute | solution.py:260
  57.7 5.6 %collective-permute-start.18 = (f32[16,256]{1,0:T(8,128)S(1)}, f32[16,256]{1,0:T(8,128)S(1)}, u32[]{:S(2)}, u32[]{:S(2)}) collective-permute-start(f32[16,256]{1,0:T(8,128)S(1)} %add_add_fusion.8), channel_id=1, source_target_pairs={{0,8},{4,12},{8,0},{12,4},{1,9},{5,13},{9,1},{13,5},{2,10},{6,14},... | collective-permute-start | bytes 49160 | tf_op jit(solution)/shard_map/ppermute | solution.py:264
  63.6 5.3 %collective-permute-start.22 = (f32[16,256]{1,0:T(8,128)S(1)}, f32[16,256]{1,0:T(8,128)S(1)}, u32[]{:S(2)}, u32[]{:S(2)}) collective-permute-start(f32[16,256]{1,0:T(8,128)S(1)} %add_add_fusion.7), channel_id=1, source_target_pairs={{0,3},{1,2},{2,1},{3,0},{4,7},{5,6},{6,5},{7,4},{8,11},{9,10},{10,... | collective-permute-start | bytes 49160 | tf_op jit(solution)/shard_map/ppermute | solution.py:264
  65.0 5.6 %collective-permute-start.21 = (f32[16,256]{1,0:T(8,128)S(1)}, f32[16,256]{1,0:T(8,128)S(1)}, u32[]{:S(2)}, u32[]{:S(2)}) collective-permute-start(f32[16,256]{1,0:T(8,128)S(1)} %add_add_fusion.7), channel_id=1, source_target_pairs={{0,2},{1,3},{2,0},{3,1},{4,6},{5,7},{6,4},{7,5},{8,10},{9,11},{10,... | collective-permute-start | bytes 49160 | tf_op jit(solution)/shard_map/ppermute | solution.py:264
  66.3 4.3 %collective-permute-start.20 = (f32[16,256]{1,0:T(8,128)S(1)}, f32[16,256]{1,0:T(8,128)S(1)}, u32[]{:S(2)}, u32[]{:S(2)}) collective-permute-start(f32[16,256]{1,0:T(8,128)S(1)} %add_add_fusion.7), channel_id=1, source_target_pairs={{0,1},{1,0},{2,3},{3,2},{4,5},{5,4},{6,7},{7,6},{8,9},{9,8},{10,11... | collective-permute-start | bytes 49160 | tf_op jit(solution)/shard_map/ppermute | solution.py:264
  70.6 5.3 %collective-permute-start.23 = (f32[16,256]{1,0:T(8,128)S(1)}, f32[16,256]{1,0:T(8,128)S(1)}, u32[]{:S(2)}, u32[]{:S(2)}) collective-permute-start(f32[16,256]{1,0:T(8,128)S(1)} %add_add_fusion.6), channel_id=1, source_target_pairs={{0,16},{16,0},{1,17},{17,1},{2,18},{18,2},{3,19},{19,3},{4,20},{20... | collective-permute-start | bytes 49160 | tf_op jit(solution)/shard_map/ppermute | solution.py:253
  78.5 5.5 %collective-permute-start.28 = (f32[16,256]{1,0:T(8,128)S(1)}, f32[16,256]{1,0:T(8,128)S(1)}, u32[]{:S(2)}, u32[]{:S(2)}) collective-permute-start(f32[16,256]{1,0:T(8,128)S(1)} %add.173), channel_id=1, source_target_pairs={{0,96},{16,240},{32,64},{48,208},{64,32},{80,176},{96,0},{112,144}... | collective-permute-start | bytes 49160 | tf_op jit(solution)/shard_map/ppermute | solution.py:260
  80.3 4.7 %collective-permute-start.27 = (f32[16,256]{1,0:T(8,128)S(1)}, f32[16,256]{1,0:T(8,128)S(1)}, u32[]{:S(2)}, u32[]{:S(2)}) collective-permute-start(f32[16,256]{1,0:T(8,128)S(1)} %add.173), channel_id=1, source_target_pairs={{0,64},{16,208},{32,96},{48,240},{64,0},{80,144},{96,32},{112,176}... | collective-permute-start | bytes 49160 | tf_op jit(solution)/shard_map/ppermute | solution.py:260
  80.6 4.5 %collective-permute-start.26 = (f32[16,256]{1,0:T(8,128)S(1)}, f32[16,256]{1,0:T(8,128)S(1)}, u32[]{:S(2)}, u32[]{:S(2)}) collective-permute-start(f32[16,256]{1,0:T(8,128)S(1)} %add.173), channel_id=1, source_target_pairs={{0,32},{16,176},{32,0},{48,144},{64,96},{80,240},{96,64},{112,208}... | collective-permute-start | bytes 49160 | tf_op jit(solution)/shard_map/ppermute | solution.py:260
  86.2 5.6 %collective-permute-start.30 = (f32[16,256]{1,0:T(8,128)S(1)}, f32[16,256]{1,0:T(8,128)S(1)}, u32[]{:S(2)}, u32[]{:S(2)}) collective-permute-start(f32[16,256]{1,0:T(8,128)S(1)} %add_add_fusion.5), channel_id=1, source_target_pairs={{0,8},{4,12},{8,0},{12,4},{1,9},{5,13},{9,1},{13,5},{2,10},{6,14},... | collective-permute-start | bytes 49160 | tf_op jit(solution)/shard_map/ppermute | solution.py:264
  92.2 5.4 %collective-permute-start.34 = (f32[16,256]{1,0:T(8,128)S(1)}, f32[16,256]{1,0:T(8,128)S(1)}, u32[]{:S(2)}, u32[]{:S(2)}) collective-permute-start(f32[16,256]{1,0:T(8,128)S(1)} %add_add_fusion.4), channel_id=1, source_target_pairs={{0,3},{1,2},{2,1},{3,0},{4,7},{5,6},{6,5},{7,4},{8,11},{9,10},{10,... | collective-permute-start | bytes 49160 | tf_op jit(solution)/shard_map/ppermute | solution.py:264
  94.3 5.6 %collective-permute-start.33 = (f32[16,256]{1,0:T(8,128)S(1)}, f32[16,256]{1,0:T(8,128)S(1)}, u32[]{:S(2)}, u32[]{:S(2)}) collective-permute-start(f32[16,256]{1,0:T(8,128)S(1)} %add_add_fusion.4), channel_id=1, source_target_pairs={{0,2},{1,3},{2,0},{3,1},{4,6},{5,7},{6,4},{7,5},{8,10},{9,11},{10,... | collective-permute-start | bytes 49160 | tf_op jit(solution)/shard_map/ppermute | solution.py:264
  95.6 4.3 %collective-permute-start.32 = (f32[16,256]{1,0:T(8,128)S(1)}, f32[16,256]{1,0:T(8,128)S(1)}, u32[]{:S(2)}, u32[]{:S(2)}) collective-permute-start(f32[16,256]{1,0:T(8,128)S(1)} %add_add_fusion.4), channel_id=1, source_target_pairs={{0,1},{1,0},{2,3},{3,2},{4,5},{5,4},{6,7},{7,6},{8,9},{9,8},{10,11... | collective-permute-start | bytes 49160 | tf_op jit(solution)/shard_map/ppermute | solution.py:264
  99.9 5.5 %collective-permute-start.35 = (f32[16,256]{1,0:T(8,128)S(1)}, f32[16,256]{1,0:T(8,128)S(1)}, u32[]{:S(2)}, u32[]{:S(2)}) collective-permute-start(f32[16,256]{1,0:T(8,128)S(1)} %add_add_fusion.3), channel_id=1, source_target_pairs={{0,16},{16,0},{1,17},{17,1},{2,18},{18,2},{3,19},{19,3},{4,20},{20... | collective-permute-start | bytes 49160 | tf_op jit(solution)/shard_map/ppermute | solution.py:253
  108.1 6.2 %collective-permute-start.40 = (f32[16,256]{1,0:T(8,128)S(1)}, f32[16,256]{1,0:T(8,128)S(1)}, u32[]{:S(2)}, u32[]{:S(2)}) collective-permute-start(f32[16,256]{1,0:T(8,128)S(1)} %add.184), channel_id=1, source_target_pairs={{0,96},{16,240},{32,64},{48,208},{64,32},{80,176},{96,0},{112,144}... | collective-permute-start | bytes 49160 | tf_op jit(solution)/shard_map/ppermute | solution.py:260
  110.1 5.2 %collective-permute-start.39 = (f32[16,256]{1,0:T(8,128)S(1)}, f32[16,256]{1,0:T(8,128)S(1)}, u32[]{:S(2)}, u32[]{:S(2)}) collective-permute-start(f32[16,256]{1,0:T(8,128)S(1)} %add.184), channel_id=1, source_target_pairs={{0,64},{16,208},{32,96},{48,240},{64,0},{80,144},{96,32},{112,176}... | collective-permute-start | bytes 49160 | tf_op jit(solution)/shard_map/ppermute | solution.py:260
  141.9 9.3 %collective-permute-start.41 = (bf16[512,1024]{1,0:T(8,128)(2,1)S(1)}, bf16[512,1024]{1,0:T(8,128)(2,1)S(1)}, u32[]{:S(2)}, u32[]{:S(2)}) collective-permute-start(bf16[512,1024]{1,0:T(8,128)(2,1)S(1)} %get-tuple-element.19), channel_id=1, source_target_pairs={{0,16},{16,0},{1,17},{17,1},{2,18},{18,2},{3,19},{19,3},{4,20},{20... | collective-permute-start | bytes 3145736 | tf_op jit(solution)/shard_map/ppermute | solution.py:368
  154.6 4.2 %collective-permute-start.44 = (f32[16,256]{1,0:T(8,128)S(1)}, f32[16,256]{1,0:T(8,128)S(1)}, u32[]{:S(2)}, u32[]{:S(2)}) collective-permute-start(f32[16,256]{1,0:T(8,128)S(1)} %add_add_fusion.2), channel_id=1, source_target_pairs={{0,12},{4,8},{8,4},{12,0},{1,13},{5,9},{9,5},{13,1},{2,14},{6,10},... | collective-permute-start | bytes 49160 | tf_op jit(solution)/shard_map/ppermute | solution.py:264
  156.0 5.2 %collective-permute-start.43 = (f32[16,256]{1,0:T(8,128)S(1)}, f32[16,256]{1,0:T(8,128)S(1)}, u32[]{:S(2)}, u32[]{:S(2)}) collective-permute-start(f32[16,256]{1,0:T(8,128)S(1)} %add_add_fusion.2), channel_id=1, source_target_pairs={{0,8},{4,12},{8,0},{12,4},{1,9},{5,13},{9,1},{13,5},{2,10},{6,14},... | collective-permute-start | bytes 49160 | tf_op jit(solution)/shard_map/ppermute | solution.py:264
  161.8 5.0 %collective-permute-start.47 = (f32[16,256]{1,0:T(8,128)S(1)}, f32[16,256]{1,0:T(8,128)S(1)}, u32[]{:S(2)}, u32[]{:S(2)}) collective-permute-start(f32[16,256]{1,0:T(8,128)S(1)} %add_add_fusion.1), channel_id=1, source_target_pairs={{0,3},{1,2},{2,1},{3,0},{4,7},{5,6},{6,5},{7,4},{8,11},{9,10},{10,... | collective-permute-start | bytes 49160 | tf_op jit(solution)/shard_map/ppermute | solution.py:264
  163.3 5.2 %collective-permute-start.46 = (f32[16,256]{1,0:T(8,128)S(1)}, f32[16,256]{1,0:T(8,128)S(1)}, u32[]{:S(2)}, u32[]{:S(2)}) collective-permute-start(f32[16,256]{1,0:T(8,128)S(1)} %add_add_fusion.1), channel_id=1, source_target_pairs={{0,2},{1,3},{2,0},{3,1},{4,6},{5,7},{6,4},{7,5},{8,10},{9,11},{10,... | collective-permute-start | bytes 49160 | tf_op jit(solution)/shard_map/ppermute | solution.py:264
  (26 other events, 159.3 us)
Sparse Core Ops, SparseCore 0:
  12.8 100.2 all-gather.2
  154.7 40.6 reduce-scatter.1

commit v5 on v4

--- a/solution.py
+++ b/solution.py
@@ -255,15 +255,26 @@
 
 def all_sum(value, n_z, n_row, n_col, between=None):
     value = core_sum(value)
-    far = n_z // 2
-    pairs = [[(2 * z + c, 2 * (z ^ (j + c * far)) + c) for z in range(n_z) for c in range(2)] for j in range(far)]
-    value = tree([lax.ppermute(value, ("z", "core"), p) for p in pairs])
+    for axis, size, reach in (("row", n_row, n_row), ("col", n_col, n_col), ("z", n_z, min(n_z, 4))):
+        far = reach // 2
+        by_core, by_place = (1, 2) if axis == "z" else (size, 1)
+        pairs = [
+            [
+                (c * by_core + i * by_place, c * by_core + (i ^ (j + c * far)) * by_place)
+                for i in range(size)
+                for c in range(2)
+            ]
+            for j in range(far)
+        ]
+        axes = ("z", "core") if axis == "z" else ("core", axis)
+        value = core_sum(tree([lax.ppermute(value, axes, p) for p in pairs]))
     if between is not None:
         value = between(value)
-    for axis, size in (("row", n_row), ("col", n_col)):
-        swaps = [lax.ppermute(value, axis, [(i, i ^ b) for i in range(size)]) for b in range(1, size)]
-        value = tree([value] + swaps)
-    return core_sum(value)
+    bit = 4
+    while bit < n_z:
+        value = value + lax.ppermute(value, "z", [(i, i ^ bit) for i in range(n_z)])
+        bit *= 2
+    return value
 
 
 def per_device(weights, visibility, inverses, grad_points, camera_blocks, grad_cams):
@@ -307,7 +318,6 @@
         ),
         in_specs=[vmem] * 5,
         out_specs=(vmem,) * 3,
-        compiler_params=small,
         name="prepare",
     )(w_flat, visibility, inverses, grad_points, cams_placed)
 

time: 203 us -> 230 us (1.13)
  waiting for transfers between devices: 68.7 us -> 88 us
  starting transfers between devices: 79.7 us -> 87.9 us
  local copies, waits for them, and re-layouts: 3.29 us -> 0.13 us
    ppermute x8 -> x16, starting transfers between devices: 17 us -> 46.1 us  [core_sum(): return value + lax.ppermute(value, 'core', [(0, 1), (1, 0)])]
    ppermute x40 -> x28, starting transfers between devices: 55.6 us -> 41.4 us  [the longest x4 21.1 us: all_sum(): value = value + lax.ppermute(value, 'z', [(i, i ^ bit) for i in range(n_z)])]
    reduce_scatter x1, waiting for transfers between devices: 23.8 us -> 34.8 us  [make_tile(): held['schur'] = lax.psum_scatter(tile, 'z', scatter_dimension=0, tiled=True)]
    ppermute x8 -> x16, waiting for transfers between devices: 7.3 us -> 14.9 us  [core_sum(): return value + lax.ppermute(value, 'core', [(0, 1), (1, 0)])]
    ppermute x1, starting transfers between devices: 6.99 us -> 0.35 us  [make_tile(): taken = lax.ppermute(peer_half, 'core', [(0, 1), (1, 0)])]
    unnamed x14 -> x8, local copies, waits for them, and re-layouts: 3.19 us -> 0.02 us
    ppermute x40 -> x28, waiting for transfers between devices: 35.3 us -> 35.9 us  [the longest x24 26.2 us: all_sum(): value = core_sum(tree([lax.ppermute(value, axes, p) for p in pairs]))]
  transfers between devices with their start and end apart: 51 -> 47, of which waited for: 34 -> 34; matrix products, arithmetic and copies ran while one was open for 0% -> 0% of each run, Pallas kernels for 3% -> 3%
where the time goes in v5:
time: 230 us; the launch traced here: 229 us
  waiting for transfers between devices  88 us (38%)
  starting transfers between devices  87.9 us (38%)
  Pallas kernels  33.4 us (15%)
  between operations  14.3 us (6%)
  other arithmetic  5.73 us (2%)
    ppermute x16, starting transfers between devices, core_sum(): return value + lax.ppermute(value, 'core', [(0, 1), (1, 0)])  46.1 us
    reduce_scatter x1, waiting for transfers between devices, make_tile(): held['schur'] = lax.psum_scatter(tile, 'z', scatter_dimension=0, tiled=True)  34.8 us
    ppermute x24, waiting for transfers between devices, all_sum(): value = core_sum(tree([lax.ppermute(value, axes, p) for p in pairs]))  26.2 us
    pallas_call x1, Pallas kernels, make_tile(): own_half, peer_half = make_halves(place, here, camera_blocks)  24.7 us
    ppermute x4, starting transfers between devices, all_sum(): value = value + lax.ppermute(value, 'z', [(i, i ^ bit) for i in range(n_z)])  21.1 us
    ppermute x24, starting transfers between devices, all_sum(): value = core_sum(tree([lax.ppermute(value, axes, p) for p in pairs]))  20.3 us
    ppermute x16, waiting for transfers between devices, core_sum(): return value + lax.ppermute(value, 'core', [(0, 1), (1, 0)])  14.9 us
    ppermute x4, waiting for transfers between devices, all_sum(): value = value + lax.ppermute(value, 'z', [(i, i ^ bit) for i in range(n_z)])  9.75 us
  transfers between devices with their start and end apart: 47, of which 34 were waited for; matrix products, arithmetic and copies ran while one was open for 0% of the time, Pallas kernels for 3%

profile of v5, /device:TPU:2, one launch (start us, length us, event | category | flops | bytes accessed | tf_op | source)
XLA Modules:
  0.0 229.4 jit_solution(18114386416242638096)
XLA Ops:
  8.8 2.8 %prepare.1 = (bf16[3088,128]{1,0:T(8,128)(2,1)}, bf16[256,1536]{1,0:T(8,128)(2,1)}, f32[16,256]{1,0:T(8,128)}) custom-call(bf16[1536,256]{1,0:T(8,128)(2,1)} %bitcast.8, s32[4,128]{1,0:T(4,128)} %refs_1_.5, bf16[6,128]{1,0:T(8,128)(2,1)} %inv_ref.1, bf16[3,128]{1,0:T(4,128)(2,1)} %grad_ref.1, f32[16,256]{1,0:T(8,128)} %and_select_fusion.cams_ref), custom_call_target="tpu_custom_call" | custom-call | tf_op jit(solution)/shard_map/prepare/pallas_call | solution.py:312
  13.9 2.3 collective-permute-start.2
  17.9 3.4 %collective-permute-start.3 = (f32[16,256]{1,0:T(8,128)S(1)}, f32[16,256]{1,0:T(8,128)S(1)}, u32[]{:S(2)}, u32[]{:S(2)}) collective-permute-start(f32[16,256]{1,0:T(8,128)S(1)} %add.116), channel_id=1, source_target_pairs={{0,16},{16,0},{1,17},{17,1},{2,18},{18,2},{3,19},{19,3},{4,20},{20... | collective-permute-start | bytes 49160 | tf_op jit(solution)/shard_map/ppermute | solution.py:253
  25.8 5.3 %collective-permute-start.6 = (f32[16,256]{1,0:T(8,128)S(1)}, f32[16,256]{1,0:T(8,128)S(1)}, u32[]{:S(2)}, u32[]{:S(2)}) collective-permute-start(f32[16,256]{1,0:T(8,128)S(1)} %add.118), channel_id=1, source_target_pairs={{0,16},{16,0},{1,17},{17,1},{2,18},{18,2},{3,19},{19,3},{4,20},{20... | collective-permute-start | bytes 49160 | tf_op jit(solution)/shard_map/ppermute | solution.py:253
  32.0 1.9 collective-permute-start.8
  35.7 6.8 %collective-permute-start.9 = (f32[16,256]{1,0:T(8,128)S(1)}, f32[16,256]{1,0:T(8,128)S(1)}, u32[]{:S(2)}, u32[]{:S(2)}) collective-permute-start(f32[16,256]{1,0:T(8,128)S(1)} %add.120), channel_id=1, source_target_pairs={{0,16},{16,0},{1,17},{17,1},{2,18},{18,2},{3,19},{19,3},{4,20},{20... | collective-permute-start | bytes 49160 | tf_op jit(solution)/shard_map/ppermute | solution.py:253
  43.4 4.6 %collective-permute-start.10 = (f32[16,256]{1,0:T(8,128)S(1)}, f32[16,256]{1,0:T(8,128)S(1)}, u32[]{:S(2)}, u32[]{:S(2)}) collective-permute-start(f32[16,256]{1,0:T(8,128)S(1)} %add.121), channel_id=1, source_target_pairs={{0,128},{32,160},{64,192},{96,224},{128,0},{160,32},{192,64},{224,... | collective-permute-start | bytes 49160 | tf_op jit(solution)/shard_map/ppermute | solution.py:275
  48.1 2.9 %collective-permute-done.10 = f32[16,256]{1,0:T(8,128)S(1)} collective-permute-done((f32[16,256]{1,0:T(8,128)S(1)}, f32[16,256]{1,0:T(8,128)S(1)}, u32[]{:S(2)}, u32[]{:S(2)}) %collective-permute-start.10) | collective-permute-done | bytes 16416 | tf_op jit(solution)/shard_map/ppermute | solution.py:275
  57.2 3.5 %collective-permute-start.14 = (f32[16,256]{1,0:T(8,128)S(1)}, f32[16,256]{1,0:T(8,128)S(1)}, u32[]{:S(2)}, u32[]{:S(2)}) collective-permute-start(f32[16,256]{1,0:T(8,128)S(1)} %add.124), channel_id=1, source_target_pairs={{0,16},{16,0},{1,17},{17,1},{2,18},{18,2},{3,19},{19,3},{4,20},{20... | collective-permute-start | bytes 49160 | tf_op jit(solution)/shard_map/ppermute | solution.py:253
  62.2 3.4 %collective-permute-done.16 = f32[16,256]{1,0:T(8,128)S(1)} collective-permute-done((f32[16,256]{1,0:T(8,128)S(1)}, f32[16,256]{1,0:T(8,128)S(1)}, u32[]{:S(2)}, u32[]{:S(2)}) %collective-permute-start.16) | collective-permute-done | bytes 16416 | tf_op jit(solution)/shard_map/ppermute | solution.py:270
  65.6 2.6 %collective-permute-start.17 = (f32[16,256]{1,0:T(8,128)S(1)}, f32[16,256]{1,0:T(8,128)S(1)}, u32[]{:S(2)}, u32[]{:S(2)}) collective-permute-start(f32[16,256]{1,0:T(8,128)S(1)} %add.126), channel_id=1, source_target_pairs={{0,16},{16,0},{1,17},{17,1},{2,18},{18,2},{3,19},{19,3},{4,20},{20... | collective-permute-start | bytes 49160 | tf_op jit(solution)/shard_map/ppermute | solution.py:253
  69.7 3.1 %collective-permute-done.19 = f32[16,256]{1,0:T(8,128)S(1)} collective-permute-done((f32[16,256]{1,0:T(8,128)S(1)}, f32[16,256]{1,0:T(8,128)S(1)}, u32[]{:S(2)}, u32[]{:S(2)}) %collective-permute-start.19) | collective-permute-done | bytes 16416 | tf_op jit(solution)/shard_map/ppermute | solution.py:270
  72.8 2.4 %collective-permute-start.20 = (f32[16,256]{1,0:T(8,128)S(1)}, f32[16,256]{1,0:T(8,128)S(1)}, u32[]{:S(2)}, u32[]{:S(2)}) collective-permute-start(f32[16,256]{1,0:T(8,128)S(1)} %add.128), channel_id=1, source_target_pairs={{0,16},{16,0},{1,17},{17,1},{2,18},{18,2},{3,19},{19,3},{4,20},{20... | collective-permute-start | bytes 49160 | tf_op jit(solution)/shard_map/ppermute | solution.py:253
  76.1 6.2 %collective-permute-start.21 = (f32[16,256]{1,0:T(8,128)S(1)}, f32[16,256]{1,0:T(8,128)S(1)}, u32[]{:S(2)}, u32[]{:S(2)}) collective-permute-start(f32[16,256]{1,0:T(8,128)S(1)} %add.129), channel_id=1, source_target_pairs={{0,128},{32,160},{64,192},{96,224},{128,0},{160,32},{192,64},{224,... | collective-permute-start | bytes 49160 | tf_op jit(solution)/shard_map/ppermute | solution.py:275
  88.2 2.3 %collective-permute-done.24 = f32[16,256]{1,0:T(8,128)S(1)} collective-permute-done((f32[16,256]{1,0:T(8,128)S(1)}, f32[16,256]{1,0:T(8,128)S(1)}, u32[]{:S(2)}, u32[]{:S(2)}) %collective-permute-start.24) | collective-permute-done | bytes 16416 | tf_op jit(solution)/shard_map/ppermute | solution.py:270
  90.6 3.8 %collective-permute-start.25 = (f32[16,256]{1,0:T(8,128)S(1)}, f32[16,256]{1,0:T(8,128)S(1)}, u32[]{:S(2)}, u32[]{:S(2)}) collective-permute-start(f32[16,256]{1,0:T(8,128)S(1)} %add.132), channel_id=1, source_target_pairs={{0,16},{16,0},{1,17},{17,1},{2,18},{18,2},{3,19},{19,3},{4,20},{20... | collective-permute-start | bytes 49160 | tf_op jit(solution)/shard_map/ppermute | solution.py:253
  95.9 3.4 %collective-permute-done.27 = f32[16,256]{1,0:T(8,128)S(1)} collective-permute-done((f32[16,256]{1,0:T(8,128)S(1)}, f32[16,256]{1,0:T(8,128)S(1)}, u32[]{:S(2)}, u32[]{:S(2)}) %collective-permute-start.27) | collective-permute-done | bytes 16416 | tf_op jit(solution)/shard_map/ppermute | solution.py:270
  99.3 5.2 %collective-permute-start.28 = (f32[16,256]{1,0:T(8,128)S(1)}, f32[16,256]{1,0:T(8,128)S(1)}, u32[]{:S(2)}, u32[]{:S(2)}) collective-permute-start(f32[16,256]{1,0:T(8,128)S(1)} %add.134), channel_id=1, source_target_pairs={{0,16},{16,0},{1,17},{17,1},{2,18},{18,2},{3,19},{19,3},{4,20},{20... | collective-permute-start | bytes 49160 | tf_op jit(solution)/shard_map/ppermute | solution.py:253
  109.1 5.1 %collective-permute-start.31 = (f32[16,256]{1,0:T(8,128)S(1)}, f32[16,256]{1,0:T(8,128)S(1)}, u32[]{:S(2)}, u32[]{:S(2)}) collective-permute-start(f32[16,256]{1,0:T(8,128)S(1)} %add.136), channel_id=1, source_target_pairs={{0,16},{16,0},{1,17},{17,1},{2,18},{18,2},{3,19},{19,3},{4,20},{20... | collective-permute-start | bytes 49160 | tf_op jit(solution)/shard_map/ppermute | solution.py:253
  115.0 4.3 %collective-permute-start.32 = (f32[16,256]{1,0:T(8,128)S(1)}, f32[16,256]{1,0:T(8,128)S(1)}, u32[]{:S(2)}, u32[]{:S(2)}) collective-permute-start(f32[16,256]{1,0:T(8,128)S(1)} %add.137), channel_id=1, source_target_pairs={{0,128},{32,160},{64,192},{96,224},{128,0},{160,32},{192,64},{224,... | collective-permute-start | bytes 49160 | tf_op jit(solution)/shard_map/ppermute | solution.py:275
  119.3 3.4 %collective-permute-done.32 = f32[16,256]{1,0:T(8,128)S(1)} collective-permute-done((f32[16,256]{1,0:T(8,128)S(1)}, f32[16,256]{1,0:T(8,128)S(1)}, u32[]{:S(2)}, u32[]{:S(2)}) %collective-permute-start.32) | collective-permute-done | bytes 16416 | tf_op jit(solution)/shard_map/ppermute | solution.py:275
  125.4 2.4 %collective-permute-start.35 = (f32[16,256]{1,0:T(8,128)S(1)}, f32[16,256]{1,0:T(8,128)S(1)}, u32[]{:S(2)}, u32[]{:S(2)}) collective-permute-start(f32[16,256]{1,0:T(8,128)S(1)} %add.139), channel_id=1, source_target_pairs={{0,4},{16,28},{4,0},{20,24},{8,12},{24,20},{12,8},{28,16},{1,5},{1... | collective-permute-start | bytes 49160 | tf_op jit(solution)/shard_map/ppermute | solution.py:270
  129.5 3.0 %collective-permute-start.36 = (f32[16,256]{1,0:T(8,128)S(1)}, f32[16,256]{1,0:T(8,128)S(1)}, u32[]{:S(2)}, u32[]{:S(2)}) collective-permute-start(f32[16,256]{1,0:T(8,128)S(1)} %add.140), channel_id=1, source_target_pairs={{0,16},{16,0},{1,17},{17,1},{2,18},{18,2},{3,19},{19,3},{4,20},{20... | collective-permute-start | bytes 49160 | tf_op jit(solution)/shard_map/ppermute | solution.py:253
  134.0 3.1 %collective-permute-done.38 = f32[16,256]{1,0:T(8,128)S(1)} collective-permute-done((f32[16,256]{1,0:T(8,128)S(1)}, f32[16,256]{1,0:T(8,128)S(1)}, u32[]{:S(2)}, u32[]{:S(2)}) %collective-permute-start.38) | collective-permute-done | bytes 16416 | tf_op jit(solution)/shard_map/ppermute | solution.py:270
  137.1 2.6 %collective-permute-start.39 = (f32[16,256]{1,0:T(8,128)S(1)}, f32[16,256]{1,0:T(8,128)S(1)}, u32[]{:S(2)}, u32[]{:S(2)}) collective-permute-start(f32[16,256]{1,0:T(8,128)S(1)} %add.142), channel_id=1, source_target_pairs={{0,16},{16,0},{1,17},{17,1},{2,18},{18,2},{3,19},{19,3},{4,20},{20... | collective-permute-start | bytes 49160 | tf_op jit(solution)/shard_map/ppermute | solution.py:253
  141.2 3.1 %collective-permute-done.41 = f32[16,256]{1,0:T(8,128)S(1)} collective-permute-done((f32[16,256]{1,0:T(8,128)S(1)}, f32[16,256]{1,0:T(8,128)S(1)}, u32[]{:S(2)}, u32[]{:S(2)}) %collective-permute-start.41) | collective-permute-done | bytes 16416 | tf_op jit(solution)/shard_map/ppermute | solution.py:270
  144.3 2.3 collective-permute-start.42
  147.4 24.7 %tile.8 = (f32[512,1024]{1,0:T(8,128)}, bf16[512,1024]{1,0:T(8,128)(2,1)S(1)}) custom-call(s32[4]{0:T(128)S(1)} %pad_add_fusion.refs_0_.place_ref, bf16[16,3088,128]{2,1,0:T(8,128)(2,1)} %bitcast.12, f32[64,256]{1,0:T(8,128)S(1)} %copy-done.2), custom_call_target="tpu_custom_call" | custom-call | flops 12884901888 | bytes 16842752 | tf_op jit(solution)/shard_map/tile/pallas_call | solution.py:377
  172.4 2.3 %collective-permute-done.43 = bf16[512,1024]{1,0:T(8,128)(2,1)S(1)} collective-permute-done((bf16[512,1024]{1,0:T(8,128)(2,1)S(1)}, bf16[512,1024]{1,0:T(8,128)(2,1)S(1)}, u32[]{:S(2)}, u32[]{:S(2)}) %collective-permute-start.43) | collective-permute-done | bytes 1048608 | tf_op jit(solution)/shard_map/ppermute | solution.py:378
  174.7 3.4 %convert_add_fusion = f32[512,1024]{1,0:T(8,128)} fusion(f32[512,1024]{1,0:T(8,128)} %get-tuple-element.18, bf16[512,1024]{1,0:T(8,128)(2,1)S(1)} %collective-permute-done.43), kind=kLoop, calls=%fused_computation | loop fusion | flops 1048576 | bytes 5242880 | tf_op jit(solution)/shard_map/add | solution.py:379
  178.1 6.0 %collective-permute-start.44 = (f32[16,256]{1,0:T(8,128)S(1)}, f32[16,256]{1,0:T(8,128)S(1)}, u32[]{:S(2)}, u32[]{:S(2)}) collective-permute-start(f32[16,256]{1,0:T(8,128)S(1)} %add.145), channel_id=1, source_target_pairs={{0,128},{32,160},{64,192},{96,224},{128,0},{160,32},{192,64},{224,... | collective-permute-start | bytes 49160 | tf_op jit(solution)/shard_map/ppermute | solution.py:275
  187.8 34.8 %reduce-scatter.2.cloned.1.call-done = f32[64,1024]{1,0:T(8,128)} async-done(((f32[512,1024]{1,0:T(8,128)}), f32[64,1024]{1,0:T(8,128)}) %reduce-scatter.2.cloned.1.call-update) | async-done | bytes 262160 | tf_op jit(solution)/shard_map/reduce_scatter | solution.py:380
  (120 shorter events, 48.8 us)
Async XLA Ops:
  7.2 140.2 %all-gather.3.cloned.1.call-start = ((), (), s32[]{:S(2)}) async-start(), calls=%async_computation.2 | async-start | bytes 13438976 | tf_op jit(solution)/shard_map/all_gather | solution.py:324
  11.6 210.9 %reduce-scatter.2.cloned.1.call-start = ((), (), s32[]{:S(2)}) async-start(), calls=%async_computation.1 | async-start | bytes 2359296 | tf_op jit(solution)/shard_map/reduce_scatter | solution.py:380
  13.9 4.0 %collective-permute-start.2 = (f32[16,256]{1,0:T(8,128)S(1)}, f32[16,256]{1,0:T(8,128)S(1)}, u32[]{:S(2)}, u32[]{:S(2)}) collective-permute-start(f32[16,256]{1,0:T(8,128)S(1)} %add.115), channel_id=1, source_target_pairs={{0,4},{16,28},{4,0},{20,24},{8,12},{24,20},{12,8},{28,16},{1,5},{1... | collective-permute-start | bytes 49160 | tf_op jit(solution)/shard_map/ppermute | solution.py:270
  17.9 4.2 %collective-permute-start.3 = (f32[16,256]{1,0:T(8,128)S(1)}, f32[16,256]{1,0:T(8,128)S(1)}, u32[]{:S(2)}, u32[]{:S(2)}) collective-permute-start(f32[16,256]{1,0:T(8,128)S(1)} %add.116), channel_id=1, source_target_pairs={{0,16},{16,0},{1,17},{17,1},{2,18},{18,2},{3,19},{19,3},{4,20},{20... | collective-permute-start | bytes 49160 | tf_op jit(solution)/shard_map/ppermute | solution.py:253
  22.1 3.7 %collective-permute-start.5 = (f32[16,256]{1,0:T(8,128)S(1)}, f32[16,256]{1,0:T(8,128)S(1)}, u32[]{:S(2)}, u32[]{:S(2)}) collective-permute-start(f32[16,256]{1,0:T(8,128)S(1)} %add.117), channel_id=1, source_target_pairs={{0,1},{16,19},{1,0},{17,18},{2,3},{18,17},{3,2},{19,16},{4,5},{20,... | collective-permute-start | bytes 49160 | tf_op jit(solution)/shard_map/ppermute | solution.py:270
  25.8 6.1 %collective-permute-start.6 = (f32[16,256]{1,0:T(8,128)S(1)}, f32[16,256]{1,0:T(8,128)S(1)}, u32[]{:S(2)}, u32[]{:S(2)}) collective-permute-start(f32[16,256]{1,0:T(8,128)S(1)} %add.118), channel_id=1, source_target_pairs={{0,16},{16,0},{1,17},{17,1},{2,18},{18,2},{3,19},{19,3},{4,20},{20... | collective-permute-start | bytes 49160 | tf_op jit(solution)/shard_map/ppermute | solution.py:253
  32.0 3.7 %collective-permute-start.8 = (f32[16,256]{1,0:T(8,128)S(1)}, f32[16,256]{1,0:T(8,128)S(1)}, u32[]{:S(2)}, u32[]{:S(2)}) collective-permute-start(f32[16,256]{1,0:T(8,128)S(1)} %add.119), channel_id=1, source_target_pairs={{0,32},{16,112},{32,0},{48,80},{64,96},{80,48},{96,64},{112,16},{1... | collective-permute-start | bytes 49160 | tf_op jit(solution)/shard_map/ppermute | solution.py:270
  35.7 7.7 %collective-permute-start.9 = (f32[16,256]{1,0:T(8,128)S(1)}, f32[16,256]{1,0:T(8,128)S(1)}, u32[]{:S(2)}, u32[]{:S(2)}) collective-permute-start(f32[16,256]{1,0:T(8,128)S(1)} %add.120), channel_id=1, source_target_pairs={{0,16},{16,0},{1,17},{17,1},{2,18},{18,2},{3,19},{19,3},{4,20},{20... | collective-permute-start | bytes 49160 | tf_op jit(solution)/shard_map/ppermute | solution.py:253
  43.4 7.6 %collective-permute-start.10 = (f32[16,256]{1,0:T(8,128)S(1)}, f32[16,256]{1,0:T(8,128)S(1)}, u32[]{:S(2)}, u32[]{:S(2)}) collective-permute-start(f32[16,256]{1,0:T(8,128)S(1)} %add.121), channel_id=1, source_target_pairs={{0,128},{32,160},{64,192},{96,224},{128,0},{160,32},{192,64},{224,... | collective-permute-start | bytes 49160 | tf_op jit(solution)/shard_map/ppermute | solution.py:275
  53.4 3.8 %collective-permute-start.13 = (f32[16,256]{1,0:T(8,128)S(1)}, f32[16,256]{1,0:T(8,128)S(1)}, u32[]{:S(2)}, u32[]{:S(2)}) collective-permute-start(f32[16,256]{1,0:T(8,128)S(1)} %add.123), channel_id=1, source_target_pairs={{0,4},{16,28},{4,0},{20,24},{8,12},{24,20},{12,8},{28,16},{1,5},{1... | collective-permute-start | bytes 49160 | tf_op jit(solution)/shard_map/ppermute | solution.py:270
  57.2 4.3 %collective-permute-start.14 = (f32[16,256]{1,0:T(8,128)S(1)}, f32[16,256]{1,0:T(8,128)S(1)}, u32[]{:S(2)}, u32[]{:S(2)}) collective-permute-start(f32[16,256]{1,0:T(8,128)S(1)} %add.124), channel_id=1, source_target_pairs={{0,16},{16,0},{1,17},{17,1},{2,18},{18,2},{3,19},{19,3},{4,20},{20... | collective-permute-start | bytes 49160 | tf_op jit(solution)/shard_map/ppermute | solution.py:253
  61.5 4.1 %collective-permute-start.16 = (f32[16,256]{1,0:T(8,128)S(1)}, f32[16,256]{1,0:T(8,128)S(1)}, u32[]{:S(2)}, u32[]{:S(2)}) collective-permute-start(f32[16,256]{1,0:T(8,128)S(1)} %add.125), channel_id=1, source_target_pairs={{0,1},{16,19},{1,0},{17,18},{2,3},{18,17},{3,2},{19,16},{4,5},{20,... | collective-permute-start | bytes 49160 | tf_op jit(solution)/shard_map/ppermute | solution.py:270
  61.5 4.1 %collective-permute-start.15 = (f32[16,256]{1,0:T(8,128)S(1)}, f32[16,256]{1,0:T(8,128)S(1)}, u32[]{:S(2)}, u32[]{:S(2)}) collective-permute-start(f32[16,256]{1,0:T(8,128)S(1)} %add.125), channel_id=1, source_target_pairs={{0,0},{16,18},{1,1},{17,19},{2,2},{18,16},{3,3},{19,17},{4,4},{20,... | collective-permute-start | bytes 49160 | tf_op jit(solution)/shard_map/ppermute | solution.py:270
  65.6 3.5 %collective-permute-start.17 = (f32[16,256]{1,0:T(8,128)S(1)}, f32[16,256]{1,0:T(8,128)S(1)}, u32[]{:S(2)}, u32[]{:S(2)}) collective-permute-start(f32[16,256]{1,0:T(8,128)S(1)} %add.126), channel_id=1, source_target_pairs={{0,16},{16,0},{1,17},{17,1},{2,18},{18,2},{3,19},{19,3},{4,20},{20... | collective-permute-start | bytes 49160 | tf_op jit(solution)/shard_map/ppermute | solution.py:253
  69.1 3.7 %collective-permute-start.19 = (f32[16,256]{1,0:T(8,128)S(1)}, f32[16,256]{1,0:T(8,128)S(1)}, u32[]{:S(2)}, u32[]{:S(2)}) collective-permute-start(f32[16,256]{1,0:T(8,128)S(1)} %add.127), channel_id=1, source_target_pairs={{0,32},{16,112},{32,0},{48,80},{64,96},{80,48},{96,64},{112,16},{1... | collective-permute-start | bytes 49160 | tf_op jit(solution)/shard_map/ppermute | solution.py:270
  69.1 3.7 %collective-permute-start.18 = (f32[16,256]{1,0:T(8,128)S(1)}, f32[16,256]{1,0:T(8,128)S(1)}, u32[]{:S(2)}, u32[]{:S(2)}) collective-permute-start(f32[16,256]{1,0:T(8,128)S(1)} %add.127), channel_id=1, source_target_pairs={{0,0},{16,80},{32,32},{48,112},{64,64},{80,16},{96,96},{112,48},{1... | collective-permute-start | bytes 49160 | tf_op jit(solution)/shard_map/ppermute | solution.py:270
  76.1 7.9 %collective-permute-start.21 = (f32[16,256]{1,0:T(8,128)S(1)}, f32[16,256]{1,0:T(8,128)S(1)}, u32[]{:S(2)}, u32[]{:S(2)}) collective-permute-start(f32[16,256]{1,0:T(8,128)S(1)} %add.129), channel_id=1, source_target_pairs={{0,128},{32,160},{64,192},{96,224},{128,0},{160,32},{192,64},{224,... | collective-permute-start | bytes 49160 | tf_op jit(solution)/shard_map/ppermute | solution.py:275
  86.5 4.1 %collective-permute-start.24 = (f32[16,256]{1,0:T(8,128)S(1)}, f32[16,256]{1,0:T(8,128)S(1)}, u32[]{:S(2)}, u32[]{:S(2)}) collective-permute-start(f32[16,256]{1,0:T(8,128)S(1)} %add.131), channel_id=1, source_target_pairs={{0,4},{16,28},{4,0},{20,24},{8,12},{24,20},{12,8},{28,16},{1,5},{1... | collective-permute-start | bytes 49160 | tf_op jit(solution)/shard_map/ppermute | solution.py:270
  90.6 4.6 %collective-permute-start.25 = (f32[16,256]{1,0:T(8,128)S(1)}, f32[16,256]{1,0:T(8,128)S(1)}, u32[]{:S(2)}, u32[]{:S(2)}) collective-permute-start(f32[16,256]{1,0:T(8,128)S(1)} %add.132), channel_id=1, source_target_pairs={{0,16},{16,0},{1,17},{17,1},{2,18},{18,2},{3,19},{19,3},{4,20},{20... | collective-permute-start | bytes 49160 | tf_op jit(solution)/shard_map/ppermute | solution.py:253
  95.2 4.1 %collective-permute-start.27 = (f32[16,256]{1,0:T(8,128)S(1)}, f32[16,256]{1,0:T(8,128)S(1)}, u32[]{:S(2)}, u32[]{:S(2)}) collective-permute-start(f32[16,256]{1,0:T(8,128)S(1)} %add.133), channel_id=1, source_target_pairs={{0,1},{16,19},{1,0},{17,18},{2,3},{18,17},{3,2},{19,16},{4,5},{20,... | collective-permute-start | bytes 49160 | tf_op jit(solution)/shard_map/ppermute | solution.py:270
  95.2 4.1 %collective-permute-start.26 = (f32[16,256]{1,0:T(8,128)S(1)}, f32[16,256]{1,0:T(8,128)S(1)}, u32[]{:S(2)}, u32[]{:S(2)}) collective-permute-start(f32[16,256]{1,0:T(8,128)S(1)} %add.133), channel_id=1, source_target_pairs={{0,0},{16,18},{1,1},{17,19},{2,2},{18,16},{3,3},{19,17},{4,4},{20,... | collective-permute-start | bytes 49160 | tf_op jit(solution)/shard_map/ppermute | solution.py:270
  99.3 6.1 %collective-permute-start.28 = (f32[16,256]{1,0:T(8,128)S(1)}, f32[16,256]{1,0:T(8,128)S(1)}, u32[]{:S(2)}, u32[]{:S(2)}) collective-permute-start(f32[16,256]{1,0:T(8,128)S(1)} %add.134), channel_id=1, source_target_pairs={{0,16},{16,0},{1,17},{17,1},{2,18},{18,2},{3,19},{19,3},{4,20},{20... | collective-permute-start | bytes 49160 | tf_op jit(solution)/shard_map/ppermute | solution.py:253
  105.4 3.7 %collective-permute-start.30 = (f32[16,256]{1,0:T(8,128)S(1)}, f32[16,256]{1,0:T(8,128)S(1)}, u32[]{:S(2)}, u32[]{:S(2)}) collective-permute-start(f32[16,256]{1,0:T(8,128)S(1)} %add.135), channel_id=1, source_target_pairs={{0,32},{16,112},{32,0},{48,80},{64,96},{80,48},{96,64},{112,16},{1... | collective-permute-start | bytes 49160 | tf_op jit(solution)/shard_map/ppermute | solution.py:270
  109.1 5.9 %collective-permute-start.31 = (f32[16,256]{1,0:T(8,128)S(1)}, f32[16,256]{1,0:T(8,128)S(1)}, u32[]{:S(2)}, u32[]{:S(2)}) collective-permute-start(f32[16,256]{1,0:T(8,128)S(1)} %add.136), channel_id=1, source_target_pairs={{0,16},{16,0},{1,17},{17,1},{2,18},{18,2},{3,19},{19,3},{4,20},{20... | collective-permute-start | bytes 49160 | tf_op jit(solution)/shard_map/ppermute | solution.py:253
  115.0 7.6 %collective-permute-start.32 = (f32[16,256]{1,0:T(8,128)S(1)}, f32[16,256]{1,0:T(8,128)S(1)}, u32[]{:S(2)}, u32[]{:S(2)}) collective-permute-start(f32[16,256]{1,0:T(8,128)S(1)} %add.137), channel_id=1, source_target_pairs={{0,128},{32,160},{64,192},{96,224},{128,0},{160,32},{192,64},{224,... | collective-permute-start | bytes 49160 | tf_op jit(solution)/shard_map/ppermute | solution.py:275
  125.4 4.1 %collective-permute-start.35 = (f32[16,256]{1,0:T(8,128)S(1)}, f32[16,256]{1,0:T(8,128)S(1)}, u32[]{:S(2)}, u32[]{:S(2)}) collective-permute-start(f32[16,256]{1,0:T(8,128)S(1)} %add.139), channel_id=1, source_target_pairs={{0,4},{16,28},{4,0},{20,24},{8,12},{24,20},{12,8},{28,16},{1,5},{1... | collective-permute-start | bytes 49160 | tf_op jit(solution)/shard_map/ppermute | solution.py:270
  129.5 3.8 %collective-permute-start.36 = (f32[16,256]{1,0:T(8,128)S(1)}, f32[16,256]{1,0:T(8,128)S(1)}, u32[]{:S(2)}, u32[]{:S(2)}) collective-permute-start(f32[16,256]{1,0:T(8,128)S(1)} %add.140), channel_id=1, source_target_pairs={{0,16},{16,0},{1,17},{17,1},{2,18},{18,2},{3,19},{19,3},{4,20},{20... | collective-permute-start | bytes 49160 | tf_op jit(solution)/shard_map/ppermute | solution.py:253
  133.3 3.7 %collective-permute-start.38 = (f32[16,256]{1,0:T(8,128)S(1)}, f32[16,256]{1,0:T(8,128)S(1)}, u32[]{:S(2)}, u32[]{:S(2)}) collective-permute-start(f32[16,256]{1,0:T(8,128)S(1)} %add.141), channel_id=1, source_target_pairs={{0,1},{16,19},{1,0},{17,18},{2,3},{18,17},{3,2},{19,16},{4,5},{20,... | collective-permute-start | bytes 49160 | tf_op jit(solution)/shard_map/ppermute | solution.py:270
  133.3 3.7 %collective-permute-start.37 = (f32[16,256]{1,0:T(8,128)S(1)}, f32[16,256]{1,0:T(8,128)S(1)}, u32[]{:S(2)}, u32[]{:S(2)}) collective-permute-start(f32[16,256]{1,0:T(8,128)S(1)} %add.141), channel_id=1, source_target_pairs={{0,0},{16,18},{1,1},{17,19},{2,2},{18,16},{3,3},{19,17},{4,4},{20,... | collective-permute-start | bytes 49160 | tf_op jit(solution)/shard_map/ppermute | solution.py:270
  140.5 3.7 %collective-permute-start.41 = (f32[16,256]{1,0:T(8,128)S(1)}, f32[16,256]{1,0:T(8,128)S(1)}, u32[]{:S(2)}, u32[]{:S(2)}) collective-permute-start(f32[16,256]{1,0:T(8,128)S(1)} %add.143), channel_id=1, source_target_pairs={{0,32},{16,112},{32,0},{48,80},{64,96},{80,48},{96,64},{112,16},{1... | collective-permute-start | bytes 49160 | tf_op jit(solution)/shard_map/ppermute | solution.py:270
  140.5 3.7 %collective-permute-start.40 = (f32[16,256]{1,0:T(8,128)S(1)}, f32[16,256]{1,0:T(8,128)S(1)}, u32[]{:S(2)}, u32[]{:S(2)}) collective-permute-start(f32[16,256]{1,0:T(8,128)S(1)} %add.143), channel_id=1, source_target_pairs={{0,0},{16,80},{32,32},{48,112},{64,64},{80,16},{96,96},{112,48},{1... | collective-permute-start | bytes 49160 | tf_op jit(solution)/shard_map/ppermute | solution.py:270
  178.1 7.7 %collective-permute-start.44 = (f32[16,256]{1,0:T(8,128)S(1)}, f32[16,256]{1,0:T(8,128)S(1)}, u32[]{:S(2)}, u32[]{:S(2)}) collective-permute-start(f32[16,256]{1,0:T(8,128)S(1)} %add.145), channel_id=1, source_target_pairs={{0,128},{32,160},{64,192},{96,224},{128,0},{160,32},{192,64},{224,... | collective-permute-start | bytes 49160 | tf_op jit(solution)/shard_map/ppermute | solution.py:275
  (19 other events, 194.9 us)
Sparse Core Ops, SparseCore 0:
  11.8 98.9 all-gather.2
  178.3 44.2 reduce-scatter.1

commit v6 on v4

--- a/solution.py
+++ b/solution.py
@@ -77,27 +77,31 @@
     return [(vis[k : k + 1, :] == ids).astype(jnp.float32) for k in range(vis.shape[0])]
 
 
-def prepare_kernel(slots, blocks, w_ref, vis_ref, inv_ref, grad_ref, cams_ref, send_ref, zw_ref, part_ref):
+def turned_rows(w_ref, at, points):
+    return jnp.transpose(w_ref[at * points : (at + 1) * points, :].astype(jnp.float32))
+
+
+def send_kernel(slots, w_ref, vis_ref, inv_ref, send_ref):
     points = vis_ref.shape[1]
     width = w_ref.shape[1]
+    for at in range(3 * slots):
+        send_ref[at * width : (at + 1) * width, :] = turned_rows(w_ref, at, points).astype(jnp.bfloat16)
+    pad = jnp.zeros((AUX - slots - 6, points), jnp.float32)
+    aux = jnp.concatenate([vis_ref[...].astype(jnp.float32), inv_ref[...].astype(jnp.float32), pad], axis=0)
+    send_ref[3 * slots * width :, :] = aux.astype(jnp.bfloat16)
+
+
+def prepare_kernel(slots, blocks, w_ref, vis_ref, inv_ref, grad_ref, cams_ref, zw_ref, part_ref):
+    points = vis_ref.shape[1]
     inv = inv_ref[...].astype(jnp.float32)
     inv_rows = [inv[e : e + 1, :] for e in range(6)]
     grad = grad_ref[...].astype(jnp.float32)
-    vis = vis_ref[...]
     for k in range(slots):
-        turned = []
-        for a in range(3):
-            at = 3 * k + a
-            t = jnp.transpose(w_ref[at * points : (at + 1) * points, :].astype(jnp.float32))
-            turned.append(t)
-            send_ref[at * width : (at + 1) * width, :] = t.astype(jnp.bfloat16)
+        turned = [turned_rows(w_ref, 3 * k + a, points) for a in range(3)]
         for a, z in enumerate(apply_inverse(inv_rows, turned)):
             at = 3 * k + a
             zw_ref[:, at * points : (at + 1) * points] = z.astype(jnp.bfloat16)
-    pad = jnp.zeros((AUX - slots - 6, points), jnp.float32)
-    aux = jnp.concatenate([vis.astype(jnp.float32), inv, pad], axis=0)
-    send_ref[3 * slots * width :, :] = aux.astype(jnp.bfloat16)
-    masks = slot_masks(vis, blocks)
+    masks = slot_masks(vis_ref[...], blocks)
     moved = apply_inverse(inv_rows, [grad[a : a + 1, :] for a in range(3)])
     moved = [e.astype(jnp.bfloat16).astype(jnp.float32) for e in moved]
     lhs = jnp.concatenate([masks[k] * moved[a] for k in range(slots) for a in range(3)], axis=1)
@@ -253,13 +257,11 @@
     return value + lax.ppermute(value, "core", [(0, 1), (1, 0)])
 
 
-def all_sum(value, n_z, n_row, n_col, between=None):
+def all_sum(value, n_z, n_row, n_col):
     value = core_sum(value)
     far = n_z // 2
     pairs = [[(2 * z + c, 2 * (z ^ (j + c * far)) + c) for z in range(n_z) for c in range(2)] for j in range(far)]
     value = tree([lax.ppermute(value, ("z", "core"), p) for p in pairs])
-    if between is not None:
-        value = between(value)
     for axis, size in (("row", n_row), ("col", n_col)):
         swaps = [lax.ppermute(value, axis, [(i, i ^ b) for i in range(size)]) for b in range(1, size)]
         value = tree([value] + swaps)
@@ -298,20 +300,22 @@
     vec = jax.ShapeDtypeStruct((blocks, width), jnp.float32)
     small = pltpu.CompilerParams(vmem_limit_bytes=16 * 1024 * 1024)
 
-    send, zw, part = pl.pallas_call(
+    send = pl.pallas_call(
+        functools.partial(send_kernel, slots),
+        out_shape=jax.ShapeDtypeStruct((send_rows, points), jnp.bfloat16),
+        in_specs=[vmem] * 3,
+        out_specs=vmem,
+        name="send",
+    )(w_flat, visibility, inverses)
+    got = lax.all_gather(send, ("row", "col"), axis=0, tiled=False)
+    zw, part = pl.pallas_call(
         functools.partial(prepare_kernel, slots, blocks),
-        out_shape=(
-            jax.ShapeDtypeStruct((send_rows, points), jnp.bfloat16),
-            jax.ShapeDtypeStruct((width, 3 * slots * points), jnp.bfloat16),
-            vec,
-        ),
+        out_shape=(jax.ShapeDtypeStruct((width, 3 * slots * points), jnp.bfloat16), vec),
         in_specs=[vmem] * 5,
-        out_specs=(vmem,) * 3,
+        out_specs=(vmem, vmem),
         compiler_params=small,
         name="prepare",
     )(w_flat, visibility, inverses, grad_points, cams_placed)
-
-    got = lax.all_gather(send, ("row", "col"), axis=0, tiled=False)
 
     def product(known):
         return pl.pallas_call(
@@ -360,19 +364,15 @@
         name="tile",
     )
 
-    held = {}
-
-    def make_tile(value):
-        here, value = lax.optimization_barrier((got, value))
-        own_half, peer_half = make_halves(place, here, camera_blocks)
-        taken = lax.ppermute(peer_half, "core", [(0, 1), (1, 0)])
-        tile, value = lax.optimization_barrier((own_half + taken.astype(jnp.float32), value))
-        held["schur"] = lax.psum_scatter(tile, "z", scatter_dimension=0, tiled=True)
-        return value
-
     known = [all_sum(part, n_z, n_row, n_col)]
-    for between in (None,) * (ITERS - 1) + (make_tile,):
-        known.append(all_sum(product(known), n_z, n_row, n_col, between))
+    for _ in range(1, ITERS):
+        known.append(all_sum(product(known), n_z, n_row, n_col))
+    got, known = lax.optimization_barrier((got, known))
+    own_half, peer_half = make_halves(place, got, camera_blocks)
+    taken = lax.ppermute(peer_half, "core", [(0, 1), (1, 0)])
+    tile, known = lax.optimization_barrier((own_half + taken.astype(jnp.float32), known))
+    schur = lax.psum_scatter(tile, "z", scatter_dimension=0, tiled=True)
+    known.append(all_sum(product(known), n_z, n_row, n_col))
     own = jax.ShapeDtypeStruct((1, strip), jnp.float32)
     own_rhs, answer = pl.pallas_call(
         functools.partial(answer_kernel, strip),
@@ -382,7 +382,7 @@
         compiler_params=small,
         name="answer",
     )(place, *known)
-    return (held["schur"], own_rhs.reshape(strip), answer.reshape(strip))
+    return (schur, own_rhs.reshape(strip), answer.reshape(strip))
 
 
 def solution(mesh):

time: 203 us -> 191 us (0.941)
  waiting for transfers between devices: 68.7 us -> 61.4 us
  local copies, waits for them, and re-layouts: 3.29 us -> 0.13 us
  starting transfers between devices: 79.7 us -> 77.4 us
    reduce_scatter x1, waiting for transfers between devices: 23.8 us -> 8.02 us  [per_device(): schur = lax.psum_scatter(tile, 'z', scatter_dimension=0, tiled=True)]
    all_gather x1, waiting for transfers between devices: 0.02 us -> 7.53 us  [per_device(): got = lax.all_gather(send, ('row', 'col'), axis=0, tiled=False)]
    ppermute x1, starting transfers between devices: 6.99 us -> 0.01 us  [per_device(): taken = lax.ppermute(peer_half, 'core', [(0, 1), (1, 0)])]
    ppermute x8, starting transfers between devices: 17 us -> 22.7 us  [core_sum(): return value + lax.ppermute(value, 'core', [(0, 1), (1, 0)])]
    unnamed x14 -> x12, local copies, waits for them, and re-layouts: 3.19 us -> 0.03 us
    pallas_call x1 -> x2, Pallas kernels: 24.7 us -> 27.1 us  [the longest x1 24.7 us: per_device(): own_half, peer_half = make_halves(place, got, camera_blocks)]
where the time goes in v6:
time: 191 us; the launch traced here: 190 us
  starting transfers between devices  77.4 us (41%)
  waiting for transfers between devices  61.4 us (32%)
  Pallas kernels  33.4 us (17%)
  between operations  14.3 us (7%)
  other arithmetic  3.7 us (2%)
    ppermute x24, starting transfers between devices, all_sum(): lax.ppermute(value, axis, [(i, i ^ b) for i in range(size)])  33.6 us
    ppermute x24, waiting for transfers between devices, all_sum(): lax.ppermute(value, axis, [(i, i ^ b) for i in range(size)])  25.7 us
    pallas_call x1, Pallas kernels, per_device(): own_half, peer_half = make_halves(place, got, camera_blocks)  24.7 us
    ppermute x8, starting transfers between devices, core_sum(): return value + lax.ppermute(value, 'core', [(0, 1), (1, 0)])  22.7 us
    ppermute x16, starting transfers between devices, all_sum(): value = tree([lax.ppermute(value, ('z', 'core'), p) for p in pairs])  21 us
    ppermute x16, waiting for transfers between devices, all_sum(): value = tree([lax.ppermute(value, ('z', 'core'), p) for p in pairs])  10.3 us
    reduce_scatter x1, waiting for transfers between devices, per_device(): schur = lax.psum_scatter(tile, 'z', scatter_dimension=0, tiled=True)  8.02 us
    all_gather x1, waiting for transfers between devices, per_device(): got = lax.all_gather(send, ('row', 'col'), axis=0, tiled=False)  7.53 us
  transfers between devices with their start and end apart: 51, of which 34 were waited for; matrix products, arithmetic and copies ran while one was open for 0% of the time, Pallas kernels for 3%

profile of v6, /device:TPU:2, one launch (start us, length us, event | category | flops | bytes accessed | tf_op | source)
XLA Modules:
  0.0 190.4 jit_solution(9776638980361447589)
XLA Ops:
  7.3 2.4 %send.1 = bf16[3088,128]{1,0:T(8,128)(2,1)} custom-call(bf16[1536,256]{1,0:T(8,128)(2,1)} %bitcast.8, s32[4,128]{1,0:T(4,128)} %refs_1_.5, bf16[6,128]{1,0:T(8,128)(2,1)} %inv_ref.3), custom_call_target="tpu_custom_call" | custom-call | tf_op jit(solution)/shard_map/send/pallas_call | solution.py:303
  11.8 4.6 %collective-permute-start.4 = (f32[16,256]{1,0:T(8,128)S(1)}, f32[16,256]{1,0:T(8,128)S(1)}, u32[]{:S(2)}, u32[]{:S(2)}) collective-permute-start(f32[16,256]{1,0:T(8,128)S(1)} %add.150), channel_id=1, source_target_pairs={{0,96},{16,240},{32,64},{48,208},{64,32},{80,176},{96,0},{112,144}... | collective-permute-start | bytes 49160 | tf_op jit(solution)/shard_map/ppermute | solution.py:264
  18.1 2.9 %collective-permute-done.3 = f32[16,256]{1,0:T(8,128)S(1)} collective-permute-done((f32[16,256]{1,0:T(8,128)S(1)}, f32[16,256]{1,0:T(8,128)S(1)}, u32[]{:S(2)}, u32[]{:S(2)}) %collective-permute-start.3) | collective-permute-done | bytes 16416 | tf_op jit(solution)/shard_map/ppermute | solution.py:264
  25.2 2.6 %collective-permute-done.6 = f32[16,256]{1,0:T(8,128)S(1)} collective-permute-done((f32[16,256]{1,0:T(8,128)S(1)}, f32[16,256]{1,0:T(8,128)S(1)}, u32[]{:S(2)}, u32[]{:S(2)}) %collective-permute-start.6) | collective-permute-done | bytes 16416 | tf_op jit(solution)/shard_map/ppermute | solution.py:266
  27.9 3.1 %collective-permute-start.10 = (f32[16,256]{1,0:T(8,128)S(1)}, f32[16,256]{1,0:T(8,128)S(1)}, u32[]{:S(2)}, u32[]{:S(2)}) collective-permute-start(f32[16,256]{1,0:T(8,128)S(1)} %add_add_fusion.10), channel_id=1, source_target_pairs={{0,3},{1,2},{2,1},{3,0},{4,7},{5,6},{6,5},{7,4},{8,11},{9,10},{10,... | collective-permute-start | bytes 49160 | tf_op jit(solution)/shard_map/ppermute | solution.py:266
  33.2 3.3 %collective-permute-done.9 = f32[16,256]{1,0:T(8,128)S(1)} collective-permute-done((f32[16,256]{1,0:T(8,128)S(1)}, f32[16,256]{1,0:T(8,128)S(1)}, u32[]{:S(2)}, u32[]{:S(2)}) %collective-permute-start.9) | collective-permute-done | bytes 16416 | tf_op jit(solution)/shard_map/ppermute | solution.py:266
  36.6 6.6 %collective-permute-start.11 = (f32[16,256]{1,0:T(8,128)S(1)}, f32[16,256]{1,0:T(8,128)S(1)}, u32[]{:S(2)}, u32[]{:S(2)}) collective-permute-start(f32[16,256]{1,0:T(8,128)S(1)} %add_add_fusion.9), channel_id=1, source_target_pairs={{0,16},{16,0},{1,17},{17,1},{2,18},{18,2},{3,19},{19,3},{4,20},{20... | collective-permute-start | bytes 49160 | tf_op jit(solution)/shard_map/ppermute | solution.py:257
  46.4 2.3 %collective-permute-start.16 = (f32[16,256]{1,0:T(8,128)S(1)}, f32[16,256]{1,0:T(8,128)S(1)}, u32[]{:S(2)}, u32[]{:S(2)}) collective-permute-start(f32[16,256]{1,0:T(8,128)S(1)} %add.162), channel_id=1, source_target_pairs={{0,96},{16,240},{32,64},{48,208},{64,32},{80,176},{96,0},{112,144}... | collective-permute-start | bytes 49160 | tf_op jit(solution)/shard_map/ppermute | solution.py:264
  53.7 1.7 collective-permute-start.19
  55.4 1.8 collective-permute-start.18
  57.9 3.1 %collective-permute-done.18 = f32[16,256]{1,0:T(8,128)S(1)} collective-permute-done((f32[16,256]{1,0:T(8,128)S(1)}, f32[16,256]{1,0:T(8,128)S(1)}, u32[]{:S(2)}, u32[]{:S(2)}) %collective-permute-start.18) | collective-permute-done | bytes 16416 | tf_op jit(solution)/shard_map/ppermute | solution.py:266
  66.8 1.7 collective-permute-done.21
  68.5 4.5 %collective-permute-start.23 = (f32[16,256]{1,0:T(8,128)S(1)}, f32[16,256]{1,0:T(8,128)S(1)}, u32[]{:S(2)}, u32[]{:S(2)}) collective-permute-start(f32[16,256]{1,0:T(8,128)S(1)} %add_add_fusion.6), channel_id=1, source_target_pairs={{0,16},{16,0},{1,17},{17,1},{2,18},{18,2},{3,19},{19,3},{4,20},{20... | collective-permute-start | bytes 49160 | tf_op jit(solution)/shard_map/ppermute | solution.py:257
  76.4 1.9 collective-permute-start.28
  78.5 2.3 %collective-permute-start.26 = (f32[16,256]{1,0:T(8,128)S(1)}, f32[16,256]{1,0:T(8,128)S(1)}, u32[]{:S(2)}, u32[]{:S(2)}) collective-permute-start(f32[16,256]{1,0:T(8,128)S(1)} %add.173), channel_id=1, source_target_pairs={{0,32},{16,176},{32,0},{48,144},{64,96},{80,240},{96,64},{112,208}... | collective-permute-start | bytes 49160 | tf_op jit(solution)/shard_map/ppermute | solution.py:264
  84.1 1.9 %collective-permute-start.30 = (f32[16,256]{1,0:T(8,128)S(1)}, f32[16,256]{1,0:T(8,128)S(1)}, u32[]{:S(2)}, u32[]{:S(2)}) collective-permute-start(f32[16,256]{1,0:T(8,128)S(1)} %add_add_fusion.5), channel_id=1, source_target_pairs={{0,8},{4,12},{8,0},{12,4},{1,9},{5,13},{9,1},{13,5},{2,10},{6,14},... | collective-permute-start | bytes 49160 | tf_op jit(solution)/shard_map/ppermute | solution.py:266
  87.1 2.5 %collective-permute-done.30 = f32[16,256]{1,0:T(8,128)S(1)} collective-permute-done((f32[16,256]{1,0:T(8,128)S(1)}, f32[16,256]{1,0:T(8,128)S(1)}, u32[]{:S(2)}, u32[]{:S(2)}) %collective-permute-start.30) | collective-permute-done | bytes 16416 | tf_op jit(solution)/shard_map/ppermute | solution.py:266
  90.1 2.1 %collective-permute-start.34 = (f32[16,256]{1,0:T(8,128)S(1)}, f32[16,256]{1,0:T(8,128)S(1)}, u32[]{:S(2)}, u32[]{:S(2)}) collective-permute-start(f32[16,256]{1,0:T(8,128)S(1)} %add_add_fusion.4), channel_id=1, source_target_pairs={{0,3},{1,2},{2,1},{3,0},{4,7},{5,6},{6,5},{7,4},{8,11},{9,10},{10,... | collective-permute-start | bytes 49160 | tf_op jit(solution)/shard_map/ppermute | solution.py:266
  95.5 2.3 %collective-permute-done.33 = f32[16,256]{1,0:T(8,128)S(1)} collective-permute-done((f32[16,256]{1,0:T(8,128)S(1)}, f32[16,256]{1,0:T(8,128)S(1)}, u32[]{:S(2)}, u32[]{:S(2)}) %collective-permute-start.33) | collective-permute-done | bytes 16416 | tf_op jit(solution)/shard_map/ppermute | solution.py:266
  97.8 4.7 %collective-permute-start.35 = (f32[16,256]{1,0:T(8,128)S(1)}, f32[16,256]{1,0:T(8,128)S(1)}, u32[]{:S(2)}, u32[]{:S(2)}) collective-permute-start(f32[16,256]{1,0:T(8,128)S(1)} %add_add_fusion.3), channel_id=1, source_target_pairs={{0,16},{16,0},{1,17},{17,1},{2,18},{18,2},{3,19},{19,3},{4,20},{20... | collective-permute-start | bytes 49160 | tf_op jit(solution)/shard_map/ppermute | solution.py:257
  103.3 7.5 %all-gather.3.cloned.1.call-done = bf16[49408,128]{1,0:T(8,128)(2,1)} async-done(((bf16[3088,128]{1,0:T(8,128)(2,1)}), bf16[49408,128]{1,0:T(8,128)(2,1)}) %all-gather.3.cloned.1.call-update) | async-done | bytes 12648464 | tf_op jit(solution)/shard_map/all_gather | solution.py:310
  110.8 24.7 %tile.8 = (f32[512,1024]{1,0:T(8,128)}, bf16[512,1024]{1,0:T(8,128)(2,1)S(1)}) custom-call(s32[4]{0:T(128)S(1)} %pad_add_fusion.refs_0_.place_ref, bf16[16,3088,128]{2,1,0:T(8,128)(2,1)} %bitcast.13, f32[64,256]{1,0:T(8,128)S(1)} %copy-done.1), custom_call_target="tpu_custom_call" | custom-call | flops 12884901888 | bytes 16842752 | tf_op jit(solution)/shard_map/tile/pallas_call | solution.py:371
  135.5 2.7 %collective-permute-done.36 = bf16[512,1024]{1,0:T(8,128)(2,1)S(1)} collective-permute-done((bf16[512,1024]{1,0:T(8,128)(2,1)S(1)}, bf16[512,1024]{1,0:T(8,128)(2,1)S(1)}, u32[]{:S(2)}, u32[]{:S(2)}) %collective-permute-start.36) | collective-permute-done | bytes 1048608 | tf_op jit(solution)/shard_map/ppermute | solution.py:372
  138.2 3.4 %convert_add_fusion = f32[512,1024]{1,0:T(8,128)} fusion(f32[512,1024]{1,0:T(8,128)} %get-tuple-element.20, bf16[512,1024]{1,0:T(8,128)(2,1)S(1)} %collective-permute-done.36), kind=kLoop, calls=%fused_computation | loop fusion | flops 1048576 | bytes 5242880 | tf_op jit(solution)/shard_map/add | solution.py:373
  144.3 3.5 %collective-permute-start.41 = (f32[16,256]{1,0:T(8,128)S(1)}, f32[16,256]{1,0:T(8,128)S(1)}, u32[]{:S(2)}, u32[]{:S(2)}) collective-permute-start(f32[16,256]{1,0:T(8,128)S(1)} %add.185), channel_id=1, source_target_pairs={{0,96},{16,240},{32,64},{48,208},{64,32},{80,176},{96,0},{112,144}... | collective-permute-start | bytes 49160 | tf_op jit(solution)/shard_map/ppermute | solution.py:264
  149.8 2.6 %collective-permute-done.40 = f32[16,256]{1,0:T(8,128)S(1)} collective-permute-done((f32[16,256]{1,0:T(8,128)S(1)}, f32[16,256]{1,0:T(8,128)S(1)}, u32[]{:S(2)}, u32[]{:S(2)}) %collective-permute-start.40) | collective-permute-done | bytes 16416 | tf_op jit(solution)/shard_map/ppermute | solution.py:264
  156.7 2.6 %collective-permute-done.43 = f32[16,256]{1,0:T(8,128)S(1)} collective-permute-done((f32[16,256]{1,0:T(8,128)S(1)}, f32[16,256]{1,0:T(8,128)S(1)}, u32[]{:S(2)}, u32[]{:S(2)}) %collective-permute-start.43) | collective-permute-done | bytes 16416 | tf_op jit(solution)/shard_map/ppermute | solution.py:266
  159.3 2.3 %collective-permute-start.47 = (f32[16,256]{1,0:T(8,128)S(1)}, f32[16,256]{1,0:T(8,128)S(1)}, u32[]{:S(2)}, u32[]{:S(2)}) collective-permute-start(f32[16,256]{1,0:T(8,128)S(1)} %add_add_fusion.1), channel_id=1, source_target_pairs={{0,3},{1,2},{2,1},{3,0},{4,7},{5,6},{6,5},{7,4},{8,11},{9,10},{10,... | collective-permute-start | bytes 49160 | tf_op jit(solution)/shard_map/ppermute | solution.py:266
  164.3 2.5 %collective-permute-done.46 = f32[16,256]{1,0:T(8,128)S(1)} collective-permute-done((f32[16,256]{1,0:T(8,128)S(1)}, f32[16,256]{1,0:T(8,128)S(1)}, u32[]{:S(2)}, u32[]{:S(2)}) %collective-permute-start.46) | collective-permute-done | bytes 16416 | tf_op jit(solution)/shard_map/ppermute | solution.py:266
  166.9 5.9 %collective-permute-start.48 = (f32[16,256]{1,0:T(8,128)S(1)}, f32[16,256]{1,0:T(8,128)S(1)}, u32[]{:S(2)}, u32[]{:S(2)}) collective-permute-start(f32[16,256]{1,0:T(8,128)S(1)} %add_add_fusion), channel_id=1, source_target_pairs={{0,16},{16,0},{1,17},{17,1},{2,18},{18,2},{3,19},{19,3},{4,20},{20... | collective-permute-start | bytes 49160 | tf_op jit(solution)/shard_map/ppermute | solution.py:257
  173.6 1.9 answer.1
  175.5 8.0 %reduce-scatter.2.cloned.1.call-done = f32[64,1024]{1,0:T(8,128)} async-done(((f32[512,1024]{1,0:T(8,128)}), f32[64,1024]{1,0:T(8,128)}) %reduce-scatter.2.cloned.1.call-update) | async-done | bytes 262160 | tf_op jit(solution)/shard_map/reduce_scatter | solution.py:374
  (121 shorter events, 50.1 us)
Async XLA Ops:
  7.2 103.6 %all-gather.3.cloned.1.call-start = ((), (), s32[]{:S(2)}) async-start(), calls=%async_computation.2 | async-start | bytes 13438976 | tf_op jit(solution)/shard_map/all_gather | solution.py:310
  9.7 173.8 %reduce-scatter.2.cloned.1.call-start = ((), (), s32[]{:S(2)}) async-start(), calls=%async_computation.1 | async-start | bytes 2359296 | tf_op jit(solution)/shard_map/reduce_scatter | solution.py:374
  11.8 6.3 %collective-permute-start.4 = (f32[16,256]{1,0:T(8,128)S(1)}, f32[16,256]{1,0:T(8,128)S(1)}, u32[]{:S(2)}, u32[]{:S(2)}) collective-permute-start(f32[16,256]{1,0:T(8,128)S(1)} %add.150), channel_id=1, source_target_pairs={{0,96},{16,240},{32,64},{48,208},{64,32},{80,176},{96,0},{112,144}... | collective-permute-start | bytes 49160 | tf_op jit(solution)/shard_map/ppermute | solution.py:264
  16.4 4.6 %collective-permute-start.3 = (f32[16,256]{1,0:T(8,128)S(1)}, f32[16,256]{1,0:T(8,128)S(1)}, u32[]{:S(2)}, u32[]{:S(2)}) collective-permute-start(f32[16,256]{1,0:T(8,128)S(1)} %add.150), channel_id=1, source_target_pairs={{0,64},{16,208},{32,96},{48,240},{64,0},{80,144},{96,32},{112,176}... | collective-permute-start | bytes 49160 | tf_op jit(solution)/shard_map/ppermute | solution.py:264
  16.4 4.6 %collective-permute-start.2 = (f32[16,256]{1,0:T(8,128)S(1)}, f32[16,256]{1,0:T(8,128)S(1)}, u32[]{:S(2)}, u32[]{:S(2)}) collective-permute-start(f32[16,256]{1,0:T(8,128)S(1)} %add.150), channel_id=1, source_target_pairs={{0,32},{16,176},{32,0},{48,144},{64,96},{80,240},{96,64},{112,208}... | collective-permute-start | bytes 49160 | tf_op jit(solution)/shard_map/ppermute | solution.py:264
  22.6 5.2 %collective-permute-start.6 = (f32[16,256]{1,0:T(8,128)S(1)}, f32[16,256]{1,0:T(8,128)S(1)}, u32[]{:S(2)}, u32[]{:S(2)}) collective-permute-start(f32[16,256]{1,0:T(8,128)S(1)} %add_add_fusion.11), channel_id=1, source_target_pairs={{0,8},{4,12},{8,0},{12,4},{1,9},{5,13},{9,1},{13,5},{2,10},{6,14},... | collective-permute-start | bytes 49160 | tf_op jit(solution)/shard_map/ppermute | solution.py:266
  27.9 5.4 %collective-permute-start.10 = (f32[16,256]{1,0:T(8,128)S(1)}, f32[16,256]{1,0:T(8,128)S(1)}, u32[]{:S(2)}, u32[]{:S(2)}) collective-permute-start(f32[16,256]{1,0:T(8,128)S(1)} %add_add_fusion.10), channel_id=1, source_target_pairs={{0,3},{1,2},{2,1},{3,0},{4,7},{5,6},{6,5},{7,4},{8,11},{9,10},{10,... | collective-permute-start | bytes 49160 | tf_op jit(solution)/shard_map/ppermute | solution.py:266
  31.0 5.6 %collective-permute-start.9 = (f32[16,256]{1,0:T(8,128)S(1)}, f32[16,256]{1,0:T(8,128)S(1)}, u32[]{:S(2)}, u32[]{:S(2)}) collective-permute-start(f32[16,256]{1,0:T(8,128)S(1)} %add_add_fusion.10), channel_id=1, source_target_pairs={{0,2},{1,3},{2,0},{3,1},{4,6},{5,7},{6,4},{7,5},{8,10},{9,11},{10,... | collective-permute-start | bytes 49160 | tf_op jit(solution)/shard_map/ppermute | solution.py:266
  31.6 4.9 %collective-permute-start.8 = (f32[16,256]{1,0:T(8,128)S(1)}, f32[16,256]{1,0:T(8,128)S(1)}, u32[]{:S(2)}, u32[]{:S(2)}) collective-permute-start(f32[16,256]{1,0:T(8,128)S(1)} %add_add_fusion.10), channel_id=1, source_target_pairs={{0,1},{1,0},{2,3},{3,2},{4,5},{5,4},{6,7},{7,6},{8,9},{9,8},{10,11... | collective-permute-start | bytes 49160 | tf_op jit(solution)/shard_map/ppermute | solution.py:266
  36.6 7.4 %collective-permute-start.11 = (f32[16,256]{1,0:T(8,128)S(1)}, f32[16,256]{1,0:T(8,128)S(1)}, u32[]{:S(2)}, u32[]{:S(2)}) collective-permute-start(f32[16,256]{1,0:T(8,128)S(1)} %add_add_fusion.9), channel_id=1, source_target_pairs={{0,16},{16,0},{1,17},{17,1},{2,18},{18,2},{3,19},{19,3},{4,20},{20... | collective-permute-start | bytes 49160 | tf_op jit(solution)/shard_map/ppermute | solution.py:257
  46.4 5.6 %collective-permute-start.16 = (f32[16,256]{1,0:T(8,128)S(1)}, f32[16,256]{1,0:T(8,128)S(1)}, u32[]{:S(2)}, u32[]{:S(2)}) collective-permute-start(f32[16,256]{1,0:T(8,128)S(1)} %add.162), channel_id=1, source_target_pairs={{0,96},{16,240},{32,64},{48,208},{64,32},{80,176},{96,0},{112,144}... | collective-permute-start | bytes 49160 | tf_op jit(solution)/shard_map/ppermute | solution.py:264
  48.6 4.6 %collective-permute-start.15 = (f32[16,256]{1,0:T(8,128)S(1)}, f32[16,256]{1,0:T(8,128)S(1)}, u32[]{:S(2)}, u32[]{:S(2)}) collective-permute-start(f32[16,256]{1,0:T(8,128)S(1)} %add.162), channel_id=1, source_target_pairs={{0,64},{16,208},{32,96},{48,240},{64,0},{80,144},{96,32},{112,176}... | collective-permute-start | bytes 49160 | tf_op jit(solution)/shard_map/ppermute | solution.py:264
  55.4 5.6 %collective-permute-start.18 = (f32[16,256]{1,0:T(8,128)S(1)}, f32[16,256]{1,0:T(8,128)S(1)}, u32[]{:S(2)}, u32[]{:S(2)}) collective-permute-start(f32[16,256]{1,0:T(8,128)S(1)} %add_add_fusion.8), channel_id=1, source_target_pairs={{0,8},{4,12},{8,0},{12,4},{1,9},{5,13},{9,1},{13,5},{2,10},{6,14},... | collective-permute-start | bytes 49160 | tf_op jit(solution)/shard_map/ppermute | solution.py:266
  61.3 5.5 %collective-permute-start.22 = (f32[16,256]{1,0:T(8,128)S(1)}, f32[16,256]{1,0:T(8,128)S(1)}, u32[]{:S(2)}, u32[]{:S(2)}) collective-permute-start(f32[16,256]{1,0:T(8,128)S(1)} %add_add_fusion.7), channel_id=1, source_target_pairs={{0,3},{1,2},{2,1},{3,0},{4,7},{5,6},{6,5},{7,4},{8,11},{9,10},{10,... | collective-permute-start | bytes 49160 | tf_op jit(solution)/shard_map/ppermute | solution.py:266
  62.9 5.6 %collective-permute-start.21 = (f32[16,256]{1,0:T(8,128)S(1)}, f32[16,256]{1,0:T(8,128)S(1)}, u32[]{:S(2)}, u32[]{:S(2)}) collective-permute-start(f32[16,256]{1,0:T(8,128)S(1)} %add_add_fusion.7), channel_id=1, source_target_pairs={{0,2},{1,3},{2,0},{3,1},{4,6},{5,7},{6,4},{7,5},{8,10},{9,11},{10,... | collective-permute-start | bytes 49160 | tf_op jit(solution)/shard_map/ppermute | solution.py:266
  64.2 4.3 %collective-permute-start.20 = (f32[16,256]{1,0:T(8,128)S(1)}, f32[16,256]{1,0:T(8,128)S(1)}, u32[]{:S(2)}, u32[]{:S(2)}) collective-permute-start(f32[16,256]{1,0:T(8,128)S(1)} %add_add_fusion.7), channel_id=1, source_target_pairs={{0,1},{1,0},{2,3},{3,2},{4,5},{5,4},{6,7},{7,6},{8,9},{9,8},{10,11... | collective-permute-start | bytes 49160 | tf_op jit(solution)/shard_map/ppermute | solution.py:266
  68.5 5.3 %collective-permute-start.23 = (f32[16,256]{1,0:T(8,128)S(1)}, f32[16,256]{1,0:T(8,128)S(1)}, u32[]{:S(2)}, u32[]{:S(2)}) collective-permute-start(f32[16,256]{1,0:T(8,128)S(1)} %add_add_fusion.6), channel_id=1, source_target_pairs={{0,16},{16,0},{1,17},{17,1},{2,18},{18,2},{3,19},{19,3},{4,20},{20... | collective-permute-start | bytes 49160 | tf_op jit(solution)/shard_map/ppermute | solution.py:257
  76.4 5.5 %collective-permute-start.28 = (f32[16,256]{1,0:T(8,128)S(1)}, f32[16,256]{1,0:T(8,128)S(1)}, u32[]{:S(2)}, u32[]{:S(2)}) collective-permute-start(f32[16,256]{1,0:T(8,128)S(1)} %add.173), channel_id=1, source_target_pairs={{0,96},{16,240},{32,64},{48,208},{64,32},{80,176},{96,0},{112,144}... | collective-permute-start | bytes 49160 | tf_op jit(solution)/shard_map/ppermute | solution.py:264
  78.2 4.7 %collective-permute-start.27 = (f32[16,256]{1,0:T(8,128)S(1)}, f32[16,256]{1,0:T(8,128)S(1)}, u32[]{:S(2)}, u32[]{:S(2)}) collective-permute-start(f32[16,256]{1,0:T(8,128)S(1)} %add.173), channel_id=1, source_target_pairs={{0,64},{16,208},{32,96},{48,240},{64,0},{80,144},{96,32},{112,176}... | collective-permute-start | bytes 49160 | tf_op jit(solution)/shard_map/ppermute | solution.py:264
  78.5 4.5 %collective-permute-start.26 = (f32[16,256]{1,0:T(8,128)S(1)}, f32[16,256]{1,0:T(8,128)S(1)}, u32[]{:S(2)}, u32[]{:S(2)}) collective-permute-start(f32[16,256]{1,0:T(8,128)S(1)} %add.173), channel_id=1, source_target_pairs={{0,32},{16,176},{32,0},{48,144},{64,96},{80,240},{96,64},{112,208}... | collective-permute-start | bytes 49160 | tf_op jit(solution)/shard_map/ppermute | solution.py:264
  84.1 5.6 %collective-permute-start.30 = (f32[16,256]{1,0:T(8,128)S(1)}, f32[16,256]{1,0:T(8,128)S(1)}, u32[]{:S(2)}, u32[]{:S(2)}) collective-permute-start(f32[16,256]{1,0:T(8,128)S(1)} %add_add_fusion.5), channel_id=1, source_target_pairs={{0,8},{4,12},{8,0},{12,4},{1,9},{5,13},{9,1},{13,5},{2,10},{6,14},... | collective-permute-start | bytes 49160 | tf_op jit(solution)/shard_map/ppermute | solution.py:266
  90.1 5.3 %collective-permute-start.34 = (f32[16,256]{1,0:T(8,128)S(1)}, f32[16,256]{1,0:T(8,128)S(1)}, u32[]{:S(2)}, u32[]{:S(2)}) collective-permute-start(f32[16,256]{1,0:T(8,128)S(1)} %add_add_fusion.4), channel_id=1, source_target_pairs={{0,3},{1,2},{2,1},{3,0},{4,7},{5,6},{6,5},{7,4},{8,11},{9,10},{10,... | collective-permute-start | bytes 49160 | tf_op jit(solution)/shard_map/ppermute | solution.py:266
  92.2 5.6 %collective-permute-start.33 = (f32[16,256]{1,0:T(8,128)S(1)}, f32[16,256]{1,0:T(8,128)S(1)}, u32[]{:S(2)}, u32[]{:S(2)}) collective-permute-start(f32[16,256]{1,0:T(8,128)S(1)} %add_add_fusion.4), channel_id=1, source_target_pairs={{0,2},{1,3},{2,0},{3,1},{4,6},{5,7},{6,4},{7,5},{8,10},{9,11},{10,... | collective-permute-start | bytes 49160 | tf_op jit(solution)/shard_map/ppermute | solution.py:266
  97.8 5.5 %collective-permute-start.35 = (f32[16,256]{1,0:T(8,128)S(1)}, f32[16,256]{1,0:T(8,128)S(1)}, u32[]{:S(2)}, u32[]{:S(2)}) collective-permute-start(f32[16,256]{1,0:T(8,128)S(1)} %add_add_fusion.3), channel_id=1, source_target_pairs={{0,16},{16,0},{1,17},{17,1},{2,18},{18,2},{3,19},{19,3},{4,20},{20... | collective-permute-start | bytes 49160 | tf_op jit(solution)/shard_map/ppermute | solution.py:257
  144.3 5.5 %collective-permute-start.41 = (f32[16,256]{1,0:T(8,128)S(1)}, f32[16,256]{1,0:T(8,128)S(1)}, u32[]{:S(2)}, u32[]{:S(2)}) collective-permute-start(f32[16,256]{1,0:T(8,128)S(1)} %add.185), channel_id=1, source_target_pairs={{0,96},{16,240},{32,64},{48,208},{64,32},{80,176},{96,0},{112,144}... | collective-permute-start | bytes 49160 | tf_op jit(solution)/shard_map/ppermute | solution.py:264
  147.8 4.6 %collective-permute-start.40 = (f32[16,256]{1,0:T(8,128)S(1)}, f32[16,256]{1,0:T(8,128)S(1)}, u32[]{:S(2)}, u32[]{:S(2)}) collective-permute-start(f32[16,256]{1,0:T(8,128)S(1)} %add.185), channel_id=1, source_target_pairs={{0,64},{16,208},{32,96},{48,240},{64,0},{80,144},{96,32},{112,176}... | collective-permute-start | bytes 49160 | tf_op jit(solution)/shard_map/ppermute | solution.py:264
  147.9 4.6 %collective-permute-start.39 = (f32[16,256]{1,0:T(8,128)S(1)}, f32[16,256]{1,0:T(8,128)S(1)}, u32[]{:S(2)}, u32[]{:S(2)}) collective-permute-start(f32[16,256]{1,0:T(8,128)S(1)} %add.185), channel_id=1, source_target_pairs={{0,32},{16,176},{32,0},{48,144},{64,96},{80,240},{96,64},{112,208}... | collective-permute-start | bytes 49160 | tf_op jit(solution)/shard_map/ppermute | solution.py:264
  154.0 5.2 %collective-permute-start.43 = (f32[16,256]{1,0:T(8,128)S(1)}, f32[16,256]{1,0:T(8,128)S(1)}, u32[]{:S(2)}, u32[]{:S(2)}) collective-permute-start(f32[16,256]{1,0:T(8,128)S(1)} %add_add_fusion.2), channel_id=1, source_target_pairs={{0,8},{4,12},{8,0},{12,4},{1,9},{5,13},{9,1},{13,5},{2,10},{6,14},... | collective-permute-start | bytes 49160 | tf_op jit(solution)/shard_map/ppermute | solution.py:266
  159.3 5.0 %collective-permute-start.47 = (f32[16,256]{1,0:T(8,128)S(1)}, f32[16,256]{1,0:T(8,128)S(1)}, u32[]{:S(2)}, u32[]{:S(2)}) collective-permute-start(f32[16,256]{1,0:T(8,128)S(1)} %add_add_fusion.1), channel_id=1, source_target_pairs={{0,3},{1,2},{2,1},{3,0},{4,7},{5,6},{6,5},{7,4},{8,11},{9,10},{10,... | collective-permute-start | bytes 49160 | tf_op jit(solution)/shard_map/ppermute | solution.py:266
  161.6 5.2 %collective-permute-start.46 = (f32[16,256]{1,0:T(8,128)S(1)}, f32[16,256]{1,0:T(8,128)S(1)}, u32[]{:S(2)}, u32[]{:S(2)}) collective-permute-start(f32[16,256]{1,0:T(8,128)S(1)} %add_add_fusion.1), channel_id=1, source_target_pairs={{0,2},{1,3},{2,0},{3,1},{4,6},{5,7},{6,4},{7,5},{8,10},{9,11},{10,... | collective-permute-start | bytes 49160 | tf_op jit(solution)/shard_map/ppermute | solution.py:266
  162.4 4.4 %collective-permute-start.45 = (f32[16,256]{1,0:T(8,128)S(1)}, f32[16,256]{1,0:T(8,128)S(1)}, u32[]{:S(2)}, u32[]{:S(2)}) collective-permute-start(f32[16,256]{1,0:T(8,128)S(1)} %add_add_fusion.1), channel_id=1, source_target_pairs={{0,1},{1,0},{2,3},{3,2},{4,5},{5,4},{6,7},{7,6},{8,9},{9,8},{10,11... | collective-permute-start | bytes 49160 | tf_op jit(solution)/shard_map/ppermute | solution.py:266
  166.9 6.8 %collective-permute-start.48 = (f32[16,256]{1,0:T(8,128)S(1)}, f32[16,256]{1,0:T(8,128)S(1)}, u32[]{:S(2)}, u32[]{:S(2)}) collective-permute-start(f32[16,256]{1,0:T(8,128)S(1)} %add_add_fusion), channel_id=1, source_target_pairs={{0,16},{16,0},{1,17},{17,1},{2,18},{18,2},{3,19},{19,3},{4,20},{20... | collective-permute-start | bytes 49160 | tf_op jit(solution)/shard_map/ppermute | solution.py:257
  (25 other events, 100.1 us)
Sparse Core Ops, SparseCore 0:
  10.5 100.2 all-gather.2
  141.7 41.7 reduce-scatter.1

commit v7 on v6

--- a/solution.py
+++ b/solution.py
@@ -354,7 +354,7 @@
             pltpu.VMEM((col_count, 3 * pair * points), jnp.bfloat16),
         ],
         compiler_params=pltpu.CompilerParams(
-            dimension_semantics=("arbitrary",), vmem_limit_bytes=52 * 1024 * 1024
+            dimension_semantics=("arbitrary",), vmem_limit_bytes=50 * 1024 * 1024
         ),
         cost_estimate=pl.CostEstimate(
             flops=2 * set_rows * col_count * 3 * shards * points,

time: 191 us -> 188 us (0.984)
  no operation moved by 1% of the time
where the time goes in v7:
time: 188 us
  starting transfers between devices  77.7 us (41%)
  waiting for transfers between devices  61.4 us (33%)
  Pallas kernels  32.5 us (17%)
  between operations  14.3 us (8%)
  other arithmetic  1.97 us (1%)
    ppermute x24, starting transfers between devices, all_sum(): lax.ppermute(value, axis, [(i, i ^ b) for i in range(size)])  33.6 us
    ppermute x24, waiting for transfers between devices, all_sum(): lax.ppermute(value, axis, [(i, i ^ b) for i in range(size)])  25.7 us
    pallas_call x1, Pallas kernels, per_device(): own_half, peer_half = make_halves(place, got, camera_blocks)  23.7 us
    ppermute x8, starting transfers between devices, core_sum(): return value + lax.ppermute(value, 'core', [(0, 1), (1, 0)])  22.7 us
    ppermute x16, starting transfers between devices, all_sum(): value = tree([lax.ppermute(value, ('z', 'core'), p) for p in pairs])  21 us
    ppermute x16, waiting for transfers between devices, all_sum(): value = tree([lax.ppermute(value, ('z', 'core'), p) for p in pairs])  10.3 us
    reduce_scatter x1, waiting for transfers between devices, per_device(): schur = lax.psum_scatter(tile, 'z', scatter_dimension=0, tiled=True)  8.02 us
    all_gather x1, waiting for transfers between devices, per_device(): got = lax.all_gather(send, ('row', 'col'), axis=0, tiled=False)  7.53 us
  transfers between devices with their start and end apart: 51, of which 34 were waited for; matrix products, arithmetic and copies ran while one was open for 0% of the time, Pallas kernels for 3%

profile of v7, /device:TPU:2, one launch (start us, length us, event | category | flops | bytes accessed | tf_op | source)
XLA Modules:
  0.0 188.0 jit_solution(7546752244633516536)
XLA Ops:
  7.3 2.4 %send.1 = bf16[3088,128]{1,0:T(8,128)(2,1)} custom-call(bf16[1536,256]{1,0:T(8,128)(2,1)} %bitcast.8, s32[4,128]{1,0:T(4,128)} %refs_1_.5, bf16[6,128]{1,0:T(8,128)(2,1)} %inv_ref.3), custom_call_target="tpu_custom_call" | custom-call | tf_op jit(solution)/shard_map/send/pallas_call | solution.py:303
  11.8 4.6 %collective-permute-start.4 = (f32[16,256]{1,0:T(8,128)S(1)}, f32[16,256]{1,0:T(8,128)S(1)}, u32[]{:S(2)}, u32[]{:S(2)}) collective-permute-start(f32[16,256]{1,0:T(8,128)S(1)} %add.150), channel_id=1, source_target_pairs={{0,96},{16,240},{32,64},{48,208},{64,32},{80,176},{96,0},{112,144}... | collective-permute-start | bytes 49160 | tf_op jit(solution)/shard_map/ppermute | solution.py:264
  18.1 2.9 %collective-permute-done.3 = f32[16,256]{1,0:T(8,128)S(1)} collective-permute-done((f32[16,256]{1,0:T(8,128)S(1)}, f32[16,256]{1,0:T(8,128)S(1)}, u32[]{:S(2)}, u32[]{:S(2)}) %collective-permute-start.3) | collective-permute-done | bytes 16416 | tf_op jit(solution)/shard_map/ppermute | solution.py:264
  25.2 2.6 %collective-permute-done.6 = f32[16,256]{1,0:T(8,128)S(1)} collective-permute-done((f32[16,256]{1,0:T(8,128)S(1)}, f32[16,256]{1,0:T(8,128)S(1)}, u32[]{:S(2)}, u32[]{:S(2)}) %collective-permute-start.6) | collective-permute-done | bytes 16416 | tf_op jit(solution)/shard_map/ppermute | solution.py:266
  27.9 3.1 %collective-permute-start.10 = (f32[16,256]{1,0:T(8,128)S(1)}, f32[16,256]{1,0:T(8,128)S(1)}, u32[]{:S(2)}, u32[]{:S(2)}) collective-permute-start(f32[16,256]{1,0:T(8,128)S(1)} %add_add_fusion.10), channel_id=1, source_target_pairs={{0,3},{1,2},{2,1},{3,0},{4,7},{5,6},{6,5},{7,4},{8,11},{9,10},{10,... | collective-permute-start | bytes 49160 | tf_op jit(solution)/shard_map/ppermute | solution.py:266
  33.2 3.3 %collective-permute-done.9 = f32[16,256]{1,0:T(8,128)S(1)} collective-permute-done((f32[16,256]{1,0:T(8,128)S(1)}, f32[16,256]{1,0:T(8,128)S(1)}, u32[]{:S(2)}, u32[]{:S(2)}) %collective-permute-start.9) | collective-permute-done | bytes 16416 | tf_op jit(solution)/shard_map/ppermute | solution.py:266
  36.6 6.6 %collective-permute-start.11 = (f32[16,256]{1,0:T(8,128)S(1)}, f32[16,256]{1,0:T(8,128)S(1)}, u32[]{:S(2)}, u32[]{:S(2)}) collective-permute-start(f32[16,256]{1,0:T(8,128)S(1)} %add_add_fusion.9), channel_id=1, source_target_pairs={{0,16},{16,0},{1,17},{17,1},{2,18},{18,2},{3,19},{19,3},{4,20},{20... | collective-permute-start | bytes 49160 | tf_op jit(solution)/shard_map/ppermute | solution.py:257
  46.4 2.3 %collective-permute-start.16 = (f32[16,256]{1,0:T(8,128)S(1)}, f32[16,256]{1,0:T(8,128)S(1)}, u32[]{:S(2)}, u32[]{:S(2)}) collective-permute-start(f32[16,256]{1,0:T(8,128)S(1)} %add.162), channel_id=1, source_target_pairs={{0,96},{16,240},{32,64},{48,208},{64,32},{80,176},{96,0},{112,144}... | collective-permute-start | bytes 49160 | tf_op jit(solution)/shard_map/ppermute | solution.py:264
  53.7 1.7 collective-permute-start.19
  55.4 1.8 collective-permute-start.18
  57.9 3.1 %collective-permute-done.18 = f32[16,256]{1,0:T(8,128)S(1)} collective-permute-done((f32[16,256]{1,0:T(8,128)S(1)}, f32[16,256]{1,0:T(8,128)S(1)}, u32[]{:S(2)}, u32[]{:S(2)}) %collective-permute-start.18) | collective-permute-done | bytes 16416 | tf_op jit(solution)/shard_map/ppermute | solution.py:266
  66.8 1.7 collective-permute-done.21
  68.5 4.5 %collective-permute-start.23 = (f32[16,256]{1,0:T(8,128)S(1)}, f32[16,256]{1,0:T(8,128)S(1)}, u32[]{:S(2)}, u32[]{:S(2)}) collective-permute-start(f32[16,256]{1,0:T(8,128)S(1)} %add_add_fusion.6), channel_id=1, source_target_pairs={{0,16},{16,0},{1,17},{17,1},{2,18},{18,2},{3,19},{19,3},{4,20},{20... | collective-permute-start | bytes 49160 | tf_op jit(solution)/shard_map/ppermute | solution.py:257
  76.4 1.9 collective-permute-start.28
  78.5 2.3 %collective-permute-start.26 = (f32[16,256]{1,0:T(8,128)S(1)}, f32[16,256]{1,0:T(8,128)S(1)}, u32[]{:S(2)}, u32[]{:S(2)}) collective-permute-start(f32[16,256]{1,0:T(8,128)S(1)} %add.173), channel_id=1, source_target_pairs={{0,32},{16,176},{32,0},{48,144},{64,96},{80,240},{96,64},{112,208}... | collective-permute-start | bytes 49160 | tf_op jit(solution)/shard_map/ppermute | solution.py:264
  84.1 1.9 %collective-permute-start.30 = (f32[16,256]{1,0:T(8,128)S(1)}, f32[16,256]{1,0:T(8,128)S(1)}, u32[]{:S(2)}, u32[]{:S(2)}) collective-permute-start(f32[16,256]{1,0:T(8,128)S(1)} %add_add_fusion.5), channel_id=1, source_target_pairs={{0,8},{4,12},{8,0},{12,4},{1,9},{5,13},{9,1},{13,5},{2,10},{6,14},... | collective-permute-start | bytes 49160 | tf_op jit(solution)/shard_map/ppermute | solution.py:266
  87.1 2.5 %collective-permute-done.30 = f32[16,256]{1,0:T(8,128)S(1)} collective-permute-done((f32[16,256]{1,0:T(8,128)S(1)}, f32[16,256]{1,0:T(8,128)S(1)}, u32[]{:S(2)}, u32[]{:S(2)}) %collective-permute-start.30) | collective-permute-done | bytes 16416 | tf_op jit(solution)/shard_map/ppermute | solution.py:266
  90.1 2.1 %collective-permute-start.34 = (f32[16,256]{1,0:T(8,128)S(1)}, f32[16,256]{1,0:T(8,128)S(1)}, u32[]{:S(2)}, u32[]{:S(2)}) collective-permute-start(f32[16,256]{1,0:T(8,128)S(1)} %add_add_fusion.4), channel_id=1, source_target_pairs={{0,3},{1,2},{2,1},{3,0},{4,7},{5,6},{6,5},{7,4},{8,11},{9,10},{10,... | collective-permute-start | bytes 49160 | tf_op jit(solution)/shard_map/ppermute | solution.py:266
  95.5 2.3 %collective-permute-done.33 = f32[16,256]{1,0:T(8,128)S(1)} collective-permute-done((f32[16,256]{1,0:T(8,128)S(1)}, f32[16,256]{1,0:T(8,128)S(1)}, u32[]{:S(2)}, u32[]{:S(2)}) %collective-permute-start.33) | collective-permute-done | bytes 16416 | tf_op jit(solution)/shard_map/ppermute | solution.py:266
  97.8 4.7 %collective-permute-start.35 = (f32[16,256]{1,0:T(8,128)S(1)}, f32[16,256]{1,0:T(8,128)S(1)}, u32[]{:S(2)}, u32[]{:S(2)}) collective-permute-start(f32[16,256]{1,0:T(8,128)S(1)} %add_add_fusion.3), channel_id=1, source_target_pairs={{0,16},{16,0},{1,17},{17,1},{2,18},{18,2},{3,19},{19,3},{4,20},{20... | collective-permute-start | bytes 49160 | tf_op jit(solution)/shard_map/ppermute | solution.py:257
  103.3 7.5 %all-gather.3.cloned.1.call-done = bf16[49408,128]{1,0:T(8,128)(2,1)} async-done(((bf16[3088,128]{1,0:T(8,128)(2,1)}), bf16[49408,128]{1,0:T(8,128)(2,1)}) %all-gather.3.cloned.1.call-update) | async-done | bytes 12648464 | tf_op jit(solution)/shard_map/all_gather | solution.py:310
  110.8 23.7 %tile.8 = (f32[512,1024]{1,0:T(8,128)S(1)}, bf16[512,1024]{1,0:T(8,128)(2,1)S(1)}) custom-call(s32[4]{0:T(128)S(1)} %pad_add_fusion.refs_0_.place_ref, bf16[16,3088,128]{2,1,0:T(8,128)(2,1)} %bitcast.13, f32[64,256]{1,0:T(8,128)S(1)} %copy-done.1), custom_call_target="tpu_custom_call" | custom-call | flops 12884901888 | bytes 16842752 | tf_op jit(solution)/shard_map/tile/pallas_call | solution.py:371
  134.9 2.6 %collective-permute-done.36 = bf16[512,1024]{1,0:T(8,128)(2,1)S(1)} collective-permute-done((bf16[512,1024]{1,0:T(8,128)(2,1)S(1)}, bf16[512,1024]{1,0:T(8,128)(2,1)S(1)}, u32[]{:S(2)}, u32[]{:S(2)}) %collective-permute-start.36) | collective-permute-done | bytes 1048608 | tf_op jit(solution)/shard_map/ppermute | solution.py:372
  137.6 1.7 convert_add_fusion
  142.0 3.5 %collective-permute-start.41 = (f32[16,256]{1,0:T(8,128)S(1)}, f32[16,256]{1,0:T(8,128)S(1)}, u32[]{:S(2)}, u32[]{:S(2)}) collective-permute-start(f32[16,256]{1,0:T(8,128)S(1)} %add.185), channel_id=1, source_target_pairs={{0,96},{16,240},{32,64},{48,208},{64,32},{80,176},{96,0},{112,144}... | collective-permute-start | bytes 49160 | tf_op jit(solution)/shard_map/ppermute | solution.py:264
  147.5 2.6 %collective-permute-done.40 = f32[16,256]{1,0:T(8,128)S(1)} collective-permute-done((f32[16,256]{1,0:T(8,128)S(1)}, f32[16,256]{1,0:T(8,128)S(1)}, u32[]{:S(2)}, u32[]{:S(2)}) %collective-permute-start.40) | collective-permute-done | bytes 16416 | tf_op jit(solution)/shard_map/ppermute | solution.py:264
  154.3 2.6 %collective-permute-done.43 = f32[16,256]{1,0:T(8,128)S(1)} collective-permute-done((f32[16,256]{1,0:T(8,128)S(1)}, f32[16,256]{1,0:T(8,128)S(1)}, u32[]{:S(2)}, u32[]{:S(2)}) %collective-permute-start.43) | collective-permute-done | bytes 16416 | tf_op jit(solution)/shard_map/ppermute | solution.py:266
  157.0 2.3 %collective-permute-start.47 = (f32[16,256]{1,0:T(8,128)S(1)}, f32[16,256]{1,0:T(8,128)S(1)}, u32[]{:S(2)}, u32[]{:S(2)}) collective-permute-start(f32[16,256]{1,0:T(8,128)S(1)} %add_add_fusion.1), channel_id=1, source_target_pairs={{0,3},{1,2},{2,1},{3,0},{4,7},{5,6},{6,5},{7,4},{8,11},{9,10},{10,... | collective-permute-start | bytes 49160 | tf_op jit(solution)/shard_map/ppermute | solution.py:266
  162.0 2.5 %collective-permute-done.46 = f32[16,256]{1,0:T(8,128)S(1)} collective-permute-done((f32[16,256]{1,0:T(8,128)S(1)}, f32[16,256]{1,0:T(8,128)S(1)}, u32[]{:S(2)}, u32[]{:S(2)}) %collective-permute-start.46) | collective-permute-done | bytes 16416 | tf_op jit(solution)/shard_map/ppermute | solution.py:266
  164.5 5.9 %collective-permute-start.48 = (f32[16,256]{1,0:T(8,128)S(1)}, f32[16,256]{1,0:T(8,128)S(1)}, u32[]{:S(2)}, u32[]{:S(2)}) collective-permute-start(f32[16,256]{1,0:T(8,128)S(1)} %add_add_fusion), channel_id=1, source_target_pairs={{0,16},{16,0},{1,17},{17,1},{2,18},{18,2},{3,19},{19,3},{4,20},{20... | collective-permute-start | bytes 49160 | tf_op jit(solution)/shard_map/ppermute | solution.py:257
  171.3 1.9 answer.1
  173.1 8.0 %reduce-scatter.2.cloned.1.call-done = f32[64,1024]{1,0:T(8,128)} async-done(((f32[512,1024]{1,0:T(8,128)}), f32[64,1024]{1,0:T(8,128)}) %reduce-scatter.2.cloned.1.call-update) | async-done | bytes 262160 | tf_op jit(solution)/shard_map/reduce_scatter | solution.py:374
  (121 shorter events, 50.4 us)
Async XLA Ops:
  7.2 103.6 %all-gather.3.cloned.1.call-start = ((), (), s32[]{:S(2)}) async-start(), calls=%async_computation.2 | async-start | bytes 13438976 | tf_op jit(solution)/shard_map/all_gather | solution.py:310
  9.7 171.4 %reduce-scatter.2.cloned.1.call-start = ((), (), s32[]{:S(2)}) async-start(), calls=%async_computation.1 | async-start | bytes 2359296 | tf_op jit(solution)/shard_map/reduce_scatter | solution.py:374
  11.8 6.3 %collective-permute-start.4 = (f32[16,256]{1,0:T(8,128)S(1)}, f32[16,256]{1,0:T(8,128)S(1)}, u32[]{:S(2)}, u32[]{:S(2)}) collective-permute-start(f32[16,256]{1,0:T(8,128)S(1)} %add.150), channel_id=1, source_target_pairs={{0,96},{16,240},{32,64},{48,208},{64,32},{80,176},{96,0},{112,144}... | collective-permute-start | bytes 49160 | tf_op jit(solution)/shard_map/ppermute | solution.py:264
  16.4 4.6 %collective-permute-start.3 = (f32[16,256]{1,0:T(8,128)S(1)}, f32[16,256]{1,0:T(8,128)S(1)}, u32[]{:S(2)}, u32[]{:S(2)}) collective-permute-start(f32[16,256]{1,0:T(8,128)S(1)} %add.150), channel_id=1, source_target_pairs={{0,64},{16,208},{32,96},{48,240},{64,0},{80,144},{96,32},{112,176}... | collective-permute-start | bytes 49160 | tf_op jit(solution)/shard_map/ppermute | solution.py:264
  16.4 4.6 %collective-permute-start.2 = (f32[16,256]{1,0:T(8,128)S(1)}, f32[16,256]{1,0:T(8,128)S(1)}, u32[]{:S(2)}, u32[]{:S(2)}) collective-permute-start(f32[16,256]{1,0:T(8,128)S(1)} %add.150), channel_id=1, source_target_pairs={{0,32},{16,176},{32,0},{48,144},{64,96},{80,240},{96,64},{112,208}... | collective-permute-start | bytes 49160 | tf_op jit(solution)/shard_map/ppermute | solution.py:264
  22.6 5.2 %collective-permute-start.6 = (f32[16,256]{1,0:T(8,128)S(1)}, f32[16,256]{1,0:T(8,128)S(1)}, u32[]{:S(2)}, u32[]{:S(2)}) collective-permute-start(f32[16,256]{1,0:T(8,128)S(1)} %add_add_fusion.11), channel_id=1, source_target_pairs={{0,8},{4,12},{8,0},{12,4},{1,9},{5,13},{9,1},{13,5},{2,10},{6,14},... | collective-permute-start | bytes 49160 | tf_op jit(solution)/shard_map/ppermute | solution.py:266
  27.9 5.4 %collective-permute-start.10 = (f32[16,256]{1,0:T(8,128)S(1)}, f32[16,256]{1,0:T(8,128)S(1)}, u32[]{:S(2)}, u32[]{:S(2)}) collective-permute-start(f32[16,256]{1,0:T(8,128)S(1)} %add_add_fusion.10), channel_id=1, source_target_pairs={{0,3},{1,2},{2,1},{3,0},{4,7},{5,6},{6,5},{7,4},{8,11},{9,10},{10,... | collective-permute-start | bytes 49160 | tf_op jit(solution)/shard_map/ppermute | solution.py:266
  31.0 5.6 %collective-permute-start.9 = (f32[16,256]{1,0:T(8,128)S(1)}, f32[16,256]{1,0:T(8,128)S(1)}, u32[]{:S(2)}, u32[]{:S(2)}) collective-permute-start(f32[16,256]{1,0:T(8,128)S(1)} %add_add_fusion.10), channel_id=1, source_target_pairs={{0,2},{1,3},{2,0},{3,1},{4,6},{5,7},{6,4},{7,5},{8,10},{9,11},{10,... | collective-permute-start | bytes 49160 | tf_op jit(solution)/shard_map/ppermute | solution.py:266
  31.6 4.9 %collective-permute-start.8 = (f32[16,256]{1,0:T(8,128)S(1)}, f32[16,256]{1,0:T(8,128)S(1)}, u32[]{:S(2)}, u32[]{:S(2)}) collective-permute-start(f32[16,256]{1,0:T(8,128)S(1)} %add_add_fusion.10), channel_id=1, source_target_pairs={{0,1},{1,0},{2,3},{3,2},{4,5},{5,4},{6,7},{7,6},{8,9},{9,8},{10,11... | collective-permute-start | bytes 49160 | tf_op jit(solution)/shard_map/ppermute | solution.py:266
  36.6 7.4 %collective-permute-start.11 = (f32[16,256]{1,0:T(8,128)S(1)}, f32[16,256]{1,0:T(8,128)S(1)}, u32[]{:S(2)}, u32[]{:S(2)}) collective-permute-start(f32[16,256]{1,0:T(8,128)S(1)} %add_add_fusion.9), channel_id=1, source_target_pairs={{0,16},{16,0},{1,17},{17,1},{2,18},{18,2},{3,19},{19,3},{4,20},{20... | collective-permute-start | bytes 49160 | tf_op jit(solution)/shard_map/ppermute | solution.py:257
  46.4 5.6 %collective-permute-start.16 = (f32[16,256]{1,0:T(8,128)S(1)}, f32[16,256]{1,0:T(8,128)S(1)}, u32[]{:S(2)}, u32[]{:S(2)}) collective-permute-start(f32[16,256]{1,0:T(8,128)S(1)} %add.162), channel_id=1, source_target_pairs={{0,96},{16,240},{32,64},{48,208},{64,32},{80,176},{96,0},{112,144}... | collective-permute-start | bytes 49160 | tf_op jit(solution)/shard_map/ppermute | solution.py:264
  48.6 4.6 %collective-permute-start.15 = (f32[16,256]{1,0:T(8,128)S(1)}, f32[16,256]{1,0:T(8,128)S(1)}, u32[]{:S(2)}, u32[]{:S(2)}) collective-permute-start(f32[16,256]{1,0:T(8,128)S(1)} %add.162), channel_id=1, source_target_pairs={{0,64},{16,208},{32,96},{48,240},{64,0},{80,144},{96,32},{112,176}... | collective-permute-start | bytes 49160 | tf_op jit(solution)/shard_map/ppermute | solution.py:264
  55.4 5.6 %collective-permute-start.18 = (f32[16,256]{1,0:T(8,128)S(1)}, f32[16,256]{1,0:T(8,128)S(1)}, u32[]{:S(2)}, u32[]{:S(2)}) collective-permute-start(f32[16,256]{1,0:T(8,128)S(1)} %add_add_fusion.8), channel_id=1, source_target_pairs={{0,8},{4,12},{8,0},{12,4},{1,9},{5,13},{9,1},{13,5},{2,10},{6,14},... | collective-permute-start | bytes 49160 | tf_op jit(solution)/shard_map/ppermute | solution.py:266
  61.3 5.5 %collective-permute-start.22 = (f32[16,256]{1,0:T(8,128)S(1)}, f32[16,256]{1,0:T(8,128)S(1)}, u32[]{:S(2)}, u32[]{:S(2)}) collective-permute-start(f32[16,256]{1,0:T(8,128)S(1)} %add_add_fusion.7), channel_id=1, source_target_pairs={{0,3},{1,2},{2,1},{3,0},{4,7},{5,6},{6,5},{7,4},{8,11},{9,10},{10,... | collective-permute-start | bytes 49160 | tf_op jit(solution)/shard_map/ppermute | solution.py:266
  62.9 5.6 %collective-permute-start.21 = (f32[16,256]{1,0:T(8,128)S(1)}, f32[16,256]{1,0:T(8,128)S(1)}, u32[]{:S(2)}, u32[]{:S(2)}) collective-permute-start(f32[16,256]{1,0:T(8,128)S(1)} %add_add_fusion.7), channel_id=1, source_target_pairs={{0,2},{1,3},{2,0},{3,1},{4,6},{5,7},{6,4},{7,5},{8,10},{9,11},{10,... | collective-permute-start | bytes 49160 | tf_op jit(solution)/shard_map/ppermute | solution.py:266
  64.2 4.3 %collective-permute-start.20 = (f32[16,256]{1,0:T(8,128)S(1)}, f32[16,256]{1,0:T(8,128)S(1)}, u32[]{:S(2)}, u32[]{:S(2)}) collective-permute-start(f32[16,256]{1,0:T(8,128)S(1)} %add_add_fusion.7), channel_id=1, source_target_pairs={{0,1},{1,0},{2,3},{3,2},{4,5},{5,4},{6,7},{7,6},{8,9},{9,8},{10,11... | collective-permute-start | bytes 49160 | tf_op jit(solution)/shard_map/ppermute | solution.py:266
  68.5 5.3 %collective-permute-start.23 = (f32[16,256]{1,0:T(8,128)S(1)}, f32[16,256]{1,0:T(8,128)S(1)}, u32[]{:S(2)}, u32[]{:S(2)}) collective-permute-start(f32[16,256]{1,0:T(8,128)S(1)} %add_add_fusion.6), channel_id=1, source_target_pairs={{0,16},{16,0},{1,17},{17,1},{2,18},{18,2},{3,19},{19,3},{4,20},{20... | collective-permute-start | bytes 49160 | tf_op jit(solution)/shard_map/ppermute | solution.py:257
  76.4 5.5 %collective-permute-start.28 = (f32[16,256]{1,0:T(8,128)S(1)}, f32[16,256]{1,0:T(8,128)S(1)}, u32[]{:S(2)}, u32[]{:S(2)}) collective-permute-start(f32[16,256]{1,0:T(8,128)S(1)} %add.173), channel_id=1, source_target_pairs={{0,96},{16,240},{32,64},{48,208},{64,32},{80,176},{96,0},{112,144}... | collective-permute-start | bytes 49160 | tf_op jit(solution)/shard_map/ppermute | solution.py:264
  78.2 4.7 %collective-permute-start.27 = (f32[16,256]{1,0:T(8,128)S(1)}, f32[16,256]{1,0:T(8,128)S(1)}, u32[]{:S(2)}, u32[]{:S(2)}) collective-permute-start(f32[16,256]{1,0:T(8,128)S(1)} %add.173), channel_id=1, source_target_pairs={{0,64},{16,208},{32,96},{48,240},{64,0},{80,144},{96,32},{112,176}... | collective-permute-start | bytes 49160 | tf_op jit(solution)/shard_map/ppermute | solution.py:264
  78.5 4.5 %collective-permute-start.26 = (f32[16,256]{1,0:T(8,128)S(1)}, f32[16,256]{1,0:T(8,128)S(1)}, u32[]{:S(2)}, u32[]{:S(2)}) collective-permute-start(f32[16,256]{1,0:T(8,128)S(1)} %add.173), channel_id=1, source_target_pairs={{0,32},{16,176},{32,0},{48,144},{64,96},{80,240},{96,64},{112,208}... | collective-permute-start | bytes 49160 | tf_op jit(solution)/shard_map/ppermute | solution.py:264
  84.1 5.6 %collective-permute-start.30 = (f32[16,256]{1,0:T(8,128)S(1)}, f32[16,256]{1,0:T(8,128)S(1)}, u32[]{:S(2)}, u32[]{:S(2)}) collective-permute-start(f32[16,256]{1,0:T(8,128)S(1)} %add_add_fusion.5), channel_id=1, source_target_pairs={{0,8},{4,12},{8,0},{12,4},{1,9},{5,13},{9,1},{13,5},{2,10},{6,14},... | collective-permute-start | bytes 49160 | tf_op jit(solution)/shard_map/ppermute | solution.py:266
  90.1 5.3 %collective-permute-start.34 = (f32[16,256]{1,0:T(8,128)S(1)}, f32[16,256]{1,0:T(8,128)S(1)}, u32[]{:S(2)}, u32[]{:S(2)}) collective-permute-start(f32[16,256]{1,0:T(8,128)S(1)} %add_add_fusion.4), channel_id=1, source_target_pairs={{0,3},{1,2},{2,1},{3,0},{4,7},{5,6},{6,5},{7,4},{8,11},{9,10},{10,... | collective-permute-start | bytes 49160 | tf_op jit(solution)/shard_map/ppermute | solution.py:266
  92.2 5.6 %collective-permute-start.33 = (f32[16,256]{1,0:T(8,128)S(1)}, f32[16,256]{1,0:T(8,128)S(1)}, u32[]{:S(2)}, u32[]{:S(2)}) collective-permute-start(f32[16,256]{1,0:T(8,128)S(1)} %add_add_fusion.4), channel_id=1, source_target_pairs={{0,2},{1,3},{2,0},{3,1},{4,6},{5,7},{6,4},{7,5},{8,10},{9,11},{10,... | collective-permute-start | bytes 49160 | tf_op jit(solution)/shard_map/ppermute | solution.py:266
  97.8 5.5 %collective-permute-start.35 = (f32[16,256]{1,0:T(8,128)S(1)}, f32[16,256]{1,0:T(8,128)S(1)}, u32[]{:S(2)}, u32[]{:S(2)}) collective-permute-start(f32[16,256]{1,0:T(8,128)S(1)} %add_add_fusion.3), channel_id=1, source_target_pairs={{0,16},{16,0},{1,17},{17,1},{2,18},{18,2},{3,19},{19,3},{4,20},{20... | collective-permute-start | bytes 49160 | tf_op jit(solution)/shard_map/ppermute | solution.py:257
  142.0 5.5 %collective-permute-start.41 = (f32[16,256]{1,0:T(8,128)S(1)}, f32[16,256]{1,0:T(8,128)S(1)}, u32[]{:S(2)}, u32[]{:S(2)}) collective-permute-start(f32[16,256]{1,0:T(8,128)S(1)} %add.185), channel_id=1, source_target_pairs={{0,96},{16,240},{32,64},{48,208},{64,32},{80,176},{96,0},{112,144}... | collective-permute-start | bytes 49160 | tf_op jit(solution)/shard_map/ppermute | solution.py:264
  145.5 4.6 %collective-permute-start.40 = (f32[16,256]{1,0:T(8,128)S(1)}, f32[16,256]{1,0:T(8,128)S(1)}, u32[]{:S(2)}, u32[]{:S(2)}) collective-permute-start(f32[16,256]{1,0:T(8,128)S(1)} %add.185), channel_id=1, source_target_pairs={{0,64},{16,208},{32,96},{48,240},{64,0},{80,144},{96,32},{112,176}... | collective-permute-start | bytes 49160 | tf_op jit(solution)/shard_map/ppermute | solution.py:264
  145.5 4.6 %collective-permute-start.39 = (f32[16,256]{1,0:T(8,128)S(1)}, f32[16,256]{1,0:T(8,128)S(1)}, u32[]{:S(2)}, u32[]{:S(2)}) collective-permute-start(f32[16,256]{1,0:T(8,128)S(1)} %add.185), channel_id=1, source_target_pairs={{0,32},{16,176},{32,0},{48,144},{64,96},{80,240},{96,64},{112,208}... | collective-permute-start | bytes 49160 | tf_op jit(solution)/shard_map/ppermute | solution.py:264
  151.7 5.2 %collective-permute-start.43 = (f32[16,256]{1,0:T(8,128)S(1)}, f32[16,256]{1,0:T(8,128)S(1)}, u32[]{:S(2)}, u32[]{:S(2)}) collective-permute-start(f32[16,256]{1,0:T(8,128)S(1)} %add_add_fusion.2), channel_id=1, source_target_pairs={{0,8},{4,12},{8,0},{12,4},{1,9},{5,13},{9,1},{13,5},{2,10},{6,14},... | collective-permute-start | bytes 49160 | tf_op jit(solution)/shard_map/ppermute | solution.py:266
  157.0 5.0 %collective-permute-start.47 = (f32[16,256]{1,0:T(8,128)S(1)}, f32[16,256]{1,0:T(8,128)S(1)}, u32[]{:S(2)}, u32[]{:S(2)}) collective-permute-start(f32[16,256]{1,0:T(8,128)S(1)} %add_add_fusion.1), channel_id=1, source_target_pairs={{0,3},{1,2},{2,1},{3,0},{4,7},{5,6},{6,5},{7,4},{8,11},{9,10},{10,... | collective-permute-start | bytes 49160 | tf_op jit(solution)/shard_map/ppermute | solution.py:266
  159.2 5.2 %collective-permute-start.46 = (f32[16,256]{1,0:T(8,128)S(1)}, f32[16,256]{1,0:T(8,128)S(1)}, u32[]{:S(2)}, u32[]{:S(2)}) collective-permute-start(f32[16,256]{1,0:T(8,128)S(1)} %add_add_fusion.1), channel_id=1, source_target_pairs={{0,2},{1,3},{2,0},{3,1},{4,6},{5,7},{6,4},{7,5},{8,10},{9,11},{10,... | collective-permute-start | bytes 49160 | tf_op jit(solution)/shard_map/ppermute | solution.py:266
  160.1 4.4 %collective-permute-start.45 = (f32[16,256]{1,0:T(8,128)S(1)}, f32[16,256]{1,0:T(8,128)S(1)}, u32[]{:S(2)}, u32[]{:S(2)}) collective-permute-start(f32[16,256]{1,0:T(8,128)S(1)} %add_add_fusion.1), channel_id=1, source_target_pairs={{0,1},{1,0},{2,3},{3,2},{4,5},{5,4},{6,7},{7,6},{8,9},{9,8},{10,11... | collective-permute-start | bytes 49160 | tf_op jit(solution)/shard_map/ppermute | solution.py:266
  164.5 6.8 %collective-permute-start.48 = (f32[16,256]{1,0:T(8,128)S(1)}, f32[16,256]{1,0:T(8,128)S(1)}, u32[]{:S(2)}, u32[]{:S(2)}) collective-permute-start(f32[16,256]{1,0:T(8,128)S(1)} %add_add_fusion), channel_id=1, source_target_pairs={{0,16},{16,0},{1,17},{17,1},{2,18},{18,2},{3,19},{19,3},{4,20},{20... | collective-permute-start | bytes 49160 | tf_op jit(solution)/shard_map/ppermute | solution.py:257
  (25 other events, 100.4 us)
Sparse Core Ops, SparseCore 0:
  10.5 100.2 all-gather.2
  139.4 41.7 reduce-scatter.1

commit v8 on v7

--- a/solution.py
+++ b/solution.py
@@ -163,8 +163,8 @@
     return value
 
 
-def tile_kernel(slots, blocks, width, strip, parts, place_ref, got_ref, cam_ref, own_ref, peer_ref, acc_ref, *operands):
-    z_idx, core_idx, row_idx, col_idx = place_ref[0], place_ref[1], place_ref[2], place_ref[3]
+def tile_kernel(slots, blocks, width, strip, parts, place_ref, got_ref, own_ref, peer_ref, acc_ref, *operands):
+    core_idx, row_idx, col_idx = place_ref[1], place_ref[2], place_ref[3]
     sources, _, points = got_ref.shape
     half, col_count = own_ref.shape
     col_blocks = col_count // width
@@ -176,12 +176,6 @@
     def _():
         own_ref[...] = jnp.zeros_like(own_ref)
         acc_ref[...] = jnp.zeros_like(acc_ref)
-        for c in range(col_blocks):
-
-            @pl.when(col_idx * col_blocks + c == 2 * z_idx + core_idx)
-            def _():
-                start = pl.multiple_of(z_idx * strip, strip)
-                own_ref[pl.ds(start, strip), c * width : (c + 1) * width] = cam_ref[...]
 
     def build(part, row_ref, col_ref):
         for s in range(sources):
@@ -340,7 +334,6 @@
         in_specs=[
             smem,
             pl.BlockSpec((pair, send_rows, points), lambda i: (jnp.minimum(i, steps - 1), 0, 0)),
-            pl.BlockSpec((strip, width), lambda i: (0, 0)),
         ],
         out_specs=(
             pl.BlockSpec((half, col_count), lambda i: (0, 0)),
@@ -368,10 +361,14 @@
     for _ in range(1, ITERS):
         known.append(all_sum(product(known), n_z, n_row, n_col))
     got, known = lax.optimization_barrier((got, known))
-    own_half, peer_half = make_halves(place, got, camera_blocks)
+    own_half, peer_half = make_halves(place, got)
     taken = lax.ppermute(peer_half, "core", [(0, 1), (1, 0)])
-    tile, known = lax.optimization_barrier((own_half + taken.astype(jnp.float32), known))
-    schur = lax.psum_scatter(tile, "z", scatter_dimension=0, tiled=True)
+    tile, known = lax.optimization_barrier(((own_half + taken.astype(jnp.float32)).astype(jnp.bfloat16), known))
+    minus_g = lax.psum_scatter(tile, "z", scatter_dimension=0, tiled=True)
+    col_blocks = col_count // width
+    block_at = jnp.arange(col_count, dtype=jnp.int32)[None, :] // width + col_idx * col_blocks
+    cams = jnp.where(block_at == pts_idx, jnp.tile(camera_blocks, (1, col_blocks)), 0.0)
+    schur = minus_g.astype(jnp.float32) + cams
     known.append(all_sum(product(known), n_z, n_row, n_col))
     own = jax.ShapeDtypeStruct((1, strip), jnp.float32)
     own_rhs, answer = pl.pallas_call(

time: 188 us -> 187 us (level)
  starting transfers between devices: 77.7 us -> 65.7 us
  waiting for transfers between devices: 61.4 us -> 70.2 us
    ppermute x8, starting transfers between devices: 22.7 us -> 8.74 us  [core_sum(): return value + lax.ppermute(value, 'core', [(0, 1), (1, 0)])]
    ppermute x16, waiting for transfers between devices: 10.3 us -> 18.3 us  [all_sum(): value = tree([lax.ppermute(value, ('z', 'core'), p) for p in pairs])]
    ppermute x24, waiting for transfers between devices: 25.7 us -> 29 us  [all_sum(): lax.ppermute(value, axis, [(i, i ^ b) for i in range(size)])]
  transfers between devices with their start and end apart: 51 -> 51, of which waited for: 34 -> 39; matrix products, arithmetic and copies ran while one was open for 0% -> 0% of each run, Pallas kernels for 3% -> 3%
where the time goes in v8:
time: 187 us; the launch traced here: 186 us
  waiting for transfers between devices  70.2 us (38%)
  starting transfers between devices  65.7 us (35%)
  Pallas kernels  32.5 us (17%)
  between operations  14.3 us (8%)
  other arithmetic  3.34 us (2%)
    ppermute x24, starting transfers between devices, all_sum(): lax.ppermute(value, axis, [(i, i ^ b) for i in range(size)])  34.4 us
    ppermute x24, waiting for transfers between devices, all_sum(): lax.ppermute(value, axis, [(i, i ^ b) for i in range(size)])  29 us
    pallas_call x1, Pallas kernels, per_device(): own_half, peer_half = make_halves(place, got)  23.8 us
    ppermute x16, starting transfers between devices, all_sum(): value = tree([lax.ppermute(value, ('z', 'core'), p) for p in pairs])  22.1 us
    ppermute x16, waiting for transfers between devices, all_sum(): value = tree([lax.ppermute(value, ('z', 'core'), p) for p in pairs])  18.3 us
    ppermute x8, starting transfers between devices, core_sum(): return value + lax.ppermute(value, 'core', [(0, 1), (1, 0)])  8.74 us
    reduce_scatter x1, waiting for transfers between devices, per_device(): minus_g = lax.psum_scatter(tile, 'z', scatter_dimension=0, tiled=True)  7.15 us
    ppermute x8, waiting for transfers between devices, core_sum(): return value + lax.ppermute(value, 'core', [(0, 1), (1, 0)])  7.06 us
  transfers between devices with their start and end apart: 51, of which 39 were waited for; matrix products, arithmetic and copies ran while one was open for 0% of the time, Pallas kernels for 3%

profile of v8, /device:TPU:2, one launch (start us, length us, event | category | flops | bytes accessed | tf_op | source)
XLA Modules:
  0.0 186.4 jit_solution(8265104969054721108)
XLA Ops:
  7.3 2.4 %send.1 = bf16[3088,128]{1,0:T(8,128)(2,1)} custom-call(bf16[1536,256]{1,0:T(8,128)(2,1)} %bitcast.10, s32[4,128]{1,0:T(4,128)} %refs_1_.5, bf16[6,128]{1,0:T(8,128)(2,1)} %inv_ref.3), custom_call_target="tpu_custom_call" | custom-call | tf_op jit(solution)/shard_map/send/pallas_call | solution.py:297
  12.4 2.0 %collective-permute-start.2 = (f32[16,256]{1,0:T(8,128)S(1)}, f32[16,256]{1,0:T(8,128)S(1)}, u32[]{:S(2)}, u32[]{:S(2)}) collective-permute-start(f32[16,256]{1,0:T(8,128)S(1)} %add.170), channel_id=1, source_target_pairs={{0,32},{16,176},{32,0},{48,144},{64,96},{80,240},{96,64},{112,208}... | collective-permute-start | bytes 49160 | tf_op jit(solution)/shard_map/ppermute | solution.py:258
  14.4 3.3 %collective-permute-start.3 = (f32[16,256]{1,0:T(8,128)S(1)}, f32[16,256]{1,0:T(8,128)S(1)}, u32[]{:S(2)}, u32[]{:S(2)}) collective-permute-start(f32[16,256]{1,0:T(8,128)S(1)} %add.170), channel_id=1, source_target_pairs={{0,64},{16,208},{32,96},{48,240},{64,0},{80,144},{96,32},{112,176}... | collective-permute-start | bytes 49160 | tf_op jit(solution)/shard_map/ppermute | solution.py:258
  19.4 3.8 %collective-permute-done.4 = f32[16,256]{1,0:T(8,128)S(1)} collective-permute-done((f32[16,256]{1,0:T(8,128)S(1)}, f32[16,256]{1,0:T(8,128)S(1)}, u32[]{:S(2)}, u32[]{:S(2)}) %collective-permute-start.4) | collective-permute-done | bytes 16416 | tf_op jit(solution)/shard_map/ppermute | solution.py:258
  23.9 2.4 %collective-permute-start.6 = (f32[16,256]{1,0:T(8,128)S(1)}, f32[16,256]{1,0:T(8,128)S(1)}, u32[]{:S(2)}, u32[]{:S(2)}) collective-permute-start(f32[16,256]{1,0:T(8,128)S(1)} %add_add_fusion.11), channel_id=1, source_target_pairs={{0,8},{4,12},{8,0},{12,4},{1,9},{5,13},{9,1},{13,5},{2,10},{6,14},... | collective-permute-start | bytes 49160 | tf_op jit(solution)/shard_map/ppermute | solution.py:260
  27.1 2.0 %collective-permute-done.6 = f32[16,256]{1,0:T(8,128)S(1)} collective-permute-done((f32[16,256]{1,0:T(8,128)S(1)}, f32[16,256]{1,0:T(8,128)S(1)}, u32[]{:S(2)}, u32[]{:S(2)}) %collective-permute-start.6) | collective-permute-done | bytes 16416 | tf_op jit(solution)/shard_map/ppermute | solution.py:260
  30.0 3.1 %collective-permute-start.10 = (f32[16,256]{1,0:T(8,128)S(1)}, f32[16,256]{1,0:T(8,128)S(1)}, u32[]{:S(2)}, u32[]{:S(2)}) collective-permute-start(f32[16,256]{1,0:T(8,128)S(1)} %add_add_fusion.10), channel_id=1, source_target_pairs={{0,3},{1,2},{2,1},{3,0},{4,7},{5,6},{6,5},{7,4},{8,11},{9,10},{10,... | collective-permute-start | bytes 49160 | tf_op jit(solution)/shard_map/ppermute | solution.py:260
  38.7 3.5 %collective-permute-start.11 = (f32[16,256]{1,0:T(8,128)S(1)}, f32[16,256]{1,0:T(8,128)S(1)}, u32[]{:S(2)}, u32[]{:S(2)}) collective-permute-start(f32[16,256]{1,0:T(8,128)S(1)} %add_add_fusion.9), channel_id=1, source_target_pairs={{0,16},{16,0},{1,17},{17,1},{2,18},{18,2},{3,19},{19,3},{4,20},{20... | collective-permute-start | bytes 49160 | tf_op jit(solution)/shard_map/ppermute | solution.py:251
  46.1 2.5 %collective-permute-start.14 = (f32[16,256]{1,0:T(8,128)S(1)}, f32[16,256]{1,0:T(8,128)S(1)}, u32[]{:S(2)}, u32[]{:S(2)}) collective-permute-start(f32[16,256]{1,0:T(8,128)S(1)} %add.182), channel_id=1, source_target_pairs={{0,32},{16,176},{32,0},{48,144},{64,96},{80,240},{96,64},{112,208}... | collective-permute-start | bytes 49160 | tf_op jit(solution)/shard_map/ppermute | solution.py:258
  49.1 1.9 %collective-permute-start.16 = (f32[16,256]{1,0:T(8,128)S(1)}, f32[16,256]{1,0:T(8,128)S(1)}, u32[]{:S(2)}, u32[]{:S(2)}) collective-permute-start(f32[16,256]{1,0:T(8,128)S(1)} %add.182), channel_id=1, source_target_pairs={{0,96},{16,240},{32,64},{48,208},{64,32},{80,176},{96,0},{112,144}... | collective-permute-start | bytes 49160 | tf_op jit(solution)/shard_map/ppermute | solution.py:258
  51.0 2.2 %collective-permute-done.15 = f32[16,256]{1,0:T(8,128)S(1)} collective-permute-done((f32[16,256]{1,0:T(8,128)S(1)}, f32[16,256]{1,0:T(8,128)S(1)}, u32[]{:S(2)}, u32[]{:S(2)}) %collective-permute-start.15) | collective-permute-done | bytes 16416 | tf_op jit(solution)/shard_map/ppermute | solution.py:258
  54.7 2.8 %collective-permute-start.17 = (f32[16,256]{1,0:T(8,128)S(1)}, f32[16,256]{1,0:T(8,128)S(1)}, u32[]{:S(2)}, u32[]{:S(2)}) collective-permute-start(f32[16,256]{1,0:T(8,128)S(1)} %add_add_fusion.8), channel_id=1, source_target_pairs={{0,4},{4,0},{8,12},{12,8},{1,5},{5,1},{9,13},{13,9},{2,6},{6,2},{1... | collective-permute-start | bytes 49160 | tf_op jit(solution)/shard_map/ppermute | solution.py:260
  59.6 3.5 %collective-permute-done.18 = f32[16,256]{1,0:T(8,128)S(1)} collective-permute-done((f32[16,256]{1,0:T(8,128)S(1)}, f32[16,256]{1,0:T(8,128)S(1)}, u32[]{:S(2)}, u32[]{:S(2)}) %collective-permute-start.18) | collective-permute-done | bytes 16416 | tf_op jit(solution)/shard_map/ppermute | solution.py:260
  63.1 1.9 %collective-permute-start.20 = (f32[16,256]{1,0:T(8,128)S(1)}, f32[16,256]{1,0:T(8,128)S(1)}, u32[]{:S(2)}, u32[]{:S(2)}) collective-permute-start(f32[16,256]{1,0:T(8,128)S(1)} %add_add_fusion.7), channel_id=1, source_target_pairs={{0,1},{1,0},{2,3},{3,2},{4,5},{5,4},{6,7},{7,6},{8,9},{9,8},{10,11... | collective-permute-start | bytes 49160 | tf_op jit(solution)/shard_map/ppermute | solution.py:260
  68.1 2.6 %collective-permute-done.21 = f32[16,256]{1,0:T(8,128)S(1)} collective-permute-done((f32[16,256]{1,0:T(8,128)S(1)}, f32[16,256]{1,0:T(8,128)S(1)}, u32[]{:S(2)}, u32[]{:S(2)}) %collective-permute-start.21) | collective-permute-done | bytes 16416 | tf_op jit(solution)/shard_map/ppermute | solution.py:260
  77.3 2.4 %collective-permute-start.26 = (f32[16,256]{1,0:T(8,128)S(1)}, f32[16,256]{1,0:T(8,128)S(1)}, u32[]{:S(2)}, u32[]{:S(2)}) collective-permute-start(f32[16,256]{1,0:T(8,128)S(1)} %add.193), channel_id=1, source_target_pairs={{0,32},{16,176},{32,0},{48,144},{64,96},{80,240},{96,64},{112,208}... | collective-permute-start | bytes 49160 | tf_op jit(solution)/shard_map/ppermute | solution.py:258
  82.1 2.2 %collective-permute-done.27 = f32[16,256]{1,0:T(8,128)S(1)} collective-permute-done((f32[16,256]{1,0:T(8,128)S(1)}, f32[16,256]{1,0:T(8,128)S(1)}, u32[]{:S(2)}, u32[]{:S(2)}) %collective-permute-start.27) | collective-permute-done | bytes 16416 | tf_op jit(solution)/shard_map/ppermute | solution.py:258
  90.2 2.9 %collective-permute-done.30 = f32[16,256]{1,0:T(8,128)S(1)} collective-permute-done((f32[16,256]{1,0:T(8,128)S(1)}, f32[16,256]{1,0:T(8,128)S(1)}, u32[]{:S(2)}, u32[]{:S(2)}) %collective-permute-start.30) | collective-permute-done | bytes 16416 | tf_op jit(solution)/shard_map/ppermute | solution.py:260
  93.4 3.4 %collective-permute-start.33 = (f32[16,256]{1,0:T(8,128)S(1)}, f32[16,256]{1,0:T(8,128)S(1)}, u32[]{:S(2)}, u32[]{:S(2)}) collective-permute-start(f32[16,256]{1,0:T(8,128)S(1)} %add_add_fusion.4), channel_id=1, source_target_pairs={{0,2},{1,3},{2,0},{3,1},{4,6},{5,7},{6,4},{7,5},{8,10},{9,11},{10,... | collective-permute-start | bytes 49160 | tf_op jit(solution)/shard_map/ppermute | solution.py:260
  99.4 2.7 %collective-permute-done.34 = f32[16,256]{1,0:T(8,128)S(1)} collective-permute-done((f32[16,256]{1,0:T(8,128)S(1)}, f32[16,256]{1,0:T(8,128)S(1)}, u32[]{:S(2)}, u32[]{:S(2)}) %collective-permute-start.34) | collective-permute-done | bytes 16416 | tf_op jit(solution)/shard_map/ppermute | solution.py:260
  104.8 6.0 %all-gather.3.cloned.1.call-done = bf16[49408,128]{1,0:T(8,128)(2,1)} async-done(((bf16[3088,128]{1,0:T(8,128)(2,1)}), bf16[49408,128]{1,0:T(8,128)(2,1)}) %all-gather.3.cloned.1.call-update) | async-done | bytes 12648464 | tf_op jit(solution)/shard_map/all_gather | solution.py:304
  110.9 23.8 %tile.19 = (f32[512,1024]{1,0:T(8,128)S(1)}, bf16[512,1024]{1,0:T(8,128)(2,1)S(1)}) custom-call(s32[4]{0:T(128)S(1)} %pad_add_fusion.refs_0_.place_ref, bf16[16,3088,128]{2,1,0:T(8,128)(2,1)} %bitcast.17), custom_call_target="tpu_custom_call" | custom-call | flops 12884901888 | bytes 16842752 | tf_op jit(solution)/shard_map/tile/pallas_call | solution.py:364
  134.9 2.6 %collective-permute-done.36 = bf16[512,1024]{1,0:T(8,128)(2,1)S(1)} collective-permute-done((bf16[512,1024]{1,0:T(8,128)(2,1)S(1)}, bf16[512,1024]{1,0:T(8,128)(2,1)S(1)}, u32[]{:S(2)}, u32[]{:S(2)}) %collective-permute-start.36) | collective-permute-done | bytes 1048608 | tf_op jit(solution)/shard_map/ppermute | solution.py:365
  144.0 2.5 %collective-permute-start.40 = (f32[16,256]{1,0:T(8,128)S(1)}, f32[16,256]{1,0:T(8,128)S(1)}, u32[]{:S(2)}, u32[]{:S(2)}) collective-permute-start(f32[16,256]{1,0:T(8,128)S(1)} %add.208), channel_id=1, source_target_pairs={{0,64},{16,208},{32,96},{48,240},{64,0},{80,144},{96,32},{112,176}... | collective-permute-start | bytes 49160 | tf_op jit(solution)/shard_map/ppermute | solution.py:258
  146.8 1.9 %collective-permute-done.40 = f32[16,256]{1,0:T(8,128)S(1)} collective-permute-done((f32[16,256]{1,0:T(8,128)S(1)}, f32[16,256]{1,0:T(8,128)S(1)}, u32[]{:S(2)}, u32[]{:S(2)}) %collective-permute-start.40) | collective-permute-done | bytes 16416 | tf_op jit(solution)/shard_map/ppermute | solution.py:258
  148.7 3.4 %collective-permute-done.41 = f32[16,256]{1,0:T(8,128)S(1)} collective-permute-done((f32[16,256]{1,0:T(8,128)S(1)}, f32[16,256]{1,0:T(8,128)S(1)}, u32[]{:S(2)}, u32[]{:S(2)}) %collective-permute-start.41) | collective-permute-done | bytes 16416 | tf_op jit(solution)/shard_map/ppermute | solution.py:258
  152.8 2.3 %collective-permute-start.43 = (f32[16,256]{1,0:T(8,128)S(1)}, f32[16,256]{1,0:T(8,128)S(1)}, u32[]{:S(2)}, u32[]{:S(2)}) collective-permute-start(f32[16,256]{1,0:T(8,128)S(1)} %add_add_fusion.2), channel_id=1, source_target_pairs={{0,8},{4,12},{8,0},{12,4},{1,9},{5,13},{9,1},{13,5},{2,10},{6,14},... | collective-permute-start | bytes 49160 | tf_op jit(solution)/shard_map/ppermute | solution.py:260
  155.9 2.1 %collective-permute-done.43 = f32[16,256]{1,0:T(8,128)S(1)} collective-permute-done((f32[16,256]{1,0:T(8,128)S(1)}, f32[16,256]{1,0:T(8,128)S(1)}, u32[]{:S(2)}, u32[]{:S(2)}) %collective-permute-start.43) | collective-permute-done | bytes 16416 | tf_op jit(solution)/shard_map/ppermute | solution.py:260
  159.5 2.7 %collective-permute-start.46 = (f32[16,256]{1,0:T(8,128)S(1)}, f32[16,256]{1,0:T(8,128)S(1)}, u32[]{:S(2)}, u32[]{:S(2)}) collective-permute-start(f32[16,256]{1,0:T(8,128)S(1)} %add_add_fusion.1), channel_id=1, source_target_pairs={{0,2},{1,3},{2,0},{3,1},{4,6},{5,7},{6,4},{7,5},{8,10},{9,11},{10,... | collective-permute-start | bytes 49160 | tf_op jit(solution)/shard_map/ppermute | solution.py:260
  164.8 2.4 %collective-permute-done.47 = f32[16,256]{1,0:T(8,128)S(1)} collective-permute-done((f32[16,256]{1,0:T(8,128)S(1)}, f32[16,256]{1,0:T(8,128)S(1)}, u32[]{:S(2)}, u32[]{:S(2)}) %collective-permute-start.47) | collective-permute-done | bytes 16416 | tf_op jit(solution)/shard_map/ppermute | solution.py:260
  168.8 1.9 %answer.1 = (f32[1,64]{1,0:T(1,128)}, f32[1,64]{1,0:T(1,128)}) custom-call(s32[4]{0:T(128)S(1)} %pad_add_fusion.refs_0_.place_ref, f32[16,256]{1,0:T(8,128)S(1)} %add.180.refs_5_.rhs_ref, f32[16,256]{1,0:T(8,128)S(1)} %add.192.refs_6_.s1_ref, f32[16,256]{1,0:T(8,128)S(1)} %add.203.refs_7_.s2_ref, f32[16,256]{1,0:T(8,128)S(1)} %add.218.s3_ref), custom_call_target="tpu_custom_call" | custom-call | tf_op jit(solution)/shard_map/answer/pallas_call | solution.py:374
  170.7 7.1 %reduce-scatter.2.cloned.1.call-done = bf16[64,1024]{1,0:T(8,128)(2,1)} async-done(((bf16[512,1024]{1,0:T(8,128)(2,1)}), bf16[64,1024]{1,0:T(8,128)(2,1)}) %reduce-scatter.2.cloned.1.call-update) | async-done | bytes 131088 | tf_op jit(solution)/shard_map/reduce_scatter | solution.py:367
  (125 shorter events, 59.6 us)
Async XLA Ops:
  7.2 103.6 %all-gather.3.cloned.1.call-start = ((), (), s32[]{:S(2)}) async-start(), calls=%async_computation.2 | async-start | bytes 13438976 | tf_op jit(solution)/shard_map/all_gather | solution.py:304
  9.7 168.2 %reduce-scatter.2.cloned.1.call-start = ((), (), s32[]{:S(2)}) async-start(), calls=%async_computation.1 | async-start | bytes 1179648 | tf_op jit(solution)/shard_map/reduce_scatter | solution.py:367
  11.8 5.9 %collective-permute-start.1 = (f32[16,256]{1,0:T(8,128)S(1)}, f32[16,256]{1,0:T(8,128)S(1)}, u32[]{:S(2)}, u32[]{:S(2)}) collective-permute-start(f32[16,256]{1,0:T(8,128)S(1)} %add.170), channel_id=1, source_target_pairs={{0,0},{16,144},{32,32},{48,176},{64,64},{80,208},{96,96},{112,240}... | collective-permute-start | bytes 49160 | tf_op jit(solution)/shard_map/ppermute | solution.py:258
  12.4 5.3 %collective-permute-start.2 = (f32[16,256]{1,0:T(8,128)S(1)}, f32[16,256]{1,0:T(8,128)S(1)}, u32[]{:S(2)}, u32[]{:S(2)}) collective-permute-start(f32[16,256]{1,0:T(8,128)S(1)} %add.170), channel_id=1, source_target_pairs={{0,32},{16,176},{32,0},{48,144},{64,96},{80,240},{96,64},{112,208}... | collective-permute-start | bytes 49160 | tf_op jit(solution)/shard_map/ppermute | solution.py:258
  14.4 5.0 %collective-permute-start.3 = (f32[16,256]{1,0:T(8,128)S(1)}, f32[16,256]{1,0:T(8,128)S(1)}, u32[]{:S(2)}, u32[]{:S(2)}) collective-permute-start(f32[16,256]{1,0:T(8,128)S(1)} %add.170), channel_id=1, source_target_pairs={{0,64},{16,208},{32,96},{48,240},{64,0},{80,144},{96,32},{112,176}... | collective-permute-start | bytes 49160 | tf_op jit(solution)/shard_map/ppermute | solution.py:258
  17.7 5.5 %collective-permute-start.4 = (f32[16,256]{1,0:T(8,128)S(1)}, f32[16,256]{1,0:T(8,128)S(1)}, u32[]{:S(2)}, u32[]{:S(2)}) collective-permute-start(f32[16,256]{1,0:T(8,128)S(1)} %add.170), channel_id=1, source_target_pairs={{0,96},{16,240},{32,64},{48,208},{64,32},{80,176},{96,0},{112,144}... | collective-permute-start | bytes 49160 | tf_op jit(solution)/shard_map/ppermute | solution.py:258
  23.9 5.2 %collective-permute-start.6 = (f32[16,256]{1,0:T(8,128)S(1)}, f32[16,256]{1,0:T(8,128)S(1)}, u32[]{:S(2)}, u32[]{:S(2)}) collective-permute-start(f32[16,256]{1,0:T(8,128)S(1)} %add_add_fusion.11), channel_id=1, source_target_pairs={{0,8},{4,12},{8,0},{12,4},{1,9},{5,13},{9,1},{13,5},{2,10},{6,14},... | collective-permute-start | bytes 49160 | tf_op jit(solution)/shard_map/ppermute | solution.py:260
  30.0 5.3 %collective-permute-start.10 = (f32[16,256]{1,0:T(8,128)S(1)}, f32[16,256]{1,0:T(8,128)S(1)}, u32[]{:S(2)}, u32[]{:S(2)}) collective-permute-start(f32[16,256]{1,0:T(8,128)S(1)} %add_add_fusion.10), channel_id=1, source_target_pairs={{0,3},{1,2},{2,1},{3,0},{4,7},{5,6},{6,5},{7,4},{8,11},{9,10},{10,... | collective-permute-start | bytes 49160 | tf_op jit(solution)/shard_map/ppermute | solution.py:260
  33.3 5.4 %collective-permute-start.9 = (f32[16,256]{1,0:T(8,128)S(1)}, f32[16,256]{1,0:T(8,128)S(1)}, u32[]{:S(2)}, u32[]{:S(2)}) collective-permute-start(f32[16,256]{1,0:T(8,128)S(1)} %add_add_fusion.10), channel_id=1, source_target_pairs={{0,2},{1,3},{2,0},{3,1},{4,6},{5,7},{6,4},{7,5},{8,10},{9,11},{10,... | collective-permute-start | bytes 49160 | tf_op jit(solution)/shard_map/ppermute | solution.py:260
  45.4 5.6 %collective-permute-start.13 = (f32[16,256]{1,0:T(8,128)S(1)}, f32[16,256]{1,0:T(8,128)S(1)}, u32[]{:S(2)}, u32[]{:S(2)}) collective-permute-start(f32[16,256]{1,0:T(8,128)S(1)} %add.182), channel_id=1, source_target_pairs={{0,0},{16,144},{32,32},{48,176},{64,64},{80,208},{96,96},{112,240}... | collective-permute-start | bytes 49160 | tf_op jit(solution)/shard_map/ppermute | solution.py:258
  46.1 4.9 %collective-permute-start.14 = (f32[16,256]{1,0:T(8,128)S(1)}, f32[16,256]{1,0:T(8,128)S(1)}, u32[]{:S(2)}, u32[]{:S(2)}) collective-permute-start(f32[16,256]{1,0:T(8,128)S(1)} %add.182), channel_id=1, source_target_pairs={{0,32},{16,176},{32,0},{48,144},{64,96},{80,240},{96,64},{112,208}... | collective-permute-start | bytes 49160 | tf_op jit(solution)/shard_map/ppermute | solution.py:258
  49.1 5.5 %collective-permute-start.16 = (f32[16,256]{1,0:T(8,128)S(1)}, f32[16,256]{1,0:T(8,128)S(1)}, u32[]{:S(2)}, u32[]{:S(2)}) collective-permute-start(f32[16,256]{1,0:T(8,128)S(1)} %add.182), channel_id=1, source_target_pairs={{0,96},{16,240},{32,64},{48,208},{64,32},{80,176},{96,0},{112,144}... | collective-permute-start | bytes 49160 | tf_op jit(solution)/shard_map/ppermute | solution.py:258
  54.7 4.9 %collective-permute-start.17 = (f32[16,256]{1,0:T(8,128)S(1)}, f32[16,256]{1,0:T(8,128)S(1)}, u32[]{:S(2)}, u32[]{:S(2)}) collective-permute-start(f32[16,256]{1,0:T(8,128)S(1)} %add_add_fusion.8), channel_id=1, source_target_pairs={{0,4},{4,0},{8,12},{12,8},{1,5},{5,1},{9,13},{13,9},{2,6},{6,2},{1... | collective-permute-start | bytes 49160 | tf_op jit(solution)/shard_map/ppermute | solution.py:260
  57.5 5.6 %collective-permute-start.18 = (f32[16,256]{1,0:T(8,128)S(1)}, f32[16,256]{1,0:T(8,128)S(1)}, u32[]{:S(2)}, u32[]{:S(2)}) collective-permute-start(f32[16,256]{1,0:T(8,128)S(1)} %add_add_fusion.8), channel_id=1, source_target_pairs={{0,8},{4,12},{8,0},{12,4},{1,9},{5,13},{9,1},{13,5},{2,10},{6,14},... | collective-permute-start | bytes 49160 | tf_op jit(solution)/shard_map/ppermute | solution.py:260
  57.5 5.6 %collective-permute-start.19 = (f32[16,256]{1,0:T(8,128)S(1)}, f32[16,256]{1,0:T(8,128)S(1)}, u32[]{:S(2)}, u32[]{:S(2)}) collective-permute-start(f32[16,256]{1,0:T(8,128)S(1)} %add_add_fusion.8), channel_id=1, source_target_pairs={{0,12},{4,8},{8,4},{12,0},{1,13},{5,9},{9,5},{13,1},{2,14},{6,10},... | collective-permute-start | bytes 49160 | tf_op jit(solution)/shard_map/ppermute | solution.py:260
  63.1 5.0 %collective-permute-start.20 = (f32[16,256]{1,0:T(8,128)S(1)}, f32[16,256]{1,0:T(8,128)S(1)}, u32[]{:S(2)}, u32[]{:S(2)}) collective-permute-start(f32[16,256]{1,0:T(8,128)S(1)} %add_add_fusion.7), channel_id=1, source_target_pairs={{0,1},{1,0},{2,3},{3,2},{4,5},{5,4},{6,7},{7,6},{8,9},{9,8},{10,11... | collective-permute-start | bytes 49160 | tf_op jit(solution)/shard_map/ppermute | solution.py:260
  65.1 5.6 %collective-permute-start.21 = (f32[16,256]{1,0:T(8,128)S(1)}, f32[16,256]{1,0:T(8,128)S(1)}, u32[]{:S(2)}, u32[]{:S(2)}) collective-permute-start(f32[16,256]{1,0:T(8,128)S(1)} %add_add_fusion.7), channel_id=1, source_target_pairs={{0,2},{1,3},{2,0},{3,1},{4,6},{5,7},{6,4},{7,5},{8,10},{9,11},{10,... | collective-permute-start | bytes 49160 | tf_op jit(solution)/shard_map/ppermute | solution.py:260
  66.3 5.3 %collective-permute-start.22 = (f32[16,256]{1,0:T(8,128)S(1)}, f32[16,256]{1,0:T(8,128)S(1)}, u32[]{:S(2)}, u32[]{:S(2)}) collective-permute-start(f32[16,256]{1,0:T(8,128)S(1)} %add_add_fusion.7), channel_id=1, source_target_pairs={{0,3},{1,2},{2,1},{3,0},{4,7},{5,6},{6,5},{7,4},{8,11},{9,10},{10,... | collective-permute-start | bytes 49160 | tf_op jit(solution)/shard_map/ppermute | solution.py:260
  76.6 5.5 %collective-permute-start.25 = (f32[16,256]{1,0:T(8,128)S(1)}, f32[16,256]{1,0:T(8,128)S(1)}, u32[]{:S(2)}, u32[]{:S(2)}) collective-permute-start(f32[16,256]{1,0:T(8,128)S(1)} %add.193), channel_id=1, source_target_pairs={{0,0},{16,144},{32,32},{48,176},{64,64},{80,208},{96,96},{112,240}... | collective-permute-start | bytes 49160 | tf_op jit(solution)/shard_map/ppermute | solution.py:258
  77.3 4.9 %collective-permute-start.26 = (f32[16,256]{1,0:T(8,128)S(1)}, f32[16,256]{1,0:T(8,128)S(1)}, u32[]{:S(2)}, u32[]{:S(2)}) collective-permute-start(f32[16,256]{1,0:T(8,128)S(1)} %add.193), channel_id=1, source_target_pairs={{0,32},{16,176},{32,0},{48,144},{64,96},{80,240},{96,64},{112,208}... | collective-permute-start | bytes 49160 | tf_op jit(solution)/shard_map/ppermute | solution.py:258
  80.5 5.5 %collective-permute-start.28 = (f32[16,256]{1,0:T(8,128)S(1)}, f32[16,256]{1,0:T(8,128)S(1)}, u32[]{:S(2)}, u32[]{:S(2)}) collective-permute-start(f32[16,256]{1,0:T(8,128)S(1)} %add.193), channel_id=1, source_target_pairs={{0,96},{16,240},{32,64},{48,208},{64,32},{80,176},{96,0},{112,144}... | collective-permute-start | bytes 49160 | tf_op jit(solution)/shard_map/ppermute | solution.py:258
  87.5 5.6 %collective-permute-start.30 = (f32[16,256]{1,0:T(8,128)S(1)}, f32[16,256]{1,0:T(8,128)S(1)}, u32[]{:S(2)}, u32[]{:S(2)}) collective-permute-start(f32[16,256]{1,0:T(8,128)S(1)} %add_add_fusion.5), channel_id=1, source_target_pairs={{0,8},{4,12},{8,0},{12,4},{1,9},{5,13},{9,1},{13,5},{2,10},{6,14},... | collective-permute-start | bytes 49160 | tf_op jit(solution)/shard_map/ppermute | solution.py:260
  93.3 4.8 %collective-permute-start.32 = (f32[16,256]{1,0:T(8,128)S(1)}, f32[16,256]{1,0:T(8,128)S(1)}, u32[]{:S(2)}, u32[]{:S(2)}) collective-permute-start(f32[16,256]{1,0:T(8,128)S(1)} %add_add_fusion.4), channel_id=1, source_target_pairs={{0,1},{1,0},{2,3},{3,2},{4,5},{5,4},{6,7},{7,6},{8,9},{9,8},{10,11... | collective-permute-start | bytes 49160 | tf_op jit(solution)/shard_map/ppermute | solution.py:260
  93.4 6.0 %collective-permute-start.33 = (f32[16,256]{1,0:T(8,128)S(1)}, f32[16,256]{1,0:T(8,128)S(1)}, u32[]{:S(2)}, u32[]{:S(2)}) collective-permute-start(f32[16,256]{1,0:T(8,128)S(1)} %add_add_fusion.4), channel_id=1, source_target_pairs={{0,2},{1,3},{2,0},{3,1},{4,6},{5,7},{6,4},{7,5},{8,10},{9,11},{10,... | collective-permute-start | bytes 49160 | tf_op jit(solution)/shard_map/ppermute | solution.py:260
  96.9 5.3 %collective-permute-start.34 = (f32[16,256]{1,0:T(8,128)S(1)}, f32[16,256]{1,0:T(8,128)S(1)}, u32[]{:S(2)}, u32[]{:S(2)}) collective-permute-start(f32[16,256]{1,0:T(8,128)S(1)} %add_add_fusion.4), channel_id=1, source_target_pairs={{0,3},{1,2},{2,1},{3,0},{4,7},{5,6},{6,5},{7,4},{8,11},{9,10},{10,... | collective-permute-start | bytes 49160 | tf_op jit(solution)/shard_map/ppermute | solution.py:260
  141.7 5.1 %collective-permute-start.38 = (f32[16,256]{1,0:T(8,128)S(1)}, f32[16,256]{1,0:T(8,128)S(1)}, u32[]{:S(2)}, u32[]{:S(2)}) collective-permute-start(f32[16,256]{1,0:T(8,128)S(1)} %add.208), channel_id=1, source_target_pairs={{0,0},{16,144},{32,32},{48,176},{64,64},{80,208},{96,96},{112,240}... | collective-permute-start | bytes 49160 | tf_op jit(solution)/shard_map/ppermute | solution.py:258
  144.0 4.7 %collective-permute-start.40 = (f32[16,256]{1,0:T(8,128)S(1)}, f32[16,256]{1,0:T(8,128)S(1)}, u32[]{:S(2)}, u32[]{:S(2)}) collective-permute-start(f32[16,256]{1,0:T(8,128)S(1)} %add.208), channel_id=1, source_target_pairs={{0,64},{16,208},{32,96},{48,240},{64,0},{80,144},{96,32},{112,176}... | collective-permute-start | bytes 49160 | tf_op jit(solution)/shard_map/ppermute | solution.py:258
  146.5 5.5 %collective-permute-start.41 = (f32[16,256]{1,0:T(8,128)S(1)}, f32[16,256]{1,0:T(8,128)S(1)}, u32[]{:S(2)}, u32[]{:S(2)}) collective-permute-start(f32[16,256]{1,0:T(8,128)S(1)} %add.208), channel_id=1, source_target_pairs={{0,96},{16,240},{32,64},{48,208},{64,32},{80,176},{96,0},{112,144}... | collective-permute-start | bytes 49160 | tf_op jit(solution)/shard_map/ppermute | solution.py:258
  152.8 5.2 %collective-permute-start.43 = (f32[16,256]{1,0:T(8,128)S(1)}, f32[16,256]{1,0:T(8,128)S(1)}, u32[]{:S(2)}, u32[]{:S(2)}) collective-permute-start(f32[16,256]{1,0:T(8,128)S(1)} %add_add_fusion.2), channel_id=1, source_target_pairs={{0,8},{4,12},{8,0},{12,4},{1,9},{5,13},{9,1},{13,5},{2,10},{6,14},... | collective-permute-start | bytes 49160 | tf_op jit(solution)/shard_map/ppermute | solution.py:260
  158.9 4.8 %collective-permute-start.45 = (f32[16,256]{1,0:T(8,128)S(1)}, f32[16,256]{1,0:T(8,128)S(1)}, u32[]{:S(2)}, u32[]{:S(2)}) collective-permute-start(f32[16,256]{1,0:T(8,128)S(1)} %add_add_fusion.1), channel_id=1, source_target_pairs={{0,1},{1,0},{2,3},{3,2},{4,5},{5,4},{6,7},{7,6},{8,9},{9,8},{10,11... | collective-permute-start | bytes 49160 | tf_op jit(solution)/shard_map/ppermute | solution.py:260
  159.5 5.2 %collective-permute-start.46 = (f32[16,256]{1,0:T(8,128)S(1)}, f32[16,256]{1,0:T(8,128)S(1)}, u32[]{:S(2)}, u32[]{:S(2)}) collective-permute-start(f32[16,256]{1,0:T(8,128)S(1)} %add_add_fusion.1), channel_id=1, source_target_pairs={{0,2},{1,3},{2,0},{3,1},{4,6},{5,7},{6,4},{7,5},{8,10},{9,11},{10,... | collective-permute-start | bytes 49160 | tf_op jit(solution)/shard_map/ppermute | solution.py:260
  162.3 4.9 %collective-permute-start.47 = (f32[16,256]{1,0:T(8,128)S(1)}, f32[16,256]{1,0:T(8,128)S(1)}, u32[]{:S(2)}, u32[]{:S(2)}) collective-permute-start(f32[16,256]{1,0:T(8,128)S(1)} %add_add_fusion.1), channel_id=1, source_target_pairs={{0,3},{1,2},{2,1},{3,0},{4,7},{5,6},{6,5},{7,4},{8,11},{9,10},{10,... | collective-permute-start | bytes 49160 | tf_op jit(solution)/shard_map/ppermute | solution.py:260
  (25 other events, 101.3 us)
Sparse Core Ops, SparseCore 0:
  10.5 100.2 all-gather.2
  139.1 38.7 reduce-scatter.1

commit v9 on v7

--- a/solution.py
+++ b/solution.py
@@ -81,14 +81,28 @@
     return jnp.transpose(w_ref[at * points : (at + 1) * points, :].astype(jnp.float32))
 
 
-def send_kernel(slots, w_ref, vis_ref, inv_ref, send_ref):
+def send_kernel(slots, w_ref, vis_ref, inv_ref, send_ref, held_ref, made_ref, in_sem, out_sem):
     points = vis_ref.shape[1]
     width = w_ref.shape[1]
-    for at in range(3 * slots):
-        send_ref[at * width : (at + 1) * width, :] = turned_rows(w_ref, at, points).astype(jnp.bfloat16)
+    rows, made = 3 * points, 3 * width
+    arrivals, leaves = [], []
+    for k in range(slots):
+        span = pl.ds(k * rows, rows)
+        arrivals.append(pltpu.make_async_copy(w_ref.at[span, :], held_ref.at[span, :], in_sem.at[k]))
+        arrivals[k].start()
     pad = jnp.zeros((AUX - slots - 6, points), jnp.float32)
     aux = jnp.concatenate([vis_ref[...].astype(jnp.float32), inv_ref[...].astype(jnp.float32), pad], axis=0)
-    send_ref[3 * slots * width :, :] = aux.astype(jnp.bfloat16)
+    made_ref[slots * made :, :] = aux.astype(jnp.bfloat16)
+    for k in range(slots + 1):
+        if k < slots:
+            arrivals[k].wait()
+            for at in range(3 * k, 3 * k + 3):
+                made_ref[at * width : (at + 1) * width, :] = turned_rows(held_ref, at, points).astype(jnp.bfloat16)
+        span = pl.ds(k * made, made if k < slots else AUX)
+        leaves.append(pltpu.make_async_copy(made_ref.at[span, :], send_ref.at[span, :], out_sem.at[k]))
+        leaves[k].start()
+    for leave in leaves:
+        leave.wait()
 
 
 def prepare_kernel(slots, blocks, w_ref, vis_ref, inv_ref, grad_ref, cams_ref, zw_ref, part_ref):
@@ -303,8 +317,14 @@
     send = pl.pallas_call(
         functools.partial(send_kernel, slots),
         out_shape=jax.ShapeDtypeStruct((send_rows, points), jnp.bfloat16),
-        in_specs=[vmem] * 3,
-        out_specs=vmem,
+        in_specs=[pl.BlockSpec(memory_space=pl.ANY), vmem, vmem],
+        out_specs=pl.BlockSpec(memory_space=pl.ANY),
+        scratch_shapes=[
+            pltpu.VMEM((3 * slots * points, width), jnp.bfloat16),
+            pltpu.VMEM((send_rows, points), jnp.bfloat16),
+            pltpu.SemaphoreType.DMA((slots,)),
+            pltpu.SemaphoreType.DMA((slots + 1,)),
+        ],
         name="send",
     )(w_flat, visibility, inverses)
     got = lax.all_gather(send, ("row", "col"), axis=0, tiled=False)

time: 188 us -> 188 us (level)
  transfers between devices with their start and end apart: 51 -> 51, of which waited for: 34 -> 35; matrix products, arithmetic and copies ran while one was open for 0% -> 0% of each run, Pallas kernels for 3% -> 3%
where the time goes in v9:
time: 188 us
  starting transfers between devices  78 us (41%)
  waiting for transfers between devices  60.5 us (32%)
  Pallas kernels  33.1 us (18%)
  between operations  14.3 us (8%)
  other arithmetic  1.97 us (1%)
    ppermute x24, starting transfers between devices, all_sum(): lax.ppermute(value, axis, [(i, i ^ b) for i in range(size)])  33.6 us
    ppermute x24, waiting for transfers between devices, all_sum(): lax.ppermute(value, axis, [(i, i ^ b) for i in range(size)])  25.6 us
    pallas_call x1, Pallas kernels, per_device(): own_half, peer_half = make_halves(place, got, camera_blocks)  23.7 us
    ppermute x8, starting transfers between devices, core_sum(): return value + lax.ppermute(value, 'core', [(0, 1), (1, 0)])  23 us
    ppermute x16, starting transfers between devices, all_sum(): value = tree([lax.ppermute(value, ('z', 'core'), p) for p in pairs])  21 us
    ppermute x16, waiting for transfers between devices, all_sum(): value = tree([lax.ppermute(value, ('z', 'core'), p) for p in pairs])  10.2 us
    reduce_scatter x1, waiting for transfers between devices, per_device(): schur = lax.psum_scatter(tile, 'z', scatter_dimension=0, tiled=True)  8.02 us
    ppermute x8, waiting for transfers between devices, core_sum(): return value + lax.ppermute(value, 'core', [(0, 1), (1, 0)])  7.17 us
  transfers between devices with their start and end apart: 51, of which 35 were waited for; matrix products, arithmetic and copies ran while one was open for 0% of the time, Pallas kernels for 3%

profile of v9, /device:TPU:2, one launch (start us, length us, event | category | flops | bytes accessed | tf_op | source)
XLA Modules:
  0.0 188.0 jit_solution(6626083588958608216)
XLA Ops:
  7.3 3.0 %send.1 = bf16[3088,128]{1,0:T(8,128)(2,1)} custom-call(bf16[1536,256]{1,0:T(8,128)(2,1)} %bitcast.8, s32[4,128]{1,0:T(4,128)} %refs_1_.5, bf16[6,128]{1,0:T(8,128)(2,1)} %inv_ref.3), custom_call_target="tpu_custom_call" | custom-call | tf_op jit(solution)/shard_map/send/pallas_call | solution.py:317
  12.4 4.6 %collective-permute-start.4 = (f32[16,256]{1,0:T(8,128)S(1)}, f32[16,256]{1,0:T(8,128)S(1)}, u32[]{:S(2)}, u32[]{:S(2)}) collective-permute-start(f32[16,256]{1,0:T(8,128)S(1)} %add.150), channel_id=1, source_target_pairs={{0,96},{16,240},{32,64},{48,208},{64,32},{80,176},{96,0},{112,144}... | collective-permute-start | bytes 49160 | tf_op jit(solution)/shard_map/ppermute | solution.py:278
  18.7 2.9 %collective-permute-done.3 = f32[16,256]{1,0:T(8,128)S(1)} collective-permute-done((f32[16,256]{1,0:T(8,128)S(1)}, f32[16,256]{1,0:T(8,128)S(1)}, u32[]{:S(2)}, u32[]{:S(2)}) %collective-permute-start.3) | collective-permute-done | bytes 16416 | tf_op jit(solution)/shard_map/ppermute | solution.py:278
  25.8 2.6 %collective-permute-done.6 = f32[16,256]{1,0:T(8,128)S(1)} collective-permute-done((f32[16,256]{1,0:T(8,128)S(1)}, f32[16,256]{1,0:T(8,128)S(1)}, u32[]{:S(2)}, u32[]{:S(2)}) %collective-permute-start.6) | collective-permute-done | bytes 16416 | tf_op jit(solution)/shard_map/ppermute | solution.py:280
  28.5 3.1 %collective-permute-start.10 = (f32[16,256]{1,0:T(8,128)S(1)}, f32[16,256]{1,0:T(8,128)S(1)}, u32[]{:S(2)}, u32[]{:S(2)}) collective-permute-start(f32[16,256]{1,0:T(8,128)S(1)} %add_add_fusion.10), channel_id=1, source_target_pairs={{0,3},{1,2},{2,1},{3,0},{4,7},{5,6},{6,5},{7,4},{8,11},{9,10},{10,... | collective-permute-start | bytes 49160 | tf_op jit(solution)/shard_map/ppermute | solution.py:280
  33.8 3.3 %collective-permute-done.9 = f32[16,256]{1,0:T(8,128)S(1)} collective-permute-done((f32[16,256]{1,0:T(8,128)S(1)}, f32[16,256]{1,0:T(8,128)S(1)}, u32[]{:S(2)}, u32[]{:S(2)}) %collective-permute-start.9) | collective-permute-done | bytes 16416 | tf_op jit(solution)/shard_map/ppermute | solution.py:280
  37.2 6.6 %collective-permute-start.11 = (f32[16,256]{1,0:T(8,128)S(1)}, f32[16,256]{1,0:T(8,128)S(1)}, u32[]{:S(2)}, u32[]{:S(2)}) collective-permute-start(f32[16,256]{1,0:T(8,128)S(1)} %add_add_fusion.9), channel_id=1, source_target_pairs={{0,16},{16,0},{1,17},{17,1},{2,18},{18,2},{3,19},{19,3},{4,20},{20... | collective-permute-start | bytes 49160 | tf_op jit(solution)/shard_map/ppermute | solution.py:271
  47.0 2.1 %collective-permute-start.16 = (f32[16,256]{1,0:T(8,128)S(1)}, f32[16,256]{1,0:T(8,128)S(1)}, u32[]{:S(2)}, u32[]{:S(2)}) collective-permute-start(f32[16,256]{1,0:T(8,128)S(1)} %add.162), channel_id=1, source_target_pairs={{0,96},{16,240},{32,64},{48,208},{64,32},{80,176},{96,0},{112,144}... | collective-permute-start | bytes 49160 | tf_op jit(solution)/shard_map/ppermute | solution.py:278
  55.8 2.0 %collective-permute-start.18 = (f32[16,256]{1,0:T(8,128)S(1)}, f32[16,256]{1,0:T(8,128)S(1)}, u32[]{:S(2)}, u32[]{:S(2)}) collective-permute-start(f32[16,256]{1,0:T(8,128)S(1)} %add_add_fusion.8), channel_id=1, source_target_pairs={{0,8},{4,12},{8,0},{12,4},{1,9},{5,13},{9,1},{13,5},{2,10},{6,14},... | collective-permute-start | bytes 49160 | tf_op jit(solution)/shard_map/ppermute | solution.py:280
  58.4 2.9 %collective-permute-done.18 = f32[16,256]{1,0:T(8,128)S(1)} collective-permute-done((f32[16,256]{1,0:T(8,128)S(1)}, f32[16,256]{1,0:T(8,128)S(1)}, u32[]{:S(2)}, u32[]{:S(2)}) %collective-permute-start.18) | collective-permute-done | bytes 16416 | tf_op jit(solution)/shard_map/ppermute | solution.py:280
  61.8 1.7 collective-permute-start.22
  64.3 1.8 collective-permute-start.20
  67.4 1.7 collective-permute-done.21
  69.1 4.4 %collective-permute-start.23 = (f32[16,256]{1,0:T(8,128)S(1)}, f32[16,256]{1,0:T(8,128)S(1)}, u32[]{:S(2)}, u32[]{:S(2)}) collective-permute-start(f32[16,256]{1,0:T(8,128)S(1)} %add_add_fusion.6), channel_id=1, source_target_pairs={{0,16},{16,0},{1,17},{17,1},{2,18},{18,2},{3,19},{19,3},{4,20},{20... | collective-permute-start | bytes 49160 | tf_op jit(solution)/shard_map/ppermute | solution.py:271
  76.9 1.9 collective-permute-start.28
  79.1 2.2 %collective-permute-start.26 = (f32[16,256]{1,0:T(8,128)S(1)}, f32[16,256]{1,0:T(8,128)S(1)}, u32[]{:S(2)}, u32[]{:S(2)}) collective-permute-start(f32[16,256]{1,0:T(8,128)S(1)} %add.173), channel_id=1, source_target_pairs={{0,32},{16,176},{32,0},{48,144},{64,96},{80,240},{96,64},{112,208}... | collective-permute-start | bytes 49160 | tf_op jit(solution)/shard_map/ppermute | solution.py:278
  84.4 2.1 %collective-permute-start.30 = (f32[16,256]{1,0:T(8,128)S(1)}, f32[16,256]{1,0:T(8,128)S(1)}, u32[]{:S(2)}, u32[]{:S(2)}) collective-permute-start(f32[16,256]{1,0:T(8,128)S(1)} %add_add_fusion.5), channel_id=1, source_target_pairs={{0,8},{4,12},{8,0},{12,4},{1,9},{5,13},{9,1},{13,5},{2,10},{6,14},... | collective-permute-start | bytes 49160 | tf_op jit(solution)/shard_map/ppermute | solution.py:280
  87.7 2.3 %collective-permute-done.30 = f32[16,256]{1,0:T(8,128)S(1)} collective-permute-done((f32[16,256]{1,0:T(8,128)S(1)}, f32[16,256]{1,0:T(8,128)S(1)}, u32[]{:S(2)}, u32[]{:S(2)}) %collective-permute-start.30) | collective-permute-done | bytes 16416 | tf_op jit(solution)/shard_map/ppermute | solution.py:280
  90.6 1.8 collective-permute-start.34
  96.0 2.0 %collective-permute-done.33 = f32[16,256]{1,0:T(8,128)S(1)} collective-permute-done((f32[16,256]{1,0:T(8,128)S(1)}, f32[16,256]{1,0:T(8,128)S(1)}, u32[]{:S(2)}, u32[]{:S(2)}) %collective-permute-start.33) | collective-permute-done | bytes 16416 | tf_op jit(solution)/shard_map/ppermute | solution.py:280
  98.1 5.1 %collective-permute-start.35 = (f32[16,256]{1,0:T(8,128)S(1)}, f32[16,256]{1,0:T(8,128)S(1)}, u32[]{:S(2)}, u32[]{:S(2)}) collective-permute-start(f32[16,256]{1,0:T(8,128)S(1)} %add_add_fusion.3), channel_id=1, source_target_pairs={{0,16},{16,0},{1,17},{17,1},{2,18},{18,2},{3,19},{19,3},{4,20},{20... | collective-permute-start | bytes 49160 | tf_op jit(solution)/shard_map/ppermute | solution.py:271
  104.0 6.8 %all-gather.3.cloned.1.call-done = bf16[49408,128]{1,0:T(8,128)(2,1)} async-done(((bf16[3088,128]{1,0:T(8,128)(2,1)}), bf16[49408,128]{1,0:T(8,128)(2,1)}) %all-gather.3.cloned.1.call-update) | async-done | bytes 12648464 | tf_op jit(solution)/shard_map/all_gather | solution.py:330
  110.8 23.7 %tile.8 = (f32[512,1024]{1,0:T(8,128)S(1)}, bf16[512,1024]{1,0:T(8,128)(2,1)S(1)}) custom-call(s32[4]{0:T(128)S(1)} %pad_add_fusion.refs_0_.place_ref, bf16[16,3088,128]{2,1,0:T(8,128)(2,1)} %bitcast.13, f32[64,256]{1,0:T(8,128)S(1)} %copy-done.1), custom_call_target="tpu_custom_call" | custom-call | flops 12884901888 | bytes 16842752 | tf_op jit(solution)/shard_map/tile/pallas_call | solution.py:391
  134.9 2.6 %collective-permute-done.36 = bf16[512,1024]{1,0:T(8,128)(2,1)S(1)} collective-permute-done((bf16[512,1024]{1,0:T(8,128)(2,1)S(1)}, bf16[512,1024]{1,0:T(8,128)(2,1)S(1)}, u32[]{:S(2)}, u32[]{:S(2)}) %collective-permute-start.36) | collective-permute-done | bytes 1048608 | tf_op jit(solution)/shard_map/ppermute | solution.py:392
  142.0 3.5 %collective-permute-start.41 = (f32[16,256]{1,0:T(8,128)S(1)}, f32[16,256]{1,0:T(8,128)S(1)}, u32[]{:S(2)}, u32[]{:S(2)}) collective-permute-start(f32[16,256]{1,0:T(8,128)S(1)} %add.185), channel_id=1, source_target_pairs={{0,96},{16,240},{32,64},{48,208},{64,32},{80,176},{96,0},{112,144}... | collective-permute-start | bytes 49160 | tf_op jit(solution)/shard_map/ppermute | solution.py:278
  147.5 2.6 %collective-permute-done.40 = f32[16,256]{1,0:T(8,128)S(1)} collective-permute-done((f32[16,256]{1,0:T(8,128)S(1)}, f32[16,256]{1,0:T(8,128)S(1)}, u32[]{:S(2)}, u32[]{:S(2)}) %collective-permute-start.40) | collective-permute-done | bytes 16416 | tf_op jit(solution)/shard_map/ppermute | solution.py:278
  154.3 2.6 %collective-permute-done.43 = f32[16,256]{1,0:T(8,128)S(1)} collective-permute-done((f32[16,256]{1,0:T(8,128)S(1)}, f32[16,256]{1,0:T(8,128)S(1)}, u32[]{:S(2)}, u32[]{:S(2)}) %collective-permute-start.43) | collective-permute-done | bytes 16416 | tf_op jit(solution)/shard_map/ppermute | solution.py:280
  157.0 2.3 %collective-permute-start.47 = (f32[16,256]{1,0:T(8,128)S(1)}, f32[16,256]{1,0:T(8,128)S(1)}, u32[]{:S(2)}, u32[]{:S(2)}) collective-permute-start(f32[16,256]{1,0:T(8,128)S(1)} %add_add_fusion.1), channel_id=1, source_target_pairs={{0,3},{1,2},{2,1},{3,0},{4,7},{5,6},{6,5},{7,4},{8,11},{9,10},{10,... | collective-permute-start | bytes 49160 | tf_op jit(solution)/shard_map/ppermute | solution.py:280
  162.0 2.5 %collective-permute-done.46 = f32[16,256]{1,0:T(8,128)S(1)} collective-permute-done((f32[16,256]{1,0:T(8,128)S(1)}, f32[16,256]{1,0:T(8,128)S(1)}, u32[]{:S(2)}, u32[]{:S(2)}) %collective-permute-start.46) | collective-permute-done | bytes 16416 | tf_op jit(solution)/shard_map/ppermute | solution.py:280
  164.5 5.9 %collective-permute-start.48 = (f32[16,256]{1,0:T(8,128)S(1)}, f32[16,256]{1,0:T(8,128)S(1)}, u32[]{:S(2)}, u32[]{:S(2)}) collective-permute-start(f32[16,256]{1,0:T(8,128)S(1)} %add_add_fusion), channel_id=1, source_target_pairs={{0,16},{16,0},{1,17},{17,1},{2,18},{18,2},{3,19},{19,3},{4,20},{20... | collective-permute-start | bytes 49160 | tf_op jit(solution)/shard_map/ppermute | solution.py:271
  171.3 1.9 answer.1
  173.1 8.0 %reduce-scatter.2.cloned.1.call-done = f32[64,1024]{1,0:T(8,128)} async-done(((f32[512,1024]{1,0:T(8,128)}), f32[64,1024]{1,0:T(8,128)}) %reduce-scatter.2.cloned.1.call-update) | async-done | bytes 262160 | tf_op jit(solution)/shard_map/reduce_scatter | solution.py:394
  (121 shorter events, 50.9 us)
Async XLA Ops:
  7.2 103.6 %all-gather.3.cloned.1.call-start = ((), (), s32[]{:S(2)}) async-start(), calls=%async_computation.2 | async-start | bytes 13438976 | tf_op jit(solution)/shard_map/all_gather | solution.py:330
  10.3 170.8 %reduce-scatter.2.cloned.1.call-start = ((), (), s32[]{:S(2)}) async-start(), calls=%async_computation.1 | async-start | bytes 2359296 | tf_op jit(solution)/shard_map/reduce_scatter | solution.py:394
  12.4 6.3 %collective-permute-start.4 = (f32[16,256]{1,0:T(8,128)S(1)}, f32[16,256]{1,0:T(8,128)S(1)}, u32[]{:S(2)}, u32[]{:S(2)}) collective-permute-start(f32[16,256]{1,0:T(8,128)S(1)} %add.150), channel_id=1, source_target_pairs={{0,96},{16,240},{32,64},{48,208},{64,32},{80,176},{96,0},{112,144}... | collective-permute-start | bytes 49160 | tf_op jit(solution)/shard_map/ppermute | solution.py:278
  17.0 4.6 %collective-permute-start.3 = (f32[16,256]{1,0:T(8,128)S(1)}, f32[16,256]{1,0:T(8,128)S(1)}, u32[]{:S(2)}, u32[]{:S(2)}) collective-permute-start(f32[16,256]{1,0:T(8,128)S(1)} %add.150), channel_id=1, source_target_pairs={{0,64},{16,208},{32,96},{48,240},{64,0},{80,144},{96,32},{112,176}... | collective-permute-start | bytes 49160 | tf_op jit(solution)/shard_map/ppermute | solution.py:278
  17.0 4.6 %collective-permute-start.2 = (f32[16,256]{1,0:T(8,128)S(1)}, f32[16,256]{1,0:T(8,128)S(1)}, u32[]{:S(2)}, u32[]{:S(2)}) collective-permute-start(f32[16,256]{1,0:T(8,128)S(1)} %add.150), channel_id=1, source_target_pairs={{0,32},{16,176},{32,0},{48,144},{64,96},{80,240},{96,64},{112,208}... | collective-permute-start | bytes 49160 | tf_op jit(solution)/shard_map/ppermute | solution.py:278
  23.2 5.2 %collective-permute-start.6 = (f32[16,256]{1,0:T(8,128)S(1)}, f32[16,256]{1,0:T(8,128)S(1)}, u32[]{:S(2)}, u32[]{:S(2)}) collective-permute-start(f32[16,256]{1,0:T(8,128)S(1)} %add_add_fusion.11), channel_id=1, source_target_pairs={{0,8},{4,12},{8,0},{12,4},{1,9},{5,13},{9,1},{13,5},{2,10},{6,14},... | collective-permute-start | bytes 49160 | tf_op jit(solution)/shard_map/ppermute | solution.py:280
  28.5 5.4 %collective-permute-start.10 = (f32[16,256]{1,0:T(8,128)S(1)}, f32[16,256]{1,0:T(8,128)S(1)}, u32[]{:S(2)}, u32[]{:S(2)}) collective-permute-start(f32[16,256]{1,0:T(8,128)S(1)} %add_add_fusion.10), channel_id=1, source_target_pairs={{0,3},{1,2},{2,1},{3,0},{4,7},{5,6},{6,5},{7,4},{8,11},{9,10},{10,... | collective-permute-start | bytes 49160 | tf_op jit(solution)/shard_map/ppermute | solution.py:280
  31.6 5.6 %collective-permute-start.9 = (f32[16,256]{1,0:T(8,128)S(1)}, f32[16,256]{1,0:T(8,128)S(1)}, u32[]{:S(2)}, u32[]{:S(2)}) collective-permute-start(f32[16,256]{1,0:T(8,128)S(1)} %add_add_fusion.10), channel_id=1, source_target_pairs={{0,2},{1,3},{2,0},{3,1},{4,6},{5,7},{6,4},{7,5},{8,10},{9,11},{10,... | collective-permute-start | bytes 49160 | tf_op jit(solution)/shard_map/ppermute | solution.py:280
  32.2 4.9 %collective-permute-start.8 = (f32[16,256]{1,0:T(8,128)S(1)}, f32[16,256]{1,0:T(8,128)S(1)}, u32[]{:S(2)}, u32[]{:S(2)}) collective-permute-start(f32[16,256]{1,0:T(8,128)S(1)} %add_add_fusion.10), channel_id=1, source_target_pairs={{0,1},{1,0},{2,3},{3,2},{4,5},{5,4},{6,7},{7,6},{8,9},{9,8},{10,11... | collective-permute-start | bytes 49160 | tf_op jit(solution)/shard_map/ppermute | solution.py:280
  37.2 7.4 %collective-permute-start.11 = (f32[16,256]{1,0:T(8,128)S(1)}, f32[16,256]{1,0:T(8,128)S(1)}, u32[]{:S(2)}, u32[]{:S(2)}) collective-permute-start(f32[16,256]{1,0:T(8,128)S(1)} %add_add_fusion.9), channel_id=1, source_target_pairs={{0,16},{16,0},{1,17},{17,1},{2,18},{18,2},{3,19},{19,3},{4,20},{20... | collective-permute-start | bytes 49160 | tf_op jit(solution)/shard_map/ppermute | solution.py:271
  47.0 5.6 %collective-permute-start.16 = (f32[16,256]{1,0:T(8,128)S(1)}, f32[16,256]{1,0:T(8,128)S(1)}, u32[]{:S(2)}, u32[]{:S(2)}) collective-permute-start(f32[16,256]{1,0:T(8,128)S(1)} %add.162), channel_id=1, source_target_pairs={{0,96},{16,240},{32,64},{48,208},{64,32},{80,176},{96,0},{112,144}... | collective-permute-start | bytes 49160 | tf_op jit(solution)/shard_map/ppermute | solution.py:278
  49.1 4.6 %collective-permute-start.15 = (f32[16,256]{1,0:T(8,128)S(1)}, f32[16,256]{1,0:T(8,128)S(1)}, u32[]{:S(2)}, u32[]{:S(2)}) collective-permute-start(f32[16,256]{1,0:T(8,128)S(1)} %add.162), channel_id=1, source_target_pairs={{0,64},{16,208},{32,96},{48,240},{64,0},{80,144},{96,32},{112,176}... | collective-permute-start | bytes 49160 | tf_op jit(solution)/shard_map/ppermute | solution.py:278
  55.8 5.6 %collective-permute-start.18 = (f32[16,256]{1,0:T(8,128)S(1)}, f32[16,256]{1,0:T(8,128)S(1)}, u32[]{:S(2)}, u32[]{:S(2)}) collective-permute-start(f32[16,256]{1,0:T(8,128)S(1)} %add_add_fusion.8), channel_id=1, source_target_pairs={{0,8},{4,12},{8,0},{12,4},{1,9},{5,13},{9,1},{13,5},{2,10},{6,14},... | collective-permute-start | bytes 49160 | tf_op jit(solution)/shard_map/ppermute | solution.py:280
  61.8 5.5 %collective-permute-start.22 = (f32[16,256]{1,0:T(8,128)S(1)}, f32[16,256]{1,0:T(8,128)S(1)}, u32[]{:S(2)}, u32[]{:S(2)}) collective-permute-start(f32[16,256]{1,0:T(8,128)S(1)} %add_add_fusion.7), channel_id=1, source_target_pairs={{0,3},{1,2},{2,1},{3,0},{4,7},{5,6},{6,5},{7,4},{8,11},{9,10},{10,... | collective-permute-start | bytes 49160 | tf_op jit(solution)/shard_map/ppermute | solution.py:280
  63.5 5.6 %collective-permute-start.21 = (f32[16,256]{1,0:T(8,128)S(1)}, f32[16,256]{1,0:T(8,128)S(1)}, u32[]{:S(2)}, u32[]{:S(2)}) collective-permute-start(f32[16,256]{1,0:T(8,128)S(1)} %add_add_fusion.7), channel_id=1, source_target_pairs={{0,2},{1,3},{2,0},{3,1},{4,6},{5,7},{6,4},{7,5},{8,10},{9,11},{10,... | collective-permute-start | bytes 49160 | tf_op jit(solution)/shard_map/ppermute | solution.py:280
  64.3 4.7 %collective-permute-start.20 = (f32[16,256]{1,0:T(8,128)S(1)}, f32[16,256]{1,0:T(8,128)S(1)}, u32[]{:S(2)}, u32[]{:S(2)}) collective-permute-start(f32[16,256]{1,0:T(8,128)S(1)} %add_add_fusion.7), channel_id=1, source_target_pairs={{0,1},{1,0},{2,3},{3,2},{4,5},{5,4},{6,7},{7,6},{8,9},{9,8},{10,11... | collective-permute-start | bytes 49160 | tf_op jit(solution)/shard_map/ppermute | solution.py:280
  69.1 5.3 %collective-permute-start.23 = (f32[16,256]{1,0:T(8,128)S(1)}, f32[16,256]{1,0:T(8,128)S(1)}, u32[]{:S(2)}, u32[]{:S(2)}) collective-permute-start(f32[16,256]{1,0:T(8,128)S(1)} %add_add_fusion.6), channel_id=1, source_target_pairs={{0,16},{16,0},{1,17},{17,1},{2,18},{18,2},{3,19},{19,3},{4,20},{20... | collective-permute-start | bytes 49160 | tf_op jit(solution)/shard_map/ppermute | solution.py:271
  76.9 5.5 %collective-permute-start.28 = (f32[16,256]{1,0:T(8,128)S(1)}, f32[16,256]{1,0:T(8,128)S(1)}, u32[]{:S(2)}, u32[]{:S(2)}) collective-permute-start(f32[16,256]{1,0:T(8,128)S(1)} %add.173), channel_id=1, source_target_pairs={{0,96},{16,240},{32,64},{48,208},{64,32},{80,176},{96,0},{112,144}... | collective-permute-start | bytes 49160 | tf_op jit(solution)/shard_map/ppermute | solution.py:278
  78.7 4.7 %collective-permute-start.27 = (f32[16,256]{1,0:T(8,128)S(1)}, f32[16,256]{1,0:T(8,128)S(1)}, u32[]{:S(2)}, u32[]{:S(2)}) collective-permute-start(f32[16,256]{1,0:T(8,128)S(1)} %add.173), channel_id=1, source_target_pairs={{0,64},{16,208},{32,96},{48,240},{64,0},{80,144},{96,32},{112,176}... | collective-permute-start | bytes 49160 | tf_op jit(solution)/shard_map/ppermute | solution.py:278
  79.1 4.4 %collective-permute-start.26 = (f32[16,256]{1,0:T(8,128)S(1)}, f32[16,256]{1,0:T(8,128)S(1)}, u32[]{:S(2)}, u32[]{:S(2)}) collective-permute-start(f32[16,256]{1,0:T(8,128)S(1)} %add.173), channel_id=1, source_target_pairs={{0,32},{16,176},{32,0},{48,144},{64,96},{80,240},{96,64},{112,208}... | collective-permute-start | bytes 49160 | tf_op jit(solution)/shard_map/ppermute | solution.py:278
  84.4 5.6 %collective-permute-start.30 = (f32[16,256]{1,0:T(8,128)S(1)}, f32[16,256]{1,0:T(8,128)S(1)}, u32[]{:S(2)}, u32[]{:S(2)}) collective-permute-start(f32[16,256]{1,0:T(8,128)S(1)} %add_add_fusion.5), channel_id=1, source_target_pairs={{0,8},{4,12},{8,0},{12,4},{1,9},{5,13},{9,1},{13,5},{2,10},{6,14},... | collective-permute-start | bytes 49160 | tf_op jit(solution)/shard_map/ppermute | solution.py:280
  90.6 5.4 %collective-permute-start.34 = (f32[16,256]{1,0:T(8,128)S(1)}, f32[16,256]{1,0:T(8,128)S(1)}, u32[]{:S(2)}, u32[]{:S(2)}) collective-permute-start(f32[16,256]{1,0:T(8,128)S(1)} %add_add_fusion.4), channel_id=1, source_target_pairs={{0,3},{1,2},{2,1},{3,0},{4,7},{5,6},{6,5},{7,4},{8,11},{9,10},{10,... | collective-permute-start | bytes 49160 | tf_op jit(solution)/shard_map/ppermute | solution.py:280
  92.4 5.6 %collective-permute-start.33 = (f32[16,256]{1,0:T(8,128)S(1)}, f32[16,256]{1,0:T(8,128)S(1)}, u32[]{:S(2)}, u32[]{:S(2)}) collective-permute-start(f32[16,256]{1,0:T(8,128)S(1)} %add_add_fusion.4), channel_id=1, source_target_pairs={{0,2},{1,3},{2,0},{3,1},{4,6},{5,7},{6,4},{7,5},{8,10},{9,11},{10,... | collective-permute-start | bytes 49160 | tf_op jit(solution)/shard_map/ppermute | solution.py:280
  98.1 5.9 %collective-permute-start.35 = (f32[16,256]{1,0:T(8,128)S(1)}, f32[16,256]{1,0:T(8,128)S(1)}, u32[]{:S(2)}, u32[]{:S(2)}) collective-permute-start(f32[16,256]{1,0:T(8,128)S(1)} %add_add_fusion.3), channel_id=1, source_target_pairs={{0,16},{16,0},{1,17},{17,1},{2,18},{18,2},{3,19},{19,3},{4,20},{20... | collective-permute-start | bytes 49160 | tf_op jit(solution)/shard_map/ppermute | solution.py:271
  142.0 5.5 %collective-permute-start.41 = (f32[16,256]{1,0:T(8,128)S(1)}, f32[16,256]{1,0:T(8,128)S(1)}, u32[]{:S(2)}, u32[]{:S(2)}) collective-permute-start(f32[16,256]{1,0:T(8,128)S(1)} %add.185), channel_id=1, source_target_pairs={{0,96},{16,240},{32,64},{48,208},{64,32},{80,176},{96,0},{112,144}... | collective-permute-start | bytes 49160 | tf_op jit(solution)/shard_map/ppermute | solution.py:278
  145.5 4.6 %collective-permute-start.40 = (f32[16,256]{1,0:T(8,128)S(1)}, f32[16,256]{1,0:T(8,128)S(1)}, u32[]{:S(2)}, u32[]{:S(2)}) collective-permute-start(f32[16,256]{1,0:T(8,128)S(1)} %add.185), channel_id=1, source_target_pairs={{0,64},{16,208},{32,96},{48,240},{64,0},{80,144},{96,32},{112,176}... | collective-permute-start | bytes 49160 | tf_op jit(solution)/shard_map/ppermute | solution.py:278
  145.5 4.6 %collective-permute-start.39 = (f32[16,256]{1,0:T(8,128)S(1)}, f32[16,256]{1,0:T(8,128)S(1)}, u32[]{:S(2)}, u32[]{:S(2)}) collective-permute-start(f32[16,256]{1,0:T(8,128)S(1)} %add.185), channel_id=1, source_target_pairs={{0,32},{16,176},{32,0},{48,144},{64,96},{80,240},{96,64},{112,208}... | collective-permute-start | bytes 49160 | tf_op jit(solution)/shard_map/ppermute | solution.py:278
  151.7 5.2 %collective-permute-start.43 = (f32[16,256]{1,0:T(8,128)S(1)}, f32[16,256]{1,0:T(8,128)S(1)}, u32[]{:S(2)}, u32[]{:S(2)}) collective-permute-start(f32[16,256]{1,0:T(8,128)S(1)} %add_add_fusion.2), channel_id=1, source_target_pairs={{0,8},{4,12},{8,0},{12,4},{1,9},{5,13},{9,1},{13,5},{2,10},{6,14},... | collective-permute-start | bytes 49160 | tf_op jit(solution)/shard_map/ppermute | solution.py:280
  157.0 5.0 %collective-permute-start.47 = (f32[16,256]{1,0:T(8,128)S(1)}, f32[16,256]{1,0:T(8,128)S(1)}, u32[]{:S(2)}, u32[]{:S(2)}) collective-permute-start(f32[16,256]{1,0:T(8,128)S(1)} %add_add_fusion.1), channel_id=1, source_target_pairs={{0,3},{1,2},{2,1},{3,0},{4,7},{5,6},{6,5},{7,4},{8,11},{9,10},{10,... | collective-permute-start | bytes 49160 | tf_op jit(solution)/shard_map/ppermute | solution.py:280
  159.2 5.2 %collective-permute-start.46 = (f32[16,256]{1,0:T(8,128)S(1)}, f32[16,256]{1,0:T(8,128)S(1)}, u32[]{:S(2)}, u32[]{:S(2)}) collective-permute-start(f32[16,256]{1,0:T(8,128)S(1)} %add_add_fusion.1), channel_id=1, source_target_pairs={{0,2},{1,3},{2,0},{3,1},{4,6},{5,7},{6,4},{7,5},{8,10},{9,11},{10,... | collective-permute-start | bytes 49160 | tf_op jit(solution)/shard_map/ppermute | solution.py:280
  160.1 4.4 %collective-permute-start.45 = (f32[16,256]{1,0:T(8,128)S(1)}, f32[16,256]{1,0:T(8,128)S(1)}, u32[]{:S(2)}, u32[]{:S(2)}) collective-permute-start(f32[16,256]{1,0:T(8,128)S(1)} %add_add_fusion.1), channel_id=1, source_target_pairs={{0,1},{1,0},{2,3},{3,2},{4,5},{5,4},{6,7},{7,6},{8,9},{9,8},{10,11... | collective-permute-start | bytes 49160 | tf_op jit(solution)/shard_map/ppermute | solution.py:280
  164.5 6.8 %collective-permute-start.48 = (f32[16,256]{1,0:T(8,128)S(1)}, f32[16,256]{1,0:T(8,128)S(1)}, u32[]{:S(2)}, u32[]{:S(2)}) collective-permute-start(f32[16,256]{1,0:T(8,128)S(1)} %add_add_fusion), channel_id=1, source_target_pairs={{0,16},{16,0},{1,17},{17,1},{2,18},{18,2},{3,19},{19,3},{4,20},{20... | collective-permute-start | bytes 49160 | tf_op jit(solution)/shard_map/ppermute | solution.py:271
  (25 other events, 103.7 us)
Sparse Core Ops, SparseCore 0:
  10.5 100.2 all-gather.2
  139.4 41.7 reduce-scatter.1
